TPU v7x, 32 devices: a whole 2x2x4 slice. The times are simulated.
32 devices in a mesh: dp: 8 (over y, x, core), grp: 4 (over z).
Axes of the slice: x: 2, y: 2, z: 4, core: 2. Of those that a mesh axis runs over, the one named last changes fastest.
Arguments:
- activations: bfloat16 [64, 14, 14, 512], P(('dp', 'grp')), may hold values from -6 to 6
- out_grads: bfloat16 [64, 14, 14, 512], P(('dp', 'grp')), may hold values from -60 to 60
- input_basis: bfloat16 [4608, 4608], P('grp'), may hold values from -0.09375 to 0.09375
- output_basis: bfloat16 [512, 512], replicated, may hold values from -0.25 to 0.25
- input_eigen: float32 [4608], P('grp'), may hold values from 0.02 to 2
Outputs:
- update: bfloat16 [4608, 512], P('grp', 'dp')
All inputs are finite; a program needn't handle non-finite values.
Results may differ from a plain program's by a relative error of at most 0.015.
Values may be sent and summed in bfloat16 or wider, within the bound.
No kernel may reach another device: no remote copies, remote signals or barrier semaphores. Data moves between devices by JAX's collectives and lax.ppermute only.
A program may use at most 64 MiB of HBM per device.

v0:
```python
import jax
import jax.numpy as jnp
from jax import lax
from jax.sharding import PartitionSpec as P

damping = 1.0


def unfold(images):
    side = images.shape[1]
    channels = images.shape[3]
    padded = jnp.pad(images, ((0, 0), (1, 1), (1, 1), (0, 0)))
    pieces = [
        padded[:, row : row + side, col : col + side, :] for row in range(3) for col in range(3)
    ]
    return jnp.concatenate(pieces, axis=-1).reshape(-1, 9 * channels)


def rounded(value):
    return lax.optimization_barrier(value.astype(jnp.bfloat16)).astype(jnp.float32)


def on_device(activations, out_grads, input_basis, output_basis, input_eigen):
    channels = output_basis.shape[0]
    side = activations.shape[1]
    local_images = activations.shape[0]
    replicas = lax.axis_size("dp")
    groups = lax.axis_size("grp")
    images_all = local_images * replicas * groups
    contract_rows = (((0,), (0,)), ((), ()))
    flat = out_grads.reshape(-1, channels)
    turned = jnp.dot(flat, output_basis, preferred_element_type=jnp.float32)
    turned_b = turned.astype(jnp.bfloat16)
    moment = rounded(jnp.sum(turned * turned, axis=0))
    patches = unfold(activations)
    term = lax.dot_general(patches, turned_b, contract_rows, preferred_element_type=jnp.float32)
    tiled = jnp.broadcast_to(moment[None, :], (groups, channels))
    group_sum, group_moment = (
        lax.psum_scatter(term.astype(jnp.bfloat16), "grp", scatter_dimension=0, tiled=True).astype(
            jnp.float32
        ),
        lax.psum_scatter(tiled.astype(jnp.bfloat16), "grp", scatter_dimension=0, tiled=True).astype(
            jnp.float32
        ),
    )
    grad_total, moment_rows = lax.psum((group_sum, group_moment), "dp")
    moment_total = moment_rows[0]
    grad_mean = (grad_total / images_all).astype(jnp.bfloat16)
    eigen_out = moment_total / (images_all * side * side)
    width = channels // replicas
    offset = lax.axis_index("dp") * width
    columns = lax.dynamic_slice_in_dim(grad_mean, offset, width, 1)
    rotated = lax.psum_scatter(
        lax.dot_general(
            input_basis, columns, contract_rows, preferred_element_type=jnp.float32
        ).astype(jnp.bfloat16),
        "grp",
        scatter_dimension=0,
        tiled=True,
    ).astype(jnp.float32)
    eigen_cols = lax.dynamic_slice_in_dim(eigen_out, offset, width, 0)
    scaled = (rotated / (input_eigen[:, None] * eigen_cols[None, :] + damping)).astype(jnp.bfloat16)
    back = jnp.dot(
        input_basis,
        lax.all_gather(scaled, "grp", axis=0, tiled=True),
        preferred_element_type=jnp.float32,
    )
    block = back.astype(jnp.bfloat16)
    out_rows = lax.dynamic_slice_in_dim(output_basis, offset, width, 0)
    final = lax.dot_general(
        lax.all_gather(block, "dp", axis=1, tiled=True),
        out_rows,
        (((1,), (1,)), ((), ())),
        preferred_element_type=jnp.float32,
    )
    return final.astype(jnp.bfloat16)


def solution(mesh):
    in_specs = (
        P(("dp", "grp"), None, None, None),
        P(("dp", "grp"), None, None, None),
        P("grp", None),
        P(),
        P("grp"),
    )
    out_specs = P("grp", "dp")
    return jax.shard_map(
        on_device, mesh=mesh, in_specs=in_specs, out_specs=out_specs, check_vma=False
    )
```

profile of v0, /device:TPU:0, one launch (start us, length us, event | category | flops | bytes accessed | tf_op | source)
XLA Modules:
  0.0 271.9 jit_solution(17372503339787427760)
XLA Ops:
  6.5 1.4 slice_dynamic-update-slice_fusion.7
  7.9 1.4 slice_dynamic-update-slice_fusion.6
  9.3 1.4 slice_dynamic-update-slice_fusion.5
  10.7 1.4 slice_dynamic-update-slice_fusion.4
  12.1 1.3 constant_dynamic-update-slice_fusion
  13.5 0.4 slice_dynamic-update-slice_fusion.3
  13.9 0.4 slice_dynamic-update-slice_fusion.2
  14.3 0.4 slice_dynamic-update-slice_fusion.1
  14.7 0.4 slice_dynamic-update-slice_fusion
  15.2 2.6 copy.8
  17.7 6.6 %reshape.12 = bf16[392,4608]{1,0:T(8,128)(2,1)} reshape(bf16[2,14,14,4608]{3,2,1,0:T(8,128)(2,1)} %copy.8) | data formatting | bytes 7225344 | tf_op jit(solution)/shard_map/reshape | solution.py:16
  24.3 0.1 copy.9
  24.4 0.1 reshape.13
  24.5 0.4 multiply_reduce_fusion
  24.9 6.6 %convolution_convert_fusion = bf16[4608,512]{1,0:T(8,128)(2,1)} fusion(bf16[392,4608]{1,0:T(8,128)(2,1)} %reshape.12, bf16[392,512]{1,0:T(8,128)(2,1)S(1)} %get-tuple-element.8), kind=kOutput, calls=%fused_computation | convolution fusion | flops 1852047360 | bytes 8732672 | tf_op jit(solution)/shard_map/dot_general | solution.py:36
  31.5 0.0 reduce-scatter.7.cloned.1.call-start
  31.6 0.6 copy-done.4
  32.1 0.6 dynamic-slice.1
  32.7 13.6 %all-reduce.1 = bf16[4,512]{1,0:T(4,128)(2,1)S(1)} all-reduce(bf16[4,512]{1,0:T(4,128)(2,1)S(1)} %broadcast_in_dim.2), channel_id=4, replica_groups=mesh['dp'=8,'grp'=4] {'grp'}, use_global_device_ids=true, to_apply=%region_4.5.clone | all-reduce | flops 2048 | bytes 8192
  46.4 0.7 dynamic-slice_convert_fusion
  47.0 72.7 %reduce-scatter.5.cloned.1.call-done = bf16[1152,512]{1,0:T(8,128)(2,1)} async-done(((bf16[4608,512]{1,0:T(8,128)(2,1)}), bf16[1152,512]{1,0:T(8,128)(2,1)}) %reduce-scatter.5.cloned.1.call-update) | async-done | bytes 1179664 | tf_op jit(solution)/shard_map/reduce_scatter | solution.py:39
  119.7 58.4 %all-reduce.4 = (f32[1152,512]{1,0:T(8,128)S(1)}, f32[1,512]{1,0:T(1,128)S(1)}) all-reduce(bf16[1152,512]{1,0:T(8,128)(2,1)} %reduce-scatter.5.cloned.1.call-done, f32[1,512]{1,0:T(1,128)S(1)} %dynamic-slice_convert_fusion), channel_id=1, replica_groups=mesh['dp'=8,'grp'=4] {'dp'}, use_global_device_ids=true, to_apply=%region_1.2 | all-reduce | flops 590336 | bytes 3543040 | tf_op jit(solution)/shard_map/psum | solution.py:46
  178.1 6.1 %fusion = bf16[4608,64]{0,1:T(8,128)(2,1)S(1)} fusion(bf16[1152,4608]{1,0:T(8,128)(2,1)} %param.7, f32[1152,512]{1,0:T(8,128)S(1)} %get-tuple-element.5, s32[]{:T(128)S(6)} %select_n.2), kind=kOutput, calls=%fused_computation.2 | convolution fusion | flops 679919616 | bytes 11796484 | tf_op jit(solution)/shard_map/dot_general | solution.py:54
  184.2 1.4 copy.10
  185.6 0.1 fusion.10
  185.7 29.0 %reduce-scatter.7.cloned.1.call-done = bf16[1152,64]{1,0:T(8,128)(2,1)} async-done(((bf16[4608,64]{1,0:T(8,128)(2,1)}), bf16[1152,64]{1,0:T(8,128)(2,1)}) %reduce-scatter.7.cloned.1.call-update) | async-done | bytes 147472
  214.8 1.1 copy.11
  215.9 0.1 divide_convert_fusion
  216.0 16.4 %all_gather.6 = bf16[4608,64]{0,1:T(8,128)(2,1)S(1)} all-gather(bf16[1152,64]{0,1:T(8,128)(2,1)S(1)} %divide_convert_fusion), channel_id=1, replica_groups=mesh['dp'=8,'grp'=4] {'grp'}, dimensions={0}, use_global_device_ids=true | all-gather | bytes 737280 | tf_op jit(solution)/shard_map/all_gather | solution.py:65
  232.4 8.0 %fusion.1 = bf16[1152,64]{0,1:T(8,128)(2,1)} fusion(bf16[4608,64]{0,1:T(8,128)(2,1)S(1)} %all_gather.6, bf16[1152,4608]{1,0:T(8,128)(2,1)} %param.7), kind=kOutput, calls=%fused_computation.5 | convolution fusion | flops 679550976 | bytes 11354112 | tf_op jit(solution)/shard_map/dot_general | solution.py:63
  240.4 22.7 %all-gather.2.cloned.1.call-done = bf16[1152,512]{0,1:T(8,128)(2,1)} async-done(((bf16[1152,64]{0,1:T(8,128)(2,1)}), bf16[1152,512]{0,1:T(8,128)(2,1)}) %all-gather.2.cloned.1.call-update) | async-done | bytes 1179664 | tf_op jit(solution)/shard_map/all_gather | solution.py:71
  263.1 2.3 convolution_convert_fusion.3
  (15 shorter events, 0.1 us)
Async XLA Ops:
  6.5 18.0 %copy-start = (bf16[512,512]{1,0:T(8,128)(2,1)S(1)}, bf16[512,512]{1,0:T(8,128)(2,1)}, u32[]{:S(2)}) copy-start(bf16[512,512]{1,0:T(8,128)(2,1)} %param.8) | copy-start | bytes 1572868
  6.5 7.0 %copy-start.1 = (bf16[2,14,14,512]{3,0,2,1:T(2,128)(2,1)S(1)}, bf16[2,14,14,512]{3,0,2,1:T(2,128)(2,1)}, u32[]{:S(2)}) copy-start(bf16[2,14,14,512]{3,0,2,1:T(2,128)(2,1)} %param.5) | copy-start | bytes 1204228
  6.5 113.2 %reduce-scatter.5.cloned.1.call-start = ((), (), s32[]{:S(2)}) async-start(), calls=%async_computation.2 | async-start | bytes 5898240 | tf_op jit(solution)/shard_map/reduce_scatter | solution.py:39
  17.7 6.6 %copy-start.2 = (bf16[2,14,14,512]{3,0,2,1:T(2,128)(2,1)S(1)}, bf16[2,14,14,512]{3,0,2,1:T(2,128)(2,1)}, u32[]{:S(2)}) copy-start(bf16[2,14,14,512]{3,0,2,1:T(2,128)(2,1)} %param.6) | copy-start | bytes 1204228
  31.5 0.7 copy-start.4
  31.5 183.3 %reduce-scatter.7.cloned.1.call-start = ((), (), s32[]{:S(2)}) async-start(), calls=%async_computation.4 | async-start | bytes 1474560
  178.1 37.8 %copy-start.3 = (f32[1152]{0:T(1024)S(1)}, f32[1152]{0:T(1024)}, u32[]{:S(2)}) copy-start(f32[1152]{0:T(1024)} %param.9) | copy-start | bytes 13828
  185.6 77.5 %all-gather.2.cloned.1.call-start = ((), (), s32[]{:S(2)}) async-start(), calls=%async_computation.3 | async-start | bytes 1327104 | tf_op jit(solution)/shard_map/all_gather | solution.py:71
Sparse Core Ops, SparseCore 0:
  31.6 88.0 reduce-scatter.4
  185.7 28.9 reduce-scatter.6
  240.6 22.4 all-gather.1
where the time goes:
time: 273 us; the launch traced here: 272 us
  waiting for transfers between devices  124 us (45%)
  blocking collectives  88.4 us (32%)
  matrix products  23.3 us (9%)
  local copies, waits for them, and re-layouts  21.6 us (8%)
  between operations  13.2 us (5%)
    reduce_scatter x1, waiting for transfers between devices, on_device(): lax.psum_scatter(term.astype(jnp.bfloat16), 'grp', scatter_dimension=0, t...  72.7 us
    psum x1, blocking collectives, on_device(): grad_total, moment_rows = lax.psum((group_sum, group_moment), 'dp')  58.4 us
    unnamed x4, waiting for transfers between devices  29.1 us
    all_gather x1, waiting for transfers between devices, on_device(): lax.all_gather(block, 'dp', axis=1, tiled=True)  22.7 us
    all_gather x1, blocking collectives, on_device(): lax.all_gather(scaled, 'grp', axis=0, tiled=True)  16.4 us
    unnamed x1, blocking collectives  13.6 us
    unnamed x22, local copies, waits for them, and re-layouts  11.9 us
    dot_general x1, matrix products, on_device(): jnp.dot(input_basis, lax.all_gather(scaled, 'grp', axis=0, tiled=True), p...  7.99 us
  transfers between devices with their start and end apart: 3, of which 3 were waited for; matrix products, arithmetic and copies ran while one was open for 0% of the time, Pallas kernels for 0%

commit v1 on v0

--- a/solution.py
+++ b/solution.py
@@ -1,9 +1,15 @@
+import functools
+
 import jax
 import jax.numpy as jnp
 from jax import lax
+from jax.experimental import pallas as pl
+from jax.experimental.pallas import tpu as pltpu
 from jax.sharding import PartitionSpec as P
 
 damping = 1.0
+BF = jnp.bfloat16
+F32 = jnp.float32
 
 
 def unfold(images):
@@ -20,7 +26,7 @@
     return lax.optimization_barrier(value.astype(jnp.bfloat16)).astype(jnp.float32)
 
 
-def on_device(activations, out_grads, input_basis, output_basis, input_eigen):
+def any_mesh(activations, out_grads, input_basis, output_basis, input_eigen):
     channels = output_basis.shape[0]
     side = activations.shape[1]
     local_images = activations.shape[0]
@@ -76,6 +82,152 @@
     return final.astype(jnp.bfloat16)
 
 
+def swap(value, bit):
+    return lax.ppermute(value, "dp", [(i, i ^ bit) for i in range(lax.axis_size("dp"))])
+
+
+def shift(value, step):
+    n = lax.axis_size("grp")
+    return lax.ppermute(value, "grp", [(i, (i + step) % n) for i in range(n)])
+
+
+def grad_kernel(act_a, act_b, dout_a, dout_b, basis_t, s_a, k_a, s_b, k_b, acts, turned, lhs):
+    step = pl.program_id(0)
+    rows = act_a.shape[0]
+
+    @pl.when(step == 0)
+    def _():
+        me = lax.axis_index("dp")
+        half = basis_t.shape[0] // 2
+        sub = half // 8
+        quarter = me >> 1
+        base = (me & 1) * half
+        order = [(0, 1), (0, 3), (0, 0), (0, 2), (1, 2), (1, 3), (1, 0), (1, 1)]
+        for at, (chunk, flip) in enumerate(order):
+            start = pl.multiple_of(base + (quarter ^ flip) * 2 * sub + chunk * sub, sub)
+            turned[at * sub : (at + 1) * sub, :] = basis_t[pl.ds(start, sub), :]
+        acts[0:16, :] = jnp.zeros((16, acts.shape[1]), BF)
+        acts[16 + 2 * rows :, :] = jnp.zeros((16, acts.shape[1]), BF)
+        acts[16 : 16 + rows, :] = act_a[...]
+        acts[16 + rows : 16 + 2 * rows, :] = act_b[...]
+        own = turned[...]
+        for at, ref in enumerate((dout_a, dout_b)):
+            part = lax.dot_general(
+                own, ref[...], (((1,), (1,)), ((), ())), preferred_element_type=F32
+            )
+            for tap, turn in enumerate((rows - 1, 0, 1)):
+                moved = pltpu.roll(part, turn, 1) if turn else part
+                lhs[tap * half : (tap + 1) * half, at * rows : (at + 1) * rows] = moved.astype(BF)
+
+    window = acts[pl.ds(pl.multiple_of(16 * step, 16), 2 * rows), :]
+    out = jnp.dot(lhs[...], window, preferred_element_type=F32)
+    channels = window.shape[1]
+    quarter_rows = s_a.shape[0]
+    for tap in range(3):
+        for at, ref in enumerate((s_a, k_a, s_b, k_b)):
+            start = tap * 4 * quarter_rows + at * quarter_rows
+            ref[:, tap * channels : (tap + 1) * channels] = out[
+                start : start + quarter_rows, :
+            ].astype(BF)
+
+
+def grad_parts(act_a, act_b, dout_a, dout_b, basis_t):
+    rows, channels = act_a.shape
+    sub = channels // 8
+    whole = lambda shape: pl.BlockSpec(shape, lambda i: (0,) * len(shape))
+    piece = jax.ShapeDtypeStruct((sub, 9 * channels), BF)
+    return pl.pallas_call(
+        grad_kernel,
+        grid=(3,),
+        in_specs=[whole((rows, channels))] * 4 + [whole(basis_t.shape)],
+        out_specs=[pl.BlockSpec((sub, 3 * channels), lambda i: (0, i))] * 4,
+        out_shape=[piece] * 4,
+        scratch_shapes=[
+            pltpu.VMEM((2 * rows + 32, channels), BF),
+            pltpu.VMEM((channels // 2, channels), BF),
+            pltpu.VMEM((3 * channels // 2, 2 * rows), BF),
+        ],
+        compiler_params=pltpu.CompilerParams(
+            dimension_semantics=("arbitrary",), vmem_limit_bytes=40 << 20
+        ),
+        cost_estimate=pl.CostEstimate(
+            flops=2 * 9 * channels * channels * rows,
+            bytes_accessed=4 * rows * channels * 2 + 9 * channels * channels,
+            transcendentals=0,
+        ),
+    )(act_a, act_b, dout_a, dout_b, basis_t)
+
+
+def padded_rows(images):
+    n, h, w, c = images.shape
+    return jnp.pad(images, ((0, 0), (0, 16 - h), (0, 16 - w), (0, 0))).reshape(n * 256, c)
+
+
+def spread(value, width):
+    n = lax.axis_size("grp")
+    me = lax.axis_index("grp")
+    total = lax.dynamic_slice_in_dim(value, me * width, width, 1).astype(F32)
+    for step in range(1, n):
+        piece = lax.dynamic_slice_in_dim(value, lax.rem(me + step, n) * width, width, 1)
+        total = total + shift(piece.astype(BF), step).astype(F32)
+    return total
+
+
+def cube(activations, out_grads, input_basis, output_basis, input_eigen):
+    channels = output_basis.shape[0]
+    local_images, side = activations.shape[:2]
+    images_all = local_images * lax.axis_size("dp") * lax.axis_size("grp")
+    groups = lax.axis_size("grp")
+    me = lax.axis_index("dp")
+    width = channels // 8
+    own_rows = input_eigen.shape[0]
+    block = (me & 1) * 4 + (me >> 1)
+
+    flat = out_grads.reshape(-1, channels)
+    turned = jnp.dot(flat, output_basis, preferred_element_type=F32)
+    moment = rounded(jnp.sum(turned * turned, axis=0))
+    for bit in (1, 2, 4):
+        moment = moment + swap(moment, bit)
+    parts = [moment] + [shift(moment, step) for step in range(1, groups)]
+    eigen_out = sum(parts) / (images_all * side * side)
+    eigen_cols = lax.dynamic_slice_in_dim(eigen_out, block * width, width, 0)
+
+    acts = padded_rows(activations)
+    douts = padded_rows(out_grads)
+    s_a, k_a, s_b, k_b = grad_parts(acts, swap(acts, 1), douts, swap(douts, 1), output_basis.T)
+    half = width // 2
+    r_a, r_b = swap(s_a, 2), swap(s_b, 4)
+    sum_a, sum_b = k_a.astype(F32) + r_a.astype(F32), k_b.astype(F32) + r_b.astype(F32)
+    r_a = swap(sum_a[half:].astype(BF), 4)
+    r_b = swap(sum_b[half:].astype(BF), 2)
+    total = jnp.concatenate([sum_a[:half] + r_a.astype(F32), sum_b[:half] + r_b.astype(F32)], 0)
+    grad_mean = (spread(total, own_rows) / images_all).astype(BF)
+
+    rotated = spread(jnp.dot(grad_mean, input_basis, preferred_element_type=F32).astype(BF), own_rows)
+    scaled = (rotated / (input_eigen[None, :] * eigen_cols[:, None] + damping)).astype(BF)
+
+    near = jnp.concatenate([scaled] + [swap(scaled, bit) for bit in (2, 4, 6)], 0)
+    pieces = [
+        lax.dynamic_slice_in_dim(output_basis, (block ^ flip) * width, width, 1)
+        for flip in range(4)
+    ]
+    mine = jnp.concatenate(pieces, 1)
+    rows_of = lambda r: lax.dynamic_slice_in_dim(mine, r * width, width, 0)
+    both = jnp.concatenate([rows_of(me), rows_of(me ^ 1)], 0)
+    turned_back = jnp.dot(both, near, preferred_element_type=F32)
+    own = (turned_back[:width] + swap(turned_back[width:], 1)).astype(BF)
+
+    grp = lax.axis_index("grp")
+    update = None
+    for step in range(groups):
+        held = own if step == 0 else shift(own, step)
+        at = lax.rem(grp - step + groups, groups) * own_rows
+        basis = lax.dynamic_slice_in_dim(input_basis, at, own_rows, 1)
+        part = lax.dot_general(held, basis, (((1,), (1,)), ((), ())), preferred_element_type=F32)
+        update = part if update is None else update + part
+    return update.astype(BF).T
+
+
 def solution(mesh):
     in_specs = (
         P(("dp", "grp"), None, None, None),
@@ -85,6 +237,5 @@
         P("grp"),
     )
     out_specs = P("grp", "dp")
-    return jax.shard_map(
-        on_device, mesh=mesh, in_specs=in_specs, out_specs=out_specs, check_vma=False
-    )
+    plan = cube if mesh.shape["dp"] == 8 else any_mesh
+    return jax.shard_map(plan, mesh=mesh, in_specs=in_specs, out_specs=out_specs, check_vma=False)

time: 273 us -> 113 us (0.41)
  blocking collectives: 88.4 us -> 0 us
  waiting for transfers between devices: 124 us -> 50.7 us
  starting transfers between devices: 0.09 us -> 28.6 us
  local copies, waits for them, and re-layouts: 21.6 us -> 8.45 us
  between operations: 13.2 us -> 0.23 us
  Pallas kernels: 0 us -> 4.38 us
  matrix products: 23.3 us -> 19 us
    reduce_scatter x1 -> x0, waiting for transfers between devices: 72.7 us -> none  [on_device(): lax.psum_scatter(term.astype(jnp.bfloat16), 'grp', scatter_dimension=0, t...]
    psum x1 -> x0, blocking collectives: 58.4 us -> none  [on_device(): grad_total, moment_rows = lax.psum((group_sum, group_moment), 'dp')]
    ppermute x0 -> x25, waiting for transfers between devices: none -> 50.7 us  [the longest x13 31.7 us: swap(): lax.ppermute(value, 'dp', [(i, i ^ bit) for i in range(lax.axis_size('dp'...]
    unnamed x4 -> x0, waiting for transfers between devices: 29.1 us -> none
    ppermute x0 -> x25, starting transfers between devices: none -> 28.6 us  [the longest x12 15.9 us: shift(): return lax.ppermute(value, 'grp', [(i, (i + step) % n) for i in range(n)])]
    all_gather x1 -> x0, waiting for transfers between devices: 22.7 us -> none  [on_device(): lax.all_gather(block, 'dp', axis=1, tiled=True)]
    all_gather x1 -> x0, blocking collectives: 16.4 us -> none  [on_device(): lax.all_gather(scaled, 'grp', axis=0, tiled=True)]
    unnamed x1 -> x0, blocking collectives: 13.6 us -> none
  transfers between devices with their start and end apart: 3 -> 25, of which waited for: 3 -> 16; matrix products, arithmetic and copies ran while one was open for 0% -> 14% of each run, Pallas kernels for 0% -> 0%
where the time goes in v1:
time: 113 us; the launch traced here: 112 us
  waiting for transfers between devices  50.7 us (45%)
  starting transfers between devices  28.6 us (25%)
  matrix products  19 us (17%)
  local copies, waits for them, and re-layouts  8.45 us (7%)
  Pallas kernels  4.38 us (4%)
    ppermute x13, waiting for transfers between devices, swap(): lax.ppermute(value, 'dp', [(i, i ^ bit) for i in range(lax.axis_size('dp'...  31.7 us
    ppermute x12, waiting for transfers between devices, shift(): return lax.ppermute(value, 'grp', [(i, (i + step) % n) for i in range(n)])  19 us
    ppermute x12, starting transfers between devices, shift(): return lax.ppermute(value, 'grp', [(i, (i + step) % n) for i in range(n)])  15.9 us
    ppermute x13, starting transfers between devices, swap(): lax.ppermute(value, 'dp', [(i, i ^ bit) for i in range(lax.axis_size('dp'...  12.7 us
    dot_general x4, matrix products, cube(): lax.dot_general(held, basis, (((1,), (1,)), ((), ())), preferred_element_...  11.4 us
    unnamed x19, local copies, waits for them, and re-layouts  6.79 us
    dot_general x1, matrix products, cube(): jnp.dot(grad_mean, input_basis, preferred_element_type=F32).astype(BF)  5.97 us
    pallas_call x1, Pallas kernels, grad_parts(): pl.pallas_call(grad_kernel, grid=(3,), in_specs=[whole((rows, channels))]...  4.38 us
  transfers between devices with their start and end apart: 25, of which 16 were waited for; matrix products, arithmetic and copies ran while one was open for 14% of the time, Pallas kernels for 0%

profile of v1, /device:TPU:0, one launch (start us, length us, event | category | flops | bytes accessed | tf_op | source)
XLA Modules:
  0.0 112.2 jit_solution(11074889453627842477)
XLA Ops:
  8.4 4.4 %shard_map.55 = (bf16[64,4608]{1,0:T(8,128)(2,1)}, bf16[64,4608]{1,0:T(8,128)(2,1)S(1)}, bf16[64,4608]{1,0:T(8,128)(2,1)S(1)}, bf16[64,4608]{1,0:T(8,128)(2,1)S(1)}) custom-call(bf16[512,512]{1,0:T(8,128)(2,1)S(1)} %bitcast.11, bf16[512,512]{1,0:T(8,128)(2,1)S(1)} %copy-done.1, bf16[512,512]{1,0:T(8,128)(2,1)S(1)} %bitcast.13, ...), custom_call_target="tpu_custom_call" | custom-call | flops 2415919104 | bytes 4456448 | tf_op jit(solution)/shard_map/pallas_call | solution.py:139
  12.7 2.6 %collective-permute-start.2 = (bf16[64,4608]{1,0:T(8,128)(2,1)}, bf16[64,4608]{1,0:T(8,128)(2,1)S(1)}, u32[]{:S(2)}, u32[]{:S(2)}) collective-permute-start(bf16[64,4608]{1,0:T(8,128)(2,1)} %get-tuple-element.10), channel_id=1, source_target_pairs={{0,8},{4,12},{8,0},{12,4},{16,24},{20,28},{24,16},{28,20},{1,9},{5... | collective-permute-start | bytes 1769480 | tf_op jit(solution)/shard_map/ppermute | solution.py:86
  16.5 1.4 %fusion.20 = bf16[512]{0:T(512)(128)(2,1)S(1)} fusion(bf16[392,512]{1,0:T(8,128)(2,1)S(1)} %reshape.13, bf16[512,512]{1,0:T(8,128)(2,1)} %param.8), kind=kOutput, calls=%fused_computation.22 | convolution fusion | flops 205921792 | bytes 926720 | tf_op jit(solution)/shard_map/dot_general | solution.py:187
  18.1 1.5 %collective-permute-start.4 = (bf16[64,4608]{1,0:T(8,128)(2,1)S(1)}, bf16[64,4608]{1,0:T(8,128)(2,1)S(1)}, u32[]{:S(2)}, u32[]{:S(2)}) collective-permute-start(bf16[64,4608]{1,0:T(8,128)(2,1)S(1)} %get-tuple-element.12), channel_id=1, source_target_pairs={{0,16},{4,20},{8,24},{12,28},{16,0},{20,4},{24,8},{28,12},{1,17},{... | collective-permute-start | bytes 1769480 | tf_op jit(solution)/shard_map/ppermute | solution.py:86
  19.6 9.8 %collective-permute-done.2 = bf16[64,4608]{1,0:T(8,128)(2,1)S(1)} collective-permute-done((bf16[64,4608]{1,0:T(8,128)(2,1)}, bf16[64,4608]{1,0:T(8,128)(2,1)S(1)}, u32[]{:S(2)}, u32[]{:S(2)}) %collective-permute-start.2) | collective-permute-done | bytes 589856 | tf_op jit(solution)/shard_map/ppermute | solution.py:86
  29.6 1.8 %collective-permute-start.3 = (bf16[32,4608]{1,0:T(8,128)(2,1)S(1)}, bf16[32,4608]{1,0:T(8,128)(2,1)S(1)}, u32[]{:S(2)}, u32[]{:S(2)}) collective-permute-start(bf16[32,4608]{1,0:T(8,128)(2,1)S(1)} %slice.40), channel_id=1, source_target_pairs={{0,16},{4,20},{8,24},{12,28},{16,0},{20,4},{24,8},{28,12},{1,17},{... | collective-permute-start | bytes 884744 | tf_op jit(solution)/shard_map/ppermute | solution.py:86
  31.4 2.8 %collective-permute-done.4 = bf16[64,4608]{1,0:T(8,128)(2,1)S(1)} collective-permute-done((bf16[64,4608]{1,0:T(8,128)(2,1)S(1)}, bf16[64,4608]{1,0:T(8,128)(2,1)S(1)}, u32[]{:S(2)}, u32[]{:S(2)}) %collective-permute-start.4) | collective-permute-done | bytes 589856 | tf_op jit(solution)/shard_map/ppermute | solution.py:86
  34.7 5.4 %collective-permute-done.3 = bf16[32,4608]{1,0:T(8,128)(2,1)S(1)} collective-permute-done((bf16[32,4608]{1,0:T(8,128)(2,1)S(1)}, bf16[32,4608]{1,0:T(8,128)(2,1)S(1)}, u32[]{:S(2)}, u32[]{:S(2)}) %collective-permute-start.3) | collective-permute-done | bytes 294944 | tf_op jit(solution)/shard_map/ppermute | solution.py:86
  40.2 2.4 %collective-permute-done.5 = bf16[32,4608]{1,0:T(8,128)(2,1)S(1)} collective-permute-done((bf16[32,4608]{1,0:T(8,128)(2,1)S(1)}, bf16[32,4608]{1,0:T(8,128)(2,1)S(1)}, u32[]{:S(2)}, u32[]{:S(2)}) %collective-permute-start.5) | collective-permute-done | bytes 294944 | tf_op jit(solution)/shard_map/ppermute | solution.py:86
  42.7 1.6 %collective-permute-start.6 = (bf16[64,1152]{1,0:T(8,128)(2,1)S(1)}, bf16[64,1152]{1,0:T(8,128)(2,1)S(1)}, u32[]{:S(2)}, u32[]{:S(2)}) collective-permute-start(bf16[64,1152]{1,0:T(8,128)(2,1)S(1)} %get-tuple-element.13), channel_id=1, source_target_pairs={{0,1},{1,2},{2,3},{3,0},{4,5},{5,6},{6,7},{7,4},{8,9},{9,10},{10,1... | collective-permute-start | bytes 442376 | tf_op jit(solution)/shard_map/ppermute | solution.py:91
  44.3 2.6 %collective-permute-start.7 = (bf16[64,1152]{1,0:T(8,128)(2,1)S(1)}, bf16[64,1152]{1,0:T(8,128)(2,1)S(1)}, u32[]{:S(2)}, u32[]{:S(2)}) collective-permute-start(bf16[64,1152]{1,0:T(8,128)(2,1)S(1)} %get-tuple-element.14), channel_id=1, source_target_pairs={{0,2},{1,3},{2,0},{3,1},{4,6},{5,7},{6,4},{7,5},{8,10},{9,11},{10,... | collective-permute-start | bytes 442376 | tf_op jit(solution)/shard_map/ppermute | solution.py:91
  48.8 3.0 %collective-permute-done.13 = f32[512]{0:T(512)S(1)} collective-permute-done((f32[512]{0:T(512)S(1)}, f32[512]{0:T(512)S(1)}, u32[]{:S(2)}, u32[]{:S(2)}) %collective-permute-start.13) | collective-permute-done | bytes 2080 | tf_op jit(solution)/shard_map/ppermute | solution.py:86
  51.9 1.5 %collective-permute-start.14 = (f32[512]{0:T(512)S(1)}, f32[512]{0:T(512)S(1)}, u32[]{:S(2)}, u32[]{:S(2)}) collective-permute-start(f32[512]{0:T(512)S(1)} %add.171), channel_id=1, source_target_pairs={{0,16},{4,20},{8,24},{12,28},{16,0},{20,4},{24,8},{28,12},{1,17},{... | collective-permute-start | bytes 6152 | tf_op jit(solution)/shard_map/ppermute | solution.py:86
  53.6 1.8 %collective-permute-done.14 = f32[512]{0:T(512)S(1)} collective-permute-done((f32[512]{0:T(512)S(1)}, f32[512]{0:T(512)S(1)}, u32[]{:S(2)}, u32[]{:S(2)}) %collective-permute-start.14) | collective-permute-done | bytes 2080 | tf_op jit(solution)/shard_map/ppermute | solution.py:86
  55.9 1.7 %collective-permute-start.16 = (f32[512]{0:T(512)S(1)}, f32[512]{0:T(512)S(1)}, u32[]{:S(2)}, u32[]{:S(2)}) collective-permute-start(f32[512]{0:T(512)S(1)} %add.172), channel_id=1, source_target_pairs={{0,2},{1,3},{2,0},{3,1},{4,6},{5,7},{6,4},{7,5},{8,10},{9,11},{10,... | collective-permute-start | bytes 6152 | tf_op jit(solution)/shard_map/ppermute | solution.py:91
  57.8 6.0 %convolution_convert_fusion = bf16[64,4608]{1,0:T(8,128)(2,1)S(1)} fusion(bf16[1152,4608]{1,0:T(8,128)(2,1)} %param.7, s32[]{:T(128)S(6)} %select_n.48, f32[32,4608]{1,0:T(8,128)S(1)} %slice_add_fusion.1, f32[32,4608]{1,0:T(8,128)S(1)} %slice_add_fusion, bf16[64,1152]{1,0:T(8,128)(2,1)S(1)} %collective-permute-done.8, ...), kind=kOutput, calls=%fused_computation | convolution fusion | flops 680435712 | bytes 12828676 | tf_op jit(solution)/shard_map/dot_general | solution.py:206
  63.9 1.6 %collective-permute-start.9 = (bf16[64,1152]{1,0:T(8,128)(2,1)S(1)}, bf16[64,1152]{1,0:T(8,128)(2,1)S(1)}, u32[]{:S(2)}, u32[]{:S(2)}) collective-permute-start(bf16[64,1152]{1,0:T(8,128)(2,1)S(1)} %get-tuple-element.16), channel_id=1, source_target_pairs={{0,1},{1,2},{2,3},{3,0},{4,5},{5,6},{6,7},{7,4},{8,9},{9,10},{10,1... | collective-permute-start | bytes 442376 | tf_op jit(solution)/shard_map/ppermute | solution.py:91
  65.5 2.2 %collective-permute-start.11 = (bf16[64,1152]{1,0:T(8,128)(2,1)S(1)}, bf16[64,1152]{1,0:T(8,128)(2,1)S(1)}, u32[]{:S(2)}, u32[]{:S(2)}) collective-permute-start(bf16[64,1152]{1,0:T(8,128)(2,1)S(1)} %get-tuple-element.17), channel_id=1, source_target_pairs={{0,3},{1,0},{2,1},{3,2},{4,7},{5,4},{6,5},{7,6},{8,11},{9,8},{10,9... | collective-permute-start | bytes 442376 | tf_op jit(solution)/shard_map/ppermute | solution.py:91
  68.6 3.9 %collective-permute-done.9 = bf16[64,1152]{1,0:T(8,128)(2,1)S(1)} collective-permute-done((bf16[64,1152]{1,0:T(8,128)(2,1)S(1)}, bf16[64,1152]{1,0:T(8,128)(2,1)S(1)}, u32[]{:S(2)}, u32[]{:S(2)}) %collective-permute-start.9) | collective-permute-done | bytes 147488 | tf_op jit(solution)/shard_map/ppermute | solution.py:91
  72.9 5.2 %collective-permute-done.10 = bf16[64,1152]{1,0:T(8,128)(2,1)S(1)} collective-permute-done((bf16[64,1152]{1,0:T(8,128)(2,1)S(1)}, bf16[64,1152]{1,0:T(8,128)(2,1)S(1)}, u32[]{:S(2)}, u32[]{:S(2)}) %collective-permute-start.10) | collective-permute-done | bytes 147488 | tf_op jit(solution)/shard_map/ppermute | solution.py:91
  78.2 1.6 %collective-permute-start.20 = (bf16[64,1152]{1,0:T(8,128)(2,1)S(1)}, bf16[64,1152]{1,0:T(8,128)(2,1)S(1)}, u32[]{:S(2)}, u32[]{:S(2)}) collective-permute-start(bf16[64,1152]{1,0:T(8,128)(2,1)S(1)} %divide_convert_fusion), channel_id=1, source_target_pairs={{0,24},{4,28},{8,16},{12,20},{16,8},{20,12},{24,0},{28,4},{1,25},{... | collective-permute-start | bytes 442376 | tf_op jit(solution)/shard_map/ppermute | solution.py:86
  80.3 1.5 %collective-permute-start.18 = (bf16[64,1152]{1,0:T(8,128)(2,1)S(1)}, bf16[64,1152]{1,0:T(8,128)(2,1)S(1)}, u32[]{:S(2)}, u32[]{:S(2)}) collective-permute-start(bf16[64,1152]{1,0:T(8,128)(2,1)S(1)} %divide_convert_fusion), channel_id=1, source_target_pairs={{0,8},{4,12},{8,0},{12,4},{16,24},{20,28},{24,16},{28,20},{1,9},{5... | collective-permute-start | bytes 442376 | tf_op jit(solution)/shard_map/ppermute | solution.py:86
  82.0 2.4 %collective-permute-done.20 = bf16[64,1152]{1,0:T(8,128)(2,1)S(1)} collective-permute-done((bf16[64,1152]{1,0:T(8,128)(2,1)S(1)}, bf16[64,1152]{1,0:T(8,128)(2,1)S(1)}, u32[]{:S(2)}, u32[]{:S(2)}) %collective-permute-start.20) | collective-permute-done | bytes 147488 | tf_op jit(solution)/shard_map/ppermute | solution.py:86
  84.5 1.5 %collective-permute-done.19 = bf16[64,1152]{1,0:T(8,128)(2,1)S(1)} collective-permute-done((bf16[64,1152]{1,0:T(8,128)(2,1)S(1)}, bf16[64,1152]{1,0:T(8,128)(2,1)S(1)}, u32[]{:S(2)}, u32[]{:S(2)}) %collective-permute-start.19) | collective-permute-done | bytes 147488 | tf_op jit(solution)/shard_map/ppermute | solution.py:86
  86.4 1.6 %collective-permute-done.21 = f32[64,1152]{1,0:T(8,128)S(1)} collective-permute-done((f32[64,1152]{1,0:T(8,128)S(1)}, f32[64,1152]{1,0:T(8,128)S(1)}, u32[]{:S(2)}, u32[]{:S(2)}) %collective-permute-start.21) | collective-permute-done | bytes 294944 | tf_op jit(solution)/shard_map/ppermute | solution.py:86
  88.0 2.7 %collective-permute-start.24 = (bf16[64,1152]{1,0:T(8,128)(2,1)S(1)}, bf16[64,1152]{1,0:T(8,128)(2,1)S(1)}, u32[]{:S(2)}, u32[]{:S(2)}) collective-permute-start(bf16[64,1152]{1,0:T(8,128)(2,1)S(1)} %fusion.41), channel_id=1, source_target_pairs={{0,3},{1,0},{2,1},{3,2},{4,7},{5,4},{6,5},{7,6},{8,11},{9,8},{10,9... | collective-permute-start | bytes 442376 | tf_op jit(solution)/shard_map/ppermute | solution.py:91
  91.3 3.6 %collective-permute-done.24 = bf16[64,1152]{1,0:T(8,128)(2,1)S(1)} collective-permute-done((bf16[64,1152]{1,0:T(8,128)(2,1)S(1)}, bf16[64,1152]{1,0:T(8,128)(2,1)S(1)}, u32[]{:S(2)}, u32[]{:S(2)}) %collective-permute-start.24) | collective-permute-done | bytes 147488 | tf_op jit(solution)/shard_map/ppermute | solution.py:91
  95.0 2.7 %fusion = f32[1152,64]{0,1:T(8,128)S(1)} fusion(bf16[64,1152]{1,0:T(8,128)(2,1)S(1)} %collective-permute-done.24, bf16[1152,4608]{1,0:T(8,128)(2,1)} %param.7, s32[]{:T(128)S(6)} %select_n.49), kind=kOutput, calls=%fused_computation.1 | convolution fusion | flops 169869312 | bytes 3096580 | tf_op jit(solution)/shard_map/dot_general | solution.py:226
  97.6 5.9 %collective-permute-done.23 = bf16[64,1152]{1,0:T(8,128)(2,1)S(1)} collective-permute-done((bf16[64,1152]{1,0:T(8,128)(2,1)S(1)}, bf16[64,1152]{1,0:T(8,128)(2,1)S(1)}, u32[]{:S(2)}, u32[]{:S(2)}) %collective-permute-start.23) | collective-permute-done | bytes 147488 | tf_op jit(solution)/shard_map/ppermute | solution.py:91
  103.5 2.7 %fusion.2 = f32[1152,64]{0,1:T(8,128)S(1)} fusion(bf16[64,1152]{1,0:T(8,128)(2,1)S(1)} %collective-permute-done.23, bf16[1152,4608]{1,0:T(8,128)(2,1)} %param.7, s32[]{:T(128)S(6)} %select_n.50), kind=kOutput, calls=%fused_computation.3 | convolution fusion | flops 169869312 | bytes 3096580 | tf_op jit(solution)/shard_map/dot_general | solution.py:226
  106.2 2.7 %fusion.4 = f32[1152,64]{0,1:T(8,128)S(1)} fusion(bf16[64,1152]{1,0:T(8,128)(2,1)S(1)} %collective-permute-done.22, bf16[1152,4608]{1,0:T(8,128)(2,1)} %param.7, s32[]{:T(128)S(6)} %select_n.51), kind=kOutput, calls=%fused_computation.5 | convolution fusion | flops 169869312 | bytes 3096580 | tf_op jit(solution)/shard_map/dot_general | solution.py:226
  108.8 3.4 %fusion.17 = bf16[1152,64]{0,1:T(8,128)(2,1)} fusion(f32[1152,64]{0,1:T(8,128)S(1)} %fusion, f32[1152,64]{0,1:T(8,128)S(1)} %fusion.2, f32[1152,64]{0,1:T(8,128)S(1)} %fusion.4, bf16[64,1152]{1,0:T(8,128)(2,1)S(1)} %fusion.41, bf16[1152,4608]{1,0:T(8,128)(2,1)} %param.7, s32[]{:T(128)S(6)} %select_n.41), kind=kOutput, calls=%fused_computation.12 | convolution fusion | flops 170164224 | bytes 3833860 | tf_op jit(solution)/shard_map/dot_general | solution.py:226
  (68 shorter events, 16.4 us)
Async XLA Ops:
  0.0 3.6 %copy-start.5 = (bf16[512,512]{1,0:T(8,128)(2,1)S(1)}, bf16[512,512]{1,0:T(8,128)(2,1)}, u32[]{:S(2)}) copy-start(bf16[512,512]{1,0:T(8,128)(2,1)} %param.8) | copy-start | bytes 1572868
  1.2 2.7 %collective-permute-start = (bf16[512,512]{1,0:T(8,128)(2,1)S(1)}, bf16[512,512]{1,0:T(8,128)(2,1)S(1)}, u32[]{:S(2)}, u32[]{:S(2)}) collective-permute-start(bf16[512,512]{1,0:T(8,128)(2,1)S(1)} %bitcast.10), channel_id=1, source_target_pairs={{0,4},{4,0},{8,12},{12,8},{16,20},{20,16},{24,28},{28,24},{1,5},{5... | collective-permute-start | bytes 1572872 | tf_op jit(solution)/shard_map/ppermute | solution.py:86
  2.8 0.8 copy-start.4
  3.6 1.9 %collective-permute-start.1 = (bf16[512,512]{1,0:T(8,128)(2,1)S(1)}, bf16[512,512]{1,0:T(8,128)(2,1)S(1)}, u32[]{:S(2)}, u32[]{:S(2)}) collective-permute-start(bf16[512,512]{1,0:T(8,128)(2,1)S(1)} %bitcast.12), channel_id=1, source_target_pairs={{0,4},{4,0},{8,12},{12,8},{16,20},{20,16},{24,28},{28,24},{1,5},{5... | collective-permute-start | bytes 1572872 | tf_op jit(solution)/shard_map/ppermute | solution.py:86
  5.5 0.8 copy-start.2
  6.3 1.0 copy-start.1
  7.3 1.0 copy-start.3
  12.7 16.7 %collective-permute-start.2 = (bf16[64,4608]{1,0:T(8,128)(2,1)}, bf16[64,4608]{1,0:T(8,128)(2,1)S(1)}, u32[]{:S(2)}, u32[]{:S(2)}) collective-permute-start(bf16[64,4608]{1,0:T(8,128)(2,1)} %get-tuple-element.10), channel_id=1, source_target_pairs={{0,8},{4,12},{8,0},{12,4},{16,24},{20,28},{24,16},{28,20},{1,9},{5... | collective-permute-start | bytes 1769480 | tf_op jit(solution)/shard_map/ppermute | solution.py:86
  17.9 30.3 %collective-permute-start.12 = (f32[512]{0:T(512)S(1)}, f32[512]{0:T(512)S(1)}, u32[]{:S(2)}, u32[]{:S(2)}) collective-permute-start(f32[512]{0:T(512)S(1)} %convert_element_type.94), channel_id=1, source_target_pairs={{0,4},{4,0},{8,12},{12,8},{16,20},{20,16},{24,28},{28,24},{1,5},{5... | collective-permute-start | bytes 6152 | tf_op jit(solution)/shard_map/ppermute | solution.py:86
  18.1 16.2 %collective-permute-start.4 = (bf16[64,4608]{1,0:T(8,128)(2,1)S(1)}, bf16[64,4608]{1,0:T(8,128)(2,1)S(1)}, u32[]{:S(2)}, u32[]{:S(2)}) collective-permute-start(bf16[64,4608]{1,0:T(8,128)(2,1)S(1)} %get-tuple-element.12), channel_id=1, source_target_pairs={{0,16},{4,20},{8,24},{12,28},{16,0},{20,4},{24,8},{28,12},{1,17},{... | collective-permute-start | bytes 1769480 | tf_op jit(solution)/shard_map/ppermute | solution.py:86
  29.6 10.5 %collective-permute-start.3 = (bf16[32,4608]{1,0:T(8,128)(2,1)S(1)}, bf16[32,4608]{1,0:T(8,128)(2,1)S(1)}, u32[]{:S(2)}, u32[]{:S(2)}) collective-permute-start(bf16[32,4608]{1,0:T(8,128)(2,1)S(1)} %slice.40), channel_id=1, source_target_pairs={{0,16},{4,20},{8,24},{12,28},{16,0},{20,4},{24,8},{28,12},{1,17},{... | collective-permute-start | bytes 884744 | tf_op jit(solution)/shard_map/ppermute | solution.py:86
  34.4 19.0 %copy-start.6 = (bf16[512,512]{1,0:T(8,128)(2,1)S(1)}, bf16[512,512]{1,0:T(8,128)(2,1)}, u32[]{:S(2)}) copy-start(bf16[512,512]{1,0:T(8,128)(2,1)} %param.8) | copy-start | bytes 1572868
  34.4 8.1 %collective-permute-start.5 = (bf16[32,4608]{1,0:T(8,128)(2,1)S(1)}, bf16[32,4608]{1,0:T(8,128)(2,1)S(1)}, u32[]{:S(2)}, u32[]{:S(2)}) collective-permute-start(bf16[32,4608]{1,0:T(8,128)(2,1)S(1)} %slice.39), channel_id=1, source_target_pairs={{0,8},{4,12},{8,0},{12,4},{16,24},{20,28},{24,16},{28,20},{1,9},{5... | collective-permute-start | bytes 884744 | tf_op jit(solution)/shard_map/ppermute | solution.py:86
  42.7 14.9 %collective-permute-start.6 = (bf16[64,1152]{1,0:T(8,128)(2,1)S(1)}, bf16[64,1152]{1,0:T(8,128)(2,1)S(1)}, u32[]{:S(2)}, u32[]{:S(2)}) collective-permute-start(bf16[64,1152]{1,0:T(8,128)(2,1)S(1)} %get-tuple-element.13), channel_id=1, source_target_pairs={{0,1},{1,2},{2,3},{3,0},{4,5},{5,6},{6,7},{7,4},{8,9},{9,10},{10,1... | collective-permute-start | bytes 442376 | tf_op jit(solution)/shard_map/ppermute | solution.py:91
  44.3 13.5 %collective-permute-start.7 = (bf16[64,1152]{1,0:T(8,128)(2,1)S(1)}, bf16[64,1152]{1,0:T(8,128)(2,1)S(1)}, u32[]{:S(2)}, u32[]{:S(2)}) collective-permute-start(bf16[64,1152]{1,0:T(8,128)(2,1)S(1)} %get-tuple-element.14), channel_id=1, source_target_pairs={{0,2},{1,3},{2,0},{3,1},{4,6},{5,7},{6,4},{7,5},{8,10},{9,11},{10,... | collective-permute-start | bytes 442376 | tf_op jit(solution)/shard_map/ppermute | solution.py:91
  46.9 10.9 %collective-permute-start.8 = (bf16[64,1152]{1,0:T(8,128)(2,1)S(1)}, bf16[64,1152]{1,0:T(8,128)(2,1)S(1)}, u32[]{:S(2)}, u32[]{:S(2)}) collective-permute-start(bf16[64,1152]{1,0:T(8,128)(2,1)S(1)} %get-tuple-element.15), channel_id=1, source_target_pairs={{0,3},{1,0},{2,1},{3,2},{4,7},{5,4},{6,5},{7,6},{8,11},{9,8},{10,9... | collective-permute-start | bytes 442376 | tf_op jit(solution)/shard_map/ppermute | solution.py:91
  48.3 3.6 %collective-permute-start.13 = (f32[512]{0:T(512)S(1)}, f32[512]{0:T(512)S(1)}, u32[]{:S(2)}, u32[]{:S(2)}) collective-permute-start(f32[512]{0:T(512)S(1)} %convert_add_fusion.2), channel_id=1, source_target_pairs={{0,8},{4,12},{8,0},{12,4},{16,24},{20,28},{24,16},{28,20},{1,9},{5... | collective-permute-start | bytes 6152 | tf_op jit(solution)/shard_map/ppermute | solution.py:86
  51.9 3.6 %collective-permute-start.14 = (f32[512]{0:T(512)S(1)}, f32[512]{0:T(512)S(1)}, u32[]{:S(2)}, u32[]{:S(2)}) collective-permute-start(f32[512]{0:T(512)S(1)} %add.171), channel_id=1, source_target_pairs={{0,16},{4,20},{8,24},{12,28},{16,0},{20,4},{24,8},{28,12},{1,17},{... | collective-permute-start | bytes 6152 | tf_op jit(solution)/shard_map/ppermute | solution.py:86
  55.5 22.7 %copy-start.7 = (f32[1152]{0:T(1024)S(1)}, f32[1152]{0:T(1024)}, u32[]{:S(2)}) copy-start(f32[1152]{0:T(1024)} %param.9) | copy-start | bytes 13828
  55.5 12.3 %collective-permute-start.17 = (f32[512]{0:T(512)S(1)}, f32[512]{0:T(512)S(1)}, u32[]{:S(2)}, u32[]{:S(2)}) collective-permute-start(f32[512]{0:T(512)S(1)} %add.172), channel_id=1, source_target_pairs={{0,3},{1,0},{2,1},{3,2},{4,7},{5,4},{6,5},{7,6},{8,11},{9,8},{10,9... | collective-permute-start | bytes 6152 | tf_op jit(solution)/shard_map/ppermute | solution.py:91
  55.9 12.6 %collective-permute-start.16 = (f32[512]{0:T(512)S(1)}, f32[512]{0:T(512)S(1)}, u32[]{:S(2)}, u32[]{:S(2)}) collective-permute-start(f32[512]{0:T(512)S(1)} %add.172), channel_id=1, source_target_pairs={{0,2},{1,3},{2,0},{3,1},{4,6},{5,7},{6,4},{7,5},{8,10},{9,11},{10,... | collective-permute-start | bytes 6152 | tf_op jit(solution)/shard_map/ppermute | solution.py:91
  57.6 10.9 %collective-permute-start.15 = (f32[512]{0:T(512)S(1)}, f32[512]{0:T(512)S(1)}, u32[]{:S(2)}, u32[]{:S(2)}) collective-permute-start(f32[512]{0:T(512)S(1)} %add.172), channel_id=1, source_target_pairs={{0,1},{1,2},{2,3},{3,0},{4,5},{5,6},{6,7},{7,4},{8,9},{9,10},{10,1... | collective-permute-start | bytes 6152 | tf_op jit(solution)/shard_map/ppermute | solution.py:91
  63.9 8.6 %collective-permute-start.9 = (bf16[64,1152]{1,0:T(8,128)(2,1)S(1)}, bf16[64,1152]{1,0:T(8,128)(2,1)S(1)}, u32[]{:S(2)}, u32[]{:S(2)}) collective-permute-start(bf16[64,1152]{1,0:T(8,128)(2,1)S(1)} %get-tuple-element.16), channel_id=1, source_target_pairs={{0,1},{1,2},{2,3},{3,0},{4,5},{5,6},{6,7},{7,4},{8,9},{9,10},{10,1... | collective-permute-start | bytes 442376 | tf_op jit(solution)/shard_map/ppermute | solution.py:91
  65.5 7.4 %collective-permute-start.11 = (bf16[64,1152]{1,0:T(8,128)(2,1)S(1)}, bf16[64,1152]{1,0:T(8,128)(2,1)S(1)}, u32[]{:S(2)}, u32[]{:S(2)}) collective-permute-start(bf16[64,1152]{1,0:T(8,128)(2,1)S(1)} %get-tuple-element.17), channel_id=1, source_target_pairs={{0,3},{1,0},{2,1},{3,2},{4,7},{5,4},{6,5},{7,6},{8,11},{9,8},{10,9... | collective-permute-start | bytes 442376 | tf_op jit(solution)/shard_map/ppermute | solution.py:91
  67.8 10.4 %collective-permute-start.10 = (bf16[64,1152]{1,0:T(8,128)(2,1)S(1)}, bf16[64,1152]{1,0:T(8,128)(2,1)S(1)}, u32[]{:S(2)}, u32[]{:S(2)}) collective-permute-start(bf16[64,1152]{1,0:T(8,128)(2,1)S(1)} %get-tuple-element.18), channel_id=1, source_target_pairs={{0,2},{1,3},{2,0},{3,1},{4,6},{5,7},{6,4},{7,5},{8,10},{9,11},{10,... | collective-permute-start | bytes 442376 | tf_op jit(solution)/shard_map/ppermute | solution.py:91
  78.2 6.2 %collective-permute-start.20 = (bf16[64,1152]{1,0:T(8,128)(2,1)S(1)}, bf16[64,1152]{1,0:T(8,128)(2,1)S(1)}, u32[]{:S(2)}, u32[]{:S(2)}) collective-permute-start(bf16[64,1152]{1,0:T(8,128)(2,1)S(1)} %divide_convert_fusion), channel_id=1, source_target_pairs={{0,24},{4,28},{8,16},{12,20},{16,8},{20,12},{24,0},{28,4},{1,25},{... | collective-permute-start | bytes 442376 | tf_op jit(solution)/shard_map/ppermute | solution.py:86
  79.8 6.1 %collective-permute-start.19 = (bf16[64,1152]{1,0:T(8,128)(2,1)S(1)}, bf16[64,1152]{1,0:T(8,128)(2,1)S(1)}, u32[]{:S(2)}, u32[]{:S(2)}) collective-permute-start(bf16[64,1152]{1,0:T(8,128)(2,1)S(1)} %divide_convert_fusion), channel_id=1, source_target_pairs={{0,16},{4,20},{8,24},{12,28},{16,0},{20,4},{24,8},{28,12},{1,17},{... | collective-permute-start | bytes 442376 | tf_op jit(solution)/shard_map/ppermute | solution.py:86
  80.3 5.7 %collective-permute-start.18 = (bf16[64,1152]{1,0:T(8,128)(2,1)S(1)}, bf16[64,1152]{1,0:T(8,128)(2,1)S(1)}, u32[]{:S(2)}, u32[]{:S(2)}) collective-permute-start(bf16[64,1152]{1,0:T(8,128)(2,1)S(1)} %divide_convert_fusion), channel_id=1, source_target_pairs={{0,8},{4,12},{8,0},{12,4},{16,24},{20,28},{24,16},{28,20},{1,9},{5... | collective-permute-start | bytes 442376 | tf_op jit(solution)/shard_map/ppermute | solution.py:86
  86.3 1.6 %collective-permute-start.21 = (f32[64,1152]{1,0:T(8,128)S(1)}, f32[64,1152]{1,0:T(8,128)S(1)}, u32[]{:S(2)}, u32[]{:S(2)}) collective-permute-start(f32[64,1152]{1,0:T(8,128)S(1)} %slice.31), channel_id=1, source_target_pairs={{0,4},{4,0},{8,12},{12,8},{16,20},{20,16},{24,28},{28,24},{1,5},{5... | collective-permute-start | bytes 884744 | tf_op jit(solution)/shard_map/ppermute | solution.py:86
  88.0 7.0 %collective-permute-start.24 = (bf16[64,1152]{1,0:T(8,128)(2,1)S(1)}, bf16[64,1152]{1,0:T(8,128)(2,1)S(1)}, u32[]{:S(2)}, u32[]{:S(2)}) collective-permute-start(bf16[64,1152]{1,0:T(8,128)(2,1)S(1)} %fusion.41), channel_id=1, source_target_pairs={{0,3},{1,0},{2,1},{3,2},{4,7},{5,4},{6,5},{7,6},{8,11},{9,8},{10,9... | collective-permute-start | bytes 442376 | tf_op jit(solution)/shard_map/ppermute | solution.py:91
  90.7 12.8 %collective-permute-start.23 = (bf16[64,1152]{1,0:T(8,128)(2,1)S(1)}, bf16[64,1152]{1,0:T(8,128)(2,1)S(1)}, u32[]{:S(2)}, u32[]{:S(2)}) collective-permute-start(bf16[64,1152]{1,0:T(8,128)(2,1)S(1)} %fusion.41), channel_id=1, source_target_pairs={{0,2},{1,3},{2,0},{3,1},{4,6},{5,7},{6,4},{7,5},{8,10},{9,11},{10,... | collective-permute-start | bytes 442376 | tf_op jit(solution)/shard_map/ppermute | solution.py:91
  90.7 15.5 %collective-permute-start.22 = (bf16[64,1152]{1,0:T(8,128)(2,1)S(1)}, bf16[64,1152]{1,0:T(8,128)(2,1)S(1)}, u32[]{:S(2)}, u32[]{:S(2)}) collective-permute-start(bf16[64,1152]{1,0:T(8,128)(2,1)S(1)} %fusion.41), channel_id=1, source_target_pairs={{0,1},{1,2},{2,3},{3,0},{4,5},{5,6},{6,7},{7,4},{8,9},{9,10},{10,1... | collective-permute-start | bytes 442376 | tf_op jit(solution)/shard_map/ppermute | solution.py:91
  (1 other events, 0.8 us)

commit v2 on v1

--- a/solution.py
+++ b/solution.py
@@ -10,6 +10,7 @@
 damping = 1.0
 BF = jnp.bfloat16
 F32 = jnp.float32
+LOADS = 4
 
 
 def unfold(images):
@@ -91,35 +92,45 @@
     return lax.ppermute(value, "grp", [(i, (i + step) % n) for i in range(n)])
 
 
-def grad_kernel(act_a, act_b, dout_a, dout_b, basis_t, s_a, k_a, s_b, k_b, acts, turned, lhs):
+ORDER = ((0, 1), (0, 3), (0, 0), (0, 2), (1, 2), (1, 3), (1, 0), (1, 1))
+
+
+def grad_kernel(
+    act, dout, turn, s_a, k_a, s_b, k_b, moment, acts, flipped, turned, lhs
+):
     step = pl.program_id(0)
-    rows = act_a.shape[0]
+    rows = act.shape[0]
+    edge = rows // 16
+    images = edge // 16
 
     @pl.when(step == 0)
     def _():
         me = lax.axis_index("dp")
-        half = basis_t.shape[0] // 2
+        half = turn.shape[0] // 2
         sub = half // 8
         quarter = me >> 1
-        base = (me & 1) * half
-        order = [(0, 1), (0, 3), (0, 0), (0, 2), (1, 2), (1, 3), (1, 0), (1, 1)]
-        for at, (chunk, flip) in enumerate(order):
-            start = pl.multiple_of(base + (quarter ^ flip) * 2 * sub + chunk * sub, sub)
-            turned[at * sub : (at + 1) * sub, :] = basis_t[pl.ds(start, sub), :]
-        acts[0:16, :] = jnp.zeros((16, acts.shape[1]), BF)
-        acts[16 + 2 * rows :, :] = jnp.zeros((16, acts.shape[1]), BF)
-        acts[16 : 16 + rows, :] = act_a[...]
-        acts[16 + rows : 16 + 2 * rows, :] = act_b[...]
-        own = turned[...]
-        for at, ref in enumerate((dout_a, dout_b)):
-            part = lax.dot_general(
-                own, ref[...], (((1,), (1,)), ((), ())), preferred_element_type=F32
-            )
-            for tap, turn in enumerate((rows - 1, 0, 1)):
-                moved = pltpu.roll(part, turn, 1) if turn else part
-                lhs[tap * half : (tap + 1) * half, at * rows : (at + 1) * rows] = moved.astype(BF)
-
-    window = acts[pl.ds(pl.multiple_of(16 * step, 16), 2 * rows), :]
+        flipped[...] = turn[:, pl.ds(pl.multiple_of((me & 1) * half, half), half)].T
+        for at, (chunk, flip) in enumerate(ORDER):
+            start = pl.multiple_of((quarter ^ flip) * 2 * sub + chunk * sub, sub)
+            turned[at * sub : (at + 1) * sub, :] = flipped[pl.ds(start, sub), :]
+        acts[0:edge, :] = jnp.zeros((edge, acts.shape[1]), BF)
+        acts[edge + rows :, :] = jnp.zeros((edge, acts.shape[1]), BF)
+        acts[edge : edge + rows, :] = act[...]
+        part = lax.dot_general(
+            turned[...], dout[...], (((1,), (1,)), ((), ())), preferred_element_type=F32
+        )
+        moment[...] = lax.dot_general(
+            jnp.ones((8, rows), F32),
+            part * part,
+            (((1,), (1,)), ((), ())),
+            precision=lax.Precision.HIGHEST,
+            preferred_element_type=F32,
+        )
+        for tap, by in enumerate((rows - images, 0, images)):
+            moved = pltpu.roll(part, by, 1) if by else part
+            lhs[tap * half : (tap + 1) * half, :] = moved.astype(BF)
+
+    window = acts[pl.ds(pl.multiple_of(edge * step, edge), rows), :]
     out = jnp.dot(lhs[...], window, preferred_element_type=F32)
     channels = window.shape[1]
     quarter_rows = s_a.shape[0]
@@ -131,36 +142,89 @@
             ].astype(BF)
 
 
-def grad_parts(act_a, act_b, dout_a, dout_b, basis_t):
-    rows, channels = act_a.shape
+def grad_parts(act, dout, turn):
+    rows, channels = act.shape
     sub = channels // 8
     whole = lambda shape: pl.BlockSpec(shape, lambda i: (0,) * len(shape))
     piece = jax.ShapeDtypeStruct((sub, 9 * channels), BF)
     return pl.pallas_call(
         grad_kernel,
         grid=(3,),
-        in_specs=[whole((rows, channels))] * 4 + [whole(basis_t.shape)],
-        out_specs=[pl.BlockSpec((sub, 3 * channels), lambda i: (0, i))] * 4,
-        out_shape=[piece] * 4,
+        in_specs=[whole((rows, channels))] * 2
+        + [whole(turn.shape)],
+        out_specs=[pl.BlockSpec((sub, 3 * channels), lambda i: (0, i))] * 4
+        + [whole((8, channels // 2))],
+        out_shape=[piece] * 4 + [jax.ShapeDtypeStruct((8, channels // 2), F32)],
         scratch_shapes=[
-            pltpu.VMEM((2 * rows + 32, channels), BF),
+            pltpu.VMEM((rows + rows // 8, channels), BF),
             pltpu.VMEM((channels // 2, channels), BF),
-            pltpu.VMEM((3 * channels // 2, 2 * rows), BF),
+            pltpu.VMEM((channels // 2, channels), BF),
+            pltpu.VMEM((3 * channels // 2, rows), BF),
         ],
         compiler_params=pltpu.CompilerParams(
-            dimension_semantics=("arbitrary",), vmem_limit_bytes=40 << 20
+            dimension_semantics=("arbitrary",), vmem_limit_bytes=24 << 20
         ),
         cost_estimate=pl.CostEstimate(
-            flops=2 * 9 * channels * channels * rows,
-            bytes_accessed=4 * rows * channels * 2 + 9 * channels * channels,
+            flops=9 * channels * channels * rows,
+            bytes_accessed=2 * rows * channels * 2 + 9 * channels * channels,
             transcendentals=0,
         ),
-    )(act_a, act_b, dout_a, dout_b, basis_t)
-
-
-def padded_rows(images):
-    n, h, w, c = images.shape
-    return jnp.pad(images, ((0, 0), (0, 16 - h), (0, 16 - w), (0, 0))).reshape(n * 256, c)
+    )(act, dout, turn)
+
+
+def map_rows(own, other):
+    both = jnp.concatenate([own, other], 2)
+    h, w, n, c = both.shape
+    return jnp.pad(both, ((0, 16 - h), (0, 16 - w), (0, 0), (0, 0))).reshape(256 * n, c)
+
+
+def load_kernel(source, target, sems):
+    rows = source.shape[0] // LOADS
+    copies = [
+        pltpu.make_async_copy(
+            source.at[pl.ds(at * rows, rows)], target.at[pl.ds(at * rows, rows)], sems.at[at]
+        )
+        for at in range(LOADS)
+    ]
+    for copy in copies:
+        copy.start()
+    for copy in copies:
+        copy.wait()
+
+
+def load(value):
+    return pl.pallas_call(
+        load_kernel,
+        in_specs=[pl.BlockSpec(memory_space=pl.ANY)],
+        out_specs=pl.BlockSpec(memory_space=pl.ANY),
+        out_shape=pltpu.VMEM(value.shape, value.dtype),
+        scratch_shapes=[pltpu.SemaphoreType.DMA((LOADS,))],
+        compiler_params=pltpu.CompilerParams(vmem_limit_bytes=44 << 20),
+        cost_estimate=pl.CostEstimate(flops=0, bytes_accessed=4 * value.size, transcendentals=0),
+    )(value)
+
+
+def rotate_kernel(columns, basis, out):
+    out[...] = jnp.dot(columns[...], basis[...], preferred_element_type=F32).astype(BF)
+
+
+def restore_kernel(columns, basis, out):
+    turned = jnp.dot(basis[...], columns[...].T, preferred_element_type=F32)
+    out[...] = turned.T.astype(BF)
+
+
+def with_basis(kernel, columns, basis, width):
+    held = pl.BlockSpec(memory_space=pltpu.VMEM)
+    return pl.pallas_call(
+        kernel,
+        in_specs=[held, held],
+        out_specs=held,
+        out_shape=jax.ShapeDtypeStruct((columns.shape[0], width), BF),
+        compiler_params=pltpu.CompilerParams(vmem_limit_bytes=8 << 20),
+        cost_estimate=pl.CostEstimate(
+            flops=2 * columns.shape[0] * basis.size, bytes_accessed=2 * basis.size, transcendentals=0
+        ),
+    )(columns, basis)
 
 
 def spread(value, width):
@@ -183,27 +247,33 @@
     own_rows = input_eigen.shape[0]
     block = (me & 1) * 4 + (me >> 1)
 
-    flat = out_grads.reshape(-1, channels)
-    turned = jnp.dot(flat, output_basis, preferred_element_type=F32)
-    moment = rounded(jnp.sum(turned * turned, axis=0))
-    for bit in (1, 2, 4):
-        moment = moment + swap(moment, bit)
-    parts = [moment] + [shift(moment, step) for step in range(1, groups)]
-    eigen_out = sum(parts) / (images_all * side * side)
-    eigen_cols = lax.dynamic_slice_in_dim(eigen_out, block * width, width, 0)
-
-    acts = padded_rows(activations)
-    douts = padded_rows(out_grads)
-    s_a, k_a, s_b, k_b = grad_parts(acts, swap(acts, 1), douts, swap(douts, 1), output_basis.T)
+    act_own = activations.transpose(1, 2, 0, 3)
+    dout_own = out_grads.transpose(1, 2, 0, 3)
+    act_rows = map_rows(act_own, swap(act_own, 1))
+    dout_rows = map_rows(dout_own, swap(dout_own, 1))
+    s_a, k_a, s_b, k_b, moment = grad_parts(act_rows, dout_rows, output_basis)
+
     half = width // 2
     r_a, r_b = swap(s_a, 2), swap(s_b, 4)
+    r_a, r_b, moment = lax.optimization_barrier((r_a, r_b, moment))
     sum_a, sum_b = k_a.astype(F32) + r_a.astype(F32), k_b.astype(F32) + r_b.astype(F32)
     r_a = swap(sum_a[half:].astype(BF), 4)
     r_b = swap(sum_b[half:].astype(BF), 2)
     total = jnp.concatenate([sum_a[:half] + r_a.astype(F32), sum_b[:half] + r_b.astype(F32)], 0)
+    source, total = lax.optimization_barrier((input_basis, total))
     grad_mean = (spread(total, own_rows) / images_all).astype(BF)
-
-    rotated = spread(jnp.dot(grad_mean, input_basis, preferred_element_type=F32).astype(BF), own_rows)
+    basis = load(source)
+    rotated = spread(with_basis(rotate_kernel, grad_mean, basis, basis.shape[1]), own_rows)
+
+    def of(terms, flip):
+        places = [ORDER.index((chunk, flip)) * half for chunk in (0, 1)]
+        return jnp.concatenate([terms[0:1, at : at + half] for at in places], 1)
+
+    own_moment = of(moment, 0)
+    for flip in (1, 2, 3):
+        own_moment = own_moment + of(swap(moment, 2 * flip), flip)
+    own_moment = sum([shift(own_moment, step) for step in range(1, groups)], own_moment)
+    eigen_cols = own_moment[0] / (images_all * side * side)
     scaled = (rotated / (input_eigen[None, :] * eigen_cols[:, None] + damping)).astype(BF)
 
     near = jnp.concatenate([scaled] + [swap(scaled, bit) for bit in (2, 4, 6)], 0)
@@ -218,14 +288,14 @@
     own = (turned_back[:width] + swap(turned_back[width:], 1)).astype(BF)
 
     grp = lax.axis_index("grp")
-    update = None
+    source, own = lax.optimization_barrier((input_basis, own))
+    back = jnp.zeros((width, groups * own_rows), BF)
     for step in range(groups):
-        held = own if step == 0 else shift(own, step)
+        block_of = own if step == 0 else shift(own, step)
         at = lax.rem(grp - step + groups, groups) * own_rows
-        basis = lax.dynamic_slice_in_dim(input_basis, at, own_rows, 1)
-        part = lax.dot_general(held, basis, (((1,), (1,)), ((), ())), preferred_element_type=F32)
-        update = part if update is None else update + part
-    return update.astype(BF).T
+        back = lax.dynamic_update_slice_in_dim(back, block_of, at, 1)
+    basis = load(source)
+    return with_basis(restore_kernel, back, basis, own_rows).T
 
 
 def solution(mesh):

time: 113 us -> 103 us (0.912)
  matrix products: 19 us -> 0.25 us
  Pallas kernels: 4.38 us -> 19.3 us
  waiting for transfers between devices: 50.7 us -> 41.3 us
  local copies, waits for them, and re-layouts: 8.45 us -> 4.2 us
  other arithmetic: 0.78 us -> 4.79 us
  starting transfers between devices: 28.6 us -> 32.5 us
    dot_general x6 -> x0, matrix products: 18.8 us -> none  [the longest x4 11.4 us: cube(): lax.dot_general(held, basis, (((1,), (1,)), ((), ())), preferred_element_...]
    pallas_call x0 -> x4, Pallas kernels: none -> 13.9 us  [the longest x2 8.27 us: load(): pl.pallas_call(load_kernel, in_specs=[pl.BlockSpec(memory_space=pl.ANY)],...]
    ppermute x13, waiting for transfers between devices: 31.7 us -> 25.1 us  [swap(): lax.ppermute(value, 'dp', [(i, i ^ bit) for i in range(lax.axis_size('dp'...]
    unnamed x19 -> x6, local copies, waits for them, and re-layouts: 6.79 us -> 1.73 us
    concatenate x0 -> x3, other arithmetic: none -> 2.87 us  [the longest x2 2.79 us: map_rows(): both = jnp.concatenate([own, other], 2)]
    ppermute x12, waiting for transfers between devices: 19 us -> 16.2 us  [shift(): return lax.ppermute(value, 'grp', [(i, (i + step) % n) for i in range(n)])]
    ppermute x12, starting transfers between devices: 15.9 us -> 18.3 us  [shift(): return lax.ppermute(value, 'grp', [(i, (i + step) % n) for i in range(n)])]
    ppermute x13, starting transfers between devices: 12.7 us -> 14.2 us  [swap(): lax.ppermute(value, 'dp', [(i, i ^ bit) for i in range(lax.axis_size('dp'...]
  transfers between devices with their start and end apart: 25 -> 25, of which waited for: 16 -> 13; matrix products, arithmetic and copies ran while one was open for 14% -> 6% of each run, Pallas kernels for 0% -> 10%
where the time goes in v2:
time: 103 us
  waiting for transfers between devices  41.3 us (40%)
  starting transfers between devices  32.5 us (32%)
  Pallas kernels  19.3 us (19%)
  other arithmetic  4.79 us (5%)
  local copies, waits for them, and re-layouts  4.2 us (4%)
    ppermute x13, waiting for transfers between devices, swap(): lax.ppermute(value, 'dp', [(i, i ^ bit) for i in range(lax.axis_size('dp'...  25.1 us
    ppermute x12, starting transfers between devices, shift(): return lax.ppermute(value, 'grp', [(i, (i + step) % n) for i in range(n)])  18.3 us
    ppermute x12, waiting for transfers between devices, shift(): return lax.ppermute(value, 'grp', [(i, (i + step) % n) for i in range(n)])  16.2 us
    ppermute x13, starting transfers between devices, swap(): lax.ppermute(value, 'dp', [(i, i ^ bit) for i in range(lax.axis_size('dp'...  14.2 us
    pallas_call x2, Pallas kernels, load(): pl.pallas_call(load_kernel, in_specs=[pl.BlockSpec(memory_space=pl.ANY)],...  8.27 us
    pallas_call x2, Pallas kernels, with_basis(): pl.pallas_call(kernel, in_specs=[held, held], out_specs=held, out_shape=j...  5.62 us
    pallas_call x1, Pallas kernels, grad_parts(): pl.pallas_call(grad_kernel, grid=(3,), in_specs=[whole((rows, channels))]...  5.47 us
    concatenate x2, other arithmetic, map_rows(): both = jnp.concatenate([own, other], 2)  2.79 us
  transfers between devices with their start and end apart: 25, of which 13 were waited for; matrix products, arithmetic and copies ran while one was open for 6% of the time, Pallas kernels for 10%

profile of v2, /device:TPU:0, one launch (start us, length us, event | category | flops | bytes accessed | tf_op | source)
XLA Modules:
  0.0 102.7 jit_solution(18396140129854575175)
XLA Ops:
  0.5 1.5 %collective-permute-done = bf16[14,14,2,512]{3,2,1,0:T(2,128)(2,1)S(1)} collective-permute-done((bf16[14,14,2,512]{3,2,1,0:T(2,128)(2,1)}, bf16[14,14,2,512]{3,2,1,0:T(2,128)(2,1)S(1)}, u32[]{:S(2)}, u32[]{:S(2)}) %collective-permute-start) | collective-permute-done | bytes 401440 | tf_op jit(solution)/shard_map/ppermute | solution.py:87
  2.0 1.9 %fusion.6 = bf16[16,16,4,512]{3,2,1,0:T(4,128)(2,1)S(1)} fusion(bf16[14,14,2,512]{3,2,1,0:T(2,128)(2,1)S(1)} %collective-permute-done, bf16[14,14,2,512]{3,2,1,0:T(2,128)(2,1)} %bitcast.6), kind=kLoop, calls=%fused_computation.11 | loop fusion | flops 5767168 | bytes 1851392 | tf_op jit(solution)/shard_map/concatenate | solution.py:176
  6.1 1.0 %copy-done = bf16[512,512]{1,0:T(8,128)(2,1)S(1)} copy-done((bf16[512,512]{1,0:T(8,128)(2,1)S(1)}, bf16[512,512]{1,0:T(8,128)(2,1)}, u32[]{:S(2)}) %copy-start) | copy-done | bytes 524312
  7.2 5.5 %shard_map.55 = (bf16[64,4608]{1,0:T(8,128)(2,1)}, bf16[64,4608]{1,0:T(8,128)(2,1)S(1)}, bf16[64,4608]{1,0:T(8,128)(2,1)}, bf16[64,4608]{1,0:T(8,128)(2,1)S(1)}, f32[8,256]{1,0:T(8,128)S(1)}) custom-call(bf16[1024,512]{1,0:T(8,128)(2,1)S(1)} %reshape.66.act, bf16[1024,512]{1,0:T(8,128)(2,1)S(1)} %reshape.67.dout, bf16[512,512]{1,0:T(8,128)(2,1)S(1)} %copy-done), custom_call_target="tpu_custom_call" | custom-call | flops 2415919104 | bytes 4456448 | tf_op jit(solution)/shard_map/pallas_call | solution.py:150
  12.6 2.9 %collective-permute-start.2 = (bf16[64,4608]{1,0:T(8,128)(2,1)}, bf16[64,4608]{1,0:T(8,128)(2,1)S(1)}, u32[]{:S(2)}, u32[]{:S(2)}) collective-permute-start(bf16[64,4608]{1,0:T(8,128)(2,1)} %get-tuple-element.18), channel_id=1, source_target_pairs={{0,8},{4,12},{8,0},{12,4},{16,24},{20,28},{24,16},{28,20},{1,9},{5... | collective-permute-start | bytes 1769480 | tf_op jit(solution)/shard_map/ppermute | solution.py:87
  15.5 1.5 %collective-permute-start.3 = (bf16[64,4608]{1,0:T(8,128)(2,1)}, bf16[64,4608]{1,0:T(8,128)(2,1)}, u32[]{:S(2)}, u32[]{:S(2)}) collective-permute-start(bf16[64,4608]{1,0:T(8,128)(2,1)} %get-tuple-element.19), channel_id=1, source_target_pairs={{0,16},{4,20},{8,24},{12,28},{16,0},{20,4},{24,8},{28,12},{1,17},{... | collective-permute-start | bytes 1769480 | tf_op jit(solution)/shard_map/ppermute | solution.py:87
  17.0 1.3 %constant_dynamic-slice_fusion.8 = (bf16[512,64]{1,0:T(8,128)(2,1)S(1)}, bf16[512,64]{1,0:T(8,128)(2,1)S(1)}, bf16[512,64]{1,0:T(8,128)(2,1)S(1)}, bf16[512,64]{1,0:T(8,128)(2,1)S(1)}) fusion(bf16[512,512]{1,0:T(8,128)(2,1)} %turn.1, s32[]{:T(128)S(6)} %select_n.40, s32[]{:T(128)S(6)} %select_n.42, s32[]{:T(128)S(6)} %select_n.41, s32[]{:T(128)S(6)} %select_n.43), kind=kLoop, calls=%fused_computation.51 | loop fusion | bytes 524304 | tf_op jit(solution)/shard_map/dynamic_slice | solution.py:281
  18.3 11.0 %collective-permute-done.2 = bf16[64,4608]{1,0:T(8,128)(2,1)S(1)} collective-permute-done((bf16[64,4608]{1,0:T(8,128)(2,1)}, bf16[64,4608]{1,0:T(8,128)(2,1)S(1)}, u32[]{:S(2)}, u32[]{:S(2)}) %collective-permute-start.2) | collective-permute-done | bytes 589856 | tf_op jit(solution)/shard_map/ppermute | solution.py:87
  29.4 1.6 %collective-permute-done.3 = bf16[64,4608]{1,0:T(8,128)(2,1)} collective-permute-done((bf16[64,4608]{1,0:T(8,128)(2,1)}, bf16[64,4608]{1,0:T(8,128)(2,1)}, u32[]{:S(2)}, u32[]{:S(2)}) %collective-permute-start.3) | collective-permute-done | bytes 589856 | tf_op jit(solution)/shard_map/ppermute | solution.py:87
  30.9 1.5 %collective-permute-start.13 = (f32[8,256]{1,0:T(8,128)S(1)}, f32[8,256]{1,0:T(8,128)S(1)}, u32[]{:S(2)}, u32[]{:S(2)}) collective-permute-start(f32[8,256]{1,0:T(8,128)S(1)} %get-tuple-element.26), channel_id=1, source_target_pairs={{0,16},{4,20},{8,24},{12,28},{16,0},{20,4},{24,8},{28,12},{1,17},{... | collective-permute-start | bytes 24584 | tf_op jit(solution)/shard_map/ppermute | solution.py:87
  33.1 1.4 %collective-permute-start.14 = (f32[8,256]{1,0:T(8,128)S(1)}, f32[8,256]{1,0:T(8,128)S(1)}, u32[]{:S(2)}, u32[]{:S(2)}) collective-permute-start(f32[8,256]{1,0:T(8,128)S(1)} %get-tuple-element.26), channel_id=1, source_target_pairs={{0,24},{4,28},{8,16},{12,20},{16,8},{20,12},{24,0},{28,4},{1,25},{... | collective-permute-start | bytes 24584 | tf_op jit(solution)/shard_map/ppermute | solution.py:87
  34.5 1.2 %convert_add_fusion = f32[64,4608]{1,0:T(8,128)S(1)} fusion(bf16[64,4608]{1,0:T(8,128)(2,1)} %collective-permute-done.3, bf16[64,4608]{1,0:T(8,128)(2,1)S(1)} %get-tuple-element.22), kind=kLoop, calls=%fused_computation.8 | loop fusion | flops 884736 | bytes 2359296 | tf_op jit(solution)/shard_map/add | solution.py:259
  36.3 1.8 %collective-permute-start.4 = (bf16[32,4608]{1,0:T(8,128)(2,1)S(1)}, bf16[32,4608]{1,0:T(8,128)(2,1)S(1)}, u32[]{:S(2)}, u32[]{:S(2)}) collective-permute-start(bf16[32,4608]{1,0:T(8,128)(2,1)S(1)} %slice.71), channel_id=1, source_target_pairs={{0,16},{4,20},{8,24},{12,28},{16,0},{20,4},{24,8},{28,12},{1,17},{... | collective-permute-start | bytes 884744 | tf_op jit(solution)/shard_map/ppermute | solution.py:87
  38.2 4.6 %collective-permute-done.5 = bf16[32,4608]{1,0:T(8,128)(2,1)S(1)} collective-permute-done((bf16[32,4608]{1,0:T(8,128)(2,1)S(1)}, bf16[32,4608]{1,0:T(8,128)(2,1)S(1)}, u32[]{:S(2)}, u32[]{:S(2)}) %collective-permute-start.5) | collective-permute-done | bytes 294944 | tf_op jit(solution)/shard_map/ppermute | solution.py:87
  43.8 3.6 %collective-permute-start.8 = (bf16[64,1152]{1,0:T(8,128)(2,1)S(1)}, bf16[64,1152]{1,0:T(8,128)(2,1)S(1)}, u32[]{:S(2)}, u32[]{:S(2)}) collective-permute-start(bf16[64,1152]{1,0:T(8,128)(2,1)S(1)} %get-tuple-element.30), channel_id=1, source_target_pairs={{0,3},{1,0},{2,1},{3,2},{4,7},{5,4},{6,5},{7,6},{8,11},{9,8},{10,9... | collective-permute-start | bytes 442376 | tf_op jit(solution)/shard_map/ppermute | solution.py:92
  48.5 2.8 %collective-permute-start.17 = (f32[1,64]{1,0:T(1,128)S(1)}, f32[1,64]{1,0:T(1,128)S(1)}, u32[]{:S(2)}, u32[]{:S(2)}) collective-permute-start(f32[1,64]{1,0:T(1,128)S(1)} %fusion.23), channel_id=1, source_target_pairs={{0,3},{1,0},{2,1},{3,2},{4,7},{5,4},{6,5},{7,6},{8,11},{9,8},{10,9... | collective-permute-start | bytes 776 | tf_op jit(solution)/shard_map/ppermute | solution.py:92
  51.3 1.1 %collective-permute-start.16 = (f32[1,64]{1,0:T(1,128)S(1)}, f32[1,64]{1,0:T(1,128)S(1)}, u32[]{:S(2)}, u32[]{:S(2)}) collective-permute-start(f32[1,64]{1,0:T(1,128)S(1)} %fusion.23), channel_id=1, source_target_pairs={{0,2},{1,3},{2,0},{3,1},{4,6},{5,7},{6,4},{7,5},{8,10},{9,11},{10,... | collective-permute-start | bytes 776 | tf_op jit(solution)/shard_map/ppermute | solution.py:92
  52.4 4.1 %shard_map.56.basis = bf16[1152,4608]{1,0:T(8,128)(2,1)S(1)} custom-call(bf16[1152,4608]{1,0:T(8,128)(2,1)} %source.1), custom_call_target="tpu_custom_call" | custom-call | bytes 21233664 | tf_op jit(solution)/shard_map/pallas_call | solution.py:196
  58.3 2.0 %shard_map.57 = bf16[64,4608]{1,0:T(8,128)(2,1)S(1)} custom-call(bf16[64,1152]{1,0:T(8,128)(2,1)S(1)} %multiply_convert_fusion.columns, bf16[1152,4608]{1,0:T(8,128)(2,1)S(1)} %shard_map.56.basis), custom_call_target="tpu_custom_call" | custom-call | flops 679477248 | bytes 10616832 | tf_op jit(solution)/shard_map/pallas_call | solution.py:218
  60.4 2.3 %collective-permute-start.11 = (bf16[64,1152]{1,0:T(8,128)(2,1)S(1)}, bf16[64,1152]{1,0:T(8,128)(2,1)S(1)}, u32[]{:S(2)}, u32[]{:S(2)}) collective-permute-start(bf16[64,1152]{1,0:T(8,128)(2,1)S(1)} %get-tuple-element.33), channel_id=1, source_target_pairs={{0,3},{1,0},{2,1},{3,2},{4,7},{5,4},{6,5},{7,6},{8,11},{9,8},{10,9... | collective-permute-start | bytes 442376 | tf_op jit(solution)/shard_map/ppermute | solution.py:92
  62.7 1.5 %collective-permute-start.9 = (bf16[64,1152]{1,0:T(8,128)(2,1)S(1)}, bf16[64,1152]{1,0:T(8,128)(2,1)S(1)}, u32[]{:S(2)}, u32[]{:S(2)}) collective-permute-start(bf16[64,1152]{1,0:T(8,128)(2,1)S(1)} %get-tuple-element.32), channel_id=1, source_target_pairs={{0,1},{1,2},{2,3},{3,0},{4,5},{5,6},{6,7},{7,4},{8,9},{9,10},{10,1... | collective-permute-start | bytes 442376 | tf_op jit(solution)/shard_map/ppermute | solution.py:92
  64.2 2.2 %collective-permute-done.11 = bf16[64,1152]{1,0:T(8,128)(2,1)S(1)} collective-permute-done((bf16[64,1152]{1,0:T(8,128)(2,1)S(1)}, bf16[64,1152]{1,0:T(8,128)(2,1)S(1)}, u32[]{:S(2)}, u32[]{:S(2)}) %collective-permute-start.11) | collective-permute-done | bytes 147488 | tf_op jit(solution)/shard_map/ppermute | solution.py:92
  66.4 8.3 %collective-permute-done.10 = bf16[64,1152]{1,0:T(8,128)(2,1)S(1)} collective-permute-done((bf16[64,1152]{1,0:T(8,128)(2,1)S(1)}, bf16[64,1152]{1,0:T(8,128)(2,1)S(1)}, u32[]{:S(2)}, u32[]{:S(2)}) %collective-permute-start.10) | collective-permute-done | bytes 147488 | tf_op jit(solution)/shard_map/ppermute | solution.py:92
  74.9 2.1 %collective-permute-start.20 = (bf16[64,1152]{1,0:T(8,128)(2,1)S(1)}, bf16[64,1152]{1,0:T(8,128)(2,1)S(1)}, u32[]{:S(2)}, u32[]{:S(2)}) collective-permute-start(bf16[64,1152]{1,0:T(8,128)(2,1)S(1)} %divide_convert_fusion), channel_id=1, source_target_pairs={{0,24},{4,28},{8,16},{12,20},{16,8},{20,12},{24,0},{28,4},{1,25},{... | collective-permute-start | bytes 442376 | tf_op jit(solution)/shard_map/ppermute | solution.py:87
  78.6 2.4 %collective-permute-done.20 = bf16[64,1152]{1,0:T(8,128)(2,1)S(1)} collective-permute-done((bf16[64,1152]{1,0:T(8,128)(2,1)S(1)}, bf16[64,1152]{1,0:T(8,128)(2,1)S(1)}, u32[]{:S(2)}, u32[]{:S(2)}) %collective-permute-start.20) | collective-permute-done | bytes 147488 | tf_op jit(solution)/shard_map/ppermute | solution.py:87
  81.0 1.5 %collective-permute-done.19 = bf16[64,1152]{1,0:T(8,128)(2,1)S(1)} collective-permute-done((bf16[64,1152]{1,0:T(8,128)(2,1)S(1)}, bf16[64,1152]{1,0:T(8,128)(2,1)S(1)}, u32[]{:S(2)}, u32[]{:S(2)}) %collective-permute-start.19) | collective-permute-done | bytes 147488 | tf_op jit(solution)/shard_map/ppermute | solution.py:87
  83.2 1.6 %collective-permute-done.21 = f32[64,1152]{1,0:T(8,128)S(1)} collective-permute-done((f32[64,1152]{1,0:T(8,128)S(1)}, f32[64,1152]{1,0:T(8,128)S(1)}, u32[]{:S(2)}, u32[]{:S(2)}) %collective-permute-start.21) | collective-permute-done | bytes 294944 | tf_op jit(solution)/shard_map/ppermute | solution.py:87
  85.3 2.0 %collective-permute-start.23 = (bf16[64,1152]{1,0:T(8,128)(2,1)S(1)}, bf16[64,1152]{1,0:T(8,128)(2,1)S(1)}, u32[]{:S(2)}, u32[]{:S(2)}) collective-permute-start(bf16[64,1152]{1,0:T(8,128)(2,1)S(1)} %fusion.19), channel_id=1, source_target_pairs={{0,2},{1,3},{2,0},{3,1},{4,6},{5,7},{6,4},{7,5},{8,10},{9,11},{10,... | collective-permute-start | bytes 442376 | tf_op jit(solution)/shard_map/ppermute | solution.py:92
  87.3 2.8 %collective-permute-start.24 = (bf16[64,1152]{1,0:T(8,128)(2,1)S(1)}, bf16[64,1152]{1,0:T(8,128)(2,1)S(1)}, u32[]{:S(2)}, u32[]{:S(2)}) collective-permute-start(bf16[64,1152]{1,0:T(8,128)(2,1)S(1)} %fusion.19), channel_id=1, source_target_pairs={{0,3},{1,0},{2,1},{3,2},{4,7},{5,4},{6,5},{7,6},{8,11},{9,8},{10,9... | collective-permute-start | bytes 442376 | tf_op jit(solution)/shard_map/ppermute | solution.py:92
  90.1 4.1 %shard_map.58.basis = bf16[1152,4608]{1,0:T(8,128)(2,1)S(1)} custom-call(bf16[1152,4608]{1,0:T(8,128)(2,1)} %source.1), custom_call_target="tpu_custom_call" | custom-call | bytes 21233664 | tf_op jit(solution)/shard_map/pallas_call | solution.py:196
  94.4 4.7 %collective-permute-done.23 = bf16[64,1152]{1,0:T(8,128)(2,1)S(1)} collective-permute-done((bf16[64,1152]{1,0:T(8,128)(2,1)S(1)}, bf16[64,1152]{1,0:T(8,128)(2,1)S(1)}, u32[]{:S(2)}, u32[]{:S(2)}) %collective-permute-start.23) | collective-permute-done | bytes 147488 | tf_op jit(solution)/shard_map/ppermute | solution.py:92
  99.1 3.6 %shard_map.59 = bf16[64,1152]{1,0:T(8,128)(2,1)} custom-call(bf16[64,4608]{1,0:T(8,128)(2,1)S(1)} %constant_dynamic-update-slice_fusion.columns, bf16[1152,4608]{1,0:T(8,128)(2,1)S(1)} %shard_map.58.basis), custom_call_target="tpu_custom_call" | custom-call | flops 679477248 | bytes 10616832 | tf_op jit(solution)/shard_map/pallas_call | solution.py:218
  (60 shorter events, 10.8 us)
Async XLA Ops:
  0.0 2.0 %collective-permute-start = (bf16[14,14,2,512]{3,2,1,0:T(2,128)(2,1)}, bf16[14,14,2,512]{3,2,1,0:T(2,128)(2,1)S(1)}, u32[]{:S(2)}, u32[]{:S(2)}) collective-permute-start(bf16[14,14,2,512]{3,2,1,0:T(2,128)(2,1)} %bitcast.5), channel_id=1, source_target_pairs={{0,4},{4,0},{8,12},{12,8},{16,20},{20,16},{24,28},{28,24},{1,5},{5... | collective-permute-start | bytes 1204232 | tf_op jit(solution)/shard_map/ppermute | solution.py:87
  0.5 3.8 %collective-permute-start.1 = (bf16[14,14,2,512]{3,2,1,0:T(2,128)(2,1)}, bf16[14,14,2,512]{3,2,1,0:T(2,128)(2,1)S(1)}, u32[]{:S(2)}, u32[]{:S(2)}) collective-permute-start(bf16[14,14,2,512]{3,2,1,0:T(2,128)(2,1)} %bitcast.7), channel_id=1, source_target_pairs={{0,4},{4,0},{8,12},{12,8},{16,20},{20,16},{24,28},{28,24},{1,5},{5... | collective-permute-start | bytes 1204232 | tf_op jit(solution)/shard_map/ppermute | solution.py:87
  3.9 1.0 copy-start.1
  6.1 1.0 %copy-start = (bf16[512,512]{1,0:T(8,128)(2,1)S(1)}, bf16[512,512]{1,0:T(8,128)(2,1)}, u32[]{:S(2)}) copy-start(bf16[512,512]{1,0:T(8,128)(2,1)} %turn.1) | copy-start | bytes 1572868
  12.6 16.7 %collective-permute-start.2 = (bf16[64,4608]{1,0:T(8,128)(2,1)}, bf16[64,4608]{1,0:T(8,128)(2,1)S(1)}, u32[]{:S(2)}, u32[]{:S(2)}) collective-permute-start(bf16[64,4608]{1,0:T(8,128)(2,1)} %get-tuple-element.18), channel_id=1, source_target_pairs={{0,8},{4,12},{8,0},{12,4},{16,24},{20,28},{24,16},{28,20},{1,9},{5... | collective-permute-start | bytes 1769480 | tf_op jit(solution)/shard_map/ppermute | solution.py:87
  15.5 15.4 %collective-permute-start.3 = (bf16[64,4608]{1,0:T(8,128)(2,1)}, bf16[64,4608]{1,0:T(8,128)(2,1)}, u32[]{:S(2)}, u32[]{:S(2)}) collective-permute-start(bf16[64,4608]{1,0:T(8,128)(2,1)} %get-tuple-element.19), channel_id=1, source_target_pairs={{0,16},{4,20},{8,24},{12,28},{16,0},{20,4},{24,8},{28,12},{1,17},{... | collective-permute-start | bytes 1769480 | tf_op jit(solution)/shard_map/ppermute | solution.py:87
  30.9 17.5 %collective-permute-start.13 = (f32[8,256]{1,0:T(8,128)S(1)}, f32[8,256]{1,0:T(8,128)S(1)}, u32[]{:S(2)}, u32[]{:S(2)}) collective-permute-start(f32[8,256]{1,0:T(8,128)S(1)} %get-tuple-element.26), channel_id=1, source_target_pairs={{0,16},{4,20},{8,24},{12,28},{16,0},{20,4},{24,8},{28,12},{1,17},{... | collective-permute-start | bytes 24584 | tf_op jit(solution)/shard_map/ppermute | solution.py:87
  32.5 5.5 %collective-permute-start.12 = (f32[8,256]{1,0:T(8,128)S(1)}, f32[8,256]{1,0:T(8,128)S(1)}, u32[]{:S(2)}, u32[]{:S(2)}) collective-permute-start(f32[8,256]{1,0:T(8,128)S(1)} %get-tuple-element.26), channel_id=1, source_target_pairs={{0,8},{4,12},{8,0},{12,4},{16,24},{20,28},{24,16},{28,20},{1,9},{5... | collective-permute-start | bytes 24584 | tf_op jit(solution)/shard_map/ppermute | solution.py:87
  33.1 5.1 %collective-permute-start.14 = (f32[8,256]{1,0:T(8,128)S(1)}, f32[8,256]{1,0:T(8,128)S(1)}, u32[]{:S(2)}, u32[]{:S(2)}) collective-permute-start(f32[8,256]{1,0:T(8,128)S(1)} %get-tuple-element.26), channel_id=1, source_target_pairs={{0,24},{4,28},{8,16},{12,20},{16,8},{20,12},{24,0},{28,4},{1,25},{... | collective-permute-start | bytes 24584 | tf_op jit(solution)/shard_map/ppermute | solution.py:87
  35.7 7.1 %collective-permute-start.5 = (bf16[32,4608]{1,0:T(8,128)(2,1)S(1)}, bf16[32,4608]{1,0:T(8,128)(2,1)S(1)}, u32[]{:S(2)}, u32[]{:S(2)}) collective-permute-start(bf16[32,4608]{1,0:T(8,128)(2,1)S(1)} %slice.70), channel_id=1, source_target_pairs={{0,8},{4,12},{8,0},{12,4},{16,24},{20,28},{24,16},{28,20},{1,9},{5... | collective-permute-start | bytes 884744 | tf_op jit(solution)/shard_map/ppermute | solution.py:87
  36.3 7.3 %collective-permute-start.4 = (bf16[32,4608]{1,0:T(8,128)(2,1)S(1)}, bf16[32,4608]{1,0:T(8,128)(2,1)S(1)}, u32[]{:S(2)}, u32[]{:S(2)}) collective-permute-start(bf16[32,4608]{1,0:T(8,128)(2,1)S(1)} %slice.71), channel_id=1, source_target_pairs={{0,16},{4,20},{8,24},{12,28},{16,0},{20,4},{24,8},{28,12},{1,17},{... | collective-permute-start | bytes 884744 | tf_op jit(solution)/shard_map/ppermute | solution.py:87
  43.8 12.8 %collective-permute-start.8 = (bf16[64,1152]{1,0:T(8,128)(2,1)S(1)}, bf16[64,1152]{1,0:T(8,128)(2,1)S(1)}, u32[]{:S(2)}, u32[]{:S(2)}) collective-permute-start(bf16[64,1152]{1,0:T(8,128)(2,1)S(1)} %get-tuple-element.30), channel_id=1, source_target_pairs={{0,3},{1,0},{2,1},{3,2},{4,7},{5,4},{6,5},{7,6},{8,11},{9,8},{10,9... | collective-permute-start | bytes 442376 | tf_op jit(solution)/shard_map/ppermute | solution.py:92
  47.4 10.8 %collective-permute-start.7 = (bf16[64,1152]{1,0:T(8,128)(2,1)S(1)}, bf16[64,1152]{1,0:T(8,128)(2,1)S(1)}, u32[]{:S(2)}, u32[]{:S(2)}) collective-permute-start(bf16[64,1152]{1,0:T(8,128)(2,1)S(1)} %get-tuple-element.31), channel_id=1, source_target_pairs={{0,2},{1,3},{2,0},{3,1},{4,6},{5,7},{6,4},{7,5},{8,10},{9,11},{10,... | collective-permute-start | bytes 442376 | tf_op jit(solution)/shard_map/ppermute | solution.py:92
  47.4 10.8 %collective-permute-start.6 = (bf16[64,1152]{1,0:T(8,128)(2,1)S(1)}, bf16[64,1152]{1,0:T(8,128)(2,1)S(1)}, u32[]{:S(2)}, u32[]{:S(2)}) collective-permute-start(bf16[64,1152]{1,0:T(8,128)(2,1)S(1)} %get-tuple-element.29), channel_id=1, source_target_pairs={{0,1},{1,2},{2,3},{3,0},{4,5},{5,6},{6,7},{7,4},{8,9},{9,10},{10,1... | collective-permute-start | bytes 442376 | tf_op jit(solution)/shard_map/ppermute | solution.py:92
  48.5 14.2 %collective-permute-start.17 = (f32[1,64]{1,0:T(1,128)S(1)}, f32[1,64]{1,0:T(1,128)S(1)}, u32[]{:S(2)}, u32[]{:S(2)}) collective-permute-start(f32[1,64]{1,0:T(1,128)S(1)} %fusion.23), channel_id=1, source_target_pairs={{0,3},{1,0},{2,1},{3,2},{4,7},{5,4},{6,5},{7,6},{8,11},{9,8},{10,9... | collective-permute-start | bytes 776 | tf_op jit(solution)/shard_map/ppermute | solution.py:92
  51.3 12.9 %collective-permute-start.16 = (f32[1,64]{1,0:T(1,128)S(1)}, f32[1,64]{1,0:T(1,128)S(1)}, u32[]{:S(2)}, u32[]{:S(2)}) collective-permute-start(f32[1,64]{1,0:T(1,128)S(1)} %fusion.23), channel_id=1, source_target_pairs={{0,2},{1,3},{2,0},{3,1},{4,6},{5,7},{6,4},{7,5},{8,10},{9,11},{10,... | collective-permute-start | bytes 776 | tf_op jit(solution)/shard_map/ppermute | solution.py:92
  56.6 7.6 %collective-permute-start.15 = (f32[1,64]{1,0:T(1,128)S(1)}, f32[1,64]{1,0:T(1,128)S(1)}, u32[]{:S(2)}, u32[]{:S(2)}) collective-permute-start(f32[1,64]{1,0:T(1,128)S(1)} %fusion.23), channel_id=1, source_target_pairs={{0,1},{1,2},{2,3},{3,0},{4,5},{5,6},{6,7},{7,4},{8,9},{9,10},{10,1... | collective-permute-start | bytes 776 | tf_op jit(solution)/shard_map/ppermute | solution.py:92
  58.3 16.4 %copy-start.2 = (f32[1152]{0:T(1024)S(1)}, f32[1152]{0:T(1024)}, u32[]{:S(2)}) copy-start(f32[1152]{0:T(1024)} %param.9) | copy-start | bytes 13828
  60.4 6.1 %collective-permute-start.11 = (bf16[64,1152]{1,0:T(8,128)(2,1)S(1)}, bf16[64,1152]{1,0:T(8,128)(2,1)S(1)}, u32[]{:S(2)}, u32[]{:S(2)}) collective-permute-start(bf16[64,1152]{1,0:T(8,128)(2,1)S(1)} %get-tuple-element.33), channel_id=1, source_target_pairs={{0,3},{1,0},{2,1},{3,2},{4,7},{5,4},{6,5},{7,6},{8,11},{9,8},{10,9... | collective-permute-start | bytes 442376 | tf_op jit(solution)/shard_map/ppermute | solution.py:92
  62.7 12.0 %collective-permute-start.10 = (bf16[64,1152]{1,0:T(8,128)(2,1)S(1)}, bf16[64,1152]{1,0:T(8,128)(2,1)S(1)}, u32[]{:S(2)}, u32[]{:S(2)}) collective-permute-start(bf16[64,1152]{1,0:T(8,128)(2,1)S(1)} %get-tuple-element.34), channel_id=1, source_target_pairs={{0,2},{1,3},{2,0},{3,1},{4,6},{5,7},{6,4},{7,5},{8,10},{9,11},{10,... | collective-permute-start | bytes 442376 | tf_op jit(solution)/shard_map/ppermute | solution.py:92
  62.7 12.0 %collective-permute-start.9 = (bf16[64,1152]{1,0:T(8,128)(2,1)S(1)}, bf16[64,1152]{1,0:T(8,128)(2,1)S(1)}, u32[]{:S(2)}, u32[]{:S(2)}) collective-permute-start(bf16[64,1152]{1,0:T(8,128)(2,1)S(1)} %get-tuple-element.32), channel_id=1, source_target_pairs={{0,1},{1,2},{2,3},{3,0},{4,5},{5,6},{6,7},{7,4},{8,9},{9,10},{10,1... | collective-permute-start | bytes 442376 | tf_op jit(solution)/shard_map/ppermute | solution.py:92
  74.9 6.2 %collective-permute-start.20 = (bf16[64,1152]{1,0:T(8,128)(2,1)S(1)}, bf16[64,1152]{1,0:T(8,128)(2,1)S(1)}, u32[]{:S(2)}, u32[]{:S(2)}) collective-permute-start(bf16[64,1152]{1,0:T(8,128)(2,1)S(1)} %divide_convert_fusion), channel_id=1, source_target_pairs={{0,24},{4,28},{8,16},{12,20},{16,8},{20,12},{24,0},{28,4},{1,25},{... | collective-permute-start | bytes 442376 | tf_op jit(solution)/shard_map/ppermute | solution.py:87
  76.9 5.6 %collective-permute-start.19 = (bf16[64,1152]{1,0:T(8,128)(2,1)S(1)}, bf16[64,1152]{1,0:T(8,128)(2,1)S(1)}, u32[]{:S(2)}, u32[]{:S(2)}) collective-permute-start(bf16[64,1152]{1,0:T(8,128)(2,1)S(1)} %divide_convert_fusion), channel_id=1, source_target_pairs={{0,16},{4,20},{8,24},{12,28},{16,0},{20,4},{24,8},{28,12},{1,17},{... | collective-permute-start | bytes 442376 | tf_op jit(solution)/shard_map/ppermute | solution.py:87
  77.7 5.1 %collective-permute-start.18 = (bf16[64,1152]{1,0:T(8,128)(2,1)S(1)}, bf16[64,1152]{1,0:T(8,128)(2,1)S(1)}, u32[]{:S(2)}, u32[]{:S(2)}) collective-permute-start(bf16[64,1152]{1,0:T(8,128)(2,1)S(1)} %divide_convert_fusion), channel_id=1, source_target_pairs={{0,8},{4,12},{8,0},{12,4},{16,24},{20,28},{24,16},{28,20},{1,9},{5... | collective-permute-start | bytes 442376 | tf_op jit(solution)/shard_map/ppermute | solution.py:87
  83.1 1.6 %collective-permute-start.21 = (f32[64,1152]{1,0:T(8,128)S(1)}, f32[64,1152]{1,0:T(8,128)S(1)}, u32[]{:S(2)}, u32[]{:S(2)}) collective-permute-start(f32[64,1152]{1,0:T(8,128)S(1)} %slice.62), channel_id=1, source_target_pairs={{0,4},{4,0},{8,12},{12,8},{16,20},{20,16},{24,28},{28,24},{1,5},{5... | collective-permute-start | bytes 884744 | tf_op jit(solution)/shard_map/ppermute | solution.py:87
  84.8 9.5 %collective-permute-start.22 = (bf16[64,1152]{1,0:T(8,128)(2,1)S(1)}, bf16[64,1152]{1,0:T(8,128)(2,1)S(1)}, u32[]{:S(2)}, u32[]{:S(2)}) collective-permute-start(bf16[64,1152]{1,0:T(8,128)(2,1)S(1)} %fusion.19), channel_id=1, source_target_pairs={{0,1},{1,2},{2,3},{3,0},{4,5},{5,6},{6,7},{7,4},{8,9},{9,10},{10,1... | collective-permute-start | bytes 442376 | tf_op jit(solution)/shard_map/ppermute | solution.py:92
  85.3 13.8 %collective-permute-start.23 = (bf16[64,1152]{1,0:T(8,128)(2,1)S(1)}, bf16[64,1152]{1,0:T(8,128)(2,1)S(1)}, u32[]{:S(2)}, u32[]{:S(2)}) collective-permute-start(bf16[64,1152]{1,0:T(8,128)(2,1)S(1)} %fusion.19), channel_id=1, source_target_pairs={{0,2},{1,3},{2,0},{3,1},{4,6},{5,7},{6,4},{7,5},{8,10},{9,11},{10,... | collective-permute-start | bytes 442376 | tf_op jit(solution)/shard_map/ppermute | solution.py:92
  87.3 11.8 %collective-permute-start.24 = (bf16[64,1152]{1,0:T(8,128)(2,1)S(1)}, bf16[64,1152]{1,0:T(8,128)(2,1)S(1)}, u32[]{:S(2)}, u32[]{:S(2)}) collective-permute-start(bf16[64,1152]{1,0:T(8,128)(2,1)S(1)} %fusion.19), channel_id=1, source_target_pairs={{0,3},{1,0},{2,1},{3,2},{4,7},{5,4},{6,5},{7,6},{8,11},{9,8},{10,9... | collective-permute-start | bytes 442376 | tf_op jit(solution)/shard_map/ppermute | solution.py:92

commit v3 on v0

--- a/solution.py
+++ b/solution.py
@@ -1,9 +1,16 @@
+import functools
+
 import jax
 import jax.numpy as jnp
 from jax import lax
+from jax.experimental import pallas as pl
+from jax.experimental.pallas import tpu as pltpu
 from jax.sharding import PartitionSpec as P
 
 damping = 1.0
+BF = jnp.bfloat16
+F32 = jnp.float32
+LOADS = 8
 
 
 def unfold(images):
@@ -20,7 +27,7 @@
     return lax.optimization_barrier(value.astype(jnp.bfloat16)).astype(jnp.float32)
 
 
-def on_device(activations, out_grads, input_basis, output_basis, input_eigen):
+def any_mesh(activations, out_grads, input_basis, output_basis, input_eigen):
     channels = output_basis.shape[0]
     side = activations.shape[1]
     local_images = activations.shape[0]
@@ -76,6 +83,314 @@
     return final.astype(jnp.bfloat16)
 
 
+def swap(value, bit):
+    return lax.ppermute(value, "dp", [(i, i ^ bit) for i in range(lax.axis_size("dp"))])
+
+
+def shift(value, step):
+    n = lax.axis_size("grp")
+    return lax.ppermute(value, "grp", [(i, (i + step) % n) for i in range(n)])
+
+
+ROUTES = (((1, 3), (0, 2)), ((2, 3), (0, 1)))
+ORDER = tuple(
+    (2 * chunk + route, flip)
+    for chunk in (0, 1)
+    for route in (0, 1)
+    for flips in ROUTES[route]
+    for flip in flips
+)
+
+
+def grad_kernel(act_a, act_b, dout_a, dout_b, turn, *refs):
+    pieces, (acts, flipped, turned, lhs) = refs[:8], refs[8:]
+    rows, channels = act_a.shape
+    edge = rows // 16
+    images = edge // 16
+    half = channels // 2
+    sub = half // len(ORDER)
+    me = lax.axis_index("dp")
+    quarter = me >> 1
+    flipped[...] = turn[:, pl.ds(pl.multiple_of((me & 1) * half, half), half)].T
+    for at, (part, flip) in enumerate(ORDER):
+        start = pl.multiple_of((quarter ^ flip) * 4 * sub + part * sub, sub)
+        turned[at * sub : (at + 1) * sub, :] = flipped[pl.ds(start, sub), :]
+    acts[0:edge, :] = jnp.zeros((edge, channels), BF)
+    acts[edge + 2 * rows :, :] = jnp.zeros((edge, channels), BF)
+    acts[edge : edge + rows, :] = act_a[...]
+    acts[edge + rows : edge + 2 * rows, :] = act_b[...]
+    squares = jnp.zeros((half, 128), F32)
+    for at, ref in enumerate((dout_a, dout_b)):
+        part = lax.dot_general(
+            turned[...], ref[...], (((1,), (1,)), ((), ())), preferred_element_type=F32
+        )
+        for lane in range(0, rows, 128):
+            squares = squares + part[:, lane : lane + 128] * part[:, lane : lane + 128]
+        for tap, by in enumerate((rows - images, 0, images)):
+            moved = pltpu.roll(part, by, 1) if by else part
+            lhs[tap * half : (tap + 1) * half, at * rows : (at + 1) * rows] = moved.astype(BF)
+    for at, ref in enumerate(pieces):
+        ref[:, 9 * channels :] = squares[at * 2 * sub : (at + 1) * 2 * sub, :].astype(BF)
+    for step in range(3):
+        window = acts[edge * step : edge * step + 2 * rows, :]
+        out = jnp.dot(lhs[...], window, preferred_element_type=F32)
+        for tap in range(3):
+            column = (3 * step + tap) * channels
+            for at, ref in enumerate(pieces):
+                start = tap * half + at * 2 * sub
+                ref[:, column : column + channels] = out[start : start + 2 * sub, :].astype(BF)
+
+
+def grad_parts(act_a, act_b, dout_a, dout_b, turn):
+    rows, channels = act_a.shape
+    half = channels // 2
+    near = pl.BlockSpec(memory_space=pltpu.VMEM)
+    return pl.pallas_call(
+        grad_kernel,
+        in_specs=[near] * 5,
+        out_specs=[near] * 8,
+        out_shape=[jax.ShapeDtypeStruct((half // 8, 9 * channels + 128), BF)] * 8,
+        scratch_shapes=[
+            pltpu.VMEM((2 * rows + rows // 8, channels), BF),
+            pltpu.VMEM((half, channels), BF),
+            pltpu.VMEM((half, channels), BF),
+            pltpu.VMEM((3 * half, 2 * rows), BF),
+        ],
+        compiler_params=pltpu.CompilerParams(vmem_limit_bytes=16 << 20),
+        cost_estimate=pl.CostEstimate(
+            flops=18 * channels * channels * rows,
+            bytes_accessed=4 * rows * channels * 2 + 9 * channels * channels,
+            transcendentals=0,
+        ),
+    )(act_a, act_b, dout_a, dout_b, turn)
+
+
+def map_rows(images):
+    h, w, n, c = images.shape
+    return jnp.pad(images, ((0, 16 - h), (0, 16 - w), (0, 0), (0, 0))).reshape(256 * n, c)
+
+
+def load_kernel(source, after, target, sems):
+    del after
+    rows = source.shape[0] // LOADS
+    copies = [
+        pltpu.make_async_copy(
+            source.at[pl.ds(at * rows, rows)], target.at[pl.ds(at * rows, rows)], sems.at[at]
+        )
+        for at in range(LOADS)
+    ]
+    for copy in copies:
+        copy.start()
+    for copy in copies:
+        copy.wait()
+
+
+def load(value, after):
+    return pl.pallas_call(
+        load_kernel,
+        in_specs=[pl.BlockSpec(memory_space=pl.ANY), pl.BlockSpec(memory_space=pltpu.VMEM)],
+        out_specs=pl.BlockSpec(memory_space=pl.ANY),
+        out_shape=pltpu.VMEM(value.shape, value.dtype),
+        scratch_shapes=[pltpu.SemaphoreType.DMA((LOADS,))],
+        compiler_params=pltpu.CompilerParams(vmem_limit_bytes=44 << 20),
+        cost_estimate=pl.CostEstimate(flops=0, bytes_accessed=4 * value.size, transcendentals=0),
+    )(value, after)
+
+
+def stage(kernel, out_shape, operands, after=(), flops=0):
+    near = pl.BlockSpec(memory_space=pltpu.VMEM)
+
+    def body(*refs):
+        kernel(refs[: len(operands)], refs[len(operands) + len(after) :])
+
+    results = pl.pallas_call(
+        body,
+        in_specs=[near] * (len(operands) + len(after)),
+        out_specs=[near] * len(out_shape),
+        out_shape=out_shape,
+        compiler_params=pltpu.CompilerParams(vmem_limit_bytes=8 << 20),
+        cost_estimate=pl.CostEstimate(
+            flops=flops, bytes_accessed=sum(2 * x.size for x in operands), transcendentals=0
+        ),
+    )(*operands, *after)
+    return list(results)
+
+
+def first_sum(ins, outs):
+    kept, sent = outs[0], outs[1:]
+    sub = sent[0].shape[0]
+    for route in (0, 1):
+        mine, came = ins[2 * route], ins[2 * route + 1]
+        low, high = slice(0, sub), slice(sub, 2 * sub)
+        kept[route * sub : (route + 1) * sub, :] = mine[low, :].astype(F32) + came[low, :].astype(
+            F32
+        )
+        sent[route][...] = (mine[high, :].astype(F32) + came[high, :].astype(F32)).astype(BF)
+
+
+def deal(value, outs, width, behind=None):
+    me = lax.axis_index("grp")
+    groups = len(outs)
+    for step, out in enumerate(outs):
+        at = pl.multiple_of(lax.rem(me + step, groups) * width, 128)
+        out[:, 0:width] = value[:, pl.ds(at, width)].astype(out.dtype)
+        if behind is not None:
+            out[:, width:] = behind.astype(out.dtype)
+
+
+def second_sum(ins, outs):
+    kept, came_a, came_b = ins
+    *outs, total = outs
+    sub = came_a.shape[0]
+    total[0:sub, :] = kept[0:sub, :] + came_a[...].astype(F32)
+    total[sub:, :] = kept[sub:, :] + came_b[...].astype(F32)
+    rows, width = outs[0].shape
+    deal(total, outs, width - 128, total[:, len(outs) * (width - 128) :])
+
+
+def gathered(ins):
+    total = ins[0][...]
+    for other in ins[1:]:
+        total = total + other[...].astype(F32)
+    return total
+
+
+def rotate(ins, outs, images_all):
+    *ins, basis = ins
+    *outs, moments, product = outs
+    sums = gathered(ins)
+    rows = basis.shape[0]
+    grad_mean = (sums[:, :rows] / images_all).astype(BF)
+    moments[...] = sums[:, rows:]
+    product[...] = jnp.dot(grad_mean, basis[...], preferred_element_type=F32).astype(BF)
+    deal(product, outs, rows)
+
+
+def rescale(ins, outs, positions):
+    *ins, moments, input_eigen = ins
+    eigen_out = jnp.sum(moments[...], axis=1, keepdims=True) / positions
+    outs[0][...] = (gathered(ins) / (input_eigen[...] * eigen_out + damping)).astype(BF)
+
+
+def restore_kernel(offset, columns, basis, held, out, *, first, last):
+    width = columns.shape[1]
+    block = basis[:, pl.ds(pl.multiple_of(offset[0], 128), width)]
+    part = jnp.dot(block, columns[...].T, preferred_element_type=F32)
+    if not first:
+        part = part + held[...]
+    out[...] = part.T.astype(BF) if last else part
+
+
+def restore(offset, columns, basis, held, last):
+    first = held is None
+    rows, width = basis.shape[0], columns.shape[0]
+    near = pl.BlockSpec(memory_space=pltpu.VMEM)
+    kernel = functools.partial(restore_kernel, first=first, last=last)
+    if first:
+        held = jnp.zeros((8, 128), F32)
+    return pl.pallas_call(
+        kernel,
+        in_specs=[pl.BlockSpec(memory_space=pltpu.SMEM), near, near, near],
+        out_specs=near,
+        out_shape=jax.ShapeDtypeStruct((width, rows), BF)
+        if last
+        else jax.ShapeDtypeStruct((rows, width), F32),
+        compiler_params=pltpu.CompilerParams(vmem_limit_bytes=8 << 20),
+        cost_estimate=pl.CostEstimate(
+            flops=2 * columns.size * rows, bytes_accessed=2 * columns.size, transcendentals=0
+        ),
+    )(offset.reshape(1), columns, basis, held)
+
+
+def cube(activations, out_grads, input_basis, output_basis, input_eigen):
+    channels = output_basis.shape[0]
+    local_images, side = activations.shape[:2]
+    images_all = local_images * lax.axis_size("dp") * lax.axis_size("grp")
+    groups = lax.axis_size("grp")
+    me = lax.axis_index("dp")
+    width = channels // 8
+    own_rows = input_eigen.shape[0]
+    block = (me & 1) * 4 + (me >> 1)
+
+    act_own = activations.transpose(1, 2, 0, 3)
+    dout_own = out_grads.transpose(1, 2, 0, 3)
+    act_rows = [map_rows(act_own), map_rows(swap(act_own, 1))]
+    dout_rows = [map_rows(dout_own), map_rows(swap(dout_own, 1))]
+    parts = grad_parts(*act_rows, *dout_rows, output_basis)
+
+    sub = width // 4
+    wide = groups * own_rows + 128
+    chunks = (0, 1)
+    like = jax.ShapeDtypeStruct
+    others = groups - 1
+    came = [
+        [parts[4 * c + 1], swap(parts[4 * c], 2), parts[4 * c + 3], swap(parts[4 * c + 2], 4)]
+        for c in chunks
+    ]
+    last = ()
+    for c in chunks:
+        shapes = [like((2 * sub, wide), F32)] + [like((sub, wide), BF)] * 2
+        kept, s_a, s_b = last = stage(first_sum, shapes, came[c], last[1:2])
+        came[c] = [kept, swap(s_a, 4), swap(s_b, 2)]
+    last = ()
+    for c in chunks:
+        shapes = [like((2 * sub, own_rows + 128), t) for t in [F32] + [BF] * others]
+        last = stage(second_sum, shapes + [like((2 * sub, wide), F32)], came[c], last[1:2])
+        came[c] = [last[0]] + [shift(last[step], step) for step in range(1, groups)]
+        if c == 0:
+            basis = load(input_basis, last[1])
+    last = ()
+    for c in chunks:
+        shapes = [like((2 * sub, own_rows), t) for t in [F32] + [BF] * others]
+        shapes += [like((2 * sub, 128), F32), like((2 * sub, groups * own_rows), BF)]
+        last = stage(
+            functools.partial(rotate, images_all=images_all),
+            shapes,
+            came[c] + [basis],
+            last[1:2],
+            4 * sub * input_basis.size,
+        )
+        came[c] = [last[0]] + [shift(last[step], step) for step in range(1, groups)]
+        came[c].append(last[groups])
+        if c == 0:
+            basis = load(input_basis, last[1])
+
+    both = jnp.concatenate(
+        [lax.dynamic_slice_in_dim(output_basis, r * width, width, 0) for r in (me, me ^ 1)], 0
+    )
+    near = []
+    last = ()
+    for c in chunks:
+        last = stage(
+            functools.partial(rescale, positions=images_all * side * side),
+            [like((2 * sub, own_rows), BF)],
+            came[c] + [input_eigen.reshape(1, own_rows)],
+            last,
+        )
+        near.append(last + [swap(last[0], bit) for bit in (2, 4, 6)])
+    turned_back = 0
+    for chunk in chunks:
+        columns = [
+            lax.dynamic_slice_in_dim(both, (block ^ flip) * width + 2 * sub * chunk, 2 * sub, 1)
+            for flip in range(4)
+        ]
+        turned_back = turned_back + jnp.dot(
+            jnp.concatenate(columns, 1),
+            jnp.concatenate(near[chunk], 0),
+            preferred_element_type=F32,
+        )
+    own = (turned_back[:width] + swap(turned_back[width:], 1)).astype(BF)
+
+    grp = lax.axis_index("grp")
+    basis = load(input_basis, own)
+    update = None
+    for step in range(groups):
+        held = own if step == 0 else shift(own, step)
+        at = lax.rem(grp - step + groups, groups) * own_rows
+        update = restore(at, held, basis, update, step == groups - 1)
+    return update.T
+
+
 def solution(mesh):
     in_specs = (
         P(("dp", "grp"), None, None, None),
@@ -85,6 +400,5 @@
         P("grp"),
     )
     out_specs = P("grp", "dp")
-    return jax.shard_map(
-        on_device, mesh=mesh, in_specs=in_specs, out_specs=out_specs, check_vma=False
-    )
+    plan = cube if mesh.shape["dp"] == 8 else any_mesh
+    return jax.shard_map(plan, mesh=mesh, in_specs=in_specs, out_specs=out_specs, check_vma=False)

time: 273 us -> 101 us (0.37)
  waiting for transfers between devices: 124 us -> 22 us
  blocking collectives: 88.4 us -> 0 us
  starting transfers between devices: 0.09 us -> 39.6 us
  Pallas kernels: 0 us -> 29.7 us
  matrix products: 23.3 us -> 0.57 us
  local copies, waits for them, and re-layouts: 21.6 us -> 8.39 us
  between operations: 13.2 us -> 0.43 us
    reduce_scatter x1 -> x0, waiting for transfers between devices: 72.7 us -> none  [on_device(): lax.psum_scatter(term.astype(jnp.bfloat16), 'grp', scatter_dimension=0, t...]
    psum x1 -> x0, blocking collectives: 58.4 us -> none  [on_device(): grad_total, moment_rows = lax.psum((group_sum, group_moment), 'dp')]
    ppermute x0 -> x32, starting transfers between devices: none -> 39.6 us  [the longest x15 22.5 us: shift(): return lax.ppermute(value, 'grp', [(i, (i + step) % n) for i in range(n)])]
    pallas_call x0 -> x16, Pallas kernels: none -> 29.7 us  [the longest x3 15 us: load(): pl.pallas_call(load_kernel, in_specs=[pl.BlockSpec(memory_space=pl.ANY),...]
    unnamed x4 -> x0, waiting for transfers between devices: 29.1 us -> none
    dot_general x5 -> x2, matrix products: 23.3 us -> 0.57 us  [cube(): jnp.dot(jnp.concatenate(columns, 1), jnp.concatenate(near[chunk], 0), pre...]
    all_gather x1 -> x0, waiting for transfers between devices: 22.7 us -> none  [on_device(): lax.all_gather(block, 'dp', axis=1, tiled=True)]
    ppermute x0 -> x32, waiting for transfers between devices: none -> 22 us  [the longest x17 17.4 us: swap(): lax.ppermute(value, 'dp', [(i, i ^ bit) for i in range(lax.axis_size('dp'...]
  transfers between devices with their start and end apart: 3 -> 32, of which waited for: 3 -> 12; matrix products, arithmetic and copies ran while one was open for 0% -> 5% of each run, Pallas kernels for 0% -> 25%
where the time goes in v3:
time: 101 us
  starting transfers between devices  39.6 us (39%)
  Pallas kernels  29.7 us (29%)
  waiting for transfers between devices  22 us (22%)
  local copies, waits for them, and re-layouts  8.39 us (8%)
    ppermute x15, starting transfers between devices, shift(): return lax.ppermute(value, 'grp', [(i, (i + step) % n) for i in range(n)])  22.5 us
    ppermute x17, waiting for transfers between devices, swap(): lax.ppermute(value, 'dp', [(i, i ^ bit) for i in range(lax.axis_size('dp'...  17.4 us
    ppermute x17, starting transfers between devices, swap(): lax.ppermute(value, 'dp', [(i, i ^ bit) for i in range(lax.axis_size('dp'...  17 us
    pallas_call x3, Pallas kernels, load(): pl.pallas_call(load_kernel, in_specs=[pl.BlockSpec(memory_space=pl.ANY),...  15 us
    pallas_call x8, Pallas kernels, stage(): pl.pallas_call(body, in_specs=[near] * (len(operands) + len(after)), out_...  7.61 us
    ppermute x15, waiting for transfers between devices, shift(): return lax.ppermute(value, 'grp', [(i, (i + step) % n) for i in range(n)])  4.54 us
    pallas_call x4, Pallas kernels, restore(): pl.pallas_call(kernel, in_specs=[pl.BlockSpec(memory_space=pltpu.SMEM), n...  4.09 us
    pad x4, local copies, waits for them, and re-layouts, map_rows(): jnp.pad(images, ((0, 16 - h), (0, 16 - w), (0, 0), (0, 0)))  3.85 us
  transfers between devices with their start and end apart: 32, of which 12 were waited for; matrix products, arithmetic and copies ran while one was open for 5% of the time, Pallas kernels for 25%

profile of v3, /device:TPU:0, one launch (start us, length us, event | category | flops | bytes accessed | tf_op | source)
XLA Modules:
  0.0 100.9 jit_solution(13424246384089159873)
XLA Ops:
  0.5 1.5 %pad.13 = bf16[16,16,2,512]{3,2,1,0:T(2,128)(2,1)S(1)} pad(bf16[14,14,2,512]{3,2,1,0:T(2,128)(2,1)} %bitcast.8, bf16[]{:T(256)} %constant.46.clone.1), padding=0_2x0_2x0_0x0_0 | pad | bytes 925698 | tf_op jit(solution)/shard_map/jit(_pad)/pad | solution.py:170
  2.0 1.5 %pad.15 = bf16[16,16,2,512]{3,2,1,0:T(2,128)(2,1)S(1)} pad(bf16[14,14,2,512]{3,2,1,0:T(2,128)(2,1)} %bitcast.10, bf16[]{:T(256)} %constant.46.clone.1), padding=0_2x0_2x0_0x0_0 | pad | bytes 925698 | tf_op jit(solution)/shard_map/jit(_pad)/pad | solution.py:170
  6.3 3.0 %shard_map.55 = (bf16[32,4736]{1,0:T(8,128)(2,1)S(1)}, bf16[32,4736]{1,0:T(8,128)(2,1)S(1)}, bf16[32,4736]{1,0:T(8,128)(2,1)S(1)}, bf16[32,4736]{1,0:T(8,128)(2,...) custom-call(bf16[512,512]{1,0:T(8,128)(2,1)S(1)} %reshape.29.act_a, ...), custom_call_target="tpu_custom_call" | custom-call | flops 2415919104 | bytes 4456448 | tf_op jit(solution)/shard_map/pallas_call | solution.py:148
  9.3 3.0 %collective-permute-start.2 = (bf16[32,4736]{1,0:T(8,128)(2,1)S(1)}, bf16[32,4736]{1,0:T(8,128)(2,1)S(1)}, u32[]{:S(2)}, u32[]{:S(2)}) collective-permute-start(bf16[32,4736]{1,0:T(8,128)(2,1)S(1)} %get-tuple-element.38), channel_id=1, source_target_pairs={{0,8},{4,12},{8,0},{12,4},{16,24},{20,28},{24,16},{28,20},{1,9},{5... | collective-permute-start | bytes 909320 | tf_op jit(solution)/shard_map/ppermute | solution.py:87
  12.3 1.5 %collective-permute-start.3 = (bf16[32,4736]{1,0:T(8,128)(2,1)S(1)}, bf16[32,4736]{1,0:T(8,128)(2,1)S(1)}, u32[]{:S(2)}, u32[]{:S(2)}) collective-permute-start(bf16[32,4736]{1,0:T(8,128)(2,1)S(1)} %get-tuple-element.40), channel_id=1, source_target_pairs={{0,16},{4,20},{8,24},{12,28},{16,0},{20,4},{24,8},{28,12},{1,17},{... | collective-permute-start | bytes 909320 | tf_op jit(solution)/shard_map/ppermute | solution.py:87
  14.4 5.9 %collective-permute-done.2.refs_1_ = bf16[32,4736]{1,0:T(8,128)(2,1)S(1)} collective-permute-done((bf16[32,4736]{1,0:T(8,128)(2,1)S(1)}, bf16[32,4736]{1,0:T(8,128)(2,1)S(1)}, u32[]{:S(2)}, u32[]{:S(2)}) %collective-permute-start.2) | collective-permute-done | bytes 303136 | tf_op jit(solution)/shard_map/ppermute | solution.py:87
  20.3 2.1 %collective-permute-done.3.refs_3_ = bf16[32,4736]{1,0:T(8,128)(2,1)S(1)} collective-permute-done((bf16[32,4736]{1,0:T(8,128)(2,1)S(1)}, bf16[32,4736]{1,0:T(8,128)(2,1)S(1)}, u32[]{:S(2)}, u32[]{:S(2)}) %collective-permute-start.3) | collective-permute-done | bytes 303136 | tf_op jit(solution)/shard_map/ppermute | solution.py:87
  22.5 1.6 %collective-permute-start.4 = (bf16[16,4736]{1,0:T(8,128)(2,1)S(1)}, bf16[16,4736]{1,0:T(8,128)(2,1)S(1)}, u32[]{:S(2)}, u32[]{:S(2)}) collective-permute-start(bf16[16,4736]{1,0:T(8,128)(2,1)S(1)} %get-tuple-element.42.refs_4_), channel_id=1, source_target_pairs={{0,16},{4,20},{8,24},{12,28},{16,0},{20,4},{24,8},{28,12},{1,17},{... | collective-permute-start | bytes 454664 | tf_op jit(solution)/shard_map/ppermute | solution.py:87
  24.6 2.1 %collective-permute-done.15.refs_1_ = bf16[32,4736]{1,0:T(8,128)(2,1)S(1)} collective-permute-done((bf16[32,4736]{1,0:T(8,128)(2,1)S(1)}, bf16[32,4736]{1,0:T(8,128)(2,1)S(1)}, u32[]{:S(2)}, u32[]{:S(2)}) %collective-permute-start.15) | collective-permute-done | bytes 303136 | tf_op jit(solution)/shard_map/ppermute | solution.py:87
  26.8 2.1 %collective-permute-done.16.refs_3_ = bf16[32,4736]{1,0:T(8,128)(2,1)S(1)} collective-permute-done((bf16[32,4736]{1,0:T(8,128)(2,1)S(1)}, bf16[32,4736]{1,0:T(8,128)(2,1)S(1)}, u32[]{:S(2)}, u32[]{:S(2)}) %collective-permute-start.16) | collective-permute-done | bytes 303136 | tf_op jit(solution)/shard_map/ppermute | solution.py:87
  29.0 1.6 %collective-permute-start.17 = (bf16[16,4736]{1,0:T(8,128)(2,1)S(1)}, bf16[16,4736]{1,0:T(8,128)(2,1)S(1)}, u32[]{:S(2)}, u32[]{:S(2)}) collective-permute-start(bf16[16,4736]{1,0:T(8,128)(2,1)S(1)} %get-tuple-element.58), channel_id=1, source_target_pairs={{0,16},{4,20},{8,24},{12,28},{16,0},{20,4},{24,8},{28,12},{1,17},{... | collective-permute-start | bytes 454664 | tf_op jit(solution)/shard_map/ppermute | solution.py:87
  33.0 1.6 %collective-permute-start.6 = (bf16[32,1280]{1,0:T(8,128)(2,1)S(1)}, bf16[32,1280]{1,0:T(8,128)(2,1)S(1)}, u32[]{:S(2)}, u32[]{:S(2)}) collective-permute-start(bf16[32,1280]{1,0:T(8,128)(2,1)S(1)} %get-tuple-element.45.after.refs_3_), channel_id=1, source_target_pairs={{0,1},{1,2},{2,3},{3,0},{4,5},{5,6},{6,7},{7,4},{8,9},{9,10},{10,1... | collective-permute-start | bytes 245768 | tf_op jit(solution)/shard_map/ppermute | solution.py:92
  34.6 2.6 %collective-permute-start.7 = (bf16[32,1280]{1,0:T(8,128)(2,1)S(1)}, bf16[32,1280]{1,0:T(8,128)(2,1)S(1)}, u32[]{:S(2)}, u32[]{:S(2)}) collective-permute-start(bf16[32,1280]{1,0:T(8,128)(2,1)S(1)} %get-tuple-element.46), channel_id=1, source_target_pairs={{0,2},{1,3},{2,0},{3,1},{4,6},{5,7},{6,4},{7,5},{8,10},{9,11},{10,... | collective-permute-start | bytes 245768 | tf_op jit(solution)/shard_map/ppermute | solution.py:92
  40.9 5.0 %shard_map.58.refs_4_ = bf16[1152,4608]{1,0:T(8,128)(2,1)S(1)} custom-call(bf16[1152,4608]{1,0:T(8,128)(2,1)} %source.5, bf16[32,1280]{1,0:T(8,128)(2,1)} %copy-done.2), custom_call_target="tpu_custom_call" | custom-call | bytes 21233664 | tf_op jit(solution)/shard_map/pallas_call | solution.py:189
  45.9 2.5 %collective-permute-start.21 = (bf16[32,1280]{1,0:T(8,128)(2,1)S(1)}, bf16[32,1280]{1,0:T(8,128)(2,1)S(1)}, u32[]{:S(2)}, u32[]{:S(2)}) collective-permute-start(bf16[32,1280]{1,0:T(8,128)(2,1)S(1)} %get-tuple-element.63), channel_id=1, source_target_pairs={{0,3},{1,0},{2,1},{3,2},{4,7},{5,4},{6,5},{7,6},{8,11},{9,8},{10,9... | collective-permute-start | bytes 245768 | tf_op jit(solution)/shard_map/ppermute | solution.py:92
  48.4 2.6 %shard_map.59 = (f32[32,1152]{1,0:T(8,128)S(1)}, bf16[32,1152]{1,0:T(8,128)(2,1)S(1)}, bf16[32,1152]{1,0:T(8,128)(2,1)S(1)}, bf16[32,1152]{1,0:T(8,128)(2,1)S(1)...) custom-call(f32[32,1280]{1,0:T(8,128)S(1)} %get-tuple-element.44.refs_0_, ...), custom_call_target="tpu_custom_call" | custom-call | flops 339738624 | bytes 10944512 | tf_op jit(solution)/shard_map/pallas_call | solution.py:206
  52.6 5.0 %shard_map.63.refs_4_ = bf16[1152,4608]{1,0:T(8,128)(2,1)S(1)} custom-call(bf16[1152,4608]{1,0:T(8,128)(2,1)} %source.5, bf16[32,1152]{1,0:T(8,128)(2,1)} %copy-done.3), custom_call_target="tpu_custom_call" | custom-call | bytes 21233664 | tf_op jit(solution)/shard_map/pallas_call | solution.py:189
  58.6 2.6 %shard_map.64 = (f32[32,1152]{1,0:T(8,128)S(1)}, bf16[32,1152]{1,0:T(8,128)(2,1)S(1)}, bf16[32,1152]{1,0:T(8,128)(2,1)S(1)}, bf16[32,1152]{1,0:T(8,128)(2,1)S(1)...) custom-call(f32[32,1280]{1,0:T(8,128)S(1)} %get-tuple-element.60.refs_0_, ...), custom_call_target="tpu_custom_call" | custom-call | flops 339738624 | bytes 10944512 | tf_op jit(solution)/shard_map/pallas_call | solution.py:206
  61.2 2.0 %collective-permute-start.22 = (bf16[32,1152]{1,0:T(8,128)(2,1)S(1)}, bf16[32,1152]{1,0:T(8,128)(2,1)S(1)}, u32[]{:S(2)}, u32[]{:S(2)}) collective-permute-start(bf16[32,1152]{1,0:T(8,128)(2,1)S(1)} %get-tuple-element.65), channel_id=1, source_target_pairs={{0,1},{1,2},{2,3},{3,0},{4,5},{5,6},{6,7},{7,4},{8,9},{9,10},{10,1... | collective-permute-start | bytes 221192 | tf_op jit(solution)/shard_map/ppermute | solution.py:92
  63.2 1.8 %collective-permute-start.23 = (bf16[32,1152]{1,0:T(8,128)(2,1)S(1)}, bf16[32,1152]{1,0:T(8,128)(2,1)S(1)}, u32[]{:S(2)}, u32[]{:S(2)}) collective-permute-start(bf16[32,1152]{1,0:T(8,128)(2,1)S(1)} %get-tuple-element.66), channel_id=1, source_target_pairs={{0,2},{1,3},{2,0},{3,1},{4,6},{5,7},{6,4},{7,5},{8,10},{9,11},{10,... | collective-permute-start | bytes 221192 | tf_op jit(solution)/shard_map/ppermute | solution.py:92
  65.6 1.5 %collective-permute-start.10 = (bf16[32,1152]{1,0:T(8,128)(2,1)S(1)}, bf16[32,1152]{1,0:T(8,128)(2,1)S(1)}, u32[]{:S(2)}, u32[]{:S(2)}) collective-permute-start(bf16[32,1152]{1,0:T(8,128)(2,1)S(1)} %get-tuple-element.50), channel_id=1, source_target_pairs={{0,2},{1,3},{2,0},{3,1},{4,6},{5,7},{6,4},{7,5},{8,10},{9,11},{10,... | collective-permute-start | bytes 221192 | tf_op jit(solution)/shard_map/ppermute | solution.py:92
  67.0 2.3 %collective-permute-start.11 = (bf16[32,1152]{1,0:T(8,128)(2,1)S(1)}, bf16[32,1152]{1,0:T(8,128)(2,1)S(1)}, u32[]{:S(2)}, u32[]{:S(2)}) collective-permute-start(bf16[32,1152]{1,0:T(8,128)(2,1)S(1)} %get-tuple-element.51), channel_id=1, source_target_pairs={{0,3},{1,0},{2,1},{3,2},{4,7},{5,4},{6,5},{7,6},{8,11},{9,8},{10,9... | collective-permute-start | bytes 221192 | tf_op jit(solution)/shard_map/ppermute | solution.py:92
  69.5 1.4 %collective-permute-done.10.refs_2_ = bf16[32,1152]{1,0:T(8,128)(2,1)S(1)} collective-permute-done((bf16[32,1152]{1,0:T(8,128)(2,1)S(1)}, bf16[32,1152]{1,0:T(8,128)(2,1)S(1)}, u32[]{:S(2)}, u32[]{:S(2)}) %collective-permute-start.10) | collective-permute-done | bytes 73760 | tf_op jit(solution)/shard_map/ppermute | solution.py:92
  72.0 1.6 %collective-permute-start.27 = (bf16[32,1152]{1,0:T(8,128)(2,1)S(1)}, bf16[32,1152]{1,0:T(8,128)(2,1)S(1)}, u32[]{:S(2)}, u32[]{:S(2)}) collective-permute-start(bf16[32,1152]{1,0:T(8,128)(2,1)S(1)} %shard_map.65), channel_id=1, source_target_pairs={{0,24},{4,28},{8,16},{12,20},{16,8},{20,12},{24,0},{28,4},{1,25},{... | collective-permute-start | bytes 221192 | tf_op jit(solution)/shard_map/ppermute | solution.py:87
  75.6 1.6 %collective-permute-start.14 = (bf16[32,1152]{1,0:T(8,128)(2,1)S(1)}, bf16[32,1152]{1,0:T(8,128)(2,1)S(1)}, u32[]{:S(2)}, u32[]{:S(2)}) collective-permute-start(bf16[32,1152]{1,0:T(8,128)(2,1)S(1)} %shard_map.60.refs_6_), channel_id=1, source_target_pairs={{0,24},{4,28},{8,16},{12,20},{16,8},{20,12},{24,0},{28,4},{1,25},{... | collective-permute-start | bytes 221192 | tf_op jit(solution)/shard_map/ppermute | solution.py:87
  77.7 1.4 %collective-permute-start.12 = (bf16[32,1152]{1,0:T(8,128)(2,1)S(1)}, bf16[32,1152]{1,0:T(8,128)(2,1)S(1)}, u32[]{:S(2)}, u32[]{:S(2)}) collective-permute-start(bf16[32,1152]{1,0:T(8,128)(2,1)S(1)} %shard_map.60.refs_6_), channel_id=1, source_target_pairs={{0,8},{4,12},{8,0},{12,4},{16,24},{20,28},{24,16},{28,20},{1,9},{5... | collective-permute-start | bytes 221192 | tf_op jit(solution)/shard_map/ppermute | solution.py:87
  79.5 1.5 %collective-permute-done.14 = bf16[32,1152]{1,0:T(8,128)(2,1)S(1)} collective-permute-done((bf16[32,1152]{1,0:T(8,128)(2,1)S(1)}, bf16[32,1152]{1,0:T(8,128)(2,1)S(1)}, u32[]{:S(2)}, u32[]{:S(2)}) %collective-permute-start.14) | collective-permute-done | bytes 73760 | tf_op jit(solution)/shard_map/ppermute | solution.py:87
  82.5 1.6 %collective-permute-done.28 = f32[64,1152]{1,0:T(8,128)S(1)} collective-permute-done((f32[64,1152]{1,0:T(8,128)S(1)}, f32[64,1152]{1,0:T(8,128)S(1)}, u32[]{:S(2)}, u32[]{:S(2)}) %collective-permute-start.28) | collective-permute-done | bytes 294944 | tf_op jit(solution)/shard_map/ppermute | solution.py:87
  85.5 3.0 %collective-permute-start.30 = (bf16[64,1152]{1,0:T(8,128)(2,1)S(1)}, bf16[64,1152]{1,0:T(8,128)(2,1)S(1)}, u32[]{:S(2)}, u32[]{:S(2)}) collective-permute-start(bf16[64,1152]{1,0:T(8,128)(2,1)S(1)} %fusion.after.columns), channel_id=1, source_target_pairs={{0,2},{1,3},{2,0},{3,1},{4,6},{5,7},{6,4},{7,5},{8,10},{9,11},{10,... | collective-permute-start | bytes 442376 | tf_op jit(solution)/shard_map/ppermute | solution.py:92
  88.5 5.0 %shard_map.66.basis = bf16[1152,4608]{1,0:T(8,128)(2,1)S(1)} custom-call(bf16[1152,4608]{1,0:T(8,128)(2,1)} %source.5, bf16[64,1152]{1,0:T(8,128)(2,1)} %copy-done), custom_call_target="tpu_custom_call" | custom-call | bytes 21233664 | tf_op jit(solution)/shard_map/pallas_call | solution.py:189
  96.2 2.3 %collective-permute-done.30.columns = bf16[64,1152]{1,0:T(8,128)(2,1)S(1)} collective-permute-done((bf16[64,1152]{1,0:T(8,128)(2,1)S(1)}, bf16[64,1152]{1,0:T(8,128)(2,1)S(1)}, u32[]{:S(2)}, u32[]{:S(2)}) %collective-permute-start.30) | collective-permute-done | bytes 147488 | tf_op jit(solution)/shard_map/ppermute | solution.py:92
  99.3 1.6 %shard_map.70 = bf16[64,1152]{1,0:T(8,128)(2,1)} custom-call(s32[1]{0:T(128)} %bitcast.offset, bf16[64,1152]{1,0:T(8,128)(2,1)S(1)} %collective-permute-done.29.columns, bf16[1152,4608]{1,0:T(8,128)(2,1)S(1)} %shard_map.66.basis, f32[1152,64]{1,0:T(8,128)S(1)} %shard_map.69.held), custom_call_target="tpu_custom_call" | custom-call | flops 169869312 | bytes 147456 | tf_op jit(solution)/shard_map/pallas_call | solution.py:291
  (79 shorter events, 24.1 us)
Async XLA Ops:
  0.0 3.9 %collective-permute-start = (bf16[14,14,2,512]{3,2,1,0:T(2,128)(2,1)}, bf16[14,14,2,512]{3,2,1,0:T(2,128)(2,1)S(1)}, u32[]{:S(2)}, u32[]{:S(2)}) collective-permute-start(bf16[14,14,2,512]{3,2,1,0:T(2,128)(2,1)} %bitcast.7), channel_id=1, source_target_pairs={{0,4},{4,0},{8,12},{12,8},{16,20},{20,16},{24,28},{28,24},{1,5},{5... | collective-permute-start | bytes 1204232 | tf_op jit(solution)/shard_map/ppermute | solution.py:87
  0.5 4.1 %collective-permute-start.1 = (bf16[14,14,2,512]{3,2,1,0:T(2,128)(2,1)}, bf16[14,14,2,512]{3,2,1,0:T(2,128)(2,1)S(1)}, u32[]{:S(2)}, u32[]{:S(2)}) collective-permute-start(bf16[14,14,2,512]{3,2,1,0:T(2,128)(2,1)} %bitcast.9), channel_id=1, source_target_pairs={{0,4},{4,0},{8,12},{12,8},{16,20},{20,16},{24,28},{28,24},{1,5},{5... | collective-permute-start | bytes 1204232 | tf_op jit(solution)/shard_map/ppermute | solution.py:87
  9.3 11.0 %collective-permute-start.2 = (bf16[32,4736]{1,0:T(8,128)(2,1)S(1)}, bf16[32,4736]{1,0:T(8,128)(2,1)S(1)}, u32[]{:S(2)}, u32[]{:S(2)}) collective-permute-start(bf16[32,4736]{1,0:T(8,128)(2,1)S(1)} %get-tuple-element.38), channel_id=1, source_target_pairs={{0,8},{4,12},{8,0},{12,4},{16,24},{20,28},{24,16},{28,20},{1,9},{5... | collective-permute-start | bytes 909320 | tf_op jit(solution)/shard_map/ppermute | solution.py:87
  12.3 10.1 %collective-permute-start.3 = (bf16[32,4736]{1,0:T(8,128)(2,1)S(1)}, bf16[32,4736]{1,0:T(8,128)(2,1)S(1)}, u32[]{:S(2)}, u32[]{:S(2)}) collective-permute-start(bf16[32,4736]{1,0:T(8,128)(2,1)S(1)} %get-tuple-element.40), channel_id=1, source_target_pairs={{0,16},{4,20},{8,24},{12,28},{16,0},{20,4},{24,8},{28,12},{1,17},{... | collective-permute-start | bytes 909320 | tf_op jit(solution)/shard_map/ppermute | solution.py:87
  13.8 13.0 %collective-permute-start.15 = (bf16[32,4736]{1,0:T(8,128)(2,1)S(1)}, bf16[32,4736]{1,0:T(8,128)(2,1)S(1)}, u32[]{:S(2)}, u32[]{:S(2)}) collective-permute-start(bf16[32,4736]{1,0:T(8,128)(2,1)S(1)} %get-tuple-element.54), channel_id=1, source_target_pairs={{0,8},{4,12},{8,0},{12,4},{16,24},{20,28},{24,16},{28,20},{1,9},{5... | collective-permute-start | bytes 909320 | tf_op jit(solution)/shard_map/ppermute | solution.py:87
  14.3 14.5 %collective-permute-start.16 = (bf16[32,4736]{1,0:T(8,128)(2,1)S(1)}, bf16[32,4736]{1,0:T(8,128)(2,1)S(1)}, u32[]{:S(2)}, u32[]{:S(2)}) collective-permute-start(bf16[32,4736]{1,0:T(8,128)(2,1)S(1)} %get-tuple-element.56), channel_id=1, source_target_pairs={{0,16},{4,20},{8,24},{12,28},{16,0},{20,4},{24,8},{28,12},{1,17},{... | collective-permute-start | bytes 909320 | tf_op jit(solution)/shard_map/ppermute | solution.py:87
  22.5 9.6 %collective-permute-start.4 = (bf16[16,4736]{1,0:T(8,128)(2,1)S(1)}, bf16[16,4736]{1,0:T(8,128)(2,1)S(1)}, u32[]{:S(2)}, u32[]{:S(2)}) collective-permute-start(bf16[16,4736]{1,0:T(8,128)(2,1)S(1)} %get-tuple-element.42.refs_4_), channel_id=1, source_target_pairs={{0,16},{4,20},{8,24},{12,28},{16,0},{20,4},{24,8},{28,12},{1,17},{... | collective-permute-start | bytes 454664 | tf_op jit(solution)/shard_map/ppermute | solution.py:87
  24.1 8.0 %collective-permute-start.5 = (bf16[16,4736]{1,0:T(8,128)(2,1)S(1)}, bf16[16,4736]{1,0:T(8,128)(2,1)S(1)}, u32[]{:S(2)}, u32[]{:S(2)}) collective-permute-start(bf16[16,4736]{1,0:T(8,128)(2,1)S(1)} %get-tuple-element.43), channel_id=1, source_target_pairs={{0,8},{4,12},{8,0},{12,4},{16,24},{20,28},{24,16},{28,20},{1,9},{5... | collective-permute-start | bytes 454664 | tf_op jit(solution)/shard_map/ppermute | solution.py:87
  29.0 9.6 %collective-permute-start.17 = (bf16[16,4736]{1,0:T(8,128)(2,1)S(1)}, bf16[16,4736]{1,0:T(8,128)(2,1)S(1)}, u32[]{:S(2)}, u32[]{:S(2)}) collective-permute-start(bf16[16,4736]{1,0:T(8,128)(2,1)S(1)} %get-tuple-element.58), channel_id=1, source_target_pairs={{0,16},{4,20},{8,24},{12,28},{16,0},{20,4},{24,8},{28,12},{1,17},{... | collective-permute-start | bytes 454664 | tf_op jit(solution)/shard_map/ppermute | solution.py:87
  30.6 8.0 %collective-permute-start.18 = (bf16[16,4736]{1,0:T(8,128)(2,1)S(1)}, bf16[16,4736]{1,0:T(8,128)(2,1)S(1)}, u32[]{:S(2)}, u32[]{:S(2)}) collective-permute-start(bf16[16,4736]{1,0:T(8,128)(2,1)S(1)} %get-tuple-element.59), channel_id=1, source_target_pairs={{0,8},{4,12},{8,0},{12,4},{16,24},{20,28},{24,16},{28,20},{1,9},{5... | collective-permute-start | bytes 454664 | tf_op jit(solution)/shard_map/ppermute | solution.py:87
  33.0 12.9 %collective-permute-start.6 = (bf16[32,1280]{1,0:T(8,128)(2,1)S(1)}, bf16[32,1280]{1,0:T(8,128)(2,1)S(1)}, u32[]{:S(2)}, u32[]{:S(2)}) collective-permute-start(bf16[32,1280]{1,0:T(8,128)(2,1)S(1)} %get-tuple-element.45.after.refs_3_), channel_id=1, source_target_pairs={{0,1},{1,2},{2,3},{3,0},{4,5},{5,6},{6,7},{7,4},{8,9},{9,10},{10,1... | collective-permute-start | bytes 245768 | tf_op jit(solution)/shard_map/ppermute | solution.py:92
  34.6 13.8 %collective-permute-start.7 = (bf16[32,1280]{1,0:T(8,128)(2,1)S(1)}, bf16[32,1280]{1,0:T(8,128)(2,1)S(1)}, u32[]{:S(2)}, u32[]{:S(2)}) collective-permute-start(bf16[32,1280]{1,0:T(8,128)(2,1)S(1)} %get-tuple-element.46), channel_id=1, source_target_pairs={{0,2},{1,3},{2,0},{3,1},{4,6},{5,7},{6,4},{7,5},{8,10},{9,11},{10,... | collective-permute-start | bytes 245768 | tf_op jit(solution)/shard_map/ppermute | solution.py:92
  37.2 11.2 %collective-permute-start.8 = (bf16[32,1280]{1,0:T(8,128)(2,1)S(1)}, bf16[32,1280]{1,0:T(8,128)(2,1)S(1)}, u32[]{:S(2)}, u32[]{:S(2)}) collective-permute-start(bf16[32,1280]{1,0:T(8,128)(2,1)S(1)} %get-tuple-element.47), channel_id=1, source_target_pairs={{0,3},{1,0},{2,1},{3,2},{4,7},{5,4},{6,5},{7,6},{8,11},{9,8},{10,9... | collective-permute-start | bytes 245768 | tf_op jit(solution)/shard_map/ppermute | solution.py:92
  39.5 18.2 %collective-permute-start.19 = (bf16[32,1280]{1,0:T(8,128)(2,1)S(1)}, bf16[32,1280]{1,0:T(8,128)(2,1)S(1)}, u32[]{:S(2)}, u32[]{:S(2)}) collective-permute-start(bf16[32,1280]{1,0:T(8,128)(2,1)S(1)} %get-tuple-element.61), channel_id=1, source_target_pairs={{0,1},{1,2},{2,3},{3,0},{4,5},{5,6},{6,7},{7,4},{8,9},{9,10},{10,1... | collective-permute-start | bytes 245768 | tf_op jit(solution)/shard_map/ppermute | solution.py:92
  40.2 17.5 %collective-permute-start.20 = (bf16[32,1280]{1,0:T(8,128)(2,1)S(1)}, bf16[32,1280]{1,0:T(8,128)(2,1)S(1)}, u32[]{:S(2)}, u32[]{:S(2)}) collective-permute-start(bf16[32,1280]{1,0:T(8,128)(2,1)S(1)} %get-tuple-element.62), channel_id=1, source_target_pairs={{0,2},{1,3},{2,0},{3,1},{4,6},{5,7},{6,4},{7,5},{8,10},{9,11},{10,... | collective-permute-start | bytes 245768 | tf_op jit(solution)/shard_map/ppermute | solution.py:92
  45.9 11.8 %collective-permute-start.21 = (bf16[32,1280]{1,0:T(8,128)(2,1)S(1)}, bf16[32,1280]{1,0:T(8,128)(2,1)S(1)}, u32[]{:S(2)}, u32[]{:S(2)}) collective-permute-start(bf16[32,1280]{1,0:T(8,128)(2,1)S(1)} %get-tuple-element.63), channel_id=1, source_target_pairs={{0,3},{1,0},{2,1},{3,2},{4,7},{5,4},{6,5},{7,6},{8,11},{9,8},{10,9... | collective-permute-start | bytes 245768 | tf_op jit(solution)/shard_map/ppermute | solution.py:92
  51.1 16.0 %collective-permute-start.9 = (bf16[32,1152]{1,0:T(8,128)(2,1)S(1)}, bf16[32,1152]{1,0:T(8,128)(2,1)S(1)}, u32[]{:S(2)}, u32[]{:S(2)}) collective-permute-start(bf16[32,1152]{1,0:T(8,128)(2,1)S(1)} %get-tuple-element.49.after.refs_5_), channel_id=1, source_target_pairs={{0,1},{1,2},{2,3},{3,0},{4,5},{5,6},{6,7},{7,4},{8,9},{9,10},{10,1... | collective-permute-start | bytes 221192 | tf_op jit(solution)/shard_map/ppermute | solution.py:92
  61.2 10.6 %collective-permute-start.22 = (bf16[32,1152]{1,0:T(8,128)(2,1)S(1)}, bf16[32,1152]{1,0:T(8,128)(2,1)S(1)}, u32[]{:S(2)}, u32[]{:S(2)}) collective-permute-start(bf16[32,1152]{1,0:T(8,128)(2,1)S(1)} %get-tuple-element.65), channel_id=1, source_target_pairs={{0,1},{1,2},{2,3},{3,0},{4,5},{5,6},{6,7},{7,4},{8,9},{9,10},{10,1... | collective-permute-start | bytes 221192 | tf_op jit(solution)/shard_map/ppermute | solution.py:92
  63.2 8.7 %collective-permute-start.23 = (bf16[32,1152]{1,0:T(8,128)(2,1)S(1)}, bf16[32,1152]{1,0:T(8,128)(2,1)S(1)}, u32[]{:S(2)}, u32[]{:S(2)}) collective-permute-start(bf16[32,1152]{1,0:T(8,128)(2,1)S(1)} %get-tuple-element.66), channel_id=1, source_target_pairs={{0,2},{1,3},{2,0},{3,1},{4,6},{5,7},{6,4},{7,5},{8,10},{9,11},{10,... | collective-permute-start | bytes 221192 | tf_op jit(solution)/shard_map/ppermute | solution.py:92
  65.0 6.9 %collective-permute-start.24 = (bf16[32,1152]{1,0:T(8,128)(2,1)S(1)}, bf16[32,1152]{1,0:T(8,128)(2,1)S(1)}, u32[]{:S(2)}, u32[]{:S(2)}) collective-permute-start(bf16[32,1152]{1,0:T(8,128)(2,1)S(1)} %get-tuple-element.67), channel_id=1, source_target_pairs={{0,3},{1,0},{2,1},{3,2},{4,7},{5,4},{6,5},{7,6},{8,11},{9,8},{10,9... | collective-permute-start | bytes 221192 | tf_op jit(solution)/shard_map/ppermute | solution.py:92
  65.6 5.4 %collective-permute-start.10 = (bf16[32,1152]{1,0:T(8,128)(2,1)S(1)}, bf16[32,1152]{1,0:T(8,128)(2,1)S(1)}, u32[]{:S(2)}, u32[]{:S(2)}) collective-permute-start(bf16[32,1152]{1,0:T(8,128)(2,1)S(1)} %get-tuple-element.50), channel_id=1, source_target_pairs={{0,2},{1,3},{2,0},{3,1},{4,6},{5,7},{6,4},{7,5},{8,10},{9,11},{10,... | collective-permute-start | bytes 221192 | tf_op jit(solution)/shard_map/ppermute | solution.py:92
  67.0 4.7 %collective-permute-start.11 = (bf16[32,1152]{1,0:T(8,128)(2,1)S(1)}, bf16[32,1152]{1,0:T(8,128)(2,1)S(1)}, u32[]{:S(2)}, u32[]{:S(2)}) collective-permute-start(bf16[32,1152]{1,0:T(8,128)(2,1)S(1)} %get-tuple-element.51), channel_id=1, source_target_pairs={{0,3},{1,0},{2,1},{3,2},{4,7},{5,4},{6,5},{7,6},{8,11},{9,8},{10,9... | collective-permute-start | bytes 221192 | tf_op jit(solution)/shard_map/ppermute | solution.py:92
  72.0 5.8 %collective-permute-start.27 = (bf16[32,1152]{1,0:T(8,128)(2,1)S(1)}, bf16[32,1152]{1,0:T(8,128)(2,1)S(1)}, u32[]{:S(2)}, u32[]{:S(2)}) collective-permute-start(bf16[32,1152]{1,0:T(8,128)(2,1)S(1)} %shard_map.65), channel_id=1, source_target_pairs={{0,24},{4,28},{8,16},{12,20},{16,8},{20,12},{24,0},{28,4},{1,25},{... | collective-permute-start | bytes 221192 | tf_op jit(solution)/shard_map/ppermute | solution.py:87
  73.6 5.6 %collective-permute-start.26 = (bf16[32,1152]{1,0:T(8,128)(2,1)S(1)}, bf16[32,1152]{1,0:T(8,128)(2,1)S(1)}, u32[]{:S(2)}, u32[]{:S(2)}) collective-permute-start(bf16[32,1152]{1,0:T(8,128)(2,1)S(1)} %shard_map.65), channel_id=1, source_target_pairs={{0,16},{4,20},{8,24},{12,28},{16,0},{20,4},{24,8},{28,12},{1,17},{... | collective-permute-start | bytes 221192 | tf_op jit(solution)/shard_map/ppermute | solution.py:87
  74.1 5.1 %collective-permute-start.25 = (bf16[32,1152]{1,0:T(8,128)(2,1)S(1)}, bf16[32,1152]{1,0:T(8,128)(2,1)S(1)}, u32[]{:S(2)}, u32[]{:S(2)}) collective-permute-start(bf16[32,1152]{1,0:T(8,128)(2,1)S(1)} %shard_map.65), channel_id=1, source_target_pairs={{0,8},{4,12},{8,0},{12,4},{16,24},{20,28},{24,16},{28,20},{1,9},{5... | collective-permute-start | bytes 221192 | tf_op jit(solution)/shard_map/ppermute | solution.py:87
  75.6 5.3 %collective-permute-start.14 = (bf16[32,1152]{1,0:T(8,128)(2,1)S(1)}, bf16[32,1152]{1,0:T(8,128)(2,1)S(1)}, u32[]{:S(2)}, u32[]{:S(2)}) collective-permute-start(bf16[32,1152]{1,0:T(8,128)(2,1)S(1)} %shard_map.60.refs_6_), channel_id=1, source_target_pairs={{0,24},{4,28},{8,16},{12,20},{16,8},{20,12},{24,0},{28,4},{1,25},{... | collective-permute-start | bytes 221192 | tf_op jit(solution)/shard_map/ppermute | solution.py:87
  77.2 4.5 %collective-permute-start.13 = (bf16[32,1152]{1,0:T(8,128)(2,1)S(1)}, bf16[32,1152]{1,0:T(8,128)(2,1)S(1)}, u32[]{:S(2)}, u32[]{:S(2)}) collective-permute-start(bf16[32,1152]{1,0:T(8,128)(2,1)S(1)} %shard_map.60.refs_6_), channel_id=1, source_target_pairs={{0,16},{4,20},{8,24},{12,28},{16,0},{20,4},{24,8},{28,12},{1,17},{... | collective-permute-start | bytes 221192 | tf_op jit(solution)/shard_map/ppermute | solution.py:87
  77.7 4.4 %collective-permute-start.12 = (bf16[32,1152]{1,0:T(8,128)(2,1)S(1)}, bf16[32,1152]{1,0:T(8,128)(2,1)S(1)}, u32[]{:S(2)}, u32[]{:S(2)}) collective-permute-start(bf16[32,1152]{1,0:T(8,128)(2,1)S(1)} %shard_map.60.refs_6_), channel_id=1, source_target_pairs={{0,8},{4,12},{8,0},{12,4},{16,24},{20,28},{24,16},{28,20},{1,9},{5... | collective-permute-start | bytes 221192 | tf_op jit(solution)/shard_map/ppermute | solution.py:87
  82.4 1.6 %collective-permute-start.28 = (f32[64,1152]{1,0:T(8,128)S(1)}, f32[64,1152]{1,0:T(8,128)S(1)}, u32[]{:S(2)}, u32[]{:S(2)}) collective-permute-start(f32[64,1152]{1,0:T(8,128)S(1)} %slice.9), channel_id=1, source_target_pairs={{0,4},{4,0},{8,12},{12,8},{16,20},{20,16},{24,28},{28,24},{1,5},{5... | collective-permute-start | bytes 884744 | tf_op jit(solution)/shard_map/ppermute | solution.py:87
  84.1 11.2 %collective-permute-start.31 = (bf16[64,1152]{1,0:T(8,128)(2,1)S(1)}, bf16[64,1152]{1,0:T(8,128)(2,1)S(1)}, u32[]{:S(2)}, u32[]{:S(2)}) collective-permute-start(bf16[64,1152]{1,0:T(8,128)(2,1)S(1)} %fusion.after.columns), channel_id=1, source_target_pairs={{0,1},{1,2},{2,3},{3,0},{4,5},{5,6},{6,7},{7,4},{8,9},{9,10},{10,1... | collective-permute-start | bytes 442376 | tf_op jit(solution)/shard_map/ppermute | solution.py:92
  85.5 12.9 %collective-permute-start.30 = (bf16[64,1152]{1,0:T(8,128)(2,1)S(1)}, bf16[64,1152]{1,0:T(8,128)(2,1)S(1)}, u32[]{:S(2)}, u32[]{:S(2)}) collective-permute-start(bf16[64,1152]{1,0:T(8,128)(2,1)S(1)} %fusion.after.columns), channel_id=1, source_target_pairs={{0,2},{1,3},{2,0},{3,1},{4,6},{5,7},{6,4},{7,5},{8,10},{9,11},{10,... | collective-permute-start | bytes 442376 | tf_op jit(solution)/shard_map/ppermute | solution.py:92
  88.5 10.8 %collective-permute-start.29 = (bf16[64,1152]{1,0:T(8,128)(2,1)S(1)}, bf16[64,1152]{1,0:T(8,128)(2,1)S(1)}, u32[]{:S(2)}, u32[]{:S(2)}) collective-permute-start(bf16[64,1152]{1,0:T(8,128)(2,1)S(1)} %fusion.after.columns), channel_id=1, source_target_pairs={{0,3},{1,0},{2,1},{3,2},{4,7},{5,4},{6,5},{7,6},{8,11},{9,8},{10,9... | collective-permute-start | bytes 442376 | tf_op jit(solution)/shard_map/ppermute | solution.py:92
  (7 other events, 23.3 us)

commit v4 on v3

--- a/solution.py
+++ b/solution.py
@@ -239,11 +239,15 @@
 
 
 def second_sum(ins, outs):
-    kept, came_a, came_b = ins
     *outs, total = outs
-    sub = came_a.shape[0]
-    total[0:sub, :] = kept[0:sub, :] + came_a[...].astype(F32)
-    total[sub:, :] = kept[sub:, :] + came_b[...].astype(F32)
+    sub = ins[1].shape[0]
+    for at in (0, 1):
+        kept, *others = ins[3 * at : 3 * at + 3]
+        for route, came in enumerate(others):
+            low = 2 * sub * at + route * sub
+            total[low : low + sub, :] = kept[route * sub : (route + 1) * sub, :] + came[
+                ...
+            ].astype(F32)
     rows, width = outs[0].shape
     deal(total, outs, width - 128, total[:, len(outs) * (width - 128) :])
 
@@ -255,51 +259,67 @@
     return total
 
 
-def rotate(ins, outs, images_all):
-    *ins, basis = ins
-    *outs, moments, product = outs
+def prepare(ins, outs, images_all):
     sums = gathered(ins)
+    rows = outs[0].shape[1]
+    outs[0][...] = (sums[:, :rows] / images_all).astype(BF)
+    outs[1][...] = sums[:, rows:]
+
+
+def rotate(ins, outs, spans):
+    columns, basis = ins
+    me = lax.axis_index("grp")
     rows = basis.shape[0]
-    grad_mean = (sums[:, :rows] / images_all).astype(BF)
-    moments[...] = sums[:, rows:]
-    product[...] = jnp.dot(grad_mean, basis[...], preferred_element_type=F32).astype(BF)
-    deal(product, outs, rows)
-
-
-def rescale(ins, outs, positions):
+    groups = len(outs) // len(spans)
+    for step in range(groups):
+        at = pl.multiple_of(lax.rem(me + step, groups) * rows, 128)
+        part = jnp.dot(columns[...], basis[:, pl.ds(at, rows)], preferred_element_type=F32)
+        for c, (low, high) in enumerate(spans):
+            out = outs[groups * c + step]
+            out[...] = part[:, low:high].astype(BF).astype(out.dtype)
+
+
+def rescale(ins, outs, positions, offset):
     *ins, moments, input_eigen = ins
     eigen_out = jnp.sum(moments[...], axis=1, keepdims=True) / positions
-    outs[0][...] = (gathered(ins) / (input_eigen[...] * eigen_out + damping)).astype(BF)
-
-
-def restore_kernel(offset, columns, basis, held, out, *, first, last):
-    width = columns.shape[1]
-    block = basis[:, pl.ds(pl.multiple_of(offset[0], 128), width)]
-    part = jnp.dot(block, columns[...].T, preferred_element_type=F32)
-    if not first:
-        part = part + held[...]
-    out[...] = part.T.astype(BF) if last else part
-
-
-def restore(offset, columns, basis, held, last):
-    first = held is None
-    rows, width = basis.shape[0], columns.shape[0]
-    near = pl.BlockSpec(memory_space=pltpu.VMEM)
-    kernel = functools.partial(restore_kernel, first=first, last=last)
-    if first:
-        held = jnp.zeros((8, 128), F32)
-    return pl.pallas_call(
-        kernel,
-        in_specs=[pl.BlockSpec(memory_space=pltpu.SMEM), near, near, near],
-        out_specs=near,
-        out_shape=jax.ShapeDtypeStruct((width, rows), BF)
-        if last
-        else jax.ShapeDtypeStruct((rows, width), F32),
-        compiler_params=pltpu.CompilerParams(vmem_limit_bytes=8 << 20),
-        cost_estimate=pl.CostEstimate(
-            flops=2 * columns.size * rows, bytes_accessed=2 * columns.size, transcendentals=0
-        ),
-    )(offset.reshape(1), columns, basis, held)
+    chunk = outs[0].shape[1]
+    scale = input_eigen[:, offset : offset + chunk] * eigen_out + damping
+    outs[0][...] = (gathered(ins) / scale).astype(BF)
+
+
+def turn_back(ins, outs):
+    *near, weights = ins
+    width = near[0].shape[0]
+    total = None
+    for at, block in enumerate(near):
+        part = jnp.dot(
+            weights[:, at * width : (at + 1) * width], block[...], preferred_element_type=F32
+        )
+        total = part if total is None else total + part
+    outs[0][...] = total[:width]
+    outs[1][...] = total[width:]
+
+
+def merge(ins, outs):
+    outs[0][...] = (ins[0][...] + ins[1][...]).astype(BF)
+
+
+def restore(ins, outs, steps, offset, last):
+    *blocks, basis = ins
+    me = lax.axis_index("grp")
+    rows = basis.shape[0]
+    groups = basis.shape[1] // rows
+    total = None
+    if len(blocks) > len(steps):
+        total = blocks.pop()[...]
+    for step, block in zip(steps, blocks):
+        chunk = block.shape[1]
+        at = pl.multiple_of(lax.rem(me - step + groups, groups) * rows + offset, 128)
+        part = jnp.dot(
+            basis[:, pl.ds(at, chunk)], block[...].T, preferred_element_type=F32
+        )
+        total = part if total is None else total + part
+    outs[0][...] = total.T.astype(BF) if last else total
 
 
 def cube(activations, out_grads, input_basis, output_basis, input_eigen):
@@ -318,77 +338,87 @@
     dout_rows = [map_rows(dout_own), map_rows(swap(dout_own, 1))]
     parts = grad_parts(*act_rows, *dout_rows, output_basis)
 
+    both = jnp.concatenate(
+        [lax.dynamic_slice_in_dim(output_basis, r * width, width, 0) for r in (me, me ^ 1)], 0
+    )
+    weights = jnp.concatenate(
+        [
+            lax.dynamic_slice_in_dim(both, (block ^ flip) * width, width, 1)
+            for flip in range(4)
+        ],
+        1,
+    )
+
     sub = width // 4
     wide = groups * own_rows + 128
-    chunks = (0, 1)
     like = jax.ShapeDtypeStruct
-    others = groups - 1
+    grp_types = [F32] + [BF] * (groups - 1)
     came = [
         [parts[4 * c + 1], swap(parts[4 * c], 2), parts[4 * c + 3], swap(parts[4 * c + 2], 4)]
-        for c in chunks
+        for c in (0, 1)
     ]
-    last = ()
-    for c in chunks:
+    basis = load(input_basis, parts[1])
+    sums = ()
+    for c in (0, 1):
         shapes = [like((2 * sub, wide), F32)] + [like((sub, wide), BF)] * 2
-        kept, s_a, s_b = last = stage(first_sum, shapes, came[c], last[1:2])
+        kept, s_a, s_b = sums = stage(first_sum, shapes, came[c], sums[1:2])
         came[c] = [kept, swap(s_a, 4), swap(s_b, 2)]
-    last = ()
-    for c in chunks:
-        shapes = [like((2 * sub, own_rows + 128), t) for t in [F32] + [BF] * others]
-        last = stage(second_sum, shapes + [like((2 * sub, wide), F32)], came[c], last[1:2])
-        came[c] = [last[0]] + [shift(last[step], step) for step in range(1, groups)]
-        if c == 0:
-            basis = load(input_basis, last[1])
-    last = ()
-    for c in chunks:
-        shapes = [like((2 * sub, own_rows), t) for t in [F32] + [BF] * others]
-        shapes += [like((2 * sub, 128), F32), like((2 * sub, groups * own_rows), BF)]
-        last = stage(
-            functools.partial(rotate, images_all=images_all),
-            shapes,
-            came[c] + [basis],
-            last[1:2],
-            4 * sub * input_basis.size,
-        )
-        came[c] = [last[0]] + [shift(last[step], step) for step in range(1, groups)]
-        came[c].append(last[groups])
-        if c == 0:
-            basis = load(input_basis, last[1])
-
-    both = jnp.concatenate(
-        [lax.dynamic_slice_in_dim(output_basis, r * width, width, 0) for r in (me, me ^ 1)], 0
-    )
-    near = []
-    last = ()
-    for c in chunks:
-        last = stage(
-            functools.partial(rescale, positions=images_all * side * side),
-            [like((2 * sub, own_rows), BF)],
-            came[c] + [input_eigen.reshape(1, own_rows)],
-            last,
-        )
-        near.append(last + [swap(last[0], bit) for bit in (2, 4, 6)])
-    turned_back = 0
-    for chunk in chunks:
-        columns = [
-            lax.dynamic_slice_in_dim(both, (block ^ flip) * width + 2 * sub * chunk, 2 * sub, 1)
-            for flip in range(4)
-        ]
-        turned_back = turned_back + jnp.dot(
-            jnp.concatenate(columns, 1),
-            jnp.concatenate(near[chunk], 0),
-            preferred_element_type=F32,
-        )
-    own = (turned_back[:width] + swap(turned_back[width:], 1)).astype(BF)
-
-    grp = lax.axis_index("grp")
-    basis = load(input_basis, own)
-    update = None
-    for step in range(groups):
-        held = own if step == 0 else shift(own, step)
-        at = lax.rem(grp - step + groups, groups) * own_rows
-        update = restore(at, held, basis, update, step == groups - 1)
-    return update.T
+    shapes = [like((width, own_rows + 128), t) for t in grp_types] + [like((width, wide), F32)]
+    own, *others = stage(second_sum, shapes, came[0] + came[1])[:groups]
+    came = [own] + [shift(value, step + 1) for step, value in enumerate(others)]
+    columns, moments = stage(
+        functools.partial(prepare, images_all=images_all),
+        [like((width, own_rows), BF), like((width, 128), F32)],
+        came,
+    )
+
+    spans = ((0, own_rows // 128 // 2 * 128), (own_rows // 128 // 2 * 128, own_rows))
+    eigen_row = input_eigen.reshape(1, own_rows)
+    rotated = stage(
+        functools.partial(rotate, spans=spans),
+        [like((width, high - low), t) for low, high in spans for t in grp_types],
+        [columns, basis],
+        (),
+        2 * width * input_basis.size,
+    )
+    came = []
+    for c in (0, 1):
+        own, *others = rotated[groups * c : groups * (c + 1)]
+        came.append([own] + [shift(value, step + 1) for step, value in enumerate(others)])
+    near, scaled = [], ()
+    for (low, high), values in zip(spans, came):
+        scaled = stage(
+            functools.partial(rescale, positions=images_all * side * side, offset=low),
+            [like((width, high - low), BF)],
+            values + [moments, eigen_row],
+            scaled,
+        )
+        near.append(scaled + [swap(scaled[0], bit) for bit in (2, 4, 6)])
+    held = []
+    for (low, high), values in zip(spans, near):
+        mine, sent = stage(
+            turn_back,
+            [like((width, high - low), F32)] * 2,
+            values + [weights],
+            (),
+            16 * width * width * (high - low),
+        )
+        (own,) = stage(merge, [like((width, high - low), BF)], [mine, swap(sent, 1)])
+        held.append([own] + [shift(own, step) for step in range(1, groups)])
+
+    update = []
+    calls = [(0, (0,)), (1, (0,)), (0, tuple(range(1, groups)))]
+    calls += [(1, (step,)) for step in range(1, groups)]
+    for at, (c, steps) in enumerate(calls):
+        last = at == len(calls) - 1
+        update = stage(
+            functools.partial(restore, steps=steps, offset=spans[c][0], last=last),
+            [like((width, own_rows), BF) if last else like((own_rows, width), F32)],
+            [held[c][step] for step in steps] + update + [basis],
+            (),
+            2 * len(steps) * width * own_rows * held[c][0].shape[1],
+        )
+    return update[0].T
 
 
 def solution(mesh):

time: 101 us -> 94.7 us (0.938)
  Pallas kernels: 29.7 us -> 16.8 us
  waiting for transfers between devices: 22 us -> 29.5 us
  local copies, waits for them, and re-layouts: 8.39 us -> 6.57 us
  starting transfers between devices: 39.6 us -> 41 us
    pallas_call x3 -> x1, Pallas kernels: 15 us -> 5.09 us  [load(): pl.pallas_call(load_kernel, in_specs=[pl.BlockSpec(memory_space=pl.ANY),...]
    ppermute x15, waiting for transfers between devices: 4.54 us -> 9.2 us  [shift(): return lax.ppermute(value, 'grp', [(i, (i + step) % n) for i in range(n)])]
    pallas_call x4 -> x0, Pallas kernels: 4.09 us -> none  [restore(): pl.pallas_call(kernel, in_specs=[pl.BlockSpec(memory_space=pltpu.SMEM), n...]
    ppermute x17 -> x18, waiting for transfers between devices: 17.4 us -> 20.3 us  [swap(): lax.ppermute(value, 'dp', [(i, i ^ bit) for i in range(lax.axis_size('dp'...]
    unnamed x14 -> x6, local copies, waits for them, and re-layouts: 2.84 us -> 1.04 us
    ppermute x15, starting transfers between devices: 22.5 us -> 24.2 us  [shift(): return lax.ppermute(value, 'grp', [(i, (i + step) % n) for i in range(n)])]
    pallas_call x8 -> x17, Pallas kernels: 7.61 us -> 8.74 us  [stage(): pl.pallas_call(body, in_specs=[near] * (len(operands) + len(after)), out_...]
    ppermute x17 -> x18, starting transfers between devices: 17 us -> 16.8 us  [swap(): lax.ppermute(value, 'dp', [(i, i ^ bit) for i in range(lax.axis_size('dp'...]
  transfers between devices with their start and end apart: 32 -> 33, of which waited for: 12 -> 16; matrix products, arithmetic and copies ran while one was open for 5% -> 5% of each run, Pallas kernels for 25% -> 10%
where the time goes in v4:
time: 94.7 us; the launch traced here: 94.4 us
  starting transfers between devices  41 us (43%)
  waiting for transfers between devices  29.5 us (31%)
  Pallas kernels  16.8 us (18%)
  local copies, waits for them, and re-layouts  6.57 us (7%)
    ppermute x15, starting transfers between devices, shift(): return lax.ppermute(value, 'grp', [(i, (i + step) % n) for i in range(n)])  24.2 us
    ppermute x18, waiting for transfers between devices, swap(): lax.ppermute(value, 'dp', [(i, i ^ bit) for i in range(lax.axis_size('dp'...  20.3 us
    ppermute x18, starting transfers between devices, swap(): lax.ppermute(value, 'dp', [(i, i ^ bit) for i in range(lax.axis_size('dp'...  16.8 us
    ppermute x15, waiting for transfers between devices, shift(): return lax.ppermute(value, 'grp', [(i, (i + step) % n) for i in range(n)])  9.2 us
    pallas_call x17, Pallas kernels, stage(): pl.pallas_call(body, in_specs=[near] * (len(operands) + len(after)), out_...  8.74 us
    pallas_call x1, Pallas kernels, load(): pl.pallas_call(load_kernel, in_specs=[pl.BlockSpec(memory_space=pl.ANY),...  5.09 us
    pad x4, local copies, waits for them, and re-layouts, map_rows(): jnp.pad(images, ((0, 16 - h), (0, 16 - w), (0, 0), (0, 0)))  3.85 us
    pallas_call x1, Pallas kernels, grad_parts(): pl.pallas_call(grad_kernel, in_specs=[near] * 5, out_specs=[near] * 8, ou...  2.98 us
  transfers between devices with their start and end apart: 33, of which 16 were waited for; matrix products, arithmetic and copies ran while one was open for 5% of the time, Pallas kernels for 10%

profile of v4, /device:TPU:0, one launch (start us, length us, event | category | flops | bytes accessed | tf_op | source)
XLA Modules:
  0.0 94.4 jit_solution(12953352630659626024)
XLA Ops:
  0.5 1.5 %pad.13 = bf16[16,16,2,512]{3,2,1,0:T(2,128)(2,1)S(1)} pad(bf16[14,14,2,512]{3,2,1,0:T(2,128)(2,1)} %bitcast.4, bf16[]{:T(256)} %constant.3.clone.1), padding=0_2x0_2x0_0x0_0 | pad | bytes 925698 | tf_op jit(solution)/shard_map/jit(_pad)/pad | solution.py:170
  2.0 1.5 %pad.15 = bf16[16,16,2,512]{3,2,1,0:T(2,128)(2,1)S(1)} pad(bf16[14,14,2,512]{3,2,1,0:T(2,128)(2,1)} %bitcast.6, bf16[]{:T(256)} %constant.3.clone.1), padding=0_2x0_2x0_0x0_0 | pad | bytes 925698 | tf_op jit(solution)/shard_map/jit(_pad)/pad | solution.py:170
  6.3 3.0 %shard_map.55 = (bf16[32,4736]{1,0:T(8,128)(2,1)S(1)}, bf16[32,4736]{1,0:T(8,128)(2,1)S(1)}, bf16[32,4736]{1,0:T(8,128)(2,1)S(1)}, bf16[32,4736]{1,0:T(8,128)(2,...) custom-call(bf16[512,512]{1,0:T(8,128)(2,1)S(1)} %reshape.15.act_a, ...), custom_call_target="tpu_custom_call" | custom-call | flops 2415919104 | bytes 4456448 | tf_op jit(solution)/shard_map/pallas_call | solution.py:148
  9.3 3.0 %collective-permute-start.2 = (bf16[32,4736]{1,0:T(8,128)(2,1)S(1)}, bf16[32,4736]{1,0:T(8,128)(2,1)S(1)}, u32[]{:S(2)}, u32[]{:S(2)}) collective-permute-start(bf16[32,4736]{1,0:T(8,128)(2,1)S(1)} %get-tuple-element.38), channel_id=1, source_target_pairs={{0,8},{4,12},{8,0},{12,4},{16,24},{20,28},{24,16},{28,20},{1,9},{5... | collective-permute-start | bytes 909320 | tf_op jit(solution)/shard_map/ppermute | solution.py:87
  12.3 1.5 %collective-permute-start.3 = (bf16[32,4736]{1,0:T(8,128)(2,1)S(1)}, bf16[32,4736]{1,0:T(8,128)(2,1)S(1)}, u32[]{:S(2)}, u32[]{:S(2)}) collective-permute-start(bf16[32,4736]{1,0:T(8,128)(2,1)S(1)} %get-tuple-element.40), channel_id=1, source_target_pairs={{0,16},{4,20},{8,24},{12,28},{16,0},{20,4},{24,8},{28,12},{1,17},{... | collective-permute-start | bytes 909320 | tf_op jit(solution)/shard_map/ppermute | solution.py:87
  14.4 5.9 %collective-permute-done.2.refs_1_ = bf16[32,4736]{1,0:T(8,128)(2,1)S(1)} collective-permute-done((bf16[32,4736]{1,0:T(8,128)(2,1)S(1)}, bf16[32,4736]{1,0:T(8,128)(2,1)S(1)}, u32[]{:S(2)}, u32[]{:S(2)}) %collective-permute-start.2) | collective-permute-done | bytes 303136 | tf_op jit(solution)/shard_map/ppermute | solution.py:87
  20.3 2.1 %collective-permute-done.3.refs_3_ = bf16[32,4736]{1,0:T(8,128)(2,1)S(1)} collective-permute-done((bf16[32,4736]{1,0:T(8,128)(2,1)S(1)}, bf16[32,4736]{1,0:T(8,128)(2,1)S(1)}, u32[]{:S(2)}, u32[]{:S(2)}) %collective-permute-start.3) | collective-permute-done | bytes 303136 | tf_op jit(solution)/shard_map/ppermute | solution.py:87
  22.5 1.6 %collective-permute-start.4 = (bf16[16,4736]{1,0:T(8,128)(2,1)S(1)}, bf16[16,4736]{1,0:T(8,128)(2,1)S(1)}, u32[]{:S(2)}, u32[]{:S(2)}) collective-permute-start(bf16[16,4736]{1,0:T(8,128)(2,1)S(1)} %get-tuple-element.42.refs_4_), channel_id=1, source_target_pairs={{0,16},{4,20},{8,24},{12,28},{16,0},{20,4},{24,8},{28,12},{1,17},{... | collective-permute-start | bytes 454664 | tf_op jit(solution)/shard_map/ppermute | solution.py:87
  24.1 2.1 %collective-permute-done.6.refs_1_ = bf16[32,4736]{1,0:T(8,128)(2,1)S(1)} collective-permute-done((bf16[32,4736]{1,0:T(8,128)(2,1)S(1)}, bf16[32,4736]{1,0:T(8,128)(2,1)S(1)}, u32[]{:S(2)}, u32[]{:S(2)}) %collective-permute-start.6) | collective-permute-done | bytes 303136 | tf_op jit(solution)/shard_map/ppermute | solution.py:87
  26.2 2.7 %collective-permute-done.7.refs_3_ = bf16[32,4736]{1,0:T(8,128)(2,1)S(1)} collective-permute-done((bf16[32,4736]{1,0:T(8,128)(2,1)S(1)}, bf16[32,4736]{1,0:T(8,128)(2,1)S(1)}, u32[]{:S(2)}, u32[]{:S(2)}) %collective-permute-start.7) | collective-permute-done | bytes 303136 | tf_op jit(solution)/shard_map/ppermute | solution.py:87
  29.0 1.6 %collective-permute-start.8 = (bf16[16,4736]{1,0:T(8,128)(2,1)S(1)}, bf16[16,4736]{1,0:T(8,128)(2,1)S(1)}, u32[]{:S(2)}, u32[]{:S(2)}) collective-permute-start(bf16[16,4736]{1,0:T(8,128)(2,1)S(1)} %get-tuple-element.49), channel_id=1, source_target_pairs={{0,16},{4,20},{8,24},{12,28},{16,0},{20,4},{24,8},{28,12},{1,17},{... | collective-permute-start | bytes 454664 | tf_op jit(solution)/shard_map/ppermute | solution.py:87
  31.1 1.5 %collective-permute-start.5 = (bf16[16,4736]{1,0:T(8,128)(2,1)S(1)}, bf16[16,4736]{1,0:T(8,128)(2,1)S(1)}, u32[]{:S(2)}, u32[]{:S(2)}) collective-permute-start(bf16[16,4736]{1,0:T(8,128)(2,1)S(1)} %get-tuple-element.43), channel_id=1, source_target_pairs={{0,8},{4,12},{8,0},{12,4},{16,24},{20,28},{24,16},{28,20},{1,9},{5... | collective-permute-start | bytes 454664 | tf_op jit(solution)/shard_map/ppermute | solution.py:87
  32.6 1.6 %collective-permute-done.8.refs_4_ = bf16[16,4736]{1,0:T(8,128)(2,1)S(1)} collective-permute-done((bf16[16,4736]{1,0:T(8,128)(2,1)S(1)}, bf16[16,4736]{1,0:T(8,128)(2,1)S(1)}, u32[]{:S(2)}, u32[]{:S(2)}) %collective-permute-start.8) | collective-permute-done | bytes 151584 | tf_op jit(solution)/shard_map/ppermute | solution.py:87
  34.2 1.5 %collective-permute-done.9.refs_5_ = bf16[16,4736]{1,0:T(8,128)(2,1)S(1)} collective-permute-done((bf16[16,4736]{1,0:T(8,128)(2,1)S(1)}, bf16[16,4736]{1,0:T(8,128)(2,1)S(1)}, u32[]{:S(2)}, u32[]{:S(2)}) %collective-permute-start.9) | collective-permute-done | bytes 151584 | tf_op jit(solution)/shard_map/ppermute | solution.py:87
  35.8 1.6 %collective-permute-done.5.refs_2_ = bf16[16,4736]{1,0:T(8,128)(2,1)S(1)} collective-permute-done((bf16[16,4736]{1,0:T(8,128)(2,1)S(1)}, bf16[16,4736]{1,0:T(8,128)(2,1)S(1)}, u32[]{:S(2)}, u32[]{:S(2)}) %collective-permute-start.5) | collective-permute-done | bytes 151584 | tf_op jit(solution)/shard_map/ppermute | solution.py:87
  38.7 1.6 %collective-permute-start.10 = (bf16[64,1280]{1,0:T(8,128)(2,1)S(1)}, bf16[64,1280]{1,0:T(8,128)(2,1)S(1)}, u32[]{:S(2)}, u32[]{:S(2)}) collective-permute-start(bf16[64,1280]{1,0:T(8,128)(2,1)S(1)} %get-tuple-element.52), channel_id=1, source_target_pairs={{0,1},{1,2},{2,3},{3,0},{4,5},{5,6},{6,7},{7,4},{8,9},{9,10},{10,1... | collective-permute-start | bytes 491528 | tf_op jit(solution)/shard_map/ppermute | solution.py:92
  40.2 2.6 %collective-permute-start.11 = (bf16[64,1280]{1,0:T(8,128)(2,1)S(1)}, bf16[64,1280]{1,0:T(8,128)(2,1)S(1)}, u32[]{:S(2)}, u32[]{:S(2)}) collective-permute-start(bf16[64,1280]{1,0:T(8,128)(2,1)S(1)} %get-tuple-element.53), channel_id=1, source_target_pairs={{0,2},{1,3},{2,0},{3,1},{4,6},{5,7},{6,4},{7,5},{8,10},{9,11},{10,... | collective-permute-start | bytes 491528 | tf_op jit(solution)/shard_map/ppermute | solution.py:92
  42.8 1.3 %collective-permute-start.12 = (bf16[64,1280]{1,0:T(8,128)(2,1)S(1)}, bf16[64,1280]{1,0:T(8,128)(2,1)S(1)}, u32[]{:S(2)}, u32[]{:S(2)}) collective-permute-start(bf16[64,1280]{1,0:T(8,128)(2,1)S(1)} %get-tuple-element.54), channel_id=1, source_target_pairs={{0,3},{1,0},{2,1},{3,2},{4,7},{5,4},{6,5},{7,6},{8,11},{9,8},{10,9... | collective-permute-start | bytes 491528 | tf_op jit(solution)/shard_map/ppermute | solution.py:92
  44.2 5.1 %shard_map.60.refs_1_.refs_2_.refs_4_ = bf16[1152,4608]{1,0:T(8,128)(2,1)S(1)} custom-call(bf16[1152,4608]{1,0:T(8,128)(2,1)} %source.1, bf16[32,4736]{1,0:T(8,128)(2,1)} %copy-done), custom_call_target="tpu_custom_call" | custom-call | bytes 21233664 | tf_op jit(solution)/shard_map/pallas_call | solution.py:189
  49.3 2.2 %collective-permute-done.11.refs_2_ = bf16[64,1280]{1,0:T(8,128)(2,1)S(1)} collective-permute-done((bf16[64,1280]{1,0:T(8,128)(2,1)S(1)}, bf16[64,1280]{1,0:T(8,128)(2,1)S(1)}, u32[]{:S(2)}, u32[]{:S(2)}) %collective-permute-start.11) | collective-permute-done | bytes 163872 | tf_op jit(solution)/shard_map/ppermute | solution.py:92
  51.6 1.8 %shard_map.61 = (f32[64,512]{1,0:T(8,128)S(1)}, bf16[64,512]{1,0:T(8,128)(2,1)S(1)}, bf16[64,512]{1,0:T(8,128)(2,1)S(1)}, bf16[64,512]{1,0:T(8,128)(2,1)S(1)}, f...) custom-call(bf16[64,1152]{1,0:T(8,128)(2,1)S(1)} %get-tuple-element., ...), custom_call_target="tpu_custom_call" | custom-call | flops 679477248 | bytes 10764288 | tf_op jit(solution)/shard_map/pallas_call | solution.py:206
  53.4 2.8 %collective-permute-start.16 = (bf16[64,512]{1,0:T(8,128)(2,1)S(1)}, bf16[64,512]{1,0:T(8,128)(2,1)S(1)}, u32[]{:S(2)}, u32[]{:S(2)}) collective-permute-start(bf16[64,512]{1,0:T(8,128)(2,1)S(1)} %get-tuple-element.62), channel_id=1, source_target_pairs={{0,1},{1,2},{2,3},{3,0},{4,5},{5,6},{6,7},{7,4},{8,9},{9,10},{10,1... | collective-permute-start | bytes 196616 | tf_op jit(solution)/shard_map/ppermute | solution.py:92
  56.2 1.6 %collective-permute-start.17 = (bf16[64,512]{1,0:T(8,128)(2,1)S(1)}, bf16[64,512]{1,0:T(8,128)(2,1)S(1)}, u32[]{:S(2)}, u32[]{:S(2)}) collective-permute-start(bf16[64,512]{1,0:T(8,128)(2,1)S(1)} %get-tuple-element.63), channel_id=1, source_target_pairs={{0,2},{1,3},{2,0},{3,1},{4,6},{5,7},{6,4},{7,5},{8,10},{9,11},{10,... | collective-permute-start | bytes 196616 | tf_op jit(solution)/shard_map/ppermute | solution.py:92
  65.1 1.3 %collective-permute-done.13.refs_1_ = bf16[64,640]{1,0:T(8,128)(2,1)S(1)} collective-permute-done((bf16[64,640]{1,0:T(8,128)(2,1)S(1)}, bf16[64,640]{1,0:T(8,128)(2,1)S(1)}, u32[]{:S(2)}, u32[]{:S(2)}) %collective-permute-start.13) | collective-permute-done | bytes 81952 | tf_op jit(solution)/shard_map/ppermute | solution.py:92
  66.5 1.6 %collective-permute-start.28 = (bf16[64,512]{1,0:T(8,128)(2,1)S(1)}, bf16[64,512]{1,0:T(8,128)(2,1)S(1)}, u32[]{:S(2)}, u32[]{:S(2)}) collective-permute-start(bf16[64,512]{1,0:T(8,128)(2,1)S(1)} %shard_map.62.refs_6_.refs_0_), channel_id=1, source_target_pairs={{0,24},{4,28},{8,16},{12,20},{16,8},{20,12},{24,0},{28,4},{1,25},{... | collective-permute-start | bytes 196616 | tf_op jit(solution)/shard_map/ppermute | solution.py:87
  70.8 2.0 %collective-permute-start.21 = (bf16[64,640]{1,0:T(8,128)(2,1)S(1)}, bf16[64,640]{1,0:T(8,128)(2,1)S(1)}, u32[]{:S(2)}, u32[]{:S(2)}) collective-permute-start(bf16[64,640]{1,0:T(8,128)(2,1)S(1)} %shard_map.63.refs_0_), channel_id=1, source_target_pairs={{0,24},{4,28},{8,16},{12,20},{16,8},{20,12},{24,0},{28,4},{1,25},{... | collective-permute-start | bytes 245768 | tf_op jit(solution)/shard_map/ppermute | solution.py:87
  74.6 1.5 %collective-permute-done.21.refs_3_ = bf16[64,640]{1,0:T(8,128)(2,1)S(1)} collective-permute-done((bf16[64,640]{1,0:T(8,128)(2,1)S(1)}, bf16[64,640]{1,0:T(8,128)(2,1)S(1)}, u32[]{:S(2)}, u32[]{:S(2)}) %collective-permute-start.21) | collective-permute-done | bytes 81952 | tf_op jit(solution)/shard_map/ppermute | solution.py:87
  76.6 2.7 %collective-permute-start.30 = (bf16[64,512]{1,0:T(8,128)(2,1)S(1)}, bf16[64,512]{1,0:T(8,128)(2,1)S(1)}, u32[]{:S(2)}, u32[]{:S(2)}) collective-permute-start(bf16[64,512]{1,0:T(8,128)(2,1)S(1)} %shard_map.67.refs_0_), channel_id=1, source_target_pairs={{0,1},{1,2},{2,3},{3,0},{4,5},{5,6},{6,7},{7,4},{8,9},{9,10},{10,1... | collective-permute-start | bytes 196616 | tf_op jit(solution)/shard_map/ppermute | solution.py:92
  79.4 2.8 %collective-permute-start.32 = (bf16[64,512]{1,0:T(8,128)(2,1)S(1)}, bf16[64,512]{1,0:T(8,128)(2,1)S(1)}, u32[]{:S(2)}, u32[]{:S(2)}) collective-permute-start(bf16[64,512]{1,0:T(8,128)(2,1)S(1)} %shard_map.67.refs_0_), channel_id=1, source_target_pairs={{0,3},{1,0},{2,1},{3,2},{4,7},{5,4},{6,5},{7,6},{8,11},{9,8},{10,9... | collective-permute-start | bytes 196616 | tf_op jit(solution)/shard_map/ppermute | solution.py:92
  82.3 2.0 %collective-permute-start.24 = (bf16[64,640]{1,0:T(8,128)(2,1)S(1)}, bf16[64,640]{1,0:T(8,128)(2,1)S(1)}, u32[]{:S(2)}, u32[]{:S(2)}) collective-permute-start(bf16[64,640]{1,0:T(8,128)(2,1)S(1)} %shard_map.65.refs_0_), channel_id=1, source_target_pairs={{0,2},{1,3},{2,0},{3,1},{4,6},{5,7},{6,4},{7,5},{8,10},{9,11},{10,... | collective-permute-start | bytes 245768 | tf_op jit(solution)/shard_map/ppermute | solution.py:92
  84.3 1.8 %collective-permute-start.23 = (bf16[64,640]{1,0:T(8,128)(2,1)S(1)}, bf16[64,640]{1,0:T(8,128)(2,1)S(1)}, u32[]{:S(2)}, u32[]{:S(2)}) collective-permute-start(bf16[64,640]{1,0:T(8,128)(2,1)S(1)} %shard_map.65.refs_0_), channel_id=1, source_target_pairs={{0,3},{1,0},{2,1},{3,2},{4,7},{5,4},{6,5},{7,6},{8,11},{9,8},{10,9... | collective-permute-start | bytes 245768 | tf_op jit(solution)/shard_map/ppermute | solution.py:92
  90.0 2.6 %collective-permute-done.24.refs_0_ = bf16[64,640]{1,0:T(8,128)(2,1)S(1)} collective-permute-done((bf16[64,640]{1,0:T(8,128)(2,1)S(1)}, bf16[64,640]{1,0:T(8,128)(2,1)S(1)}, u32[]{:S(2)}, u32[]{:S(2)}) %collective-permute-start.24) | collective-permute-done | bytes 81952 | tf_op jit(solution)/shard_map/ppermute | solution.py:92
  (71 shorter events, 23.9 us)
Async XLA Ops:
  0.0 3.9 %collective-permute-start = (bf16[14,14,2,512]{3,2,1,0:T(2,128)(2,1)}, bf16[14,14,2,512]{3,2,1,0:T(2,128)(2,1)S(1)}, u32[]{:S(2)}, u32[]{:S(2)}) collective-permute-start(bf16[14,14,2,512]{3,2,1,0:T(2,128)(2,1)} %bitcast.3), channel_id=1, source_target_pairs={{0,4},{4,0},{8,12},{12,8},{16,20},{20,16},{24,28},{28,24},{1,5},{5... | collective-permute-start | bytes 1204232 | tf_op jit(solution)/shard_map/ppermute | solution.py:87
  0.5 4.1 %collective-permute-start.1 = (bf16[14,14,2,512]{3,2,1,0:T(2,128)(2,1)}, bf16[14,14,2,512]{3,2,1,0:T(2,128)(2,1)S(1)}, u32[]{:S(2)}, u32[]{:S(2)}) collective-permute-start(bf16[14,14,2,512]{3,2,1,0:T(2,128)(2,1)} %bitcast.5), channel_id=1, source_target_pairs={{0,4},{4,0},{8,12},{12,8},{16,20},{20,16},{24,28},{28,24},{1,5},{5... | collective-permute-start | bytes 1204232 | tf_op jit(solution)/shard_map/ppermute | solution.py:87
  9.3 11.0 %collective-permute-start.2 = (bf16[32,4736]{1,0:T(8,128)(2,1)S(1)}, bf16[32,4736]{1,0:T(8,128)(2,1)S(1)}, u32[]{:S(2)}, u32[]{:S(2)}) collective-permute-start(bf16[32,4736]{1,0:T(8,128)(2,1)S(1)} %get-tuple-element.38), channel_id=1, source_target_pairs={{0,8},{4,12},{8,0},{12,4},{16,24},{20,28},{24,16},{28,20},{1,9},{5... | collective-permute-start | bytes 909320 | tf_op jit(solution)/shard_map/ppermute | solution.py:87
  12.3 10.1 %collective-permute-start.3 = (bf16[32,4736]{1,0:T(8,128)(2,1)S(1)}, bf16[32,4736]{1,0:T(8,128)(2,1)S(1)}, u32[]{:S(2)}, u32[]{:S(2)}) collective-permute-start(bf16[32,4736]{1,0:T(8,128)(2,1)S(1)} %get-tuple-element.40), channel_id=1, source_target_pairs={{0,16},{4,20},{8,24},{12,28},{16,0},{20,4},{24,8},{28,12},{1,17},{... | collective-permute-start | bytes 909320 | tf_op jit(solution)/shard_map/ppermute | solution.py:87
  13.8 12.4 %collective-permute-start.6 = (bf16[32,4736]{1,0:T(8,128)(2,1)S(1)}, bf16[32,4736]{1,0:T(8,128)(2,1)S(1)}, u32[]{:S(2)}, u32[]{:S(2)}) collective-permute-start(bf16[32,4736]{1,0:T(8,128)(2,1)S(1)} %get-tuple-element.45), channel_id=1, source_target_pairs={{0,8},{4,12},{8,0},{12,4},{16,24},{20,28},{24,16},{28,20},{1,9},{5... | collective-permute-start | bytes 909320 | tf_op jit(solution)/shard_map/ppermute | solution.py:87
  14.3 14.5 %collective-permute-start.7 = (bf16[32,4736]{1,0:T(8,128)(2,1)S(1)}, bf16[32,4736]{1,0:T(8,128)(2,1)S(1)}, u32[]{:S(2)}, u32[]{:S(2)}) collective-permute-start(bf16[32,4736]{1,0:T(8,128)(2,1)S(1)} %get-tuple-element.47), channel_id=1, source_target_pairs={{0,16},{4,20},{8,24},{12,28},{16,0},{20,4},{24,8},{28,12},{1,17},{... | collective-permute-start | bytes 909320 | tf_op jit(solution)/shard_map/ppermute | solution.py:87
  22.5 13.3 %collective-permute-start.4 = (bf16[16,4736]{1,0:T(8,128)(2,1)S(1)}, bf16[16,4736]{1,0:T(8,128)(2,1)S(1)}, u32[]{:S(2)}, u32[]{:S(2)}) collective-permute-start(bf16[16,4736]{1,0:T(8,128)(2,1)S(1)} %get-tuple-element.42.refs_4_), channel_id=1, source_target_pairs={{0,16},{4,20},{8,24},{12,28},{16,0},{20,4},{24,8},{28,12},{1,17},{... | collective-permute-start | bytes 454664 | tf_op jit(solution)/shard_map/ppermute | solution.py:87
  29.0 5.3 %collective-permute-start.8 = (bf16[16,4736]{1,0:T(8,128)(2,1)S(1)}, bf16[16,4736]{1,0:T(8,128)(2,1)S(1)}, u32[]{:S(2)}, u32[]{:S(2)}) collective-permute-start(bf16[16,4736]{1,0:T(8,128)(2,1)S(1)} %get-tuple-element.49), channel_id=1, source_target_pairs={{0,16},{4,20},{8,24},{12,28},{16,0},{20,4},{24,8},{28,12},{1,17},{... | collective-permute-start | bytes 454664 | tf_op jit(solution)/shard_map/ppermute | solution.py:87
  30.6 5.2 %collective-permute-start.9 = (bf16[16,4736]{1,0:T(8,128)(2,1)S(1)}, bf16[16,4736]{1,0:T(8,128)(2,1)S(1)}, u32[]{:S(2)}, u32[]{:S(2)}) collective-permute-start(bf16[16,4736]{1,0:T(8,128)(2,1)S(1)} %get-tuple-element.50), channel_id=1, source_target_pairs={{0,8},{4,12},{8,0},{12,4},{16,24},{20,28},{24,16},{28,20},{1,9},{5... | collective-permute-start | bytes 454664 | tf_op jit(solution)/shard_map/ppermute | solution.py:87
  31.1 6.3 %collective-permute-start.5 = (bf16[16,4736]{1,0:T(8,128)(2,1)S(1)}, bf16[16,4736]{1,0:T(8,128)(2,1)S(1)}, u32[]{:S(2)}, u32[]{:S(2)}) collective-permute-start(bf16[16,4736]{1,0:T(8,128)(2,1)S(1)} %get-tuple-element.43), channel_id=1, source_target_pairs={{0,8},{4,12},{8,0},{12,4},{16,24},{20,28},{24,16},{28,20},{1,9},{5... | collective-permute-start | bytes 454664 | tf_op jit(solution)/shard_map/ppermute | solution.py:87
  38.7 10.6 %collective-permute-start.10 = (bf16[64,1280]{1,0:T(8,128)(2,1)S(1)}, bf16[64,1280]{1,0:T(8,128)(2,1)S(1)}, u32[]{:S(2)}, u32[]{:S(2)}) collective-permute-start(bf16[64,1280]{1,0:T(8,128)(2,1)S(1)} %get-tuple-element.52), channel_id=1, source_target_pairs={{0,1},{1,2},{2,3},{3,0},{4,5},{5,6},{6,7},{7,4},{8,9},{9,10},{10,1... | collective-permute-start | bytes 491528 | tf_op jit(solution)/shard_map/ppermute | solution.py:92
  40.2 11.2 %collective-permute-start.11 = (bf16[64,1280]{1,0:T(8,128)(2,1)S(1)}, bf16[64,1280]{1,0:T(8,128)(2,1)S(1)}, u32[]{:S(2)}, u32[]{:S(2)}) collective-permute-start(bf16[64,1280]{1,0:T(8,128)(2,1)S(1)} %get-tuple-element.53), channel_id=1, source_target_pairs={{0,2},{1,3},{2,0},{3,1},{4,6},{5,7},{6,4},{7,5},{8,10},{9,11},{10,... | collective-permute-start | bytes 491528 | tf_op jit(solution)/shard_map/ppermute | solution.py:92
  42.8 8.7 %collective-permute-start.12 = (bf16[64,1280]{1,0:T(8,128)(2,1)S(1)}, bf16[64,1280]{1,0:T(8,128)(2,1)S(1)}, u32[]{:S(2)}, u32[]{:S(2)}) collective-permute-start(bf16[64,1280]{1,0:T(8,128)(2,1)S(1)} %get-tuple-element.54), channel_id=1, source_target_pairs={{0,3},{1,0},{2,1},{3,2},{4,7},{5,4},{6,5},{7,6},{8,11},{9,8},{10,9... | collective-permute-start | bytes 491528 | tf_op jit(solution)/shard_map/ppermute | solution.py:92
  53.4 8.7 %collective-permute-start.16 = (bf16[64,512]{1,0:T(8,128)(2,1)S(1)}, bf16[64,512]{1,0:T(8,128)(2,1)S(1)}, u32[]{:S(2)}, u32[]{:S(2)}) collective-permute-start(bf16[64,512]{1,0:T(8,128)(2,1)S(1)} %get-tuple-element.62), channel_id=1, source_target_pairs={{0,1},{1,2},{2,3},{3,0},{4,5},{5,6},{6,7},{7,4},{8,9},{9,10},{10,1... | collective-permute-start | bytes 196616 | tf_op jit(solution)/shard_map/ppermute | solution.py:92
  56.2 7.2 %collective-permute-start.17 = (bf16[64,512]{1,0:T(8,128)(2,1)S(1)}, bf16[64,512]{1,0:T(8,128)(2,1)S(1)}, u32[]{:S(2)}, u32[]{:S(2)}) collective-permute-start(bf16[64,512]{1,0:T(8,128)(2,1)S(1)} %get-tuple-element.63), channel_id=1, source_target_pairs={{0,2},{1,3},{2,0},{3,1},{4,6},{5,7},{6,4},{7,5},{8,10},{9,11},{10,... | collective-permute-start | bytes 196616 | tf_op jit(solution)/shard_map/ppermute | solution.py:92
  57.9 6.4 %collective-permute-start.18 = (bf16[64,512]{1,0:T(8,128)(2,1)S(1)}, bf16[64,512]{1,0:T(8,128)(2,1)S(1)}, u32[]{:S(2)}, u32[]{:S(2)}) collective-permute-start(bf16[64,512]{1,0:T(8,128)(2,1)S(1)} %get-tuple-element.64), channel_id=1, source_target_pairs={{0,3},{1,0},{2,1},{3,2},{4,7},{5,4},{6,5},{7,6},{8,11},{9,8},{10,9... | collective-permute-start | bytes 196616 | tf_op jit(solution)/shard_map/ppermute | solution.py:92
  59.6 6.9 %collective-permute-start.13 = (bf16[64,640]{1,0:T(8,128)(2,1)S(1)}, bf16[64,640]{1,0:T(8,128)(2,1)S(1)}, u32[]{:S(2)}, u32[]{:S(2)}) collective-permute-start(bf16[64,640]{1,0:T(8,128)(2,1)S(1)} %get-tuple-element.57), channel_id=1, source_target_pairs={{0,1},{1,2},{2,3},{3,0},{4,5},{5,6},{6,7},{7,4},{8,9},{9,10},{10,1... | collective-permute-start | bytes 245768 | tf_op jit(solution)/shard_map/ppermute | solution.py:92
  60.9 8.3 %collective-permute-start.14 = (bf16[64,640]{1,0:T(8,128)(2,1)S(1)}, bf16[64,640]{1,0:T(8,128)(2,1)S(1)}, u32[]{:S(2)}, u32[]{:S(2)}) collective-permute-start(bf16[64,640]{1,0:T(8,128)(2,1)S(1)} %get-tuple-element.58), channel_id=1, source_target_pairs={{0,2},{1,3},{2,0},{3,1},{4,6},{5,7},{6,4},{7,5},{8,10},{9,11},{10,... | collective-permute-start | bytes 245768 | tf_op jit(solution)/shard_map/ppermute | solution.py:92
  62.1 7.0 %collective-permute-start.15 = (bf16[64,640]{1,0:T(8,128)(2,1)S(1)}, bf16[64,640]{1,0:T(8,128)(2,1)S(1)}, u32[]{:S(2)}, u32[]{:S(2)}) collective-permute-start(bf16[64,640]{1,0:T(8,128)(2,1)S(1)} %get-tuple-element.59), channel_id=1, source_target_pairs={{0,3},{1,0},{2,1},{3,2},{4,7},{5,4},{6,5},{7,6},{8,11},{9,8},{10,9... | collective-permute-start | bytes 245768 | tf_op jit(solution)/shard_map/ppermute | solution.py:92
  64.4 6.4 %collective-permute-start.26 = (bf16[64,512]{1,0:T(8,128)(2,1)S(1)}, bf16[64,512]{1,0:T(8,128)(2,1)S(1)}, u32[]{:S(2)}, u32[]{:S(2)}) collective-permute-start(bf16[64,512]{1,0:T(8,128)(2,1)S(1)} %shard_map.62.refs_6_.refs_0_), channel_id=1, source_target_pairs={{0,8},{4,12},{8,0},{12,4},{16,24},{20,28},{24,16},{28,20},{1,9},{5... | collective-permute-start | bytes 196616 | tf_op jit(solution)/shard_map/ppermute | solution.py:87
  65.0 7.9 %collective-permute-start.27 = (bf16[64,512]{1,0:T(8,128)(2,1)S(1)}, bf16[64,512]{1,0:T(8,128)(2,1)S(1)}, u32[]{:S(2)}, u32[]{:S(2)}) collective-permute-start(bf16[64,512]{1,0:T(8,128)(2,1)S(1)} %shard_map.62.refs_6_.refs_0_), channel_id=1, source_target_pairs={{0,16},{4,20},{8,24},{12,28},{16,0},{20,4},{24,8},{28,12},{1,17},{... | collective-permute-start | bytes 196616 | tf_op jit(solution)/shard_map/ppermute | solution.py:87
  66.5 6.4 %collective-permute-start.28 = (bf16[64,512]{1,0:T(8,128)(2,1)S(1)}, bf16[64,512]{1,0:T(8,128)(2,1)S(1)}, u32[]{:S(2)}, u32[]{:S(2)}) collective-permute-start(bf16[64,512]{1,0:T(8,128)(2,1)S(1)} %shard_map.62.refs_6_.refs_0_), channel_id=1, source_target_pairs={{0,24},{4,28},{8,16},{12,20},{16,8},{20,12},{24,0},{28,4},{1,25},{... | collective-permute-start | bytes 196616 | tf_op jit(solution)/shard_map/ppermute | solution.py:87
  69.3 4.5 %collective-permute-start.19 = (bf16[64,640]{1,0:T(8,128)(2,1)S(1)}, bf16[64,640]{1,0:T(8,128)(2,1)S(1)}, u32[]{:S(2)}, u32[]{:S(2)}) collective-permute-start(bf16[64,640]{1,0:T(8,128)(2,1)S(1)} %shard_map.63.refs_0_), channel_id=1, source_target_pairs={{0,8},{4,12},{8,0},{12,4},{16,24},{20,28},{24,16},{28,20},{1,9},{5... | collective-permute-start | bytes 245768 | tf_op jit(solution)/shard_map/ppermute | solution.py:87
  70.0 4.7 %collective-permute-start.20 = (bf16[64,640]{1,0:T(8,128)(2,1)S(1)}, bf16[64,640]{1,0:T(8,128)(2,1)S(1)}, u32[]{:S(2)}, u32[]{:S(2)}) collective-permute-start(bf16[64,640]{1,0:T(8,128)(2,1)S(1)} %shard_map.63.refs_0_), channel_id=1, source_target_pairs={{0,16},{4,20},{8,24},{12,28},{16,0},{20,4},{24,8},{28,12},{1,17},{... | collective-permute-start | bytes 245768 | tf_op jit(solution)/shard_map/ppermute | solution.py:87
  70.8 5.3 %collective-permute-start.21 = (bf16[64,640]{1,0:T(8,128)(2,1)S(1)}, bf16[64,640]{1,0:T(8,128)(2,1)S(1)}, u32[]{:S(2)}, u32[]{:S(2)}) collective-permute-start(bf16[64,640]{1,0:T(8,128)(2,1)S(1)} %shard_map.63.refs_0_), channel_id=1, source_target_pairs={{0,24},{4,28},{8,16},{12,20},{16,8},{20,12},{24,0},{28,4},{1,25},{... | collective-permute-start | bytes 245768 | tf_op jit(solution)/shard_map/ppermute | solution.py:87
  76.5 5.8 %collective-permute-start.22 = (f32[64,640]{1,0:T(8,128)S(1)}, f32[64,640]{1,0:T(8,128)S(1)}, u32[]{:S(2)}, u32[]{:S(2)}) collective-permute-start(f32[64,640]{1,0:T(8,128)S(1)} %get-tuple-element.66), channel_id=1, source_target_pairs={{0,4},{4,0},{8,12},{12,8},{16,20},{20,16},{24,28},{28,24},{1,5},{5... | collective-permute-start | bytes 491528 | tf_op jit(solution)/shard_map/ppermute | solution.py:87
  76.6 7.7 %collective-permute-start.30 = (bf16[64,512]{1,0:T(8,128)(2,1)S(1)}, bf16[64,512]{1,0:T(8,128)(2,1)S(1)}, u32[]{:S(2)}, u32[]{:S(2)}) collective-permute-start(bf16[64,512]{1,0:T(8,128)(2,1)S(1)} %shard_map.67.refs_0_), channel_id=1, source_target_pairs={{0,1},{1,2},{2,3},{3,0},{4,5},{5,6},{6,7},{7,4},{8,9},{9,10},{10,1... | collective-permute-start | bytes 196616 | tf_op jit(solution)/shard_map/ppermute | solution.py:92
  79.3 7.8 %collective-permute-start.31 = (bf16[64,512]{1,0:T(8,128)(2,1)S(1)}, bf16[64,512]{1,0:T(8,128)(2,1)S(1)}, u32[]{:S(2)}, u32[]{:S(2)}) collective-permute-start(bf16[64,512]{1,0:T(8,128)(2,1)S(1)} %shard_map.67.refs_0_), channel_id=1, source_target_pairs={{0,2},{1,3},{2,0},{3,1},{4,6},{5,7},{6,4},{7,5},{8,10},{9,11},{10,... | collective-permute-start | bytes 196616 | tf_op jit(solution)/shard_map/ppermute | solution.py:92
  79.4 7.7 %collective-permute-start.32 = (bf16[64,512]{1,0:T(8,128)(2,1)S(1)}, bf16[64,512]{1,0:T(8,128)(2,1)S(1)}, u32[]{:S(2)}, u32[]{:S(2)}) collective-permute-start(bf16[64,512]{1,0:T(8,128)(2,1)S(1)} %shard_map.67.refs_0_), channel_id=1, source_target_pairs={{0,3},{1,0},{2,1},{3,2},{4,7},{5,4},{6,5},{7,6},{8,11},{9,8},{10,9... | collective-permute-start | bytes 196616 | tf_op jit(solution)/shard_map/ppermute | solution.py:92
  82.3 7.2 %collective-permute-start.25 = (bf16[64,640]{1,0:T(8,128)(2,1)S(1)}, bf16[64,640]{1,0:T(8,128)(2,1)S(1)}, u32[]{:S(2)}, u32[]{:S(2)}) collective-permute-start(bf16[64,640]{1,0:T(8,128)(2,1)S(1)} %shard_map.65.refs_0_), channel_id=1, source_target_pairs={{0,1},{1,2},{2,3},{3,0},{4,5},{5,6},{6,7},{7,4},{8,9},{9,10},{10,1... | collective-permute-start | bytes 245768 | tf_op jit(solution)/shard_map/ppermute | solution.py:92
  82.3 10.3 %collective-permute-start.24 = (bf16[64,640]{1,0:T(8,128)(2,1)S(1)}, bf16[64,640]{1,0:T(8,128)(2,1)S(1)}, u32[]{:S(2)}, u32[]{:S(2)}) collective-permute-start(bf16[64,640]{1,0:T(8,128)(2,1)S(1)} %shard_map.65.refs_0_), channel_id=1, source_target_pairs={{0,2},{1,3},{2,0},{3,1},{4,6},{5,7},{6,4},{7,5},{8,10},{9,11},{10,... | collective-permute-start | bytes 245768 | tf_op jit(solution)/shard_map/ppermute | solution.py:92
  84.3 8.8 %collective-permute-start.23 = (bf16[64,640]{1,0:T(8,128)(2,1)S(1)}, bf16[64,640]{1,0:T(8,128)(2,1)S(1)}, u32[]{:S(2)}, u32[]{:S(2)}) collective-permute-start(bf16[64,640]{1,0:T(8,128)(2,1)S(1)} %shard_map.65.refs_0_), channel_id=1, source_target_pairs={{0,3},{1,0},{2,1},{3,2},{4,7},{5,4},{6,5},{7,6},{8,11},{9,8},{10,9... | collective-permute-start | bytes 245768 | tf_op jit(solution)/shard_map/ppermute | solution.py:92
  (4 other events, 83.0 us)

commit v5 on v4

--- a/solution.py
+++ b/solution.py
@@ -10,6 +10,7 @@
 damping = 1.0
 BF = jnp.bfloat16
 F32 = jnp.float32
+WORK = [[75000000, 0], [400000000, 1000000000], [75000000, 75000000], [400000000, 0], [30000000, 150000000], [400000000, 1000000000], [400000000, 400000000]]
 LOADS = 8
 
 
@@ -170,6 +171,30 @@
     return jnp.pad(images, ((0, 16 - h), (0, 16 - w), (0, 0), (0, 0))).reshape(256 * n, c)
 
 
+def fetch_kernel(*refs):
+    count = len(refs) // 2
+    sems = refs[-1]
+    copies = [
+        pltpu.make_async_copy(refs[at], refs[count + at], sems.at[at]) for at in range(count)
+    ]
+    for copy in copies:
+        copy.start()
+    for copy in copies:
+        copy.wait()
+
+
+def fetch(values):
+    anywhere = pl.BlockSpec(memory_space=pl.ANY)
+    return pl.pallas_call(
+        fetch_kernel,
+        in_specs=[anywhere] * len(values),
+        out_specs=[anywhere] * len(values),
+        out_shape=[pltpu.VMEM(value.shape, value.dtype) for value in values],
+        scratch_shapes=[pltpu.SemaphoreType.DMA((len(values),))],
+        compiler_params=pltpu.CompilerParams(vmem_limit_bytes=56 << 20),
+    )(*values)
+
+
 def load_kernel(source, after, target, sems):
     del after
     rows = source.shape[0] // LOADS
@@ -209,9 +234,7 @@
         out_specs=[near] * len(out_shape),
         out_shape=out_shape,
         compiler_params=pltpu.CompilerParams(vmem_limit_bytes=8 << 20),
-        cost_estimate=pl.CostEstimate(
-            flops=flops, bytes_accessed=sum(2 * x.size for x in operands), transcendentals=0
-        ),
+        cost_estimate=pl.CostEstimate(flops=flops, bytes_accessed=0, transcendentals=0),
     )(*operands, *after)
     return list(results)
 
@@ -315,11 +338,14 @@
     for step, block in zip(steps, blocks):
         chunk = block.shape[1]
         at = pl.multiple_of(lax.rem(me - step + groups, groups) * rows + offset, 128)
-        part = jnp.dot(
-            basis[:, pl.ds(at, chunk)], block[...].T, preferred_element_type=F32
+        part = lax.dot_general(
+            block[...],
+            basis[:, pl.ds(at, chunk)],
+            (((1,), (1,)), ((), ())),
+            preferred_element_type=F32,
         )
         total = part if total is None else total + part
-    outs[0][...] = total.T.astype(BF) if last else total
+    outs[0][...] = total.astype(outs[0].dtype)
 
 
 def cube(activations, out_grads, input_basis, output_basis, input_eigen):
@@ -332,12 +358,6 @@
     own_rows = input_eigen.shape[0]
     block = (me & 1) * 4 + (me >> 1)
 
-    act_own = activations.transpose(1, 2, 0, 3)
-    dout_own = out_grads.transpose(1, 2, 0, 3)
-    act_rows = [map_rows(act_own), map_rows(swap(act_own, 1))]
-    dout_rows = [map_rows(dout_own), map_rows(swap(dout_own, 1))]
-    parts = grad_parts(*act_rows, *dout_rows, output_basis)
-
     both = jnp.concatenate(
         [lax.dynamic_slice_in_dim(output_basis, r * width, width, 0) for r in (me, me ^ 1)], 0
     )
@@ -349,27 +369,37 @@
         1,
     )
 
+    act_own = activations.transpose(1, 2, 0, 3)
+    dout_own = out_grads.transpose(1, 2, 0, 3)
+    act_near, dout_near, basis_near = fetch([act_own, dout_own, output_basis])
+    act_rows = [map_rows(act_near), map_rows(swap(act_own, 1))]
+    dout_rows = [map_rows(dout_near), map_rows(swap(dout_own, 1))]
+    parts = list(grad_parts(*act_rows, *dout_rows, basis_near))
+
     sub = width // 4
     wide = groups * own_rows + 128
     like = jax.ShapeDtypeStruct
     grp_types = [F32] + [BF] * (groups - 1)
+    parts[1], weights = lax.optimization_barrier((parts[1], weights))
     came = [
         [parts[4 * c + 1], swap(parts[4 * c], 2), parts[4 * c + 3], swap(parts[4 * c + 2], 4)]
         for c in (0, 1)
     ]
-    basis = load(input_basis, parts[1])
+    basis = load(input_basis, parts[0])
     sums = ()
     for c in (0, 1):
         shapes = [like((2 * sub, wide), F32)] + [like((sub, wide), BF)] * 2
-        kept, s_a, s_b = sums = stage(first_sum, shapes, came[c], sums[1:2])
+        kept, s_a, s_b = sums = stage(first_sum, shapes, came[c], sums[1:2], WORK[0][c])
         came[c] = [kept, swap(s_a, 4), swap(s_b, 2)]
     shapes = [like((width, own_rows + 128), t) for t in grp_types] + [like((width, wide), F32)]
-    own, *others = stage(second_sum, shapes, came[0] + came[1])[:groups]
+    own, *others = stage(second_sum, shapes, came[0] + came[1], (), WORK[1][0])[:groups]
     came = [own] + [shift(value, step + 1) for step, value in enumerate(others)]
     columns, moments = stage(
         functools.partial(prepare, images_all=images_all),
         [like((width, own_rows), BF), like((width, 128), F32)],
         came,
+        (),
+        WORK[1][1],
     )
 
     spans = ((0, own_rows // 128 // 2 * 128), (own_rows // 128 // 2 * 128, own_rows))
@@ -379,7 +409,7 @@
         [like((width, high - low), t) for low, high in spans for t in grp_types],
         [columns, basis],
         (),
-        2 * width * input_basis.size,
+        WORK[2][0],
     )
     came = []
     for c in (0, 1):
@@ -392,6 +422,7 @@
             [like((width, high - low), BF)],
             values + [moments, eigen_row],
             scaled,
+            WORK[3][low > 0],
         )
         near.append(scaled + [swap(scaled[0], bit) for bit in (2, 4, 6)])
     held = []
@@ -401,9 +432,9 @@
             [like((width, high - low), F32)] * 2,
             values + [weights],
             (),
-            16 * width * width * (high - low),
-        )
-        (own,) = stage(merge, [like((width, high - low), BF)], [mine, swap(sent, 1)])
+            WORK[4][low > 0],
+        )
+        (own,) = stage(merge, [like((width, high - low), BF)], [mine, swap(sent, 1)], (), WORK[5][low > 0])
         held.append([own] + [shift(own, step) for step in range(1, groups)])
 
     update = []
@@ -413,10 +444,10 @@
         last = at == len(calls) - 1
         update = stage(
             functools.partial(restore, steps=steps, offset=spans[c][0], last=last),
-            [like((width, own_rows), BF) if last else like((own_rows, width), F32)],
+            [like((width, own_rows), BF) if last else like((width, own_rows), F32)],
             [held[c][step] for step in steps] + update + [basis],
             (),
-            2 * len(steps) * width * own_rows * held[c][0].shape[1],
+            len(steps) * WORK[6][c],
         )
     return update[0].T
 

time: 94.7 us -> 92.5 us (0.977)
  local copies, waits for them, and re-layouts: 6.57 us -> 3.51 us
  waiting for transfers between devices: 29.5 us -> 27.4 us
  Pallas kernels: 16.8 us -> 18.4 us
  starting transfers between devices: 41 us -> 42.4 us
    pad x4, local copies, waits for them, and re-layouts: 3.85 us -> 1.82 us  [map_rows(): jnp.pad(images, ((0, 16 - h), (0, 16 - w), (0, 0), (0, 0)))]
    ppermute x18, waiting for transfers between devices: 20.3 us -> 19 us  [swap(): lax.ppermute(value, 'dp', [(i, i ^ bit) for i in range(lax.axis_size('dp'...]
    pallas_call x0 -> x1, Pallas kernels: none -> 1.31 us  [fetch(): pl.pallas_call(fetch_kernel, in_specs=[anywhere] * len(values), out_specs...]
    ppermute x18, starting transfers between devices: 16.8 us -> 18.1 us  [swap(): lax.ppermute(value, 'dp', [(i, i ^ bit) for i in range(lax.axis_size('dp'...]
    unnamed x6 -> x4, local copies, waits for them, and re-layouts: 1.04 us -> 0.01 us
  transfers between devices with their start and end apart: 33 -> 33, of which waited for: 16 -> 15; matrix products, arithmetic and copies ran while one was open for 5% -> 3% of each run, Pallas kernels for 10% -> 12%
where the time goes in v5:
time: 92.5 us; the launch traced here: 92.2 us
  starting transfers between devices  42.4 us (46%)
  waiting for transfers between devices  27.4 us (30%)
  Pallas kernels  18.4 us (20%)
  local copies, waits for them, and re-layouts  3.51 us (4%)
    ppermute x15, starting transfers between devices, shift(): return lax.ppermute(value, 'grp', [(i, (i + step) % n) for i in range(n)])  24.4 us
    ppermute x18, waiting for transfers between devices, swap(): lax.ppermute(value, 'dp', [(i, i ^ bit) for i in range(lax.axis_size('dp'...  19 us
    ppermute x18, starting transfers between devices, swap(): lax.ppermute(value, 'dp', [(i, i ^ bit) for i in range(lax.axis_size('dp'...  18.1 us
    pallas_call x17, Pallas kernels, stage(): pl.pallas_call(body, in_specs=[near] * (len(operands) + len(after)), out_...  8.99 us
    ppermute x15, waiting for transfers between devices, shift(): return lax.ppermute(value, 'grp', [(i, (i + step) % n) for i in range(n)])  8.41 us
    pallas_call x1, Pallas kernels, load(): pl.pallas_call(load_kernel, in_specs=[pl.BlockSpec(memory_space=pl.ANY),...  5.09 us
    pallas_call x1, Pallas kernels, grad_parts(): pl.pallas_call(grad_kernel, in_specs=[near] * 5, out_specs=[near] * 8, ou...  2.99 us
  transfers between devices with their start and end apart: 33, of which 15 were waited for; matrix products, arithmetic and copies ran while one was open for 3% of the time, Pallas kernels for 12%

profile of v5, /device:TPU:0, one launch (start us, length us, event | category | flops | bytes accessed | tf_op | source)
XLA Modules:
  0.0 92.2 jit_solution(9260583226099020601)
XLA Ops:
  4.5 3.0 %shard_map.56 = (bf16[32,4736]{1,0:T(8,128)(2,1)S(1)}, bf16[32,4736]{1,0:T(8,128)(2,1)S(1)}, bf16[32,4736]{1,0:T(8,128)(2,1)S(1)}, bf16[32,4736]{1,0:T(8,128)(2,...) custom-call(bf16[512,512]{1,0:T(8,128)(2,1)S(1)} %reshape.15.act_a, ...), custom_call_target="tpu_custom_call" | custom-call | flops 2415919104 | bytes 4456448 | tf_op jit(solution)/shard_map/pallas_call | solution.py:149
  7.5 3.0 %collective-permute-start.2 = (bf16[32,4736]{1,0:T(8,128)(2,1)S(1)}, bf16[32,4736]{1,0:T(8,128)(2,1)S(1)}, u32[]{:S(2)}, u32[]{:S(2)}) collective-permute-start(bf16[32,4736]{1,0:T(8,128)(2,1)S(1)} %get-tuple-element.47.after), channel_id=1, source_target_pairs={{0,8},{4,12},{8,0},{12,4},{16,24},{20,28},{24,16},{28,20},{1,9},{5... | collective-permute-start | bytes 909320 | tf_op jit(solution)/shard_map/ppermute | solution.py:88
  10.6 1.5 %collective-permute-start.3 = (bf16[32,4736]{1,0:T(8,128)(2,1)S(1)}, bf16[32,4736]{1,0:T(8,128)(2,1)S(1)}, u32[]{:S(2)}, u32[]{:S(2)}) collective-permute-start(bf16[32,4736]{1,0:T(8,128)(2,1)S(1)} %get-tuple-element.49), channel_id=1, source_target_pairs={{0,16},{4,20},{8,24},{12,28},{16,0},{20,4},{24,8},{28,12},{1,17},{... | collective-permute-start | bytes 909320 | tf_op jit(solution)/shard_map/ppermute | solution.py:88
  13.8 4.8 %collective-permute-done.2.refs_1_ = bf16[32,4736]{1,0:T(8,128)(2,1)S(1)} collective-permute-done((bf16[32,4736]{1,0:T(8,128)(2,1)S(1)}, bf16[32,4736]{1,0:T(8,128)(2,1)S(1)}, u32[]{:S(2)}, u32[]{:S(2)}) %collective-permute-start.2) | collective-permute-done | bytes 303136 | tf_op jit(solution)/shard_map/ppermute | solution.py:88
  18.5 2.1 %collective-permute-done.3.refs_3_ = bf16[32,4736]{1,0:T(8,128)(2,1)S(1)} collective-permute-done((bf16[32,4736]{1,0:T(8,128)(2,1)S(1)}, bf16[32,4736]{1,0:T(8,128)(2,1)S(1)}, u32[]{:S(2)}, u32[]{:S(2)}) %collective-permute-start.3) | collective-permute-done | bytes 303136 | tf_op jit(solution)/shard_map/ppermute | solution.py:88
  20.8 1.6 %collective-permute-start.4 = (bf16[16,4736]{1,0:T(8,128)(2,1)S(1)}, bf16[16,4736]{1,0:T(8,128)(2,1)S(1)}, u32[]{:S(2)}, u32[]{:S(2)}) collective-permute-start(bf16[16,4736]{1,0:T(8,128)(2,1)S(1)} %get-tuple-element.51.refs_4_), channel_id=1, source_target_pairs={{0,16},{4,20},{8,24},{12,28},{16,0},{20,4},{24,8},{28,12},{1,17},{... | collective-permute-start | bytes 454664 | tf_op jit(solution)/shard_map/ppermute | solution.py:88
  22.4 2.0 %collective-permute-done.6.refs_1_ = bf16[32,4736]{1,0:T(8,128)(2,1)S(1)} collective-permute-done((bf16[32,4736]{1,0:T(8,128)(2,1)S(1)}, bf16[32,4736]{1,0:T(8,128)(2,1)S(1)}, u32[]{:S(2)}, u32[]{:S(2)}) %collective-permute-start.6) | collective-permute-done | bytes 303136 | tf_op jit(solution)/shard_map/ppermute | solution.py:88
  24.4 2.7 %collective-permute-done.7.refs_3_ = bf16[32,4736]{1,0:T(8,128)(2,1)S(1)} collective-permute-done((bf16[32,4736]{1,0:T(8,128)(2,1)S(1)}, bf16[32,4736]{1,0:T(8,128)(2,1)S(1)}, u32[]{:S(2)}, u32[]{:S(2)}) %collective-permute-start.7) | collective-permute-done | bytes 303136 | tf_op jit(solution)/shard_map/ppermute | solution.py:88
  27.3 1.6 %collective-permute-start.8 = (bf16[16,4736]{1,0:T(8,128)(2,1)S(1)}, bf16[16,4736]{1,0:T(8,128)(2,1)S(1)}, u32[]{:S(2)}, u32[]{:S(2)}) collective-permute-start(bf16[16,4736]{1,0:T(8,128)(2,1)S(1)} %get-tuple-element.58), channel_id=1, source_target_pairs={{0,16},{4,20},{8,24},{12,28},{16,0},{20,4},{24,8},{28,12},{1,17},{... | collective-permute-start | bytes 454664 | tf_op jit(solution)/shard_map/ppermute | solution.py:88
  29.4 1.5 %collective-permute-start.5 = (bf16[16,4736]{1,0:T(8,128)(2,1)S(1)}, bf16[16,4736]{1,0:T(8,128)(2,1)S(1)}, u32[]{:S(2)}, u32[]{:S(2)}) collective-permute-start(bf16[16,4736]{1,0:T(8,128)(2,1)S(1)} %get-tuple-element.52), channel_id=1, source_target_pairs={{0,8},{4,12},{8,0},{12,4},{16,24},{20,28},{24,16},{28,20},{1,9},{5... | collective-permute-start | bytes 454664 | tf_op jit(solution)/shard_map/ppermute | solution.py:88
  30.9 1.6 %collective-permute-done.8.refs_4_ = bf16[16,4736]{1,0:T(8,128)(2,1)S(1)} collective-permute-done((bf16[16,4736]{1,0:T(8,128)(2,1)S(1)}, bf16[16,4736]{1,0:T(8,128)(2,1)S(1)}, u32[]{:S(2)}, u32[]{:S(2)}) %collective-permute-start.8) | collective-permute-done | bytes 151584 | tf_op jit(solution)/shard_map/ppermute | solution.py:88
  32.5 1.5 %collective-permute-done.9.refs_5_ = bf16[16,4736]{1,0:T(8,128)(2,1)S(1)} collective-permute-done((bf16[16,4736]{1,0:T(8,128)(2,1)S(1)}, bf16[16,4736]{1,0:T(8,128)(2,1)S(1)}, u32[]{:S(2)}, u32[]{:S(2)}) %collective-permute-start.9) | collective-permute-done | bytes 151584 | tf_op jit(solution)/shard_map/ppermute | solution.py:88
  34.0 1.6 %collective-permute-done.5.refs_2_ = bf16[16,4736]{1,0:T(8,128)(2,1)S(1)} collective-permute-done((bf16[16,4736]{1,0:T(8,128)(2,1)S(1)}, bf16[16,4736]{1,0:T(8,128)(2,1)S(1)}, u32[]{:S(2)}, u32[]{:S(2)}) %collective-permute-start.5) | collective-permute-done | bytes 151584 | tf_op jit(solution)/shard_map/ppermute | solution.py:88
  36.9 1.6 %collective-permute-start.10 = (bf16[64,1280]{1,0:T(8,128)(2,1)S(1)}, bf16[64,1280]{1,0:T(8,128)(2,1)S(1)}, u32[]{:S(2)}, u32[]{:S(2)}) collective-permute-start(bf16[64,1280]{1,0:T(8,128)(2,1)S(1)} %get-tuple-element.61), channel_id=1, source_target_pairs={{0,1},{1,2},{2,3},{3,0},{4,5},{5,6},{6,7},{7,4},{8,9},{9,10},{10,1... | collective-permute-start | bytes 491528 | tf_op jit(solution)/shard_map/ppermute | solution.py:93
  38.5 2.6 %collective-permute-start.11 = (bf16[64,1280]{1,0:T(8,128)(2,1)S(1)}, bf16[64,1280]{1,0:T(8,128)(2,1)S(1)}, u32[]{:S(2)}, u32[]{:S(2)}) collective-permute-start(bf16[64,1280]{1,0:T(8,128)(2,1)S(1)} %get-tuple-element.62), channel_id=1, source_target_pairs={{0,2},{1,3},{2,0},{3,1},{4,6},{5,7},{6,4},{7,5},{8,10},{9,11},{10,... | collective-permute-start | bytes 491528 | tf_op jit(solution)/shard_map/ppermute | solution.py:93
  41.1 1.3 %collective-permute-start.12 = (bf16[64,1280]{1,0:T(8,128)(2,1)S(1)}, bf16[64,1280]{1,0:T(8,128)(2,1)S(1)}, u32[]{:S(2)}, u32[]{:S(2)}) collective-permute-start(bf16[64,1280]{1,0:T(8,128)(2,1)S(1)} %get-tuple-element.63), channel_id=1, source_target_pairs={{0,3},{1,0},{2,1},{3,2},{4,7},{5,4},{6,5},{7,6},{8,11},{9,8},{10,9... | collective-permute-start | bytes 491528 | tf_op jit(solution)/shard_map/ppermute | solution.py:93
  42.5 5.1 %shard_map.61.refs_1_.refs_2_.refs_4_ = bf16[1152,4608]{1,0:T(8,128)(2,1)S(1)} custom-call(bf16[1152,4608]{1,0:T(8,128)(2,1)} %source.1, bf16[32,4736]{1,0:T(8,128)(2,1)} %copy-done), custom_call_target="tpu_custom_call" | custom-call | bytes 21233664 | tf_op jit(solution)/shard_map/pallas_call | solution.py:214
  47.6 2.2 %collective-permute-done.11.refs_2_ = bf16[64,1280]{1,0:T(8,128)(2,1)S(1)} collective-permute-done((bf16[64,1280]{1,0:T(8,128)(2,1)S(1)}, bf16[64,1280]{1,0:T(8,128)(2,1)S(1)}, u32[]{:S(2)}, u32[]{:S(2)}) %collective-permute-start.11) | collective-permute-done | bytes 163872 | tf_op jit(solution)/shard_map/ppermute | solution.py:93
  49.9 1.8 %shard_map.62 = (f32[64,512]{1,0:T(8,128)S(1)}, bf16[64,512]{1,0:T(8,128)(2,1)S(1)}, bf16[64,512]{1,0:T(8,128)(2,1)S(1)}, bf16[64,512]{1,0:T(8,128)(2,1)S(1)}, f...) custom-call(bf16[64,1152]{1,0:T(8,128)(2,1)S(1)} %get-tuple-element., ...), custom_call_target="tpu_custom_call" | custom-call | flops 75000000 | tf_op jit(solution)/shard_map/pallas_call | solution.py:231
  51.7 2.7 %collective-permute-start.16 = (bf16[64,512]{1,0:T(8,128)(2,1)S(1)}, bf16[64,512]{1,0:T(8,128)(2,1)S(1)}, u32[]{:S(2)}, u32[]{:S(2)}) collective-permute-start(bf16[64,512]{1,0:T(8,128)(2,1)S(1)} %get-tuple-element.71), channel_id=1, source_target_pairs={{0,1},{1,2},{2,3},{3,0},{4,5},{5,6},{6,7},{7,4},{8,9},{9,10},{10,1... | collective-permute-start | bytes 196616 | tf_op jit(solution)/shard_map/ppermute | solution.py:93
  54.4 1.6 %collective-permute-start.17 = (bf16[64,512]{1,0:T(8,128)(2,1)S(1)}, bf16[64,512]{1,0:T(8,128)(2,1)S(1)}, u32[]{:S(2)}, u32[]{:S(2)}) collective-permute-start(bf16[64,512]{1,0:T(8,128)(2,1)S(1)} %get-tuple-element.72), channel_id=1, source_target_pairs={{0,2},{1,3},{2,0},{3,1},{4,6},{5,7},{6,4},{7,5},{8,10},{9,11},{10,... | collective-permute-start | bytes 196616 | tf_op jit(solution)/shard_map/ppermute | solution.py:93
  59.4 1.6 %collective-permute-start.15 = (bf16[64,640]{1,0:T(8,128)(2,1)S(1)}, bf16[64,640]{1,0:T(8,128)(2,1)S(1)}, u32[]{:S(2)}, u32[]{:S(2)}) collective-permute-start(bf16[64,640]{1,0:T(8,128)(2,1)S(1)} %get-tuple-element.68), channel_id=1, source_target_pairs={{0,3},{1,0},{2,1},{3,2},{4,7},{5,4},{6,5},{7,6},{8,11},{9,8},{10,9... | collective-permute-start | bytes 245768 | tf_op jit(solution)/shard_map/ppermute | solution.py:93
  61.0 1.7 %collective-permute-done.17.refs_2_ = bf16[64,512]{1,0:T(8,128)(2,1)S(1)} collective-permute-done((bf16[64,512]{1,0:T(8,128)(2,1)S(1)}, bf16[64,512]{1,0:T(8,128)(2,1)S(1)}, u32[]{:S(2)}, u32[]{:S(2)}) %collective-permute-start.17) | collective-permute-done | bytes 65568 | tf_op jit(solution)/shard_map/ppermute | solution.py:93
  64.5 2.9 %collective-permute-start.28 = (bf16[64,512]{1,0:T(8,128)(2,1)S(1)}, bf16[64,512]{1,0:T(8,128)(2,1)S(1)}, u32[]{:S(2)}, u32[]{:S(2)}) collective-permute-start(bf16[64,512]{1,0:T(8,128)(2,1)S(1)} %shard_map.63.refs_6_.refs_0_), channel_id=1, source_target_pairs={{0,24},{4,28},{8,16},{12,20},{16,8},{20,12},{24,0},{28,4},{1,25},{... | collective-permute-start | bytes 196616 | tf_op jit(solution)/shard_map/ppermute | solution.py:88
  68.7 2.4 %collective-permute-start.21 = (bf16[64,640]{1,0:T(8,128)(2,1)S(1)}, bf16[64,640]{1,0:T(8,128)(2,1)S(1)}, u32[]{:S(2)}, u32[]{:S(2)}) collective-permute-start(bf16[64,640]{1,0:T(8,128)(2,1)S(1)} %shard_map.64.refs_0_), channel_id=1, source_target_pairs={{0,24},{4,28},{8,16},{12,20},{16,8},{20,12},{24,0},{28,4},{1,25},{... | collective-permute-start | bytes 245768 | tf_op jit(solution)/shard_map/ppermute | solution.py:88
  72.5 1.6 %collective-permute-done.21.refs_3_ = bf16[64,640]{1,0:T(8,128)(2,1)S(1)} collective-permute-done((bf16[64,640]{1,0:T(8,128)(2,1)S(1)}, bf16[64,640]{1,0:T(8,128)(2,1)S(1)}, u32[]{:S(2)}, u32[]{:S(2)}) %collective-permute-start.21) | collective-permute-done | bytes 81952 | tf_op jit(solution)/shard_map/ppermute | solution.py:88
  74.5 2.5 %collective-permute-start.30 = (bf16[64,512]{1,0:T(8,128)(2,1)S(1)}, bf16[64,512]{1,0:T(8,128)(2,1)S(1)}, u32[]{:S(2)}, u32[]{:S(2)}) collective-permute-start(bf16[64,512]{1,0:T(8,128)(2,1)S(1)} %shard_map.68.refs_0_), channel_id=1, source_target_pairs={{0,1},{1,2},{2,3},{3,0},{4,5},{5,6},{6,7},{7,4},{8,9},{9,10},{10,1... | collective-permute-start | bytes 196616 | tf_op jit(solution)/shard_map/ppermute | solution.py:93
  77.3 2.8 %collective-permute-start.32 = (bf16[64,512]{1,0:T(8,128)(2,1)S(1)}, bf16[64,512]{1,0:T(8,128)(2,1)S(1)}, u32[]{:S(2)}, u32[]{:S(2)}) collective-permute-start(bf16[64,512]{1,0:T(8,128)(2,1)S(1)} %shard_map.68.refs_0_), channel_id=1, source_target_pairs={{0,3},{1,0},{2,1},{3,2},{4,7},{5,4},{6,5},{7,6},{8,11},{9,8},{10,9... | collective-permute-start | bytes 196616 | tf_op jit(solution)/shard_map/ppermute | solution.py:93
  80.7 1.8 %collective-permute-start.24 = (bf16[64,640]{1,0:T(8,128)(2,1)S(1)}, bf16[64,640]{1,0:T(8,128)(2,1)S(1)}, u32[]{:S(2)}, u32[]{:S(2)}) collective-permute-start(bf16[64,640]{1,0:T(8,128)(2,1)S(1)} %shard_map.66.refs_0_), channel_id=1, source_target_pairs={{0,2},{1,3},{2,0},{3,1},{4,6},{5,7},{6,4},{7,5},{8,10},{9,11},{10,... | collective-permute-start | bytes 245768 | tf_op jit(solution)/shard_map/ppermute | solution.py:93
  83.1 2.0 %collective-permute-start.23 = (bf16[64,640]{1,0:T(8,128)(2,1)S(1)}, bf16[64,640]{1,0:T(8,128)(2,1)S(1)}, u32[]{:S(2)}, u32[]{:S(2)}) collective-permute-start(bf16[64,640]{1,0:T(8,128)(2,1)S(1)} %shard_map.66.refs_0_), channel_id=1, source_target_pairs={{0,3},{1,0},{2,1},{3,2},{4,7},{5,4},{6,5},{7,6},{8,11},{9,8},{10,9... | collective-permute-start | bytes 245768 | tf_op jit(solution)/shard_map/ppermute | solution.py:93
  86.3 1.6 %collective-permute-done.25.refs_0_ = bf16[64,640]{1,0:T(8,128)(2,1)S(1)} collective-permute-done((bf16[64,640]{1,0:T(8,128)(2,1)S(1)}, bf16[64,640]{1,0:T(8,128)(2,1)S(1)}, u32[]{:S(2)}, u32[]{:S(2)}) %collective-permute-start.25) | collective-permute-done | bytes 81952 | tf_op jit(solution)/shard_map/ppermute | solution.py:93
  88.5 1.9 %collective-permute-done.24.refs_0_ = bf16[64,640]{1,0:T(8,128)(2,1)S(1)} collective-permute-done((bf16[64,640]{1,0:T(8,128)(2,1)S(1)}, bf16[64,640]{1,0:T(8,128)(2,1)S(1)}, u32[]{:S(2)}, u32[]{:S(2)}) %collective-permute-start.24) | collective-permute-done | bytes 81952 | tf_op jit(solution)/shard_map/ppermute | solution.py:93
  (70 shorter events, 21.7 us)
Async XLA Ops:
  0.0 3.2 %collective-permute-start = (bf16[14,14,2,512]{3,2,1,0:T(2,128)(2,1)}, bf16[14,14,2,512]{3,2,1,0:T(2,128)(2,1)S(1)}, u32[]{:S(2)}, u32[]{:S(2)}) collective-permute-start(bf16[14,14,2,512]{3,2,1,0:T(2,128)(2,1)} %bitcast.3), channel_id=1, source_target_pairs={{0,4},{4,0},{8,12},{12,8},{16,20},{20,16},{24,28},{28,24},{1,5},{5... | collective-permute-start | bytes 1204232 | tf_op jit(solution)/shard_map/ppermute | solution.py:88
  0.5 3.4 %collective-permute-start.1 = (bf16[14,14,2,512]{3,2,1,0:T(2,128)(2,1)}, bf16[14,14,2,512]{3,2,1,0:T(2,128)(2,1)S(1)}, u32[]{:S(2)}, u32[]{:S(2)}) collective-permute-start(bf16[14,14,2,512]{3,2,1,0:T(2,128)(2,1)} %bitcast.5), channel_id=1, source_target_pairs={{0,4},{4,0},{8,12},{12,8},{16,20},{20,16},{24,28},{28,24},{1,5},{5... | collective-permute-start | bytes 1204232 | tf_op jit(solution)/shard_map/ppermute | solution.py:88
  7.5 11.0 %collective-permute-start.2 = (bf16[32,4736]{1,0:T(8,128)(2,1)S(1)}, bf16[32,4736]{1,0:T(8,128)(2,1)S(1)}, u32[]{:S(2)}, u32[]{:S(2)}) collective-permute-start(bf16[32,4736]{1,0:T(8,128)(2,1)S(1)} %get-tuple-element.47.after), channel_id=1, source_target_pairs={{0,8},{4,12},{8,0},{12,4},{16,24},{20,28},{24,16},{28,20},{1,9},{5... | collective-permute-start | bytes 909320 | tf_op jit(solution)/shard_map/ppermute | solution.py:88
  10.6 10.1 %collective-permute-start.3 = (bf16[32,4736]{1,0:T(8,128)(2,1)S(1)}, bf16[32,4736]{1,0:T(8,128)(2,1)S(1)}, u32[]{:S(2)}, u32[]{:S(2)}) collective-permute-start(bf16[32,4736]{1,0:T(8,128)(2,1)S(1)} %get-tuple-element.49), channel_id=1, source_target_pairs={{0,16},{4,20},{8,24},{12,28},{16,0},{20,4},{24,8},{28,12},{1,17},{... | collective-permute-start | bytes 909320 | tf_op jit(solution)/shard_map/ppermute | solution.py:88
  12.1 12.3 %collective-permute-start.6 = (bf16[32,4736]{1,0:T(8,128)(2,1)S(1)}, bf16[32,4736]{1,0:T(8,128)(2,1)S(1)}, u32[]{:S(2)}, u32[]{:S(2)}) collective-permute-start(bf16[32,4736]{1,0:T(8,128)(2,1)S(1)} %get-tuple-element.54), channel_id=1, source_target_pairs={{0,8},{4,12},{8,0},{12,4},{16,24},{20,28},{24,16},{28,20},{1,9},{5... | collective-permute-start | bytes 909320 | tf_op jit(solution)/shard_map/ppermute | solution.py:88
  12.6 14.5 %collective-permute-start.7 = (bf16[32,4736]{1,0:T(8,128)(2,1)S(1)}, bf16[32,4736]{1,0:T(8,128)(2,1)S(1)}, u32[]{:S(2)}, u32[]{:S(2)}) collective-permute-start(bf16[32,4736]{1,0:T(8,128)(2,1)S(1)} %get-tuple-element.56), channel_id=1, source_target_pairs={{0,16},{4,20},{8,24},{12,28},{16,0},{20,4},{24,8},{28,12},{1,17},{... | collective-permute-start | bytes 909320 | tf_op jit(solution)/shard_map/ppermute | solution.py:88
  20.8 13.3 %collective-permute-start.4 = (bf16[16,4736]{1,0:T(8,128)(2,1)S(1)}, bf16[16,4736]{1,0:T(8,128)(2,1)S(1)}, u32[]{:S(2)}, u32[]{:S(2)}) collective-permute-start(bf16[16,4736]{1,0:T(8,128)(2,1)S(1)} %get-tuple-element.51.refs_4_), channel_id=1, source_target_pairs={{0,16},{4,20},{8,24},{12,28},{16,0},{20,4},{24,8},{28,12},{1,17},{... | collective-permute-start | bytes 454664 | tf_op jit(solution)/shard_map/ppermute | solution.py:88
  27.3 5.3 %collective-permute-start.8 = (bf16[16,4736]{1,0:T(8,128)(2,1)S(1)}, bf16[16,4736]{1,0:T(8,128)(2,1)S(1)}, u32[]{:S(2)}, u32[]{:S(2)}) collective-permute-start(bf16[16,4736]{1,0:T(8,128)(2,1)S(1)} %get-tuple-element.58), channel_id=1, source_target_pairs={{0,16},{4,20},{8,24},{12,28},{16,0},{20,4},{24,8},{28,12},{1,17},{... | collective-permute-start | bytes 454664 | tf_op jit(solution)/shard_map/ppermute | solution.py:88
  28.9 5.2 %collective-permute-start.9 = (bf16[16,4736]{1,0:T(8,128)(2,1)S(1)}, bf16[16,4736]{1,0:T(8,128)(2,1)S(1)}, u32[]{:S(2)}, u32[]{:S(2)}) collective-permute-start(bf16[16,4736]{1,0:T(8,128)(2,1)S(1)} %get-tuple-element.59), channel_id=1, source_target_pairs={{0,8},{4,12},{8,0},{12,4},{16,24},{20,28},{24,16},{28,20},{1,9},{5... | collective-permute-start | bytes 454664 | tf_op jit(solution)/shard_map/ppermute | solution.py:88
  29.4 6.3 %collective-permute-start.5 = (bf16[16,4736]{1,0:T(8,128)(2,1)S(1)}, bf16[16,4736]{1,0:T(8,128)(2,1)S(1)}, u32[]{:S(2)}, u32[]{:S(2)}) collective-permute-start(bf16[16,4736]{1,0:T(8,128)(2,1)S(1)} %get-tuple-element.52), channel_id=1, source_target_pairs={{0,8},{4,12},{8,0},{12,4},{16,24},{20,28},{24,16},{28,20},{1,9},{5... | collective-permute-start | bytes 454664 | tf_op jit(solution)/shard_map/ppermute | solution.py:88
  36.9 10.6 %collective-permute-start.10 = (bf16[64,1280]{1,0:T(8,128)(2,1)S(1)}, bf16[64,1280]{1,0:T(8,128)(2,1)S(1)}, u32[]{:S(2)}, u32[]{:S(2)}) collective-permute-start(bf16[64,1280]{1,0:T(8,128)(2,1)S(1)} %get-tuple-element.61), channel_id=1, source_target_pairs={{0,1},{1,2},{2,3},{3,0},{4,5},{5,6},{6,7},{7,4},{8,9},{9,10},{10,1... | collective-permute-start | bytes 491528 | tf_op jit(solution)/shard_map/ppermute | solution.py:93
  38.5 11.2 %collective-permute-start.11 = (bf16[64,1280]{1,0:T(8,128)(2,1)S(1)}, bf16[64,1280]{1,0:T(8,128)(2,1)S(1)}, u32[]{:S(2)}, u32[]{:S(2)}) collective-permute-start(bf16[64,1280]{1,0:T(8,128)(2,1)S(1)} %get-tuple-element.62), channel_id=1, source_target_pairs={{0,2},{1,3},{2,0},{3,1},{4,6},{5,7},{6,4},{7,5},{8,10},{9,11},{10,... | collective-permute-start | bytes 491528 | tf_op jit(solution)/shard_map/ppermute | solution.py:93
  41.1 8.7 %collective-permute-start.12 = (bf16[64,1280]{1,0:T(8,128)(2,1)S(1)}, bf16[64,1280]{1,0:T(8,128)(2,1)S(1)}, u32[]{:S(2)}, u32[]{:S(2)}) collective-permute-start(bf16[64,1280]{1,0:T(8,128)(2,1)S(1)} %get-tuple-element.63), channel_id=1, source_target_pairs={{0,3},{1,0},{2,1},{3,2},{4,7},{5,4},{6,5},{7,6},{8,11},{9,8},{10,9... | collective-permute-start | bytes 491528 | tf_op jit(solution)/shard_map/ppermute | solution.py:93
  51.7 7.7 %collective-permute-start.16 = (bf16[64,512]{1,0:T(8,128)(2,1)S(1)}, bf16[64,512]{1,0:T(8,128)(2,1)S(1)}, u32[]{:S(2)}, u32[]{:S(2)}) collective-permute-start(bf16[64,512]{1,0:T(8,128)(2,1)S(1)} %get-tuple-element.71), channel_id=1, source_target_pairs={{0,1},{1,2},{2,3},{3,0},{4,5},{5,6},{6,7},{7,4},{8,9},{9,10},{10,1... | collective-permute-start | bytes 196616 | tf_op jit(solution)/shard_map/ppermute | solution.py:93
  54.4 8.3 %collective-permute-start.17 = (bf16[64,512]{1,0:T(8,128)(2,1)S(1)}, bf16[64,512]{1,0:T(8,128)(2,1)S(1)}, u32[]{:S(2)}, u32[]{:S(2)}) collective-permute-start(bf16[64,512]{1,0:T(8,128)(2,1)S(1)} %get-tuple-element.72), channel_id=1, source_target_pairs={{0,2},{1,3},{2,0},{3,1},{4,6},{5,7},{6,4},{7,5},{8,10},{9,11},{10,... | collective-permute-start | bytes 196616 | tf_op jit(solution)/shard_map/ppermute | solution.py:93
  56.0 7.7 %collective-permute-start.18 = (bf16[64,512]{1,0:T(8,128)(2,1)S(1)}, bf16[64,512]{1,0:T(8,128)(2,1)S(1)}, u32[]{:S(2)}, u32[]{:S(2)}) collective-permute-start(bf16[64,512]{1,0:T(8,128)(2,1)S(1)} %get-tuple-element.73), channel_id=1, source_target_pairs={{0,3},{1,0},{2,1},{3,2},{4,7},{5,4},{6,5},{7,6},{8,11},{9,8},{10,9... | collective-permute-start | bytes 196616 | tf_op jit(solution)/shard_map/ppermute | solution.py:93
  56.8 7.7 %collective-permute-start.13 = (bf16[64,640]{1,0:T(8,128)(2,1)S(1)}, bf16[64,640]{1,0:T(8,128)(2,1)S(1)}, u32[]{:S(2)}, u32[]{:S(2)}) collective-permute-start(bf16[64,640]{1,0:T(8,128)(2,1)S(1)} %get-tuple-element.66), channel_id=1, source_target_pairs={{0,1},{1,2},{2,3},{3,0},{4,5},{5,6},{6,7},{7,4},{8,9},{9,10},{10,1... | collective-permute-start | bytes 245768 | tf_op jit(solution)/shard_map/ppermute | solution.py:93
  58.1 9.3 %collective-permute-start.14 = (bf16[64,640]{1,0:T(8,128)(2,1)S(1)}, bf16[64,640]{1,0:T(8,128)(2,1)S(1)}, u32[]{:S(2)}, u32[]{:S(2)}) collective-permute-start(bf16[64,640]{1,0:T(8,128)(2,1)S(1)} %get-tuple-element.67), channel_id=1, source_target_pairs={{0,2},{1,3},{2,0},{3,1},{4,6},{5,7},{6,4},{7,5},{8,10},{9,11},{10,... | collective-permute-start | bytes 245768 | tf_op jit(solution)/shard_map/ppermute | solution.py:93
  59.4 8.0 %collective-permute-start.15 = (bf16[64,640]{1,0:T(8,128)(2,1)S(1)}, bf16[64,640]{1,0:T(8,128)(2,1)S(1)}, u32[]{:S(2)}, u32[]{:S(2)}) collective-permute-start(bf16[64,640]{1,0:T(8,128)(2,1)S(1)} %get-tuple-element.68), channel_id=1, source_target_pairs={{0,3},{1,0},{2,1},{3,2},{4,7},{5,4},{6,5},{7,6},{8,11},{9,8},{10,9... | collective-permute-start | bytes 245768 | tf_op jit(solution)/shard_map/ppermute | solution.py:93
  63.8 4.9 %collective-permute-start.26 = (bf16[64,512]{1,0:T(8,128)(2,1)S(1)}, bf16[64,512]{1,0:T(8,128)(2,1)S(1)}, u32[]{:S(2)}, u32[]{:S(2)}) collective-permute-start(bf16[64,512]{1,0:T(8,128)(2,1)S(1)} %shard_map.63.refs_6_.refs_0_), channel_id=1, source_target_pairs={{0,8},{4,12},{8,0},{12,4},{16,24},{20,28},{24,16},{28,20},{1,9},{5... | collective-permute-start | bytes 196616 | tf_op jit(solution)/shard_map/ppermute | solution.py:88
  64.0 7.1 %collective-permute-start.27 = (bf16[64,512]{1,0:T(8,128)(2,1)S(1)}, bf16[64,512]{1,0:T(8,128)(2,1)S(1)}, u32[]{:S(2)}, u32[]{:S(2)}) collective-permute-start(bf16[64,512]{1,0:T(8,128)(2,1)S(1)} %shard_map.63.refs_6_.refs_0_), channel_id=1, source_target_pairs={{0,16},{4,20},{8,24},{12,28},{16,0},{20,4},{24,8},{28,12},{1,17},{... | collective-permute-start | bytes 196616 | tf_op jit(solution)/shard_map/ppermute | solution.py:88
  64.5 6.5 %collective-permute-start.28 = (bf16[64,512]{1,0:T(8,128)(2,1)S(1)}, bf16[64,512]{1,0:T(8,128)(2,1)S(1)}, u32[]{:S(2)}, u32[]{:S(2)}) collective-permute-start(bf16[64,512]{1,0:T(8,128)(2,1)S(1)} %shard_map.63.refs_6_.refs_0_), channel_id=1, source_target_pairs={{0,24},{4,28},{8,16},{12,20},{16,8},{20,12},{24,0},{28,4},{1,25},{... | collective-permute-start | bytes 196616 | tf_op jit(solution)/shard_map/ppermute | solution.py:88
  67.5 4.5 %collective-permute-start.19 = (bf16[64,640]{1,0:T(8,128)(2,1)S(1)}, bf16[64,640]{1,0:T(8,128)(2,1)S(1)}, u32[]{:S(2)}, u32[]{:S(2)}) collective-permute-start(bf16[64,640]{1,0:T(8,128)(2,1)S(1)} %shard_map.64.refs_0_), channel_id=1, source_target_pairs={{0,8},{4,12},{8,0},{12,4},{16,24},{20,28},{24,16},{28,20},{1,9},{5... | collective-permute-start | bytes 245768 | tf_op jit(solution)/shard_map/ppermute | solution.py:88
  68.0 4.4 %collective-permute-start.20 = (bf16[64,640]{1,0:T(8,128)(2,1)S(1)}, bf16[64,640]{1,0:T(8,128)(2,1)S(1)}, u32[]{:S(2)}, u32[]{:S(2)}) collective-permute-start(bf16[64,640]{1,0:T(8,128)(2,1)S(1)} %shard_map.64.refs_0_), channel_id=1, source_target_pairs={{0,16},{4,20},{8,24},{12,28},{16,0},{20,4},{24,8},{28,12},{1,17},{... | collective-permute-start | bytes 245768 | tf_op jit(solution)/shard_map/ppermute | solution.py:88
  68.7 5.3 %collective-permute-start.21 = (bf16[64,640]{1,0:T(8,128)(2,1)S(1)}, bf16[64,640]{1,0:T(8,128)(2,1)S(1)}, u32[]{:S(2)}, u32[]{:S(2)}) collective-permute-start(bf16[64,640]{1,0:T(8,128)(2,1)S(1)} %shard_map.64.refs_0_), channel_id=1, source_target_pairs={{0,24},{4,28},{8,16},{12,20},{16,8},{20,12},{24,0},{28,4},{1,25},{... | collective-permute-start | bytes 245768 | tf_op jit(solution)/shard_map/ppermute | solution.py:88
  74.4 6.2 %collective-permute-start.22 = (f32[64,640]{1,0:T(8,128)S(1)}, f32[64,640]{1,0:T(8,128)S(1)}, u32[]{:S(2)}, u32[]{:S(2)}) collective-permute-start(f32[64,640]{1,0:T(8,128)S(1)} %get-tuple-element.76), channel_id=1, source_target_pairs={{0,4},{4,0},{8,12},{12,8},{16,20},{20,16},{24,28},{28,24},{1,5},{5... | collective-permute-start | bytes 491528 | tf_op jit(solution)/shard_map/ppermute | solution.py:88
  74.5 8.6 %collective-permute-start.30 = (bf16[64,512]{1,0:T(8,128)(2,1)S(1)}, bf16[64,512]{1,0:T(8,128)(2,1)S(1)}, u32[]{:S(2)}, u32[]{:S(2)}) collective-permute-start(bf16[64,512]{1,0:T(8,128)(2,1)S(1)} %shard_map.68.refs_0_), channel_id=1, source_target_pairs={{0,1},{1,2},{2,3},{3,0},{4,5},{5,6},{6,7},{7,4},{8,9},{9,10},{10,1... | collective-permute-start | bytes 196616 | tf_op jit(solution)/shard_map/ppermute | solution.py:93
  77.0 8.1 %collective-permute-start.31 = (bf16[64,512]{1,0:T(8,128)(2,1)S(1)}, bf16[64,512]{1,0:T(8,128)(2,1)S(1)}, u32[]{:S(2)}, u32[]{:S(2)}) collective-permute-start(bf16[64,512]{1,0:T(8,128)(2,1)S(1)} %shard_map.68.refs_0_), channel_id=1, source_target_pairs={{0,2},{1,3},{2,0},{3,1},{4,6},{5,7},{6,4},{7,5},{8,10},{9,11},{10,... | collective-permute-start | bytes 196616 | tf_op jit(solution)/shard_map/ppermute | solution.py:93
  77.3 7.8 %collective-permute-start.32 = (bf16[64,512]{1,0:T(8,128)(2,1)S(1)}, bf16[64,512]{1,0:T(8,128)(2,1)S(1)}, u32[]{:S(2)}, u32[]{:S(2)}) collective-permute-start(bf16[64,512]{1,0:T(8,128)(2,1)S(1)} %shard_map.68.refs_0_), channel_id=1, source_target_pairs={{0,3},{1,0},{2,1},{3,2},{4,7},{5,4},{6,5},{7,6},{8,11},{9,8},{10,9... | collective-permute-start | bytes 196616 | tf_op jit(solution)/shard_map/ppermute | solution.py:93
  80.6 7.2 %collective-permute-start.25 = (bf16[64,640]{1,0:T(8,128)(2,1)S(1)}, bf16[64,640]{1,0:T(8,128)(2,1)S(1)}, u32[]{:S(2)}, u32[]{:S(2)}) collective-permute-start(bf16[64,640]{1,0:T(8,128)(2,1)S(1)} %shard_map.66.refs_0_), channel_id=1, source_target_pairs={{0,1},{1,2},{2,3},{3,0},{4,5},{5,6},{6,7},{7,4},{8,9},{9,10},{10,1... | collective-permute-start | bytes 245768 | tf_op jit(solution)/shard_map/ppermute | solution.py:93
  80.7 9.7 %collective-permute-start.24 = (bf16[64,640]{1,0:T(8,128)(2,1)S(1)}, bf16[64,640]{1,0:T(8,128)(2,1)S(1)}, u32[]{:S(2)}, u32[]{:S(2)}) collective-permute-start(bf16[64,640]{1,0:T(8,128)(2,1)S(1)} %shard_map.66.refs_0_), channel_id=1, source_target_pairs={{0,2},{1,3},{2,0},{3,1},{4,6},{5,7},{6,4},{7,5},{8,10},{9,11},{10,... | collective-permute-start | bytes 245768 | tf_op jit(solution)/shard_map/ppermute | solution.py:93
  83.1 7.9 %collective-permute-start.23 = (bf16[64,640]{1,0:T(8,128)(2,1)S(1)}, bf16[64,640]{1,0:T(8,128)(2,1)S(1)}, u32[]{:S(2)}, u32[]{:S(2)}) collective-permute-start(bf16[64,640]{1,0:T(8,128)(2,1)S(1)} %shard_map.66.refs_0_), channel_id=1, source_target_pairs={{0,3},{1,0},{2,1},{3,2},{4,7},{5,4},{6,5},{7,6},{8,11},{9,8},{10,9... | collective-permute-start | bytes 245768 | tf_op jit(solution)/shard_map/ppermute | solution.py:93
  (3 other events, 47.3 us)

commit v6 on v5

--- a/solution.py
+++ b/solution.py
@@ -10,7 +10,7 @@
 damping = 1.0
 BF = jnp.bfloat16
 F32 = jnp.float32
-WORK = [[75000000, 0], [400000000, 1000000000], [75000000, 75000000], [400000000, 0], [30000000, 150000000], [400000000, 1000000000], [400000000, 400000000]]
+WORK = [[0, 0], [400000000, 1000000000], [75000000, 75000000], [400000000, 0], [30000000, 150000000], [400000000, 1000000000], [400000000, 400000000], [0, 0], [300000000, 0]]
 LOADS = 8
 
 
@@ -251,28 +251,21 @@
         sent[route][...] = (mine[high, :].astype(F32) + came[high, :].astype(F32)).astype(BF)
 
 
-def deal(value, outs, width, behind=None):
+def second_sum(ins, outs):
+    *outs, total = outs
+    kept, came_a, came_b = ins
+    sub = came_a.shape[0]
+    for route, came in enumerate((came_a, came_b)):
+        rows = slice(route * sub, (route + 1) * sub)
+        total[rows, :] = kept[rows, :] + came[...].astype(F32)
+    width = outs[0].shape[1] - 128
     me = lax.axis_index("grp")
     groups = len(outs)
+    rest = total[:, groups * width :]
     for step, out in enumerate(outs):
         at = pl.multiple_of(lax.rem(me + step, groups) * width, 128)
-        out[:, 0:width] = value[:, pl.ds(at, width)].astype(out.dtype)
-        if behind is not None:
-            out[:, width:] = behind.astype(out.dtype)
-
-
-def second_sum(ins, outs):
-    *outs, total = outs
-    sub = ins[1].shape[0]
-    for at in (0, 1):
-        kept, *others = ins[3 * at : 3 * at + 3]
-        for route, came in enumerate(others):
-            low = 2 * sub * at + route * sub
-            total[low : low + sub, :] = kept[route * sub : (route + 1) * sub, :] + came[
-                ...
-            ].astype(F32)
-    rows, width = outs[0].shape
-    deal(total, outs, width - 128, total[:, len(outs) * (width - 128) :])
+        out[:, 0:width] = total[:, pl.ds(at, width)].astype(out.dtype)
+        out[:, width:] = rest.astype(out.dtype)
 
 
 def gathered(ins):
@@ -282,11 +275,15 @@
     return total
 
 
-def prepare(ins, outs, images_all):
-    sums = gathered(ins)
-    rows = outs[0].shape[1]
-    outs[0][...] = (sums[:, :rows] / images_all).astype(BF)
-    outs[1][...] = sums[:, rows:]
+def prepare(ins, outs, images_all, groups):
+    columns, moments = outs
+    low, rows = columns.shape
+    sums = gathered(ins[len(ins) - groups :])
+    low -= sums.shape[0]
+    for ref, earlier in zip(outs, ins[: len(ins) - groups]):
+        ref[:low, :] = earlier[...]
+    columns[low:, :] = (sums[:, :rows] / images_all).astype(BF)
+    moments[low:, :] = sums[:, rows:]
 
 
 def rotate(ins, outs, spans):
@@ -391,16 +388,21 @@
         shapes = [like((2 * sub, wide), F32)] + [like((sub, wide), BF)] * 2
         kept, s_a, s_b = sums = stage(first_sum, shapes, came[c], sums[1:2], WORK[0][c])
         came[c] = [kept, swap(s_a, 4), swap(s_b, 2)]
-    shapes = [like((width, own_rows + 128), t) for t in grp_types] + [like((width, wide), F32)]
-    own, *others = stage(second_sum, shapes, came[0] + came[1], (), WORK[1][0])[:groups]
-    came = [own] + [shift(value, step + 1) for step, value in enumerate(others)]
-    columns, moments = stage(
-        functools.partial(prepare, images_all=images_all),
-        [like((width, own_rows), BF), like((width, 128), F32)],
-        came,
-        (),
-        WORK[1][1],
-    )
+    held = []
+    for c in (0, 1):
+        shapes = [like((2 * sub, own_rows + 128), t) for t in grp_types] + [like((2 * sub, wide), F32)]
+        own, *others = stage(second_sum, shapes, came[c], (), WORK[7][c])[:groups]
+        came[c] = [own] + [shift(value, step + 1) for step, value in enumerate(others)]
+    for c in (0, 1):
+        rows = 2 * sub * (c + 1)
+        held = stage(
+            functools.partial(prepare, images_all=images_all, groups=groups),
+            [like((rows, own_rows), BF), like((rows, 128), F32)],
+            held + came[c],
+            (),
+            WORK[8][c],
+        )
+    columns, moments = held
 
     spans = ((0, own_rows // 128 // 2 * 128), (own_rows // 128 // 2 * 128, own_rows))
     eigen_row = input_eigen.reshape(1, own_rows)

time: 92.5 us -> 89.3 us (0.965)
  waiting for transfers between devices: 27.4 us -> 21.3 us
  starting transfers between devices: 42.4 us -> 44.7 us
    ppermute x18, waiting for transfers between devices: 19 us -> 15.5 us  [swap(): lax.ppermute(value, 'dp', [(i, i ^ bit) for i in range(lax.axis_size('dp'...]
    ppermute x15 -> x18, starting transfers between devices: 24.4 us -> 27.5 us  [shift(): return lax.ppermute(value, 'grp', [(i, (i + step) % n) for i in range(n)])]
    ppermute x15 -> x18, waiting for transfers between devices: 8.41 us -> 5.78 us  [shift(): return lax.ppermute(value, 'grp', [(i, (i + step) % n) for i in range(n)])]
    pallas_call x17 -> x19, Pallas kernels: 8.99 us -> 9.62 us  [stage(): pl.pallas_call(body, in_specs=[near] * (len(operands) + len(after)), out_...]
  transfers between devices with their start and end apart: 33 -> 36, of which waited for: 15 -> 12; matrix products, arithmetic and copies ran while one was open for 3% -> 3% of each run, Pallas kernels for 12% -> 14%
where the time goes in v6:
time: 89.3 us; the launch traced here: 89.1 us
  starting transfers between devices  44.7 us (50%)
  waiting for transfers between devices  21.3 us (24%)
  Pallas kernels  19 us (21%)
  local copies, waits for them, and re-layouts  3.51 us (4%)
    ppermute x18, starting transfers between devices, shift(): return lax.ppermute(value, 'grp', [(i, (i + step) % n) for i in range(n)])  27.5 us
    ppermute x18, starting transfers between devices, swap(): lax.ppermute(value, 'dp', [(i, i ^ bit) for i in range(lax.axis_size('dp'...  17.2 us
    ppermute x18, waiting for transfers between devices, swap(): lax.ppermute(value, 'dp', [(i, i ^ bit) for i in range(lax.axis_size('dp'...  15.5 us
    pallas_call x19, Pallas kernels, stage(): pl.pallas_call(body, in_specs=[near] * (len(operands) + len(after)), out_...  9.62 us
    ppermute x18, waiting for transfers between devices, shift(): return lax.ppermute(value, 'grp', [(i, (i + step) % n) for i in range(n)])  5.78 us
    pallas_call x1, Pallas kernels, load(): pl.pallas_call(load_kernel, in_specs=[pl.BlockSpec(memory_space=pl.ANY),...  5.09 us
    pallas_call x1, Pallas kernels, grad_parts(): pl.pallas_call(grad_kernel, in_specs=[near] * 5, out_specs=[near] * 8, ou...  2.99 us
    pad x4, local copies, waits for them, and re-layouts, map_rows(): jnp.pad(images, ((0, 16 - h), (0, 16 - w), (0, 0), (0, 0)))  1.82 us
  transfers between devices with their start and end apart: 36, of which 12 were waited for; matrix products, arithmetic and copies ran while one was open for 3% of the time, Pallas kernels for 14%

profile of v6, /device:TPU:0, one launch (start us, length us, event | category | flops | bytes accessed | tf_op | source)
XLA Modules:
  0.0 89.1 jit_solution(13895245113946027280)
XLA Ops:
  0.5 1.3 %shard_map.55 = (bf16[14,14,2,512]{3,2,1,0:T(2,128)(2,1)S(1)}, bf16[14,14,2,512]{3,2,1,0:T(2,128)(2,1)S(1)}, bf16[512,512]{1,0:T(8,128)(2,1)S(1)}) custom-call(bf16[14,14,2,512]{3,2,1,0:T(2,128)(2,1)} %bitcast.4, bf16[14,14,2,512]{3,2,1,0:T(2,128)(2,1)} %bitcast.6, bf16[512,512]{1,0:T(8,128)(2,1)} %refs_2_.1), custom_call_target="tpu_custom_call" | custom-call | tf_op jit(solution)/shard_map/pallas_call | solution.py:188
  4.5 3.0 %shard_map.56 = (bf16[32,4736]{1,0:T(8,128)(2,1)S(1)}, bf16[32,4736]{1,0:T(8,128)(2,1)S(1)}, bf16[32,4736]{1,0:T(8,128)(2,1)S(1)}, bf16[32,4736]{1,0:T(8,128)(2,...) custom-call(bf16[512,512]{1,0:T(8,128)(2,1)S(1)} %reshape.15.act_a, ...), custom_call_target="tpu_custom_call" | custom-call | flops 2415919104 | bytes 4456448 | tf_op jit(solution)/shard_map/pallas_call | solution.py:149
  7.5 3.0 %collective-permute-start.2 = (bf16[32,4736]{1,0:T(8,128)(2,1)S(1)}, bf16[32,4736]{1,0:T(8,128)(2,1)S(1)}, u32[]{:S(2)}, u32[]{:S(2)}) collective-permute-start(bf16[32,4736]{1,0:T(8,128)(2,1)S(1)} %get-tuple-element.53.after), channel_id=1, source_target_pairs={{0,8},{4,12},{8,0},{12,4},{16,24},{20,28},{24,16},{28,20},{1,9},{5... | collective-permute-start | bytes 909320 | tf_op jit(solution)/shard_map/ppermute | solution.py:88
  10.6 1.5 %collective-permute-start.3 = (bf16[32,4736]{1,0:T(8,128)(2,1)S(1)}, bf16[32,4736]{1,0:T(8,128)(2,1)S(1)}, u32[]{:S(2)}, u32[]{:S(2)}) collective-permute-start(bf16[32,4736]{1,0:T(8,128)(2,1)S(1)} %get-tuple-element.55), channel_id=1, source_target_pairs={{0,16},{4,20},{8,24},{12,28},{16,0},{20,4},{24,8},{28,12},{1,17},{... | collective-permute-start | bytes 909320 | tf_op jit(solution)/shard_map/ppermute | solution.py:88
  13.9 4.7 %collective-permute-done.2.refs_1_ = bf16[32,4736]{1,0:T(8,128)(2,1)S(1)} collective-permute-done((bf16[32,4736]{1,0:T(8,128)(2,1)S(1)}, bf16[32,4736]{1,0:T(8,128)(2,1)S(1)}, u32[]{:S(2)}, u32[]{:S(2)}) %collective-permute-start.2) | collective-permute-done | bytes 303136 | tf_op jit(solution)/shard_map/ppermute | solution.py:88
  18.5 2.1 %collective-permute-done.3.refs_3_ = bf16[32,4736]{1,0:T(8,128)(2,1)S(1)} collective-permute-done((bf16[32,4736]{1,0:T(8,128)(2,1)S(1)}, bf16[32,4736]{1,0:T(8,128)(2,1)S(1)}, u32[]{:S(2)}, u32[]{:S(2)}) %collective-permute-start.3) | collective-permute-done | bytes 303136 | tf_op jit(solution)/shard_map/ppermute | solution.py:88
  20.8 1.6 %collective-permute-start.4 = (bf16[16,4736]{1,0:T(8,128)(2,1)S(1)}, bf16[16,4736]{1,0:T(8,128)(2,1)S(1)}, u32[]{:S(2)}, u32[]{:S(2)}) collective-permute-start(bf16[16,4736]{1,0:T(8,128)(2,1)S(1)} %get-tuple-element.57.refs_4_), channel_id=1, source_target_pairs={{0,16},{4,20},{8,24},{12,28},{16,0},{20,4},{24,8},{28,12},{1,17},{... | collective-permute-start | bytes 454664 | tf_op jit(solution)/shard_map/ppermute | solution.py:88
  22.9 4.2 %collective-permute-done.10.refs_3_ = bf16[32,4736]{1,0:T(8,128)(2,1)S(1)} collective-permute-done((bf16[32,4736]{1,0:T(8,128)(2,1)S(1)}, bf16[32,4736]{1,0:T(8,128)(2,1)S(1)}, u32[]{:S(2)}, u32[]{:S(2)}) %collective-permute-start.10) | collective-permute-done | bytes 303136 | tf_op jit(solution)/shard_map/ppermute | solution.py:88
  27.3 1.6 %collective-permute-start.11 = (bf16[16,4736]{1,0:T(8,128)(2,1)S(1)}, bf16[16,4736]{1,0:T(8,128)(2,1)S(1)}, u32[]{:S(2)}, u32[]{:S(2)}) collective-permute-start(bf16[16,4736]{1,0:T(8,128)(2,1)S(1)} %get-tuple-element.70), channel_id=1, source_target_pairs={{0,16},{4,20},{8,24},{12,28},{16,0},{20,4},{24,8},{28,12},{1,17},{... | collective-permute-start | bytes 454664 | tf_op jit(solution)/shard_map/ppermute | solution.py:88
  31.3 1.6 %collective-permute-start.6 = (bf16[32,1280]{1,0:T(8,128)(2,1)S(1)}, bf16[32,1280]{1,0:T(8,128)(2,1)S(1)}, u32[]{:S(2)}, u32[]{:S(2)}) collective-permute-start(bf16[32,1280]{1,0:T(8,128)(2,1)S(1)} %get-tuple-element.60), channel_id=1, source_target_pairs={{0,1},{1,2},{2,3},{3,0},{4,5},{5,6},{6,7},{7,4},{8,9},{9,10},{10,1... | collective-permute-start | bytes 245768 | tf_op jit(solution)/shard_map/ppermute | solution.py:93
  32.9 2.6 %collective-permute-start.7 = (bf16[32,1280]{1,0:T(8,128)(2,1)S(1)}, bf16[32,1280]{1,0:T(8,128)(2,1)S(1)}, u32[]{:S(2)}, u32[]{:S(2)}) collective-permute-start(bf16[32,1280]{1,0:T(8,128)(2,1)S(1)} %get-tuple-element.61), channel_id=1, source_target_pairs={{0,2},{1,3},{2,0},{3,1},{4,6},{5,7},{6,4},{7,5},{8,10},{9,11},{10,... | collective-permute-start | bytes 245768 | tf_op jit(solution)/shard_map/ppermute | solution.py:93
  35.5 1.3 %collective-permute-start.8 = (bf16[32,1280]{1,0:T(8,128)(2,1)S(1)}, bf16[32,1280]{1,0:T(8,128)(2,1)S(1)}, u32[]{:S(2)}, u32[]{:S(2)}) collective-permute-start(bf16[32,1280]{1,0:T(8,128)(2,1)S(1)} %get-tuple-element.62), channel_id=1, source_target_pairs={{0,3},{1,0},{2,1},{3,2},{4,7},{5,4},{6,5},{7,6},{8,11},{9,8},{10,9... | collective-permute-start | bytes 245768 | tf_op jit(solution)/shard_map/ppermute | solution.py:93
  39.2 2.5 %collective-permute-start.15 = (bf16[32,1280]{1,0:T(8,128)(2,1)S(1)}, bf16[32,1280]{1,0:T(8,128)(2,1)S(1)}, u32[]{:S(2)}, u32[]{:S(2)}) collective-permute-start(bf16[32,1280]{1,0:T(8,128)(2,1)S(1)} %get-tuple-element.75), channel_id=1, source_target_pairs={{0,3},{1,0},{2,1},{3,2},{4,7},{5,4},{6,5},{7,6},{8,11},{9,8},{10,9... | collective-permute-start | bytes 245768 | tf_op jit(solution)/shard_map/ppermute | solution.py:93
  41.6 5.1 %shard_map.63.refs_1_.refs_2_.refs_4_ = bf16[1152,4608]{1,0:T(8,128)(2,1)S(1)} custom-call(bf16[1152,4608]{1,0:T(8,128)(2,1)} %source.1, bf16[32,4736]{1,0:T(8,128)(2,1)} %copy-done), custom_call_target="tpu_custom_call" | custom-call | bytes 21233664 | tf_op jit(solution)/shard_map/pallas_call | solution.py:214
  46.9 1.8 %shard_map.64 = (f32[64,512]{1,0:T(8,128)S(1)}, bf16[64,512]{1,0:T(8,128)(2,1)S(1)}, bf16[64,512]{1,0:T(8,128)(2,1)S(1)}, bf16[64,512]{1,0:T(8,128)(2,1)S(1)}, f...) custom-call(bf16[64,1152]{1,0:T(8,128)(2,1)S(1)} %get-tuple-element., ...), custom_call_target="tpu_custom_call" | custom-call | flops 75000000 | tf_op jit(solution)/shard_map/pallas_call | solution.py:231
  48.7 1.1 %collective-permute-start.19 = (bf16[64,512]{1,0:T(8,128)(2,1)S(1)}, bf16[64,512]{1,0:T(8,128)(2,1)S(1)}, u32[]{:S(2)}, u32[]{:S(2)}) collective-permute-start(bf16[64,512]{1,0:T(8,128)(2,1)S(1)} %get-tuple-element.83), channel_id=1, source_target_pairs={{0,1},{1,2},{2,3},{3,0},{4,5},{5,6},{6,7},{7,4},{8,9},{9,10},{10,1... | collective-permute-start | bytes 196616 | tf_op jit(solution)/shard_map/ppermute | solution.py:93
  49.9 2.4 %collective-permute-start.20 = (bf16[64,512]{1,0:T(8,128)(2,1)S(1)}, bf16[64,512]{1,0:T(8,128)(2,1)S(1)}, u32[]{:S(2)}, u32[]{:S(2)}) collective-permute-start(bf16[64,512]{1,0:T(8,128)(2,1)S(1)} %get-tuple-element.84), channel_id=1, source_target_pairs={{0,2},{1,3},{2,0},{3,1},{4,6},{5,7},{6,4},{7,5},{8,10},{9,11},{10,... | collective-permute-start | bytes 196616 | tf_op jit(solution)/shard_map/ppermute | solution.py:93
  52.2 1.5 %collective-permute-start.21 = (bf16[64,512]{1,0:T(8,128)(2,1)S(1)}, bf16[64,512]{1,0:T(8,128)(2,1)S(1)}, u32[]{:S(2)}, u32[]{:S(2)}) collective-permute-start(bf16[64,512]{1,0:T(8,128)(2,1)S(1)} %get-tuple-element.85), channel_id=1, source_target_pairs={{0,3},{1,0},{2,1},{3,2},{4,7},{5,4},{6,5},{7,6},{8,11},{9,8},{10,9... | collective-permute-start | bytes 196616 | tf_op jit(solution)/shard_map/ppermute | solution.py:93
  54.9 2.7 %collective-permute-start.18 = (bf16[64,640]{1,0:T(8,128)(2,1)S(1)}, bf16[64,640]{1,0:T(8,128)(2,1)S(1)}, u32[]{:S(2)}, u32[]{:S(2)}) collective-permute-start(bf16[64,640]{1,0:T(8,128)(2,1)S(1)} %get-tuple-element.80), channel_id=1, source_target_pairs={{0,3},{1,0},{2,1},{3,2},{4,7},{5,4},{6,5},{7,6},{8,11},{9,8},{10,9... | collective-permute-start | bytes 245768 | tf_op jit(solution)/shard_map/ppermute | solution.py:93
  59.3 1.6 %collective-permute-start.30 = (bf16[64,512]{1,0:T(8,128)(2,1)S(1)}, bf16[64,512]{1,0:T(8,128)(2,1)S(1)}, u32[]{:S(2)}, u32[]{:S(2)}) collective-permute-start(bf16[64,512]{1,0:T(8,128)(2,1)S(1)} %shard_map.65.refs_6_.refs_0_), channel_id=1, source_target_pairs={{0,16},{4,20},{8,24},{12,28},{16,0},{20,4},{24,8},{28,12},{1,17},{... | collective-permute-start | bytes 196616 | tf_op jit(solution)/shard_map/ppermute | solution.py:88
  60.9 1.4 %collective-permute-start.31 = (bf16[64,512]{1,0:T(8,128)(2,1)S(1)}, bf16[64,512]{1,0:T(8,128)(2,1)S(1)}, u32[]{:S(2)}, u32[]{:S(2)}) collective-permute-start(bf16[64,512]{1,0:T(8,128)(2,1)S(1)} %shard_map.65.refs_6_.refs_0_), channel_id=1, source_target_pairs={{0,24},{4,28},{8,16},{12,20},{16,8},{20,12},{24,0},{28,4},{1,25},{... | collective-permute-start | bytes 196616 | tf_op jit(solution)/shard_map/ppermute | solution.py:88
  63.8 1.5 %collective-permute-start.23 = (bf16[64,640]{1,0:T(8,128)(2,1)S(1)}, bf16[64,640]{1,0:T(8,128)(2,1)S(1)}, u32[]{:S(2)}, u32[]{:S(2)}) collective-permute-start(bf16[64,640]{1,0:T(8,128)(2,1)S(1)} %shard_map.66.refs_0_), channel_id=1, source_target_pairs={{0,16},{4,20},{8,24},{12,28},{16,0},{20,4},{24,8},{28,12},{1,17},{... | collective-permute-start | bytes 245768 | tf_op jit(solution)/shard_map/ppermute | solution.py:88
  65.3 1.4 %collective-permute-start.24 = (bf16[64,640]{1,0:T(8,128)(2,1)S(1)}, bf16[64,640]{1,0:T(8,128)(2,1)S(1)}, u32[]{:S(2)}, u32[]{:S(2)}) collective-permute-start(bf16[64,640]{1,0:T(8,128)(2,1)S(1)} %shard_map.66.refs_0_), channel_id=1, source_target_pairs={{0,24},{4,28},{8,16},{12,20},{16,8},{20,12},{24,0},{28,4},{1,25},{... | collective-permute-start | bytes 245768 | tf_op jit(solution)/shard_map/ppermute | solution.py:88
  68.2 2.4 %collective-permute-done.24.refs_3_ = bf16[64,640]{1,0:T(8,128)(2,1)S(1)} collective-permute-done((bf16[64,640]{1,0:T(8,128)(2,1)S(1)}, bf16[64,640]{1,0:T(8,128)(2,1)S(1)}, u32[]{:S(2)}, u32[]{:S(2)}) %collective-permute-start.24) | collective-permute-done | bytes 81952 | tf_op jit(solution)/shard_map/ppermute | solution.py:88
  71.2 3.0 %collective-permute-start.33 = (bf16[64,512]{1,0:T(8,128)(2,1)S(1)}, bf16[64,512]{1,0:T(8,128)(2,1)S(1)}, u32[]{:S(2)}, u32[]{:S(2)}) collective-permute-start(bf16[64,512]{1,0:T(8,128)(2,1)S(1)} %shard_map.70.refs_0_), channel_id=1, source_target_pairs={{0,1},{1,2},{2,3},{3,0},{4,5},{5,6},{6,7},{7,4},{8,9},{9,10},{10,1... | collective-permute-start | bytes 196616 | tf_op jit(solution)/shard_map/ppermute | solution.py:93
  75.2 1.4 %collective-permute-start.35 = (bf16[64,512]{1,0:T(8,128)(2,1)S(1)}, bf16[64,512]{1,0:T(8,128)(2,1)S(1)}, u32[]{:S(2)}, u32[]{:S(2)}) collective-permute-start(bf16[64,512]{1,0:T(8,128)(2,1)S(1)} %shard_map.70.refs_0_), channel_id=1, source_target_pairs={{0,3},{1,0},{2,1},{3,2},{4,7},{5,4},{6,5},{7,6},{8,11},{9,8},{10,9... | collective-permute-start | bytes 196616 | tf_op jit(solution)/shard_map/ppermute | solution.py:93
  77.8 1.9 %collective-permute-start.27 = (bf16[64,640]{1,0:T(8,128)(2,1)S(1)}, bf16[64,640]{1,0:T(8,128)(2,1)S(1)}, u32[]{:S(2)}, u32[]{:S(2)}) collective-permute-start(bf16[64,640]{1,0:T(8,128)(2,1)S(1)} %shard_map.68.refs_0_), channel_id=1, source_target_pairs={{0,2},{1,3},{2,0},{3,1},{4,6},{5,7},{6,4},{7,5},{8,10},{9,11},{10,... | collective-permute-start | bytes 245768 | tf_op jit(solution)/shard_map/ppermute | solution.py:93
  80.3 1.4 %collective-permute-start.26 = (bf16[64,640]{1,0:T(8,128)(2,1)S(1)}, bf16[64,640]{1,0:T(8,128)(2,1)S(1)}, u32[]{:S(2)}, u32[]{:S(2)}) collective-permute-start(bf16[64,640]{1,0:T(8,128)(2,1)S(1)} %shard_map.68.refs_0_), channel_id=1, source_target_pairs={{0,3},{1,0},{2,1},{3,2},{4,7},{5,4},{6,5},{7,6},{8,11},{9,8},{10,9... | collective-permute-start | bytes 245768 | tf_op jit(solution)/shard_map/ppermute | solution.py:93
  81.6 1.2 %shard_map.73.refs_1_ = f32[64,1152]{1,0:T(8,128)S(1)} custom-call(bf16[64,512]{1,0:T(8,128)(2,1)S(1)} %collective-permute-done.33.refs_0_, bf16[64,512]{1,0:T(8,128)(2,1)S(1)} %collective-permute-done.34.refs_1_, bf16[64,512]{1,0:T(8,128)(2,1)S(1)} %collective-permute-done.35.refs_2_, f32[64,1152]{1,0:T(8,128)S(1)} %shard_map.72.refs_3_, ...), custom_call_target="tpu_custom_call" | custom-call | flops 1200000000 | tf_op jit(solution)/shard_map/pallas_call | solution.py:231
  82.8 1.5 %collective-permute-done.28.refs_0_ = bf16[64,640]{1,0:T(8,128)(2,1)S(1)} collective-permute-done((bf16[64,640]{1,0:T(8,128)(2,1)S(1)}, bf16[64,640]{1,0:T(8,128)(2,1)S(1)}, u32[]{:S(2)}, u32[]{:S(2)}) %collective-permute-start.28) | collective-permute-done | bytes 81952 | tf_op jit(solution)/shard_map/ppermute | solution.py:93
  84.9 2.4 %collective-permute-done.27.refs_0_ = bf16[64,640]{1,0:T(8,128)(2,1)S(1)} collective-permute-done((bf16[64,640]{1,0:T(8,128)(2,1)S(1)}, bf16[64,640]{1,0:T(8,128)(2,1)S(1)}, u32[]{:S(2)}, u32[]{:S(2)}) %collective-permute-start.27) | collective-permute-done | bytes 81952 | tf_op jit(solution)/shard_map/ppermute | solution.py:93
  87.8 1.3 %shard_map.76 = bf16[64,1152]{1,0:T(8,128)(2,1)} custom-call(bf16[64,640]{1,0:T(8,128)(2,1)S(1)} %collective-permute-done.26.refs_0_, f32[64,1152]{1,0:T(8,128)S(1)} %shard_map.75.refs_1_, bf16[1152,4608]{1,0:T(8,128)(2,1)S(1)} %shard_map.63.refs_1_.refs_2_.refs_4_), custom_call_target="tpu_custom_call" | custom-call | flops 400000000 | tf_op jit(solution)/shard_map/pallas_call | solution.py:231
  (78 shorter events, 20.8 us)
Async XLA Ops:
  7.5 11.0 %collective-permute-start.2 = (bf16[32,4736]{1,0:T(8,128)(2,1)S(1)}, bf16[32,4736]{1,0:T(8,128)(2,1)S(1)}, u32[]{:S(2)}, u32[]{:S(2)}) collective-permute-start(bf16[32,4736]{1,0:T(8,128)(2,1)S(1)} %get-tuple-element.53.after), channel_id=1, source_target_pairs={{0,8},{4,12},{8,0},{12,4},{16,24},{20,28},{24,16},{28,20},{1,9},{5... | collective-permute-start | bytes 909320 | tf_op jit(solution)/shard_map/ppermute | solution.py:88
  10.6 10.1 %collective-permute-start.3 = (bf16[32,4736]{1,0:T(8,128)(2,1)S(1)}, bf16[32,4736]{1,0:T(8,128)(2,1)S(1)}, u32[]{:S(2)}, u32[]{:S(2)}) collective-permute-start(bf16[32,4736]{1,0:T(8,128)(2,1)S(1)} %get-tuple-element.55), channel_id=1, source_target_pairs={{0,16},{4,20},{8,24},{12,28},{16,0},{20,4},{24,8},{28,12},{1,17},{... | collective-permute-start | bytes 909320 | tf_op jit(solution)/shard_map/ppermute | solution.py:88
  13.0 14.2 %collective-permute-start.10 = (bf16[32,4736]{1,0:T(8,128)(2,1)S(1)}, bf16[32,4736]{1,0:T(8,128)(2,1)S(1)}, u32[]{:S(2)}, u32[]{:S(2)}) collective-permute-start(bf16[32,4736]{1,0:T(8,128)(2,1)S(1)} %get-tuple-element.68), channel_id=1, source_target_pairs={{0,16},{4,20},{8,24},{12,28},{16,0},{20,4},{24,8},{28,12},{1,17},{... | collective-permute-start | bytes 909320 | tf_op jit(solution)/shard_map/ppermute | solution.py:88
  13.5 13.6 %collective-permute-start.9 = (bf16[32,4736]{1,0:T(8,128)(2,1)S(1)}, bf16[32,4736]{1,0:T(8,128)(2,1)S(1)}, u32[]{:S(2)}, u32[]{:S(2)}) collective-permute-start(bf16[32,4736]{1,0:T(8,128)(2,1)S(1)} %get-tuple-element.66), channel_id=1, source_target_pairs={{0,8},{4,12},{8,0},{12,4},{16,24},{20,28},{24,16},{28,20},{1,9},{5... | collective-permute-start | bytes 909320 | tf_op jit(solution)/shard_map/ppermute | solution.py:88
  20.8 9.6 %collective-permute-start.4 = (bf16[16,4736]{1,0:T(8,128)(2,1)S(1)}, bf16[16,4736]{1,0:T(8,128)(2,1)S(1)}, u32[]{:S(2)}, u32[]{:S(2)}) collective-permute-start(bf16[16,4736]{1,0:T(8,128)(2,1)S(1)} %get-tuple-element.57.refs_4_), channel_id=1, source_target_pairs={{0,16},{4,20},{8,24},{12,28},{16,0},{20,4},{24,8},{28,12},{1,17},{... | collective-permute-start | bytes 454664 | tf_op jit(solution)/shard_map/ppermute | solution.py:88
  22.4 8.0 %collective-permute-start.5 = (bf16[16,4736]{1,0:T(8,128)(2,1)S(1)}, bf16[16,4736]{1,0:T(8,128)(2,1)S(1)}, u32[]{:S(2)}, u32[]{:S(2)}) collective-permute-start(bf16[16,4736]{1,0:T(8,128)(2,1)S(1)} %get-tuple-element.58), channel_id=1, source_target_pairs={{0,8},{4,12},{8,0},{12,4},{16,24},{20,28},{24,16},{28,20},{1,9},{5... | collective-permute-start | bytes 454664 | tf_op jit(solution)/shard_map/ppermute | solution.py:88
  27.3 9.6 %collective-permute-start.11 = (bf16[16,4736]{1,0:T(8,128)(2,1)S(1)}, bf16[16,4736]{1,0:T(8,128)(2,1)S(1)}, u32[]{:S(2)}, u32[]{:S(2)}) collective-permute-start(bf16[16,4736]{1,0:T(8,128)(2,1)S(1)} %get-tuple-element.70), channel_id=1, source_target_pairs={{0,16},{4,20},{8,24},{12,28},{16,0},{20,4},{24,8},{28,12},{1,17},{... | collective-permute-start | bytes 454664 | tf_op jit(solution)/shard_map/ppermute | solution.py:88
  28.9 8.0 %collective-permute-start.12 = (bf16[16,4736]{1,0:T(8,128)(2,1)S(1)}, bf16[16,4736]{1,0:T(8,128)(2,1)S(1)}, u32[]{:S(2)}, u32[]{:S(2)}) collective-permute-start(bf16[16,4736]{1,0:T(8,128)(2,1)S(1)} %get-tuple-element.71), channel_id=1, source_target_pairs={{0,8},{4,12},{8,0},{12,4},{16,24},{20,28},{24,16},{28,20},{1,9},{5... | collective-permute-start | bytes 454664 | tf_op jit(solution)/shard_map/ppermute | solution.py:88
  31.3 7.8 %collective-permute-start.6 = (bf16[32,1280]{1,0:T(8,128)(2,1)S(1)}, bf16[32,1280]{1,0:T(8,128)(2,1)S(1)}, u32[]{:S(2)}, u32[]{:S(2)}) collective-permute-start(bf16[32,1280]{1,0:T(8,128)(2,1)S(1)} %get-tuple-element.60), channel_id=1, source_target_pairs={{0,1},{1,2},{2,3},{3,0},{4,5},{5,6},{6,7},{7,4},{8,9},{9,10},{10,1... | collective-permute-start | bytes 245768 | tf_op jit(solution)/shard_map/ppermute | solution.py:93
  32.9 13.8 %collective-permute-start.7 = (bf16[32,1280]{1,0:T(8,128)(2,1)S(1)}, bf16[32,1280]{1,0:T(8,128)(2,1)S(1)}, u32[]{:S(2)}, u32[]{:S(2)}) collective-permute-start(bf16[32,1280]{1,0:T(8,128)(2,1)S(1)} %get-tuple-element.61), channel_id=1, source_target_pairs={{0,2},{1,3},{2,0},{3,1},{4,6},{5,7},{6,4},{7,5},{8,10},{9,11},{10,... | collective-permute-start | bytes 245768 | tf_op jit(solution)/shard_map/ppermute | solution.py:93
  35.5 11.2 %collective-permute-start.8 = (bf16[32,1280]{1,0:T(8,128)(2,1)S(1)}, bf16[32,1280]{1,0:T(8,128)(2,1)S(1)}, u32[]{:S(2)}, u32[]{:S(2)}) collective-permute-start(bf16[32,1280]{1,0:T(8,128)(2,1)S(1)} %get-tuple-element.62), channel_id=1, source_target_pairs={{0,3},{1,0},{2,1},{3,2},{4,7},{5,4},{6,5},{7,6},{8,11},{9,8},{10,9... | collective-permute-start | bytes 245768 | tf_op jit(solution)/shard_map/ppermute | solution.py:93
  37.8 9.0 %collective-permute-start.13 = (bf16[32,1280]{1,0:T(8,128)(2,1)S(1)}, bf16[32,1280]{1,0:T(8,128)(2,1)S(1)}, u32[]{:S(2)}, u32[]{:S(2)}) collective-permute-start(bf16[32,1280]{1,0:T(8,128)(2,1)S(1)} %get-tuple-element.73), channel_id=1, source_target_pairs={{0,1},{1,2},{2,3},{3,0},{4,5},{5,6},{6,7},{7,4},{8,9},{9,10},{10,1... | collective-permute-start | bytes 245768 | tf_op jit(solution)/shard_map/ppermute | solution.py:93
  38.5 8.3 %collective-permute-start.14 = (bf16[32,1280]{1,0:T(8,128)(2,1)S(1)}, bf16[32,1280]{1,0:T(8,128)(2,1)S(1)}, u32[]{:S(2)}, u32[]{:S(2)}) collective-permute-start(bf16[32,1280]{1,0:T(8,128)(2,1)S(1)} %get-tuple-element.74), channel_id=1, source_target_pairs={{0,2},{1,3},{2,0},{3,1},{4,6},{5,7},{6,4},{7,5},{8,10},{9,11},{10,... | collective-permute-start | bytes 245768 | tf_op jit(solution)/shard_map/ppermute | solution.py:93
  39.2 7.7 %collective-permute-start.15 = (bf16[32,1280]{1,0:T(8,128)(2,1)S(1)}, bf16[32,1280]{1,0:T(8,128)(2,1)S(1)}, u32[]{:S(2)}, u32[]{:S(2)}) collective-permute-start(bf16[32,1280]{1,0:T(8,128)(2,1)S(1)} %get-tuple-element.75), channel_id=1, source_target_pairs={{0,3},{1,0},{2,1},{3,2},{4,7},{5,4},{6,5},{7,6},{8,11},{9,8},{10,9... | collective-permute-start | bytes 245768 | tf_op jit(solution)/shard_map/ppermute | solution.py:93
  48.7 6.2 %collective-permute-start.19 = (bf16[64,512]{1,0:T(8,128)(2,1)S(1)}, bf16[64,512]{1,0:T(8,128)(2,1)S(1)}, u32[]{:S(2)}, u32[]{:S(2)}) collective-permute-start(bf16[64,512]{1,0:T(8,128)(2,1)S(1)} %get-tuple-element.83), channel_id=1, source_target_pairs={{0,1},{1,2},{2,3},{3,0},{4,5},{5,6},{6,7},{7,4},{8,9},{9,10},{10,1... | collective-permute-start | bytes 196616 | tf_op jit(solution)/shard_map/ppermute | solution.py:93
  49.9 8.8 %collective-permute-start.20 = (bf16[64,512]{1,0:T(8,128)(2,1)S(1)}, bf16[64,512]{1,0:T(8,128)(2,1)S(1)}, u32[]{:S(2)}, u32[]{:S(2)}) collective-permute-start(bf16[64,512]{1,0:T(8,128)(2,1)S(1)} %get-tuple-element.84), channel_id=1, source_target_pairs={{0,2},{1,3},{2,0},{3,1},{4,6},{5,7},{6,4},{7,5},{8,10},{9,11},{10,... | collective-permute-start | bytes 196616 | tf_op jit(solution)/shard_map/ppermute | solution.py:93
  52.2 6.4 %collective-permute-start.21 = (bf16[64,512]{1,0:T(8,128)(2,1)S(1)}, bf16[64,512]{1,0:T(8,128)(2,1)S(1)}, u32[]{:S(2)}, u32[]{:S(2)}) collective-permute-start(bf16[64,512]{1,0:T(8,128)(2,1)S(1)} %get-tuple-element.85), channel_id=1, source_target_pairs={{0,3},{1,0},{2,1},{3,2},{4,7},{5,4},{6,5},{7,6},{8,11},{9,8},{10,9... | collective-permute-start | bytes 196616 | tf_op jit(solution)/shard_map/ppermute | solution.py:93
  53.8 7.1 %collective-permute-start.16 = (bf16[64,640]{1,0:T(8,128)(2,1)S(1)}, bf16[64,640]{1,0:T(8,128)(2,1)S(1)}, u32[]{:S(2)}, u32[]{:S(2)}) collective-permute-start(bf16[64,640]{1,0:T(8,128)(2,1)S(1)} %get-tuple-element.78), channel_id=1, source_target_pairs={{0,1},{1,2},{2,3},{3,0},{4,5},{5,6},{6,7},{7,4},{8,9},{9,10},{10,1... | collective-permute-start | bytes 245768 | tf_op jit(solution)/shard_map/ppermute | solution.py:93
  54.3 8.8 %collective-permute-start.17 = (bf16[64,640]{1,0:T(8,128)(2,1)S(1)}, bf16[64,640]{1,0:T(8,128)(2,1)S(1)}, u32[]{:S(2)}, u32[]{:S(2)}) collective-permute-start(bf16[64,640]{1,0:T(8,128)(2,1)S(1)} %get-tuple-element.79), channel_id=1, source_target_pairs={{0,2},{1,3},{2,0},{3,1},{4,6},{5,7},{6,4},{7,5},{8,10},{9,11},{10,... | collective-permute-start | bytes 245768 | tf_op jit(solution)/shard_map/ppermute | solution.py:93
  54.9 8.2 %collective-permute-start.18 = (bf16[64,640]{1,0:T(8,128)(2,1)S(1)}, bf16[64,640]{1,0:T(8,128)(2,1)S(1)}, u32[]{:S(2)}, u32[]{:S(2)}) collective-permute-start(bf16[64,640]{1,0:T(8,128)(2,1)S(1)} %get-tuple-element.80), channel_id=1, source_target_pairs={{0,3},{1,0},{2,1},{3,2},{4,7},{5,4},{6,5},{7,6},{8,11},{9,8},{10,9... | collective-permute-start | bytes 245768 | tf_op jit(solution)/shard_map/ppermute | solution.py:93
  58.8 6.6 %collective-permute-start.29 = (bf16[64,512]{1,0:T(8,128)(2,1)S(1)}, bf16[64,512]{1,0:T(8,128)(2,1)S(1)}, u32[]{:S(2)}, u32[]{:S(2)}) collective-permute-start(bf16[64,512]{1,0:T(8,128)(2,1)S(1)} %shard_map.65.refs_6_.refs_0_), channel_id=1, source_target_pairs={{0,8},{4,12},{8,0},{12,4},{16,24},{20,28},{24,16},{28,20},{1,9},{5... | collective-permute-start | bytes 196616 | tf_op jit(solution)/shard_map/ppermute | solution.py:88
  59.3 7.5 %collective-permute-start.30 = (bf16[64,512]{1,0:T(8,128)(2,1)S(1)}, bf16[64,512]{1,0:T(8,128)(2,1)S(1)}, u32[]{:S(2)}, u32[]{:S(2)}) collective-permute-start(bf16[64,512]{1,0:T(8,128)(2,1)S(1)} %shard_map.65.refs_6_.refs_0_), channel_id=1, source_target_pairs={{0,16},{4,20},{8,24},{12,28},{16,0},{20,4},{24,8},{28,12},{1,17},{... | collective-permute-start | bytes 196616 | tf_op jit(solution)/shard_map/ppermute | solution.py:88
  60.9 5.9 %collective-permute-start.31 = (bf16[64,512]{1,0:T(8,128)(2,1)S(1)}, bf16[64,512]{1,0:T(8,128)(2,1)S(1)}, u32[]{:S(2)}, u32[]{:S(2)}) collective-permute-start(bf16[64,512]{1,0:T(8,128)(2,1)S(1)} %shard_map.65.refs_6_.refs_0_), channel_id=1, source_target_pairs={{0,24},{4,28},{8,16},{12,20},{16,8},{20,12},{24,0},{28,4},{1,25},{... | collective-permute-start | bytes 196616 | tf_op jit(solution)/shard_map/ppermute | solution.py:88
  63.2 4.5 %collective-permute-start.22 = (bf16[64,640]{1,0:T(8,128)(2,1)S(1)}, bf16[64,640]{1,0:T(8,128)(2,1)S(1)}, u32[]{:S(2)}, u32[]{:S(2)}) collective-permute-start(bf16[64,640]{1,0:T(8,128)(2,1)S(1)} %shard_map.66.refs_0_), channel_id=1, source_target_pairs={{0,8},{4,12},{8,0},{12,4},{16,24},{20,28},{24,16},{28,20},{1,9},{5... | collective-permute-start | bytes 245768 | tf_op jit(solution)/shard_map/ppermute | solution.py:88
  65.3 5.3 %collective-permute-start.24 = (bf16[64,640]{1,0:T(8,128)(2,1)S(1)}, bf16[64,640]{1,0:T(8,128)(2,1)S(1)}, u32[]{:S(2)}, u32[]{:S(2)}) collective-permute-start(bf16[64,640]{1,0:T(8,128)(2,1)S(1)} %shard_map.66.refs_0_), channel_id=1, source_target_pairs={{0,24},{4,28},{8,16},{12,20},{16,8},{20,12},{24,0},{28,4},{1,25},{... | collective-permute-start | bytes 245768 | tf_op jit(solution)/shard_map/ppermute | solution.py:88
  71.0 6.0 %collective-permute-start.25 = (f32[64,640]{1,0:T(8,128)S(1)}, f32[64,640]{1,0:T(8,128)S(1)}, u32[]{:S(2)}, u32[]{:S(2)}) collective-permute-start(f32[64,640]{1,0:T(8,128)S(1)} %get-tuple-element.88), channel_id=1, source_target_pairs={{0,4},{4,0},{8,12},{12,8},{16,20},{20,16},{24,28},{28,24},{1,5},{5... | collective-permute-start | bytes 491528 | tf_op jit(solution)/shard_map/ppermute | solution.py:88
  71.2 9.1 %collective-permute-start.33 = (bf16[64,512]{1,0:T(8,128)(2,1)S(1)}, bf16[64,512]{1,0:T(8,128)(2,1)S(1)}, u32[]{:S(2)}, u32[]{:S(2)}) collective-permute-start(bf16[64,512]{1,0:T(8,128)(2,1)S(1)} %shard_map.70.refs_0_), channel_id=1, source_target_pairs={{0,1},{1,2},{2,3},{3,0},{4,5},{5,6},{6,7},{7,4},{8,9},{9,10},{10,1... | collective-permute-start | bytes 196616 | tf_op jit(solution)/shard_map/ppermute | solution.py:93
  74.2 7.5 %collective-permute-start.34 = (bf16[64,512]{1,0:T(8,128)(2,1)S(1)}, bf16[64,512]{1,0:T(8,128)(2,1)S(1)}, u32[]{:S(2)}, u32[]{:S(2)}) collective-permute-start(bf16[64,512]{1,0:T(8,128)(2,1)S(1)} %shard_map.70.refs_0_), channel_id=1, source_target_pairs={{0,2},{1,3},{2,0},{3,1},{4,6},{5,7},{6,4},{7,5},{8,10},{9,11},{10,... | collective-permute-start | bytes 196616 | tf_op jit(solution)/shard_map/ppermute | solution.py:93
  75.2 6.4 %collective-permute-start.35 = (bf16[64,512]{1,0:T(8,128)(2,1)S(1)}, bf16[64,512]{1,0:T(8,128)(2,1)S(1)}, u32[]{:S(2)}, u32[]{:S(2)}) collective-permute-start(bf16[64,512]{1,0:T(8,128)(2,1)S(1)} %shard_map.70.refs_0_), channel_id=1, source_target_pairs={{0,3},{1,0},{2,1},{3,2},{4,7},{5,4},{6,5},{7,6},{8,11},{9,8},{10,9... | collective-permute-start | bytes 196616 | tf_op jit(solution)/shard_map/ppermute | solution.py:93
  77.1 7.2 %collective-permute-start.28 = (bf16[64,640]{1,0:T(8,128)(2,1)S(1)}, bf16[64,640]{1,0:T(8,128)(2,1)S(1)}, u32[]{:S(2)}, u32[]{:S(2)}) collective-permute-start(bf16[64,640]{1,0:T(8,128)(2,1)S(1)} %shard_map.68.refs_0_), channel_id=1, source_target_pairs={{0,1},{1,2},{2,3},{3,0},{4,5},{5,6},{6,7},{7,4},{8,9},{9,10},{10,1... | collective-permute-start | bytes 245768 | tf_op jit(solution)/shard_map/ppermute | solution.py:93
  77.8 9.4 %collective-permute-start.27 = (bf16[64,640]{1,0:T(8,128)(2,1)S(1)}, bf16[64,640]{1,0:T(8,128)(2,1)S(1)}, u32[]{:S(2)}, u32[]{:S(2)}) collective-permute-start(bf16[64,640]{1,0:T(8,128)(2,1)S(1)} %shard_map.68.refs_0_), channel_id=1, source_target_pairs={{0,2},{1,3},{2,0},{3,1},{4,6},{5,7},{6,4},{7,5},{8,10},{9,11},{10,... | collective-permute-start | bytes 245768 | tf_op jit(solution)/shard_map/ppermute | solution.py:93
  80.3 7.6 %collective-permute-start.26 = (bf16[64,640]{1,0:T(8,128)(2,1)S(1)}, bf16[64,640]{1,0:T(8,128)(2,1)S(1)}, u32[]{:S(2)}, u32[]{:S(2)}) collective-permute-start(bf16[64,640]{1,0:T(8,128)(2,1)S(1)} %shard_map.68.refs_0_), channel_id=1, source_target_pairs={{0,3},{1,0},{2,1},{3,2},{4,7},{5,4},{6,5},{7,6},{8,11},{9,8},{10,9... | collective-permute-start | bytes 245768 | tf_op jit(solution)/shard_map/ppermute | solution.py:93
  (6 other events, 56.2 us)

commit v7 on v6

--- a/solution.py
+++ b/solution.py
@@ -10,7 +10,7 @@
 damping = 1.0
 BF = jnp.bfloat16
 F32 = jnp.float32
-WORK = [[0, 0], [400000000, 1000000000], [75000000, 75000000], [400000000, 0], [30000000, 150000000], [400000000, 1000000000], [400000000, 400000000], [0, 0], [300000000, 0]]
+WORK = [[0, 0], [400000000, 1000000000], [75000000, 75000000], [400000000, 0], [30000000, 150000000], [0, 0], [1000000000, 100000000], [0, 0], [300000000, 0]]
 LOADS = 8
 
 
@@ -168,7 +168,8 @@
 
 def map_rows(images):
     h, w, n, c = images.shape
-    return jnp.pad(images, ((0, 16 - h), (0, 16 - w), (0, 0), (0, 0))).reshape(256 * n, c)
+    rows = images.reshape(h, w * n, c)
+    return jnp.pad(rows, ((0, 16 - h), (0, (16 - w) * n), (0, 0))).reshape(256 * n, c)
 
 
 def fetch_kernel(*refs):

time: 89.3 us -> 87.4 us (0.979)
  local copies, waits for them, and re-layouts: 3.51 us -> 1.72 us
    pad x4, local copies, waits for them, and re-layouts: 1.82 us -> 0.18 us  [map_rows(): jnp.pad(rows, ((0, 16 - h), (0, (16 - w) * n), (0, 0))).reshape(256 * n, c)]
  transfers between devices with their start and end apart: 36 -> 36, of which waited for: 12 -> 12; matrix products, arithmetic and copies ran while one was open for 3% -> 2% of each run, Pallas kernels for 14% -> 15%
where the time goes in v7:
time: 87.4 us; the launch traced here: 87.2 us
  starting transfers between devices  44.8 us (51%)
  waiting for transfers between devices  21.1 us (24%)
  Pallas kernels  19 us (22%)
  local copies, waits for them, and re-layouts  1.72 us (2%)
    ppermute x18, starting transfers between devices, shift(): return lax.ppermute(value, 'grp', [(i, (i + step) % n) for i in range(n)])  27.7 us
    ppermute x18, starting transfers between devices, swap(): lax.ppermute(value, 'dp', [(i, i ^ bit) for i in range(lax.axis_size('dp'...  17.1 us
    ppermute x18, waiting for transfers between devices, swap(): lax.ppermute(value, 'dp', [(i, i ^ bit) for i in range(lax.axis_size('dp'...  15.6 us
    pallas_call x19, Pallas kernels, stage(): pl.pallas_call(body, in_specs=[near] * (len(operands) + len(after)), out_...  9.62 us
    ppermute x18, waiting for transfers between devices, shift(): return lax.ppermute(value, 'grp', [(i, (i + step) % n) for i in range(n)])  5.52 us
    pallas_call x1, Pallas kernels, load(): pl.pallas_call(load_kernel, in_specs=[pl.BlockSpec(memory_space=pl.ANY),...  5.09 us
    pallas_call x1, Pallas kernels, grad_parts(): pl.pallas_call(grad_kernel, in_specs=[near] * 5, out_specs=[near] * 8, ou...  2.99 us
  transfers between devices with their start and end apart: 36, of which 12 were waited for; matrix products, arithmetic and copies ran while one was open for 2% of the time, Pallas kernels for 15%

profile of v7, /device:TPU:0, one launch (start us, length us, event | category | flops | bytes accessed | tf_op | source)
XLA Modules:
  0.0 87.2 jit_solution(8960373252038337071)
XLA Ops:
  0.5 1.3 %shard_map.55 = (bf16[14,14,2,512]{3,2,1,0:T(2,128)(2,1)S(1)}, bf16[14,14,2,512]{3,2,1,0:T(2,128)(2,1)S(1)}, bf16[512,512]{1,0:T(8,128)(2,1)S(1)}) custom-call(bf16[14,14,2,512]{3,2,1,0:T(2,128)(2,1)} %bitcast.12, bf16[14,14,2,512]{3,2,1,0:T(2,128)(2,1)} %bitcast.14, bf16[512,512]{1,0:T(8,128)(2,1)} %refs_2_.1), custom_call_target="tpu_custom_call" | custom-call | tf_op jit(solution)/shard_map/pallas_call | solution.py:189
  2.8 3.0 %shard_map.56 = (bf16[32,4736]{1,0:T(8,128)(2,1)S(1)}, bf16[32,4736]{1,0:T(8,128)(2,1)S(1)}, bf16[32,4736]{1,0:T(8,128)(2,1)S(1)}, bf16[32,4736]{1,0:T(8,128)(2,...) custom-call(bf16[512,512]{1,0:T(8,128)(2,1)S(1)} %bitcast.7, ...), custom_call_target="tpu_custom_call" | custom-call | flops 2415919104 | bytes 4456448 | tf_op jit(solution)/shard_map/pallas_call | solution.py:149
  5.8 2.9 %collective-permute-start.2 = (bf16[32,4736]{1,0:T(8,128)(2,1)S(1)}, bf16[32,4736]{1,0:T(8,128)(2,1)S(1)}, u32[]{:S(2)}, u32[]{:S(2)}) collective-permute-start(bf16[32,4736]{1,0:T(8,128)(2,1)S(1)} %get-tuple-element.53.after), channel_id=1, source_target_pairs={{0,8},{4,12},{8,0},{12,4},{16,24},{20,28},{24,16},{28,20},{1,9},{5... | collective-permute-start | bytes 909320 | tf_op jit(solution)/shard_map/ppermute | solution.py:88
  8.8 1.5 %collective-permute-start.3 = (bf16[32,4736]{1,0:T(8,128)(2,1)S(1)}, bf16[32,4736]{1,0:T(8,128)(2,1)S(1)}, u32[]{:S(2)}, u32[]{:S(2)}) collective-permute-start(bf16[32,4736]{1,0:T(8,128)(2,1)S(1)} %get-tuple-element.55), channel_id=1, source_target_pairs={{0,16},{4,20},{8,24},{12,28},{16,0},{20,4},{24,8},{28,12},{1,17},{... | collective-permute-start | bytes 909320 | tf_op jit(solution)/shard_map/ppermute | solution.py:88
  12.1 4.7 %collective-permute-done.2.refs_1_ = bf16[32,4736]{1,0:T(8,128)(2,1)S(1)} collective-permute-done((bf16[32,4736]{1,0:T(8,128)(2,1)S(1)}, bf16[32,4736]{1,0:T(8,128)(2,1)S(1)}, u32[]{:S(2)}, u32[]{:S(2)}) %collective-permute-start.2) | collective-permute-done | bytes 303136 | tf_op jit(solution)/shard_map/ppermute | solution.py:88
  16.7 2.1 %collective-permute-done.3.refs_3_ = bf16[32,4736]{1,0:T(8,128)(2,1)S(1)} collective-permute-done((bf16[32,4736]{1,0:T(8,128)(2,1)S(1)}, bf16[32,4736]{1,0:T(8,128)(2,1)S(1)}, u32[]{:S(2)}, u32[]{:S(2)}) %collective-permute-start.3) | collective-permute-done | bytes 303136 | tf_op jit(solution)/shard_map/ppermute | solution.py:88
  19.0 1.6 %collective-permute-start.4 = (bf16[16,4736]{1,0:T(8,128)(2,1)S(1)}, bf16[16,4736]{1,0:T(8,128)(2,1)S(1)}, u32[]{:S(2)}, u32[]{:S(2)}) collective-permute-start(bf16[16,4736]{1,0:T(8,128)(2,1)S(1)} %get-tuple-element.57.refs_4_), channel_id=1, source_target_pairs={{0,16},{4,20},{8,24},{12,28},{16,0},{20,4},{24,8},{28,12},{1,17},{... | collective-permute-start | bytes 454664 | tf_op jit(solution)/shard_map/ppermute | solution.py:88
  21.1 4.2 %collective-permute-done.10.refs_3_ = bf16[32,4736]{1,0:T(8,128)(2,1)S(1)} collective-permute-done((bf16[32,4736]{1,0:T(8,128)(2,1)S(1)}, bf16[32,4736]{1,0:T(8,128)(2,1)S(1)}, u32[]{:S(2)}, u32[]{:S(2)}) %collective-permute-start.10) | collective-permute-done | bytes 303136 | tf_op jit(solution)/shard_map/ppermute | solution.py:88
  25.5 1.6 %collective-permute-start.11 = (bf16[16,4736]{1,0:T(8,128)(2,1)S(1)}, bf16[16,4736]{1,0:T(8,128)(2,1)S(1)}, u32[]{:S(2)}, u32[]{:S(2)}) collective-permute-start(bf16[16,4736]{1,0:T(8,128)(2,1)S(1)} %get-tuple-element.70), channel_id=1, source_target_pairs={{0,16},{4,20},{8,24},{12,28},{16,0},{20,4},{24,8},{28,12},{1,17},{... | collective-permute-start | bytes 454664 | tf_op jit(solution)/shard_map/ppermute | solution.py:88
  29.5 1.6 %collective-permute-start.6 = (bf16[32,1280]{1,0:T(8,128)(2,1)S(1)}, bf16[32,1280]{1,0:T(8,128)(2,1)S(1)}, u32[]{:S(2)}, u32[]{:S(2)}) collective-permute-start(bf16[32,1280]{1,0:T(8,128)(2,1)S(1)} %get-tuple-element.60), channel_id=1, source_target_pairs={{0,1},{1,2},{2,3},{3,0},{4,5},{5,6},{6,7},{7,4},{8,9},{9,10},{10,1... | collective-permute-start | bytes 245768 | tf_op jit(solution)/shard_map/ppermute | solution.py:93
  31.1 2.6 %collective-permute-start.7 = (bf16[32,1280]{1,0:T(8,128)(2,1)S(1)}, bf16[32,1280]{1,0:T(8,128)(2,1)S(1)}, u32[]{:S(2)}, u32[]{:S(2)}) collective-permute-start(bf16[32,1280]{1,0:T(8,128)(2,1)S(1)} %get-tuple-element.61), channel_id=1, source_target_pairs={{0,2},{1,3},{2,0},{3,1},{4,6},{5,7},{6,4},{7,5},{8,10},{9,11},{10,... | collective-permute-start | bytes 245768 | tf_op jit(solution)/shard_map/ppermute | solution.py:93
  33.7 1.3 %collective-permute-start.8 = (bf16[32,1280]{1,0:T(8,128)(2,1)S(1)}, bf16[32,1280]{1,0:T(8,128)(2,1)S(1)}, u32[]{:S(2)}, u32[]{:S(2)}) collective-permute-start(bf16[32,1280]{1,0:T(8,128)(2,1)S(1)} %get-tuple-element.62), channel_id=1, source_target_pairs={{0,3},{1,0},{2,1},{3,2},{4,7},{5,4},{6,5},{7,6},{8,11},{9,8},{10,9... | collective-permute-start | bytes 245768 | tf_op jit(solution)/shard_map/ppermute | solution.py:93
  37.4 2.5 %collective-permute-start.15 = (bf16[32,1280]{1,0:T(8,128)(2,1)S(1)}, bf16[32,1280]{1,0:T(8,128)(2,1)S(1)}, u32[]{:S(2)}, u32[]{:S(2)}) collective-permute-start(bf16[32,1280]{1,0:T(8,128)(2,1)S(1)} %get-tuple-element.75), channel_id=1, source_target_pairs={{0,3},{1,0},{2,1},{3,2},{4,7},{5,4},{6,5},{7,6},{8,11},{9,8},{10,9... | collective-permute-start | bytes 245768 | tf_op jit(solution)/shard_map/ppermute | solution.py:93
  39.8 5.1 %shard_map.63.refs_1_.refs_2_.refs_4_ = bf16[1152,4608]{1,0:T(8,128)(2,1)S(1)} custom-call(bf16[1152,4608]{1,0:T(8,128)(2,1)} %source.1, bf16[32,4736]{1,0:T(8,128)(2,1)} %copy-done), custom_call_target="tpu_custom_call" | custom-call | bytes 21233664 | tf_op jit(solution)/shard_map/pallas_call | solution.py:215
  45.1 1.8 %shard_map.64 = (f32[64,512]{1,0:T(8,128)S(1)}, bf16[64,512]{1,0:T(8,128)(2,1)S(1)}, bf16[64,512]{1,0:T(8,128)(2,1)S(1)}, bf16[64,512]{1,0:T(8,128)(2,1)S(1)}, f...) custom-call(bf16[64,1152]{1,0:T(8,128)(2,1)S(1)} %get-tuple-element., ...), custom_call_target="tpu_custom_call" | custom-call | flops 75000000 | tf_op jit(solution)/shard_map/pallas_call | solution.py:232
  46.9 1.4 %collective-permute-start.19 = (bf16[64,512]{1,0:T(8,128)(2,1)S(1)}, bf16[64,512]{1,0:T(8,128)(2,1)S(1)}, u32[]{:S(2)}, u32[]{:S(2)}) collective-permute-start(bf16[64,512]{1,0:T(8,128)(2,1)S(1)} %get-tuple-element.83), channel_id=1, source_target_pairs={{0,1},{1,2},{2,3},{3,0},{4,5},{5,6},{6,7},{7,4},{8,9},{9,10},{10,1... | collective-permute-start | bytes 196616 | tf_op jit(solution)/shard_map/ppermute | solution.py:93
  48.3 2.2 %collective-permute-start.20 = (bf16[64,512]{1,0:T(8,128)(2,1)S(1)}, bf16[64,512]{1,0:T(8,128)(2,1)S(1)}, u32[]{:S(2)}, u32[]{:S(2)}) collective-permute-start(bf16[64,512]{1,0:T(8,128)(2,1)S(1)} %get-tuple-element.84), channel_id=1, source_target_pairs={{0,2},{1,3},{2,0},{3,1},{4,6},{5,7},{6,4},{7,5},{8,10},{9,11},{10,... | collective-permute-start | bytes 196616 | tf_op jit(solution)/shard_map/ppermute | solution.py:93
  50.5 1.4 %collective-permute-start.21 = (bf16[64,512]{1,0:T(8,128)(2,1)S(1)}, bf16[64,512]{1,0:T(8,128)(2,1)S(1)}, u32[]{:S(2)}, u32[]{:S(2)}) collective-permute-start(bf16[64,512]{1,0:T(8,128)(2,1)S(1)} %get-tuple-element.85), channel_id=1, source_target_pairs={{0,3},{1,0},{2,1},{3,2},{4,7},{5,4},{6,5},{7,6},{8,11},{9,8},{10,9... | collective-permute-start | bytes 196616 | tf_op jit(solution)/shard_map/ppermute | solution.py:93
  53.3 2.5 %collective-permute-start.18 = (bf16[64,640]{1,0:T(8,128)(2,1)S(1)}, bf16[64,640]{1,0:T(8,128)(2,1)S(1)}, u32[]{:S(2)}, u32[]{:S(2)}) collective-permute-start(bf16[64,640]{1,0:T(8,128)(2,1)S(1)} %get-tuple-element.80), channel_id=1, source_target_pairs={{0,3},{1,0},{2,1},{3,2},{4,7},{5,4},{6,5},{7,6},{8,11},{9,8},{10,9... | collective-permute-start | bytes 245768 | tf_op jit(solution)/shard_map/ppermute | solution.py:93
  57.5 1.5 %collective-permute-start.30 = (bf16[64,512]{1,0:T(8,128)(2,1)S(1)}, bf16[64,512]{1,0:T(8,128)(2,1)S(1)}, u32[]{:S(2)}, u32[]{:S(2)}) collective-permute-start(bf16[64,512]{1,0:T(8,128)(2,1)S(1)} %shard_map.65.refs_6_.refs_0_), channel_id=1, source_target_pairs={{0,16},{4,20},{8,24},{12,28},{16,0},{20,4},{24,8},{28,12},{1,17},{... | collective-permute-start | bytes 196616 | tf_op jit(solution)/shard_map/ppermute | solution.py:88
  59.0 1.4 %collective-permute-start.31 = (bf16[64,512]{1,0:T(8,128)(2,1)S(1)}, bf16[64,512]{1,0:T(8,128)(2,1)S(1)}, u32[]{:S(2)}, u32[]{:S(2)}) collective-permute-start(bf16[64,512]{1,0:T(8,128)(2,1)S(1)} %shard_map.65.refs_6_.refs_0_), channel_id=1, source_target_pairs={{0,24},{4,28},{8,16},{12,20},{16,8},{20,12},{24,0},{28,4},{1,25},{... | collective-permute-start | bytes 196616 | tf_op jit(solution)/shard_map/ppermute | solution.py:88
  62.0 1.5 %collective-permute-start.23 = (bf16[64,640]{1,0:T(8,128)(2,1)S(1)}, bf16[64,640]{1,0:T(8,128)(2,1)S(1)}, u32[]{:S(2)}, u32[]{:S(2)}) collective-permute-start(bf16[64,640]{1,0:T(8,128)(2,1)S(1)} %shard_map.66.refs_0_), channel_id=1, source_target_pairs={{0,16},{4,20},{8,24},{12,28},{16,0},{20,4},{24,8},{28,12},{1,17},{... | collective-permute-start | bytes 245768 | tf_op jit(solution)/shard_map/ppermute | solution.py:88
  63.5 1.4 %collective-permute-start.24 = (bf16[64,640]{1,0:T(8,128)(2,1)S(1)}, bf16[64,640]{1,0:T(8,128)(2,1)S(1)}, u32[]{:S(2)}, u32[]{:S(2)}) collective-permute-start(bf16[64,640]{1,0:T(8,128)(2,1)S(1)} %shard_map.66.refs_0_), channel_id=1, source_target_pairs={{0,24},{4,28},{8,16},{12,20},{16,8},{20,12},{24,0},{28,4},{1,25},{... | collective-permute-start | bytes 245768 | tf_op jit(solution)/shard_map/ppermute | solution.py:88
  66.5 2.4 %collective-permute-done.24.refs_3_ = bf16[64,640]{1,0:T(8,128)(2,1)S(1)} collective-permute-done((bf16[64,640]{1,0:T(8,128)(2,1)S(1)}, bf16[64,640]{1,0:T(8,128)(2,1)S(1)}, u32[]{:S(2)}, u32[]{:S(2)}) %collective-permute-start.24) | collective-permute-done | bytes 81952 | tf_op jit(solution)/shard_map/ppermute | solution.py:88
  69.4 2.9 %collective-permute-start.33 = (bf16[64,512]{1,0:T(8,128)(2,1)S(1)}, bf16[64,512]{1,0:T(8,128)(2,1)S(1)}, u32[]{:S(2)}, u32[]{:S(2)}) collective-permute-start(bf16[64,512]{1,0:T(8,128)(2,1)S(1)} %shard_map.70.refs_0_), channel_id=1, source_target_pairs={{0,1},{1,2},{2,3},{3,0},{4,5},{5,6},{6,7},{7,4},{8,9},{9,10},{10,1... | collective-permute-start | bytes 196616 | tf_op jit(solution)/shard_map/ppermute | solution.py:93
  72.2 1.3 %collective-permute-start.34 = (bf16[64,512]{1,0:T(8,128)(2,1)S(1)}, bf16[64,512]{1,0:T(8,128)(2,1)S(1)}, u32[]{:S(2)}, u32[]{:S(2)}) collective-permute-start(bf16[64,512]{1,0:T(8,128)(2,1)S(1)} %shard_map.70.refs_0_), channel_id=1, source_target_pairs={{0,2},{1,3},{2,0},{3,1},{4,6},{5,7},{6,4},{7,5},{8,10},{9,11},{10,... | collective-permute-start | bytes 196616 | tf_op jit(solution)/shard_map/ppermute | solution.py:93
  73.5 1.3 %collective-permute-start.35 = (bf16[64,512]{1,0:T(8,128)(2,1)S(1)}, bf16[64,512]{1,0:T(8,128)(2,1)S(1)}, u32[]{:S(2)}, u32[]{:S(2)}) collective-permute-start(bf16[64,512]{1,0:T(8,128)(2,1)S(1)} %shard_map.70.refs_0_), channel_id=1, source_target_pairs={{0,3},{1,0},{2,1},{3,2},{4,7},{5,4},{6,5},{7,6},{8,11},{9,8},{10,9... | collective-permute-start | bytes 196616 | tf_op jit(solution)/shard_map/ppermute | solution.py:93
  76.1 1.6 %collective-permute-start.27 = (bf16[64,640]{1,0:T(8,128)(2,1)S(1)}, bf16[64,640]{1,0:T(8,128)(2,1)S(1)}, u32[]{:S(2)}, u32[]{:S(2)}) collective-permute-start(bf16[64,640]{1,0:T(8,128)(2,1)S(1)} %shard_map.68.refs_0_), channel_id=1, source_target_pairs={{0,2},{1,3},{2,0},{3,1},{4,6},{5,7},{6,4},{7,5},{8,10},{9,11},{10,... | collective-permute-start | bytes 245768 | tf_op jit(solution)/shard_map/ppermute | solution.py:93
  78.3 1.5 %collective-permute-start.26 = (bf16[64,640]{1,0:T(8,128)(2,1)S(1)}, bf16[64,640]{1,0:T(8,128)(2,1)S(1)}, u32[]{:S(2)}, u32[]{:S(2)}) collective-permute-start(bf16[64,640]{1,0:T(8,128)(2,1)S(1)} %shard_map.68.refs_0_), channel_id=1, source_target_pairs={{0,3},{1,0},{2,1},{3,2},{4,7},{5,4},{6,5},{7,6},{8,11},{9,8},{10,9... | collective-permute-start | bytes 245768 | tf_op jit(solution)/shard_map/ppermute | solution.py:93
  81.1 1.5 %collective-permute-done.28.refs_0_ = bf16[64,640]{1,0:T(8,128)(2,1)S(1)} collective-permute-done((bf16[64,640]{1,0:T(8,128)(2,1)S(1)}, bf16[64,640]{1,0:T(8,128)(2,1)S(1)}, u32[]{:S(2)}, u32[]{:S(2)}) %collective-permute-start.28) | collective-permute-done | bytes 81952 | tf_op jit(solution)/shard_map/ppermute | solution.py:93
  83.1 2.2 %collective-permute-done.27.refs_0_ = bf16[64,640]{1,0:T(8,128)(2,1)S(1)} collective-permute-done((bf16[64,640]{1,0:T(8,128)(2,1)S(1)}, bf16[64,640]{1,0:T(8,128)(2,1)S(1)}, u32[]{:S(2)}, u32[]{:S(2)}) %collective-permute-start.27) | collective-permute-done | bytes 81952 | tf_op jit(solution)/shard_map/ppermute | solution.py:93
  85.9 1.3 %shard_map.76 = bf16[64,1152]{1,0:T(8,128)(2,1)} custom-call(bf16[64,640]{1,0:T(8,128)(2,1)S(1)} %collective-permute-done.26.refs_0_, f32[64,1152]{1,0:T(8,128)S(1)} %shard_map.75.refs_1_, bf16[1152,4608]{1,0:T(8,128)(2,1)S(1)} %shard_map.63.refs_1_.refs_2_.refs_4_), custom_call_target="tpu_custom_call" | custom-call | flops 100000000 | tf_op jit(solution)/shard_map/pallas_call | solution.py:232
  (78 shorter events, 19.7 us)
Async XLA Ops:
  5.8 10.9 %collective-permute-start.2 = (bf16[32,4736]{1,0:T(8,128)(2,1)S(1)}, bf16[32,4736]{1,0:T(8,128)(2,1)S(1)}, u32[]{:S(2)}, u32[]{:S(2)}) collective-permute-start(bf16[32,4736]{1,0:T(8,128)(2,1)S(1)} %get-tuple-element.53.after), channel_id=1, source_target_pairs={{0,8},{4,12},{8,0},{12,4},{16,24},{20,28},{24,16},{28,20},{1,9},{5... | collective-permute-start | bytes 909320 | tf_op jit(solution)/shard_map/ppermute | solution.py:88
  8.8 10.1 %collective-permute-start.3 = (bf16[32,4736]{1,0:T(8,128)(2,1)S(1)}, bf16[32,4736]{1,0:T(8,128)(2,1)S(1)}, u32[]{:S(2)}, u32[]{:S(2)}) collective-permute-start(bf16[32,4736]{1,0:T(8,128)(2,1)S(1)} %get-tuple-element.55), channel_id=1, source_target_pairs={{0,16},{4,20},{8,24},{12,28},{16,0},{20,4},{24,8},{28,12},{1,17},{... | collective-permute-start | bytes 909320 | tf_op jit(solution)/shard_map/ppermute | solution.py:88
  11.2 14.2 %collective-permute-start.10 = (bf16[32,4736]{1,0:T(8,128)(2,1)S(1)}, bf16[32,4736]{1,0:T(8,128)(2,1)S(1)}, u32[]{:S(2)}, u32[]{:S(2)}) collective-permute-start(bf16[32,4736]{1,0:T(8,128)(2,1)S(1)} %get-tuple-element.68), channel_id=1, source_target_pairs={{0,16},{4,20},{8,24},{12,28},{16,0},{20,4},{24,8},{28,12},{1,17},{... | collective-permute-start | bytes 909320 | tf_op jit(solution)/shard_map/ppermute | solution.py:88
  11.7 13.6 %collective-permute-start.9 = (bf16[32,4736]{1,0:T(8,128)(2,1)S(1)}, bf16[32,4736]{1,0:T(8,128)(2,1)S(1)}, u32[]{:S(2)}, u32[]{:S(2)}) collective-permute-start(bf16[32,4736]{1,0:T(8,128)(2,1)S(1)} %get-tuple-element.66), channel_id=1, source_target_pairs={{0,8},{4,12},{8,0},{12,4},{16,24},{20,28},{24,16},{28,20},{1,9},{5... | collective-permute-start | bytes 909320 | tf_op jit(solution)/shard_map/ppermute | solution.py:88
  19.0 9.6 %collective-permute-start.4 = (bf16[16,4736]{1,0:T(8,128)(2,1)S(1)}, bf16[16,4736]{1,0:T(8,128)(2,1)S(1)}, u32[]{:S(2)}, u32[]{:S(2)}) collective-permute-start(bf16[16,4736]{1,0:T(8,128)(2,1)S(1)} %get-tuple-element.57.refs_4_), channel_id=1, source_target_pairs={{0,16},{4,20},{8,24},{12,28},{16,0},{20,4},{24,8},{28,12},{1,17},{... | collective-permute-start | bytes 454664 | tf_op jit(solution)/shard_map/ppermute | solution.py:88
  20.6 8.0 %collective-permute-start.5 = (bf16[16,4736]{1,0:T(8,128)(2,1)S(1)}, bf16[16,4736]{1,0:T(8,128)(2,1)S(1)}, u32[]{:S(2)}, u32[]{:S(2)}) collective-permute-start(bf16[16,4736]{1,0:T(8,128)(2,1)S(1)} %get-tuple-element.58), channel_id=1, source_target_pairs={{0,8},{4,12},{8,0},{12,4},{16,24},{20,28},{24,16},{28,20},{1,9},{5... | collective-permute-start | bytes 454664 | tf_op jit(solution)/shard_map/ppermute | solution.py:88
  25.5 9.6 %collective-permute-start.11 = (bf16[16,4736]{1,0:T(8,128)(2,1)S(1)}, bf16[16,4736]{1,0:T(8,128)(2,1)S(1)}, u32[]{:S(2)}, u32[]{:S(2)}) collective-permute-start(bf16[16,4736]{1,0:T(8,128)(2,1)S(1)} %get-tuple-element.70), channel_id=1, source_target_pairs={{0,16},{4,20},{8,24},{12,28},{16,0},{20,4},{24,8},{28,12},{1,17},{... | collective-permute-start | bytes 454664 | tf_op jit(solution)/shard_map/ppermute | solution.py:88
  27.1 8.0 %collective-permute-start.12 = (bf16[16,4736]{1,0:T(8,128)(2,1)S(1)}, bf16[16,4736]{1,0:T(8,128)(2,1)S(1)}, u32[]{:S(2)}, u32[]{:S(2)}) collective-permute-start(bf16[16,4736]{1,0:T(8,128)(2,1)S(1)} %get-tuple-element.71), channel_id=1, source_target_pairs={{0,8},{4,12},{8,0},{12,4},{16,24},{20,28},{24,16},{28,20},{1,9},{5... | collective-permute-start | bytes 454664 | tf_op jit(solution)/shard_map/ppermute | solution.py:88
  29.5 7.8 %collective-permute-start.6 = (bf16[32,1280]{1,0:T(8,128)(2,1)S(1)}, bf16[32,1280]{1,0:T(8,128)(2,1)S(1)}, u32[]{:S(2)}, u32[]{:S(2)}) collective-permute-start(bf16[32,1280]{1,0:T(8,128)(2,1)S(1)} %get-tuple-element.60), channel_id=1, source_target_pairs={{0,1},{1,2},{2,3},{3,0},{4,5},{5,6},{6,7},{7,4},{8,9},{9,10},{10,1... | collective-permute-start | bytes 245768 | tf_op jit(solution)/shard_map/ppermute | solution.py:93
  31.1 13.8 %collective-permute-start.7 = (bf16[32,1280]{1,0:T(8,128)(2,1)S(1)}, bf16[32,1280]{1,0:T(8,128)(2,1)S(1)}, u32[]{:S(2)}, u32[]{:S(2)}) collective-permute-start(bf16[32,1280]{1,0:T(8,128)(2,1)S(1)} %get-tuple-element.61), channel_id=1, source_target_pairs={{0,2},{1,3},{2,0},{3,1},{4,6},{5,7},{6,4},{7,5},{8,10},{9,11},{10,... | collective-permute-start | bytes 245768 | tf_op jit(solution)/shard_map/ppermute | solution.py:93
  33.7 11.2 %collective-permute-start.8 = (bf16[32,1280]{1,0:T(8,128)(2,1)S(1)}, bf16[32,1280]{1,0:T(8,128)(2,1)S(1)}, u32[]{:S(2)}, u32[]{:S(2)}) collective-permute-start(bf16[32,1280]{1,0:T(8,128)(2,1)S(1)} %get-tuple-element.62), channel_id=1, source_target_pairs={{0,3},{1,0},{2,1},{3,2},{4,7},{5,4},{6,5},{7,6},{8,11},{9,8},{10,9... | collective-permute-start | bytes 245768 | tf_op jit(solution)/shard_map/ppermute | solution.py:93
  36.0 9.0 %collective-permute-start.13 = (bf16[32,1280]{1,0:T(8,128)(2,1)S(1)}, bf16[32,1280]{1,0:T(8,128)(2,1)S(1)}, u32[]{:S(2)}, u32[]{:S(2)}) collective-permute-start(bf16[32,1280]{1,0:T(8,128)(2,1)S(1)} %get-tuple-element.73), channel_id=1, source_target_pairs={{0,1},{1,2},{2,3},{3,0},{4,5},{5,6},{6,7},{7,4},{8,9},{9,10},{10,1... | collective-permute-start | bytes 245768 | tf_op jit(solution)/shard_map/ppermute | solution.py:93
  36.7 8.3 %collective-permute-start.14 = (bf16[32,1280]{1,0:T(8,128)(2,1)S(1)}, bf16[32,1280]{1,0:T(8,128)(2,1)S(1)}, u32[]{:S(2)}, u32[]{:S(2)}) collective-permute-start(bf16[32,1280]{1,0:T(8,128)(2,1)S(1)} %get-tuple-element.74), channel_id=1, source_target_pairs={{0,2},{1,3},{2,0},{3,1},{4,6},{5,7},{6,4},{7,5},{8,10},{9,11},{10,... | collective-permute-start | bytes 245768 | tf_op jit(solution)/shard_map/ppermute | solution.py:93
  37.4 7.7 %collective-permute-start.15 = (bf16[32,1280]{1,0:T(8,128)(2,1)S(1)}, bf16[32,1280]{1,0:T(8,128)(2,1)S(1)}, u32[]{:S(2)}, u32[]{:S(2)}) collective-permute-start(bf16[32,1280]{1,0:T(8,128)(2,1)S(1)} %get-tuple-element.75), channel_id=1, source_target_pairs={{0,3},{1,0},{2,1},{3,2},{4,7},{5,4},{6,5},{7,6},{8,11},{9,8},{10,9... | collective-permute-start | bytes 245768 | tf_op jit(solution)/shard_map/ppermute | solution.py:93
  46.9 6.4 %collective-permute-start.19 = (bf16[64,512]{1,0:T(8,128)(2,1)S(1)}, bf16[64,512]{1,0:T(8,128)(2,1)S(1)}, u32[]{:S(2)}, u32[]{:S(2)}) collective-permute-start(bf16[64,512]{1,0:T(8,128)(2,1)S(1)} %get-tuple-element.83), channel_id=1, source_target_pairs={{0,1},{1,2},{2,3},{3,0},{4,5},{5,6},{6,7},{7,4},{8,9},{9,10},{10,1... | collective-permute-start | bytes 196616 | tf_op jit(solution)/shard_map/ppermute | solution.py:93
  48.3 8.4 %collective-permute-start.20 = (bf16[64,512]{1,0:T(8,128)(2,1)S(1)}, bf16[64,512]{1,0:T(8,128)(2,1)S(1)}, u32[]{:S(2)}, u32[]{:S(2)}) collective-permute-start(bf16[64,512]{1,0:T(8,128)(2,1)S(1)} %get-tuple-element.84), channel_id=1, source_target_pairs={{0,2},{1,3},{2,0},{3,1},{4,6},{5,7},{6,4},{7,5},{8,10},{9,11},{10,... | collective-permute-start | bytes 196616 | tf_op jit(solution)/shard_map/ppermute | solution.py:93
  50.5 6.2 %collective-permute-start.21 = (bf16[64,512]{1,0:T(8,128)(2,1)S(1)}, bf16[64,512]{1,0:T(8,128)(2,1)S(1)}, u32[]{:S(2)}, u32[]{:S(2)}) collective-permute-start(bf16[64,512]{1,0:T(8,128)(2,1)S(1)} %get-tuple-element.85), channel_id=1, source_target_pairs={{0,3},{1,0},{2,1},{3,2},{4,7},{5,4},{6,5},{7,6},{8,11},{9,8},{10,9... | collective-permute-start | bytes 196616 | tf_op jit(solution)/shard_map/ppermute | solution.py:93
  51.9 7.1 %collective-permute-start.16 = (bf16[64,640]{1,0:T(8,128)(2,1)S(1)}, bf16[64,640]{1,0:T(8,128)(2,1)S(1)}, u32[]{:S(2)}, u32[]{:S(2)}) collective-permute-start(bf16[64,640]{1,0:T(8,128)(2,1)S(1)} %get-tuple-element.78), channel_id=1, source_target_pairs={{0,1},{1,2},{2,3},{3,0},{4,5},{5,6},{6,7},{7,4},{8,9},{9,10},{10,1... | collective-permute-start | bytes 245768 | tf_op jit(solution)/shard_map/ppermute | solution.py:93
  52.6 8.7 %collective-permute-start.17 = (bf16[64,640]{1,0:T(8,128)(2,1)S(1)}, bf16[64,640]{1,0:T(8,128)(2,1)S(1)}, u32[]{:S(2)}, u32[]{:S(2)}) collective-permute-start(bf16[64,640]{1,0:T(8,128)(2,1)S(1)} %get-tuple-element.79), channel_id=1, source_target_pairs={{0,2},{1,3},{2,0},{3,1},{4,6},{5,7},{6,4},{7,5},{8,10},{9,11},{10,... | collective-permute-start | bytes 245768 | tf_op jit(solution)/shard_map/ppermute | solution.py:93
  53.3 8.0 %collective-permute-start.18 = (bf16[64,640]{1,0:T(8,128)(2,1)S(1)}, bf16[64,640]{1,0:T(8,128)(2,1)S(1)}, u32[]{:S(2)}, u32[]{:S(2)}) collective-permute-start(bf16[64,640]{1,0:T(8,128)(2,1)S(1)} %get-tuple-element.80), channel_id=1, source_target_pairs={{0,3},{1,0},{2,1},{3,2},{4,7},{5,4},{6,5},{7,6},{8,11},{9,8},{10,9... | collective-permute-start | bytes 245768 | tf_op jit(solution)/shard_map/ppermute | solution.py:93
  56.9 6.7 %collective-permute-start.29 = (bf16[64,512]{1,0:T(8,128)(2,1)S(1)}, bf16[64,512]{1,0:T(8,128)(2,1)S(1)}, u32[]{:S(2)}, u32[]{:S(2)}) collective-permute-start(bf16[64,512]{1,0:T(8,128)(2,1)S(1)} %shard_map.65.refs_6_.refs_0_), channel_id=1, source_target_pairs={{0,8},{4,12},{8,0},{12,4},{16,24},{20,28},{24,16},{28,20},{1,9},{5... | collective-permute-start | bytes 196616 | tf_op jit(solution)/shard_map/ppermute | solution.py:88
  57.5 7.4 %collective-permute-start.30 = (bf16[64,512]{1,0:T(8,128)(2,1)S(1)}, bf16[64,512]{1,0:T(8,128)(2,1)S(1)}, u32[]{:S(2)}, u32[]{:S(2)}) collective-permute-start(bf16[64,512]{1,0:T(8,128)(2,1)S(1)} %shard_map.65.refs_6_.refs_0_), channel_id=1, source_target_pairs={{0,16},{4,20},{8,24},{12,28},{16,0},{20,4},{24,8},{28,12},{1,17},{... | collective-permute-start | bytes 196616 | tf_op jit(solution)/shard_map/ppermute | solution.py:88
  59.0 6.0 %collective-permute-start.31 = (bf16[64,512]{1,0:T(8,128)(2,1)S(1)}, bf16[64,512]{1,0:T(8,128)(2,1)S(1)}, u32[]{:S(2)}, u32[]{:S(2)}) collective-permute-start(bf16[64,512]{1,0:T(8,128)(2,1)S(1)} %shard_map.65.refs_6_.refs_0_), channel_id=1, source_target_pairs={{0,24},{4,28},{8,16},{12,20},{16,8},{20,12},{24,0},{28,4},{1,25},{... | collective-permute-start | bytes 196616 | tf_op jit(solution)/shard_map/ppermute | solution.py:88
  61.4 4.5 %collective-permute-start.22 = (bf16[64,640]{1,0:T(8,128)(2,1)S(1)}, bf16[64,640]{1,0:T(8,128)(2,1)S(1)}, u32[]{:S(2)}, u32[]{:S(2)}) collective-permute-start(bf16[64,640]{1,0:T(8,128)(2,1)S(1)} %shard_map.66.refs_0_), channel_id=1, source_target_pairs={{0,8},{4,12},{8,0},{12,4},{16,24},{20,28},{24,16},{28,20},{1,9},{5... | collective-permute-start | bytes 245768 | tf_op jit(solution)/shard_map/ppermute | solution.py:88
  63.5 5.3 %collective-permute-start.24 = (bf16[64,640]{1,0:T(8,128)(2,1)S(1)}, bf16[64,640]{1,0:T(8,128)(2,1)S(1)}, u32[]{:S(2)}, u32[]{:S(2)}) collective-permute-start(bf16[64,640]{1,0:T(8,128)(2,1)S(1)} %shard_map.66.refs_0_), channel_id=1, source_target_pairs={{0,24},{4,28},{8,16},{12,20},{16,8},{20,12},{24,0},{28,4},{1,25},{... | collective-permute-start | bytes 245768 | tf_op jit(solution)/shard_map/ppermute | solution.py:88
  69.2 6.1 %collective-permute-start.25 = (f32[64,640]{1,0:T(8,128)S(1)}, f32[64,640]{1,0:T(8,128)S(1)}, u32[]{:S(2)}, u32[]{:S(2)}) collective-permute-start(f32[64,640]{1,0:T(8,128)S(1)} %get-tuple-element.88), channel_id=1, source_target_pairs={{0,4},{4,0},{8,12},{12,8},{16,20},{20,16},{24,28},{28,24},{1,5},{5... | collective-permute-start | bytes 491528 | tf_op jit(solution)/shard_map/ppermute | solution.py:88
  69.4 9.0 %collective-permute-start.33 = (bf16[64,512]{1,0:T(8,128)(2,1)S(1)}, bf16[64,512]{1,0:T(8,128)(2,1)S(1)}, u32[]{:S(2)}, u32[]{:S(2)}) collective-permute-start(bf16[64,512]{1,0:T(8,128)(2,1)S(1)} %shard_map.70.refs_0_), channel_id=1, source_target_pairs={{0,1},{1,2},{2,3},{3,0},{4,5},{5,6},{6,7},{7,4},{8,9},{9,10},{10,1... | collective-permute-start | bytes 196616 | tf_op jit(solution)/shard_map/ppermute | solution.py:93
  72.2 7.6 %collective-permute-start.34 = (bf16[64,512]{1,0:T(8,128)(2,1)S(1)}, bf16[64,512]{1,0:T(8,128)(2,1)S(1)}, u32[]{:S(2)}, u32[]{:S(2)}) collective-permute-start(bf16[64,512]{1,0:T(8,128)(2,1)S(1)} %shard_map.70.refs_0_), channel_id=1, source_target_pairs={{0,2},{1,3},{2,0},{3,1},{4,6},{5,7},{6,4},{7,5},{8,10},{9,11},{10,... | collective-permute-start | bytes 196616 | tf_op jit(solution)/shard_map/ppermute | solution.py:93
  73.5 6.3 %collective-permute-start.35 = (bf16[64,512]{1,0:T(8,128)(2,1)S(1)}, bf16[64,512]{1,0:T(8,128)(2,1)S(1)}, u32[]{:S(2)}, u32[]{:S(2)}) collective-permute-start(bf16[64,512]{1,0:T(8,128)(2,1)S(1)} %shard_map.70.refs_0_), channel_id=1, source_target_pairs={{0,3},{1,0},{2,1},{3,2},{4,7},{5,4},{6,5},{7,6},{8,11},{9,8},{10,9... | collective-permute-start | bytes 196616 | tf_op jit(solution)/shard_map/ppermute | solution.py:93
  75.4 7.2 %collective-permute-start.28 = (bf16[64,640]{1,0:T(8,128)(2,1)S(1)}, bf16[64,640]{1,0:T(8,128)(2,1)S(1)}, u32[]{:S(2)}, u32[]{:S(2)}) collective-permute-start(bf16[64,640]{1,0:T(8,128)(2,1)S(1)} %shard_map.68.refs_0_), channel_id=1, source_target_pairs={{0,1},{1,2},{2,3},{3,0},{4,5},{5,6},{6,7},{7,4},{8,9},{9,10},{10,1... | collective-permute-start | bytes 245768 | tf_op jit(solution)/shard_map/ppermute | solution.py:93
  76.1 9.2 %collective-permute-start.27 = (bf16[64,640]{1,0:T(8,128)(2,1)S(1)}, bf16[64,640]{1,0:T(8,128)(2,1)S(1)}, u32[]{:S(2)}, u32[]{:S(2)}) collective-permute-start(bf16[64,640]{1,0:T(8,128)(2,1)S(1)} %shard_map.68.refs_0_), channel_id=1, source_target_pairs={{0,2},{1,3},{2,0},{3,1},{4,6},{5,7},{6,4},{7,5},{8,10},{9,11},{10,... | collective-permute-start | bytes 245768 | tf_op jit(solution)/shard_map/ppermute | solution.py:93
  78.3 7.6 %collective-permute-start.26 = (bf16[64,640]{1,0:T(8,128)(2,1)S(1)}, bf16[64,640]{1,0:T(8,128)(2,1)S(1)}, u32[]{:S(2)}, u32[]{:S(2)}) collective-permute-start(bf16[64,640]{1,0:T(8,128)(2,1)S(1)} %shard_map.68.refs_0_), channel_id=1, source_target_pairs={{0,3},{1,0},{2,1},{3,2},{4,7},{5,4},{6,5},{7,6},{8,11},{9,8},{10,9... | collective-permute-start | bytes 245768 | tf_op jit(solution)/shard_map/ppermute | solution.py:93
  (6 other events, 54.6 us)

commit v8 on v7

--- a/solution.py
+++ b/solution.py
@@ -103,8 +103,22 @@
 )
 
 
-def grad_kernel(act_a, act_b, dout_a, dout_b, turn, *refs):
-    pieces, (acts, flipped, turned, lhs) = refs[:8], refs[8:]
+def gradient(lhs, acts, pieces, edge, rows):
+    channels = acts.shape[1]
+    height = lhs.shape[0] // 3
+    size = pieces[0].shape[0]
+    for step in range(3):
+        window = acts[edge * step : edge * step + 2 * rows, :]
+        out = jnp.dot(lhs[...], window, preferred_element_type=F32)
+        for tap in range(3):
+            column = (3 * step + tap) * channels
+            for at, ref in enumerate(pieces):
+                start = tap * height + at * size
+                ref[:, column : column + channels] = out[start : start + size, :].astype(BF)
+
+
+def first_kernel(act_a, act_b, dout_a, dout_b, turn, *refs):
+    pieces, squared, (acts, later, flipped, turned, lhs) = refs[:4], refs[4], refs[5:]
     rows, channels = act_a.shape
     edge = rows // 16
     images = edge // 16
@@ -121,6 +135,7 @@
     acts[edge : edge + rows, :] = act_a[...]
     acts[edge + rows : edge + 2 * rows, :] = act_b[...]
     squares = jnp.zeros((half, 128), F32)
+    height = half // 2
     for at, ref in enumerate((dout_a, dout_b)):
         part = lax.dot_general(
             turned[...], ref[...], (((1,), (1,)), ((), ())), preferred_element_type=F32
@@ -128,42 +143,60 @@
         for lane in range(0, rows, 128):
             squares = squares + part[:, lane : lane + 128] * part[:, lane : lane + 128]
         for tap, by in enumerate((rows - images, 0, images)):
-            moved = pltpu.roll(part, by, 1) if by else part
-            lhs[tap * half : (tap + 1) * half, at * rows : (at + 1) * rows] = moved.astype(BF)
+            moved = (pltpu.roll(part, by, 1) if by else part).astype(BF)
+            span = slice(at * rows, (at + 1) * rows)
+            lhs[tap * height : (tap + 1) * height, span] = moved[:height, :]
+            later[tap * height : (tap + 1) * height, span] = moved[height:, :]
     for at, ref in enumerate(pieces):
-        ref[:, 9 * channels :] = squares[at * 2 * sub : (at + 1) * 2 * sub, :].astype(BF)
-    for step in range(3):
-        window = acts[edge * step : edge * step + 2 * rows, :]
-        out = jnp.dot(lhs[...], window, preferred_element_type=F32)
-        for tap in range(3):
-            column = (3 * step + tap) * channels
-            for at, ref in enumerate(pieces):
-                start = tap * half + at * 2 * sub
-                ref[:, column : column + channels] = out[start : start + 2 * sub, :].astype(BF)
+        size = ref.shape[0]
+        ref[:, 9 * channels :] = squares[at * size : (at + 1) * size, :].astype(BF)
+    squared[...] = squares[height:, :].astype(BF)
+    gradient(lhs, acts, pieces, edge, rows)
+
+
+def second_kernel(acts, later, squared, *pieces):
+    channels = acts.shape[1]
+    rows = later.shape[1] // 2
+    for at, ref in enumerate(pieces):
+        size = ref.shape[0]
+        ref[:, 9 * channels :] = squared[at * size : (at + 1) * size, :]
+    gradient(later, acts, pieces, rows // 16, rows)
 
 
 def grad_parts(act_a, act_b, dout_a, dout_b, turn):
     rows, channels = act_a.shape
     half = channels // 2
     near = pl.BlockSpec(memory_space=pltpu.VMEM)
-    return pl.pallas_call(
-        grad_kernel,
+    piece = jax.ShapeDtypeStruct((half // 8, 9 * channels + 128), BF)
+    params = pltpu.CompilerParams(vmem_limit_bytes=12 << 20)
+    *first, squared, acts, later = pl.pallas_call(
+        first_kernel,
         in_specs=[near] * 5,
-        out_specs=[near] * 8,
-        out_shape=[jax.ShapeDtypeStruct((half // 8, 9 * channels + 128), BF)] * 8,
+        out_specs=[near] * 7,
+        out_shape=[piece] * 4
+        + [
+            jax.ShapeDtypeStruct((half // 2, 128), BF),
+            jax.ShapeDtypeStruct((2 * rows + rows // 8, channels), BF),
+            jax.ShapeDtypeStruct((3 * half // 2, 2 * rows), BF),
+        ],
         scratch_shapes=[
-            pltpu.VMEM((2 * rows + rows // 8, channels), BF),
             pltpu.VMEM((half, channels), BF),
             pltpu.VMEM((half, channels), BF),
-            pltpu.VMEM((3 * half, 2 * rows), BF),
+            pltpu.VMEM((3 * half // 2, 2 * rows), BF),
         ],
-        compiler_params=pltpu.CompilerParams(vmem_limit_bytes=16 << 20),
+        compiler_params=params,
+    )(act_a, act_b, dout_a, dout_b, turn)
+    second = pl.pallas_call(
+        second_kernel,
+        in_specs=[near] * 3,
+        out_specs=[near] * 4,
+        out_shape=[piece] * 4,
+        compiler_params=params,
         cost_estimate=pl.CostEstimate(
-            flops=18 * channels * channels * rows,
-            bytes_accessed=4 * rows * channels * 2 + 9 * channels * channels,
-            transcendentals=0,
+            flops=9 * channels * channels * rows, bytes_accessed=0, transcendentals=0
         ),
-    )(act_a, act_b, dout_a, dout_b, turn)
+    )(acts, later, squared)
+    return [*first, *second]
 
 
 def map_rows(images):
@@ -356,8 +389,13 @@
     own_rows = input_eigen.shape[0]
     block = (me & 1) * 4 + (me >> 1)
 
+    act_own = activations.transpose(1, 2, 0, 3)
+    dout_own = out_grads.transpose(1, 2, 0, 3)
+    act_near, dout_near, basis_near = fetch([act_own, dout_own, output_basis])
+    act_rows = [map_rows(act_near), map_rows(swap(act_own, 1))]
+    dout_rows = [map_rows(dout_near), map_rows(swap(dout_own, 1))]
     both = jnp.concatenate(
-        [lax.dynamic_slice_in_dim(output_basis, r * width, width, 0) for r in (me, me ^ 1)], 0
+        [lax.dynamic_slice_in_dim(basis_near, r * width, width, 0) for r in (me, me ^ 1)], 0
     )
     weights = jnp.concatenate(
         [
@@ -367,11 +405,6 @@
         1,
     )
 
-    act_own = activations.transpose(1, 2, 0, 3)
-    dout_own = out_grads.transpose(1, 2, 0, 3)
-    act_near, dout_near, basis_near = fetch([act_own, dout_own, output_basis])
-    act_rows = [map_rows(act_near), map_rows(swap(act_own, 1))]
-    dout_rows = [map_rows(dout_near), map_rows(swap(dout_own, 1))]
     parts = list(grad_parts(*act_rows, *dout_rows, basis_near))
 
     sub = width // 4

time: 87.4 us -> 86.3 us (0.987)
    pallas_call x1 -> x2, Pallas kernels: 2.99 us -> 3.23 us  [the longest x1 1.85 us: grad_parts(): pl.pallas_call(first_kernel, in_specs=[near] * 5, out_specs=[near] * 7, o...]
  transfers between devices with their start and end apart: 36 -> 36, of which waited for: 12 -> 11; matrix products, arithmetic and copies ran while one was open for 2% -> 1% of each run, Pallas kernels for 15% -> 17%
where the time goes in v8:
time: 86.3 us; the launch traced here: 86.1 us
  starting transfers between devices  44.8 us (52%)
  waiting for transfers between devices  20.7 us (24%)
  Pallas kernels  19.3 us (22%)
    ppermute x18, starting transfers between devices, shift(): return lax.ppermute(value, 'grp', [(i, (i + step) % n) for i in range(n)])  27.6 us
    ppermute x18, starting transfers between devices, swap(): lax.ppermute(value, 'dp', [(i, i ^ bit) for i in range(lax.axis_size('dp'...  17.2 us
    ppermute x18, waiting for transfers between devices, swap(): lax.ppermute(value, 'dp', [(i, i ^ bit) for i in range(lax.axis_size('dp'...  15 us
    pallas_call x19, Pallas kernels, stage(): pl.pallas_call(body, in_specs=[near] * (len(operands) + len(after)), out_...  9.63 us
    ppermute x18, waiting for transfers between devices, shift(): return lax.ppermute(value, 'grp', [(i, (i + step) % n) for i in range(n)])  5.63 us
    pallas_call x1, Pallas kernels, load(): pl.pallas_call(load_kernel, in_specs=[pl.BlockSpec(memory_space=pl.ANY),...  5.09 us
    pallas_call x1, Pallas kernels, grad_parts(): pl.pallas_call(first_kernel, in_specs=[near] * 5, out_specs=[near] * 7, o...  1.85 us
  transfers between devices with their start and end apart: 36, of which 11 were waited for; matrix products, arithmetic and copies ran while one was open for 1% of the time, Pallas kernels for 17%

profile of v8, /device:TPU:0, one launch (start us, length us, event | category | flops | bytes accessed | tf_op | source)
XLA Modules:
  0.0 86.1 jit_solution(9312197011140050528)
XLA Ops:
  0.5 1.3 %shard_map.55 = (bf16[14,14,2,512]{3,2,1,0:T(2,128)(2,1)S(1)}, bf16[14,14,2,512]{3,2,1,0:T(2,128)(2,1)S(1)}, bf16[512,512]{1,0:T(8,128)(2,1)S(1)}) custom-call(bf16[14,14,2,512]{3,2,1,0:T(2,128)(2,1)} %bitcast.12, bf16[14,14,2,512]{3,2,1,0:T(2,128)(2,1)} %bitcast.14, bf16[512,512]{1,0:T(8,128)(2,1)} %refs_2_.1), custom_call_target="tpu_custom_call" | custom-call | tf_op jit(solution)/shard_map/pallas_call | solution.py:222
  2.8 1.9 %shard_map.56 = (bf16[32,4736]{1,0:T(8,128)(2,1)S(1)}, bf16[32,4736]{1,0:T(8,128)(2,1)S(1)}, bf16[32,4736]{1,0:T(8,128)(2,1)S(1)}, bf16[32,4736]{1,0:T(8,128)(2,...) custom-call(bf16[512,512]{1,0:T(8,128)(2,1)S(1)} %bitcast.7, ...), custom_call_target="tpu_custom_call" | custom-call | tf_op jit(solution)/shard_map/pallas_call | solution.py:172
  4.7 3.0 %collective-permute-start.2 = (bf16[32,4736]{1,0:T(8,128)(2,1)S(1)}, bf16[32,4736]{1,0:T(8,128)(2,1)S(1)}, u32[]{:S(2)}, u32[]{:S(2)}) collective-permute-start(bf16[32,4736]{1,0:T(8,128)(2,1)S(1)} %get-tuple-element.56.after), channel_id=1, source_target_pairs={{0,8},{4,12},{8,0},{12,4},{16,24},{20,28},{24,16},{28,20},{1,9},{5... | collective-permute-start | bytes 909320 | tf_op jit(solution)/shard_map/ppermute | solution.py:88
  7.6 1.5 %collective-permute-start.3 = (bf16[32,4736]{1,0:T(8,128)(2,1)S(1)}, bf16[32,4736]{1,0:T(8,128)(2,1)S(1)}, u32[]{:S(2)}, u32[]{:S(2)}) collective-permute-start(bf16[32,4736]{1,0:T(8,128)(2,1)S(1)} %get-tuple-element.58), channel_id=1, source_target_pairs={{0,16},{4,20},{8,24},{12,28},{16,0},{20,4},{24,8},{28,12},{1,17},{... | collective-permute-start | bytes 909320 | tf_op jit(solution)/shard_map/ppermute | solution.py:88
  9.2 1.4 %shard_map.60 = (bf16[32,4736]{1,0:T(8,128)(2,1)S(1)}, bf16[32,4736]{1,0:T(8,128)(2,1)S(1)}, bf16[32,4736]{1,0:T(8,128)(2,1)S(1)}, bf16[32,4736]{1,0:T(8,128)(2,1)S(1)}) custom-call(bf16[1088,512]{1,0:T(8,128)(2,1)S(1)} %get-tuple-element.68.acts, bf16[384,1024]{1,0:T(8,128)(2,1)S(1)} %get-tuple-element.69.later, bf16[128,128]{1,0:T(8,128)(2,1)S(1)} %get-tuple-element.70.squared), custom_call_target="tpu_custom_call" | custom-call | flops 1207959552 | tf_op jit(solution)/shard_map/pallas_call | solution.py:189
  11.5 4.2 %collective-permute-done.2.refs_1_ = bf16[32,4736]{1,0:T(8,128)(2,1)S(1)} collective-permute-done((bf16[32,4736]{1,0:T(8,128)(2,1)S(1)}, bf16[32,4736]{1,0:T(8,128)(2,1)S(1)}, u32[]{:S(2)}, u32[]{:S(2)}) %collective-permute-start.2) | collective-permute-done | bytes 303136 | tf_op jit(solution)/shard_map/ppermute | solution.py:88
  15.6 2.1 %collective-permute-done.3.refs_3_ = bf16[32,4736]{1,0:T(8,128)(2,1)S(1)} collective-permute-done((bf16[32,4736]{1,0:T(8,128)(2,1)S(1)}, bf16[32,4736]{1,0:T(8,128)(2,1)S(1)}, u32[]{:S(2)}, u32[]{:S(2)}) %collective-permute-start.3) | collective-permute-done | bytes 303136 | tf_op jit(solution)/shard_map/ppermute | solution.py:88
  17.9 1.6 %collective-permute-start.4 = (bf16[16,4736]{1,0:T(8,128)(2,1)S(1)}, bf16[16,4736]{1,0:T(8,128)(2,1)S(1)}, u32[]{:S(2)}, u32[]{:S(2)}) collective-permute-start(bf16[16,4736]{1,0:T(8,128)(2,1)S(1)} %get-tuple-element.60.refs_4_), channel_id=1, source_target_pairs={{0,16},{4,20},{8,24},{12,28},{16,0},{20,4},{24,8},{28,12},{1,17},{... | collective-permute-start | bytes 454664 | tf_op jit(solution)/shard_map/ppermute | solution.py:88
  20.0 4.2 %collective-permute-done.10.refs_3_ = bf16[32,4736]{1,0:T(8,128)(2,1)S(1)} collective-permute-done((bf16[32,4736]{1,0:T(8,128)(2,1)S(1)}, bf16[32,4736]{1,0:T(8,128)(2,1)S(1)}, u32[]{:S(2)}, u32[]{:S(2)}) %collective-permute-start.10) | collective-permute-done | bytes 303136 | tf_op jit(solution)/shard_map/ppermute | solution.py:88
  24.4 1.6 %collective-permute-start.11 = (bf16[16,4736]{1,0:T(8,128)(2,1)S(1)}, bf16[16,4736]{1,0:T(8,128)(2,1)S(1)}, u32[]{:S(2)}, u32[]{:S(2)}) collective-permute-start(bf16[16,4736]{1,0:T(8,128)(2,1)S(1)} %get-tuple-element.76), channel_id=1, source_target_pairs={{0,16},{4,20},{8,24},{12,28},{16,0},{20,4},{24,8},{28,12},{1,17},{... | collective-permute-start | bytes 454664 | tf_op jit(solution)/shard_map/ppermute | solution.py:88
  28.4 1.6 %collective-permute-start.6 = (bf16[32,1280]{1,0:T(8,128)(2,1)S(1)}, bf16[32,1280]{1,0:T(8,128)(2,1)S(1)}, u32[]{:S(2)}, u32[]{:S(2)}) collective-permute-start(bf16[32,1280]{1,0:T(8,128)(2,1)S(1)} %get-tuple-element.63), channel_id=1, source_target_pairs={{0,1},{1,2},{2,3},{3,0},{4,5},{5,6},{6,7},{7,4},{8,9},{9,10},{10,1... | collective-permute-start | bytes 245768 | tf_op jit(solution)/shard_map/ppermute | solution.py:93
  30.0 2.6 %collective-permute-start.7 = (bf16[32,1280]{1,0:T(8,128)(2,1)S(1)}, bf16[32,1280]{1,0:T(8,128)(2,1)S(1)}, u32[]{:S(2)}, u32[]{:S(2)}) collective-permute-start(bf16[32,1280]{1,0:T(8,128)(2,1)S(1)} %get-tuple-element.64), channel_id=1, source_target_pairs={{0,2},{1,3},{2,0},{3,1},{4,6},{5,7},{6,4},{7,5},{8,10},{9,11},{10,... | collective-permute-start | bytes 245768 | tf_op jit(solution)/shard_map/ppermute | solution.py:93
  32.6 1.3 %collective-permute-start.8 = (bf16[32,1280]{1,0:T(8,128)(2,1)S(1)}, bf16[32,1280]{1,0:T(8,128)(2,1)S(1)}, u32[]{:S(2)}, u32[]{:S(2)}) collective-permute-start(bf16[32,1280]{1,0:T(8,128)(2,1)S(1)} %get-tuple-element.65), channel_id=1, source_target_pairs={{0,3},{1,0},{2,1},{3,2},{4,7},{5,4},{6,5},{7,6},{8,11},{9,8},{10,9... | collective-permute-start | bytes 245768 | tf_op jit(solution)/shard_map/ppermute | solution.py:93
  36.3 2.5 %collective-permute-start.15 = (bf16[32,1280]{1,0:T(8,128)(2,1)S(1)}, bf16[32,1280]{1,0:T(8,128)(2,1)S(1)}, u32[]{:S(2)}, u32[]{:S(2)}) collective-permute-start(bf16[32,1280]{1,0:T(8,128)(2,1)S(1)} %get-tuple-element.81), channel_id=1, source_target_pairs={{0,3},{1,0},{2,1},{3,2},{4,7},{5,4},{6,5},{7,6},{8,11},{9,8},{10,9... | collective-permute-start | bytes 245768 | tf_op jit(solution)/shard_map/ppermute | solution.py:93
  38.7 5.1 %shard_map.64.refs_1_.refs_2_.refs_4_ = bf16[1152,4608]{1,0:T(8,128)(2,1)S(1)} custom-call(bf16[1152,4608]{1,0:T(8,128)(2,1)} %source.1, bf16[32,4736]{1,0:T(8,128)(2,1)} %copy-done), custom_call_target="tpu_custom_call" | custom-call | bytes 21233664 | tf_op jit(solution)/shard_map/pallas_call | solution.py:248
  44.0 1.8 %shard_map.65 = (f32[64,512]{1,0:T(8,128)S(1)}, bf16[64,512]{1,0:T(8,128)(2,1)S(1)}, bf16[64,512]{1,0:T(8,128)(2,1)S(1)}, bf16[64,512]{1,0:T(8,128)(2,1)S(1)}, f...) custom-call(bf16[64,1152]{1,0:T(8,128)(2,1)S(1)} %get-tuple-element., ...), custom_call_target="tpu_custom_call" | custom-call | flops 75000000 | tf_op jit(solution)/shard_map/pallas_call | solution.py:265
  45.8 1.4 %collective-permute-start.19 = (bf16[64,512]{1,0:T(8,128)(2,1)S(1)}, bf16[64,512]{1,0:T(8,128)(2,1)S(1)}, u32[]{:S(2)}, u32[]{:S(2)}) collective-permute-start(bf16[64,512]{1,0:T(8,128)(2,1)S(1)} %get-tuple-element.89), channel_id=1, source_target_pairs={{0,1},{1,2},{2,3},{3,0},{4,5},{5,6},{6,7},{7,4},{8,9},{9,10},{10,1... | collective-permute-start | bytes 196616 | tf_op jit(solution)/shard_map/ppermute | solution.py:93
  47.2 2.3 %collective-permute-start.20 = (bf16[64,512]{1,0:T(8,128)(2,1)S(1)}, bf16[64,512]{1,0:T(8,128)(2,1)S(1)}, u32[]{:S(2)}, u32[]{:S(2)}) collective-permute-start(bf16[64,512]{1,0:T(8,128)(2,1)S(1)} %get-tuple-element.90), channel_id=1, source_target_pairs={{0,2},{1,3},{2,0},{3,1},{4,6},{5,7},{6,4},{7,5},{8,10},{9,11},{10,... | collective-permute-start | bytes 196616 | tf_op jit(solution)/shard_map/ppermute | solution.py:93
  49.4 1.4 %collective-permute-start.21 = (bf16[64,512]{1,0:T(8,128)(2,1)S(1)}, bf16[64,512]{1,0:T(8,128)(2,1)S(1)}, u32[]{:S(2)}, u32[]{:S(2)}) collective-permute-start(bf16[64,512]{1,0:T(8,128)(2,1)S(1)} %get-tuple-element.91), channel_id=1, source_target_pairs={{0,3},{1,0},{2,1},{3,2},{4,7},{5,4},{6,5},{7,6},{8,11},{9,8},{10,9... | collective-permute-start | bytes 196616 | tf_op jit(solution)/shard_map/ppermute | solution.py:93
  52.1 2.6 %collective-permute-start.18 = (bf16[64,640]{1,0:T(8,128)(2,1)S(1)}, bf16[64,640]{1,0:T(8,128)(2,1)S(1)}, u32[]{:S(2)}, u32[]{:S(2)}) collective-permute-start(bf16[64,640]{1,0:T(8,128)(2,1)S(1)} %get-tuple-element.86), channel_id=1, source_target_pairs={{0,3},{1,0},{2,1},{3,2},{4,7},{5,4},{6,5},{7,6},{8,11},{9,8},{10,9... | collective-permute-start | bytes 245768 | tf_op jit(solution)/shard_map/ppermute | solution.py:93
  56.4 1.6 %collective-permute-start.30 = (bf16[64,512]{1,0:T(8,128)(2,1)S(1)}, bf16[64,512]{1,0:T(8,128)(2,1)S(1)}, u32[]{:S(2)}, u32[]{:S(2)}) collective-permute-start(bf16[64,512]{1,0:T(8,128)(2,1)S(1)} %shard_map.66.refs_6_.refs_0_), channel_id=1, source_target_pairs={{0,16},{4,20},{8,24},{12,28},{16,0},{20,4},{24,8},{28,12},{1,17},{... | collective-permute-start | bytes 196616 | tf_op jit(solution)/shard_map/ppermute | solution.py:88
  57.9 1.4 %collective-permute-start.31 = (bf16[64,512]{1,0:T(8,128)(2,1)S(1)}, bf16[64,512]{1,0:T(8,128)(2,1)S(1)}, u32[]{:S(2)}, u32[]{:S(2)}) collective-permute-start(bf16[64,512]{1,0:T(8,128)(2,1)S(1)} %shard_map.66.refs_6_.refs_0_), channel_id=1, source_target_pairs={{0,24},{4,28},{8,16},{12,20},{16,8},{20,12},{24,0},{28,4},{1,25},{... | collective-permute-start | bytes 196616 | tf_op jit(solution)/shard_map/ppermute | solution.py:88
  60.9 1.5 %collective-permute-start.23 = (bf16[64,640]{1,0:T(8,128)(2,1)S(1)}, bf16[64,640]{1,0:T(8,128)(2,1)S(1)}, u32[]{:S(2)}, u32[]{:S(2)}) collective-permute-start(bf16[64,640]{1,0:T(8,128)(2,1)S(1)} %shard_map.67.refs_0_), channel_id=1, source_target_pairs={{0,16},{4,20},{8,24},{12,28},{16,0},{20,4},{24,8},{28,12},{1,17},{... | collective-permute-start | bytes 245768 | tf_op jit(solution)/shard_map/ppermute | solution.py:88
  62.4 1.4 %collective-permute-start.24 = (bf16[64,640]{1,0:T(8,128)(2,1)S(1)}, bf16[64,640]{1,0:T(8,128)(2,1)S(1)}, u32[]{:S(2)}, u32[]{:S(2)}) collective-permute-start(bf16[64,640]{1,0:T(8,128)(2,1)S(1)} %shard_map.67.refs_0_), channel_id=1, source_target_pairs={{0,24},{4,28},{8,16},{12,20},{16,8},{20,12},{24,0},{28,4},{1,25},{... | collective-permute-start | bytes 245768 | tf_op jit(solution)/shard_map/ppermute | solution.py:88
  65.3 2.4 %collective-permute-done.24.refs_3_ = bf16[64,640]{1,0:T(8,128)(2,1)S(1)} collective-permute-done((bf16[64,640]{1,0:T(8,128)(2,1)S(1)}, bf16[64,640]{1,0:T(8,128)(2,1)S(1)}, u32[]{:S(2)}, u32[]{:S(2)}) %collective-permute-start.24) | collective-permute-done | bytes 81952 | tf_op jit(solution)/shard_map/ppermute | solution.py:88
  68.3 2.9 %collective-permute-start.33 = (bf16[64,512]{1,0:T(8,128)(2,1)S(1)}, bf16[64,512]{1,0:T(8,128)(2,1)S(1)}, u32[]{:S(2)}, u32[]{:S(2)}) collective-permute-start(bf16[64,512]{1,0:T(8,128)(2,1)S(1)} %shard_map.71.refs_0_), channel_id=1, source_target_pairs={{0,1},{1,2},{2,3},{3,0},{4,5},{5,6},{6,7},{7,4},{8,9},{9,10},{10,1... | collective-permute-start | bytes 196616 | tf_op jit(solution)/shard_map/ppermute | solution.py:93
  72.4 1.3 %collective-permute-start.35 = (bf16[64,512]{1,0:T(8,128)(2,1)S(1)}, bf16[64,512]{1,0:T(8,128)(2,1)S(1)}, u32[]{:S(2)}, u32[]{:S(2)}) collective-permute-start(bf16[64,512]{1,0:T(8,128)(2,1)S(1)} %shard_map.71.refs_0_), channel_id=1, source_target_pairs={{0,3},{1,0},{2,1},{3,2},{4,7},{5,4},{6,5},{7,6},{8,11},{9,8},{10,9... | collective-permute-start | bytes 196616 | tf_op jit(solution)/shard_map/ppermute | solution.py:93
  75.0 1.7 %collective-permute-start.27 = (bf16[64,640]{1,0:T(8,128)(2,1)S(1)}, bf16[64,640]{1,0:T(8,128)(2,1)S(1)}, u32[]{:S(2)}, u32[]{:S(2)}) collective-permute-start(bf16[64,640]{1,0:T(8,128)(2,1)S(1)} %shard_map.69.refs_0_), channel_id=1, source_target_pairs={{0,2},{1,3},{2,0},{3,1},{4,6},{5,7},{6,4},{7,5},{8,10},{9,11},{10,... | collective-permute-start | bytes 245768 | tf_op jit(solution)/shard_map/ppermute | solution.py:93
  77.3 1.5 %collective-permute-start.26 = (bf16[64,640]{1,0:T(8,128)(2,1)S(1)}, bf16[64,640]{1,0:T(8,128)(2,1)S(1)}, u32[]{:S(2)}, u32[]{:S(2)}) collective-permute-start(bf16[64,640]{1,0:T(8,128)(2,1)S(1)} %shard_map.69.refs_0_), channel_id=1, source_target_pairs={{0,3},{1,0},{2,1},{3,2},{4,7},{5,4},{6,5},{7,6},{8,11},{9,8},{10,9... | collective-permute-start | bytes 245768 | tf_op jit(solution)/shard_map/ppermute | solution.py:93
  79.9 1.5 %collective-permute-done.28.refs_0_ = bf16[64,640]{1,0:T(8,128)(2,1)S(1)} collective-permute-done((bf16[64,640]{1,0:T(8,128)(2,1)S(1)}, bf16[64,640]{1,0:T(8,128)(2,1)S(1)}, u32[]{:S(2)}, u32[]{:S(2)}) %collective-permute-start.28) | collective-permute-done | bytes 81952 | tf_op jit(solution)/shard_map/ppermute | solution.py:93
  82.0 2.3 %collective-permute-done.27.refs_0_ = bf16[64,640]{1,0:T(8,128)(2,1)S(1)} collective-permute-done((bf16[64,640]{1,0:T(8,128)(2,1)S(1)}, bf16[64,640]{1,0:T(8,128)(2,1)S(1)}, u32[]{:S(2)}, u32[]{:S(2)}) %collective-permute-start.27) | collective-permute-done | bytes 81952 | tf_op jit(solution)/shard_map/ppermute | solution.py:93
  84.9 1.3 %shard_map.77 = bf16[64,1152]{1,0:T(8,128)(2,1)} custom-call(bf16[64,640]{1,0:T(8,128)(2,1)S(1)} %collective-permute-done.26.refs_0_, f32[64,1152]{1,0:T(8,128)S(1)} %shard_map.76.refs_1_, bf16[1152,4608]{1,0:T(8,128)(2,1)S(1)} %shard_map.64.refs_1_.refs_2_.refs_4_), custom_call_target="tpu_custom_call" | custom-call | flops 100000000 | tf_op jit(solution)/shard_map/pallas_call | solution.py:265
  (79 shorter events, 19.8 us)
Async XLA Ops:
  4.7 10.9 %collective-permute-start.2 = (bf16[32,4736]{1,0:T(8,128)(2,1)S(1)}, bf16[32,4736]{1,0:T(8,128)(2,1)S(1)}, u32[]{:S(2)}, u32[]{:S(2)}) collective-permute-start(bf16[32,4736]{1,0:T(8,128)(2,1)S(1)} %get-tuple-element.56.after), channel_id=1, source_target_pairs={{0,8},{4,12},{8,0},{12,4},{16,24},{20,28},{24,16},{28,20},{1,9},{5... | collective-permute-start | bytes 909320 | tf_op jit(solution)/shard_map/ppermute | solution.py:88
  7.6 10.1 %collective-permute-start.3 = (bf16[32,4736]{1,0:T(8,128)(2,1)S(1)}, bf16[32,4736]{1,0:T(8,128)(2,1)S(1)}, u32[]{:S(2)}, u32[]{:S(2)}) collective-permute-start(bf16[32,4736]{1,0:T(8,128)(2,1)S(1)} %get-tuple-element.58), channel_id=1, source_target_pairs={{0,16},{4,20},{8,24},{12,28},{16,0},{20,4},{24,8},{28,12},{1,17},{... | collective-permute-start | bytes 909320 | tf_op jit(solution)/shard_map/ppermute | solution.py:88
  10.6 13.7 %collective-permute-start.10 = (bf16[32,4736]{1,0:T(8,128)(2,1)S(1)}, bf16[32,4736]{1,0:T(8,128)(2,1)S(1)}, u32[]{:S(2)}, u32[]{:S(2)}) collective-permute-start(bf16[32,4736]{1,0:T(8,128)(2,1)S(1)} %get-tuple-element.74), channel_id=1, source_target_pairs={{0,16},{4,20},{8,24},{12,28},{16,0},{20,4},{24,8},{28,12},{1,17},{... | collective-permute-start | bytes 909320 | tf_op jit(solution)/shard_map/ppermute | solution.py:88
  11.1 13.1 %collective-permute-start.9 = (bf16[32,4736]{1,0:T(8,128)(2,1)S(1)}, bf16[32,4736]{1,0:T(8,128)(2,1)S(1)}, u32[]{:S(2)}, u32[]{:S(2)}) collective-permute-start(bf16[32,4736]{1,0:T(8,128)(2,1)S(1)} %get-tuple-element.72), channel_id=1, source_target_pairs={{0,8},{4,12},{8,0},{12,4},{16,24},{20,28},{24,16},{28,20},{1,9},{5... | collective-permute-start | bytes 909320 | tf_op jit(solution)/shard_map/ppermute | solution.py:88
  17.9 9.6 %collective-permute-start.4 = (bf16[16,4736]{1,0:T(8,128)(2,1)S(1)}, bf16[16,4736]{1,0:T(8,128)(2,1)S(1)}, u32[]{:S(2)}, u32[]{:S(2)}) collective-permute-start(bf16[16,4736]{1,0:T(8,128)(2,1)S(1)} %get-tuple-element.60.refs_4_), channel_id=1, source_target_pairs={{0,16},{4,20},{8,24},{12,28},{16,0},{20,4},{24,8},{28,12},{1,17},{... | collective-permute-start | bytes 454664 | tf_op jit(solution)/shard_map/ppermute | solution.py:88
  19.4 8.0 %collective-permute-start.5 = (bf16[16,4736]{1,0:T(8,128)(2,1)S(1)}, bf16[16,4736]{1,0:T(8,128)(2,1)S(1)}, u32[]{:S(2)}, u32[]{:S(2)}) collective-permute-start(bf16[16,4736]{1,0:T(8,128)(2,1)S(1)} %get-tuple-element.61), channel_id=1, source_target_pairs={{0,8},{4,12},{8,0},{12,4},{16,24},{20,28},{24,16},{28,20},{1,9},{5... | collective-permute-start | bytes 454664 | tf_op jit(solution)/shard_map/ppermute | solution.py:88
  24.4 9.6 %collective-permute-start.11 = (bf16[16,4736]{1,0:T(8,128)(2,1)S(1)}, bf16[16,4736]{1,0:T(8,128)(2,1)S(1)}, u32[]{:S(2)}, u32[]{:S(2)}) collective-permute-start(bf16[16,4736]{1,0:T(8,128)(2,1)S(1)} %get-tuple-element.76), channel_id=1, source_target_pairs={{0,16},{4,20},{8,24},{12,28},{16,0},{20,4},{24,8},{28,12},{1,17},{... | collective-permute-start | bytes 454664 | tf_op jit(solution)/shard_map/ppermute | solution.py:88
  25.9 8.0 %collective-permute-start.12 = (bf16[16,4736]{1,0:T(8,128)(2,1)S(1)}, bf16[16,4736]{1,0:T(8,128)(2,1)S(1)}, u32[]{:S(2)}, u32[]{:S(2)}) collective-permute-start(bf16[16,4736]{1,0:T(8,128)(2,1)S(1)} %get-tuple-element.77), channel_id=1, source_target_pairs={{0,8},{4,12},{8,0},{12,4},{16,24},{20,28},{24,16},{28,20},{1,9},{5... | collective-permute-start | bytes 454664 | tf_op jit(solution)/shard_map/ppermute | solution.py:88
  28.4 7.8 %collective-permute-start.6 = (bf16[32,1280]{1,0:T(8,128)(2,1)S(1)}, bf16[32,1280]{1,0:T(8,128)(2,1)S(1)}, u32[]{:S(2)}, u32[]{:S(2)}) collective-permute-start(bf16[32,1280]{1,0:T(8,128)(2,1)S(1)} %get-tuple-element.63), channel_id=1, source_target_pairs={{0,1},{1,2},{2,3},{3,0},{4,5},{5,6},{6,7},{7,4},{8,9},{9,10},{10,1... | collective-permute-start | bytes 245768 | tf_op jit(solution)/shard_map/ppermute | solution.py:93
  30.0 13.8 %collective-permute-start.7 = (bf16[32,1280]{1,0:T(8,128)(2,1)S(1)}, bf16[32,1280]{1,0:T(8,128)(2,1)S(1)}, u32[]{:S(2)}, u32[]{:S(2)}) collective-permute-start(bf16[32,1280]{1,0:T(8,128)(2,1)S(1)} %get-tuple-element.64), channel_id=1, source_target_pairs={{0,2},{1,3},{2,0},{3,1},{4,6},{5,7},{6,4},{7,5},{8,10},{9,11},{10,... | collective-permute-start | bytes 245768 | tf_op jit(solution)/shard_map/ppermute | solution.py:93
  32.6 11.2 %collective-permute-start.8 = (bf16[32,1280]{1,0:T(8,128)(2,1)S(1)}, bf16[32,1280]{1,0:T(8,128)(2,1)S(1)}, u32[]{:S(2)}, u32[]{:S(2)}) collective-permute-start(bf16[32,1280]{1,0:T(8,128)(2,1)S(1)} %get-tuple-element.65), channel_id=1, source_target_pairs={{0,3},{1,0},{2,1},{3,2},{4,7},{5,4},{6,5},{7,6},{8,11},{9,8},{10,9... | collective-permute-start | bytes 245768 | tf_op jit(solution)/shard_map/ppermute | solution.py:93
  34.9 9.0 %collective-permute-start.13 = (bf16[32,1280]{1,0:T(8,128)(2,1)S(1)}, bf16[32,1280]{1,0:T(8,128)(2,1)S(1)}, u32[]{:S(2)}, u32[]{:S(2)}) collective-permute-start(bf16[32,1280]{1,0:T(8,128)(2,1)S(1)} %get-tuple-element.79), channel_id=1, source_target_pairs={{0,1},{1,2},{2,3},{3,0},{4,5},{5,6},{6,7},{7,4},{8,9},{9,10},{10,1... | collective-permute-start | bytes 245768 | tf_op jit(solution)/shard_map/ppermute | solution.py:93
  35.6 8.3 %collective-permute-start.14 = (bf16[32,1280]{1,0:T(8,128)(2,1)S(1)}, bf16[32,1280]{1,0:T(8,128)(2,1)S(1)}, u32[]{:S(2)}, u32[]{:S(2)}) collective-permute-start(bf16[32,1280]{1,0:T(8,128)(2,1)S(1)} %get-tuple-element.80), channel_id=1, source_target_pairs={{0,2},{1,3},{2,0},{3,1},{4,6},{5,7},{6,4},{7,5},{8,10},{9,11},{10,... | collective-permute-start | bytes 245768 | tf_op jit(solution)/shard_map/ppermute | solution.py:93
  36.3 7.7 %collective-permute-start.15 = (bf16[32,1280]{1,0:T(8,128)(2,1)S(1)}, bf16[32,1280]{1,0:T(8,128)(2,1)S(1)}, u32[]{:S(2)}, u32[]{:S(2)}) collective-permute-start(bf16[32,1280]{1,0:T(8,128)(2,1)S(1)} %get-tuple-element.81), channel_id=1, source_target_pairs={{0,3},{1,0},{2,1},{3,2},{4,7},{5,4},{6,5},{7,6},{8,11},{9,8},{10,9... | collective-permute-start | bytes 245768 | tf_op jit(solution)/shard_map/ppermute | solution.py:93
  45.8 6.3 %collective-permute-start.19 = (bf16[64,512]{1,0:T(8,128)(2,1)S(1)}, bf16[64,512]{1,0:T(8,128)(2,1)S(1)}, u32[]{:S(2)}, u32[]{:S(2)}) collective-permute-start(bf16[64,512]{1,0:T(8,128)(2,1)S(1)} %get-tuple-element.89), channel_id=1, source_target_pairs={{0,1},{1,2},{2,3},{3,0},{4,5},{5,6},{6,7},{7,4},{8,9},{9,10},{10,1... | collective-permute-start | bytes 196616 | tf_op jit(solution)/shard_map/ppermute | solution.py:93
  47.2 8.5 %collective-permute-start.20 = (bf16[64,512]{1,0:T(8,128)(2,1)S(1)}, bf16[64,512]{1,0:T(8,128)(2,1)S(1)}, u32[]{:S(2)}, u32[]{:S(2)}) collective-permute-start(bf16[64,512]{1,0:T(8,128)(2,1)S(1)} %get-tuple-element.90), channel_id=1, source_target_pairs={{0,2},{1,3},{2,0},{3,1},{4,6},{5,7},{6,4},{7,5},{8,10},{9,11},{10,... | collective-permute-start | bytes 196616 | tf_op jit(solution)/shard_map/ppermute | solution.py:93
  49.4 6.3 %collective-permute-start.21 = (bf16[64,512]{1,0:T(8,128)(2,1)S(1)}, bf16[64,512]{1,0:T(8,128)(2,1)S(1)}, u32[]{:S(2)}, u32[]{:S(2)}) collective-permute-start(bf16[64,512]{1,0:T(8,128)(2,1)S(1)} %get-tuple-element.91), channel_id=1, source_target_pairs={{0,3},{1,0},{2,1},{3,2},{4,7},{5,4},{6,5},{7,6},{8,11},{9,8},{10,9... | collective-permute-start | bytes 196616 | tf_op jit(solution)/shard_map/ppermute | solution.py:93
  50.8 7.1 %collective-permute-start.16 = (bf16[64,640]{1,0:T(8,128)(2,1)S(1)}, bf16[64,640]{1,0:T(8,128)(2,1)S(1)}, u32[]{:S(2)}, u32[]{:S(2)}) collective-permute-start(bf16[64,640]{1,0:T(8,128)(2,1)S(1)} %get-tuple-element.84), channel_id=1, source_target_pairs={{0,1},{1,2},{2,3},{3,0},{4,5},{5,6},{6,7},{7,4},{8,9},{9,10},{10,1... | collective-permute-start | bytes 245768 | tf_op jit(solution)/shard_map/ppermute | solution.py:93
  51.5 8.7 %collective-permute-start.17 = (bf16[64,640]{1,0:T(8,128)(2,1)S(1)}, bf16[64,640]{1,0:T(8,128)(2,1)S(1)}, u32[]{:S(2)}, u32[]{:S(2)}) collective-permute-start(bf16[64,640]{1,0:T(8,128)(2,1)S(1)} %get-tuple-element.85), channel_id=1, source_target_pairs={{0,2},{1,3},{2,0},{3,1},{4,6},{5,7},{6,4},{7,5},{8,10},{9,11},{10,... | collective-permute-start | bytes 245768 | tf_op jit(solution)/shard_map/ppermute | solution.py:93
  52.1 8.1 %collective-permute-start.18 = (bf16[64,640]{1,0:T(8,128)(2,1)S(1)}, bf16[64,640]{1,0:T(8,128)(2,1)S(1)}, u32[]{:S(2)}, u32[]{:S(2)}) collective-permute-start(bf16[64,640]{1,0:T(8,128)(2,1)S(1)} %get-tuple-element.86), channel_id=1, source_target_pairs={{0,3},{1,0},{2,1},{3,2},{4,7},{5,4},{6,5},{7,6},{8,11},{9,8},{10,9... | collective-permute-start | bytes 245768 | tf_op jit(solution)/shard_map/ppermute | solution.py:93
  55.8 6.6 %collective-permute-start.29 = (bf16[64,512]{1,0:T(8,128)(2,1)S(1)}, bf16[64,512]{1,0:T(8,128)(2,1)S(1)}, u32[]{:S(2)}, u32[]{:S(2)}) collective-permute-start(bf16[64,512]{1,0:T(8,128)(2,1)S(1)} %shard_map.66.refs_6_.refs_0_), channel_id=1, source_target_pairs={{0,8},{4,12},{8,0},{12,4},{16,24},{20,28},{24,16},{28,20},{1,9},{5... | collective-permute-start | bytes 196616 | tf_op jit(solution)/shard_map/ppermute | solution.py:88
  56.4 7.5 %collective-permute-start.30 = (bf16[64,512]{1,0:T(8,128)(2,1)S(1)}, bf16[64,512]{1,0:T(8,128)(2,1)S(1)}, u32[]{:S(2)}, u32[]{:S(2)}) collective-permute-start(bf16[64,512]{1,0:T(8,128)(2,1)S(1)} %shard_map.66.refs_6_.refs_0_), channel_id=1, source_target_pairs={{0,16},{4,20},{8,24},{12,28},{16,0},{20,4},{24,8},{28,12},{1,17},{... | collective-permute-start | bytes 196616 | tf_op jit(solution)/shard_map/ppermute | solution.py:88
  57.9 5.9 %collective-permute-start.31 = (bf16[64,512]{1,0:T(8,128)(2,1)S(1)}, bf16[64,512]{1,0:T(8,128)(2,1)S(1)}, u32[]{:S(2)}, u32[]{:S(2)}) collective-permute-start(bf16[64,512]{1,0:T(8,128)(2,1)S(1)} %shard_map.66.refs_6_.refs_0_), channel_id=1, source_target_pairs={{0,24},{4,28},{8,16},{12,20},{16,8},{20,12},{24,0},{28,4},{1,25},{... | collective-permute-start | bytes 196616 | tf_op jit(solution)/shard_map/ppermute | solution.py:88
  60.3 4.5 %collective-permute-start.22 = (bf16[64,640]{1,0:T(8,128)(2,1)S(1)}, bf16[64,640]{1,0:T(8,128)(2,1)S(1)}, u32[]{:S(2)}, u32[]{:S(2)}) collective-permute-start(bf16[64,640]{1,0:T(8,128)(2,1)S(1)} %shard_map.67.refs_0_), channel_id=1, source_target_pairs={{0,8},{4,12},{8,0},{12,4},{16,24},{20,28},{24,16},{28,20},{1,9},{5... | collective-permute-start | bytes 245768 | tf_op jit(solution)/shard_map/ppermute | solution.py:88
  62.4 5.3 %collective-permute-start.24 = (bf16[64,640]{1,0:T(8,128)(2,1)S(1)}, bf16[64,640]{1,0:T(8,128)(2,1)S(1)}, u32[]{:S(2)}, u32[]{:S(2)}) collective-permute-start(bf16[64,640]{1,0:T(8,128)(2,1)S(1)} %shard_map.67.refs_0_), channel_id=1, source_target_pairs={{0,24},{4,28},{8,16},{12,20},{16,8},{20,12},{24,0},{28,4},{1,25},{... | collective-permute-start | bytes 245768 | tf_op jit(solution)/shard_map/ppermute | solution.py:88
  68.1 6.0 %collective-permute-start.25 = (f32[64,640]{1,0:T(8,128)S(1)}, f32[64,640]{1,0:T(8,128)S(1)}, u32[]{:S(2)}, u32[]{:S(2)}) collective-permute-start(f32[64,640]{1,0:T(8,128)S(1)} %get-tuple-element.94), channel_id=1, source_target_pairs={{0,4},{4,0},{8,12},{12,8},{16,20},{20,16},{24,28},{28,24},{1,5},{5... | collective-permute-start | bytes 491528 | tf_op jit(solution)/shard_map/ppermute | solution.py:88
  68.3 9.0 %collective-permute-start.33 = (bf16[64,512]{1,0:T(8,128)(2,1)S(1)}, bf16[64,512]{1,0:T(8,128)(2,1)S(1)}, u32[]{:S(2)}, u32[]{:S(2)}) collective-permute-start(bf16[64,512]{1,0:T(8,128)(2,1)S(1)} %shard_map.71.refs_0_), channel_id=1, source_target_pairs={{0,1},{1,2},{2,3},{3,0},{4,5},{5,6},{6,7},{7,4},{8,9},{9,10},{10,1... | collective-permute-start | bytes 196616 | tf_op jit(solution)/shard_map/ppermute | solution.py:93
  71.2 7.6 %collective-permute-start.34 = (bf16[64,512]{1,0:T(8,128)(2,1)S(1)}, bf16[64,512]{1,0:T(8,128)(2,1)S(1)}, u32[]{:S(2)}, u32[]{:S(2)}) collective-permute-start(bf16[64,512]{1,0:T(8,128)(2,1)S(1)} %shard_map.71.refs_0_), channel_id=1, source_target_pairs={{0,2},{1,3},{2,0},{3,1},{4,6},{5,7},{6,4},{7,5},{8,10},{9,11},{10,... | collective-permute-start | bytes 196616 | tf_op jit(solution)/shard_map/ppermute | solution.py:93
  72.4 6.3 %collective-permute-start.35 = (bf16[64,512]{1,0:T(8,128)(2,1)S(1)}, bf16[64,512]{1,0:T(8,128)(2,1)S(1)}, u32[]{:S(2)}, u32[]{:S(2)}) collective-permute-start(bf16[64,512]{1,0:T(8,128)(2,1)S(1)} %shard_map.71.refs_0_), channel_id=1, source_target_pairs={{0,3},{1,0},{2,1},{3,2},{4,7},{5,4},{6,5},{7,6},{8,11},{9,8},{10,9... | collective-permute-start | bytes 196616 | tf_op jit(solution)/shard_map/ppermute | solution.py:93
  74.2 7.2 %collective-permute-start.28 = (bf16[64,640]{1,0:T(8,128)(2,1)S(1)}, bf16[64,640]{1,0:T(8,128)(2,1)S(1)}, u32[]{:S(2)}, u32[]{:S(2)}) collective-permute-start(bf16[64,640]{1,0:T(8,128)(2,1)S(1)} %shard_map.69.refs_0_), channel_id=1, source_target_pairs={{0,1},{1,2},{2,3},{3,0},{4,5},{5,6},{6,7},{7,4},{8,9},{9,10},{10,1... | collective-permute-start | bytes 245768 | tf_op jit(solution)/shard_map/ppermute | solution.py:93
  75.0 9.3 %collective-permute-start.27 = (bf16[64,640]{1,0:T(8,128)(2,1)S(1)}, bf16[64,640]{1,0:T(8,128)(2,1)S(1)}, u32[]{:S(2)}, u32[]{:S(2)}) collective-permute-start(bf16[64,640]{1,0:T(8,128)(2,1)S(1)} %shard_map.69.refs_0_), channel_id=1, source_target_pairs={{0,2},{1,3},{2,0},{3,1},{4,6},{5,7},{6,4},{7,5},{8,10},{9,11},{10,... | collective-permute-start | bytes 245768 | tf_op jit(solution)/shard_map/ppermute | solution.py:93
  77.3 7.6 %collective-permute-start.26 = (bf16[64,640]{1,0:T(8,128)(2,1)S(1)}, bf16[64,640]{1,0:T(8,128)(2,1)S(1)}, u32[]{:S(2)}, u32[]{:S(2)}) collective-permute-start(bf16[64,640]{1,0:T(8,128)(2,1)S(1)} %shard_map.69.refs_0_), channel_id=1, source_target_pairs={{0,3},{1,0},{2,1},{3,2},{4,7},{5,4},{6,5},{7,6},{8,11},{9,8},{10,9... | collective-permute-start | bytes 245768 | tf_op jit(solution)/shard_map/ppermute | solution.py:93
  (6 other events, 54.6 us)

commit v9 on v8

--- a/solution.py
+++ b/solution.py
@@ -286,20 +286,20 @@
 
 
 def second_sum(ins, outs):
-    *outs, total = outs
-    kept, came_a, came_b = ins
-    sub = came_a.shape[0]
-    for route, came in enumerate((came_a, came_b)):
-        rows = slice(route * sub, (route + 1) * sub)
-        total[rows, :] = kept[rows, :] + came[...].astype(F32)
+    kept, *others = ins
+    sub = others[0].shape[0]
     width = outs[0].shape[1] - 128
     me = lax.axis_index("grp")
     groups = len(outs)
-    rest = total[:, groups * width :]
-    for step, out in enumerate(outs):
-        at = pl.multiple_of(lax.rem(me + step, groups) * width, 128)
-        out[:, 0:width] = total[:, pl.ds(at, width)].astype(out.dtype)
-        out[:, width:] = rest.astype(out.dtype)
+    for route, came in enumerate(others):
+        rows = slice(route * sub, (route + 1) * sub)
+        end = groups * width
+        rest = kept[rows, end:] + came[:, end:].astype(F32)
+        for step, out in enumerate(outs):
+            span = pl.ds(pl.multiple_of(lax.rem(me + step, groups) * width, 128), width)
+            block = kept[rows, span] + came[:, span].astype(F32)
+            out[rows, 0:width] = block.astype(out.dtype)
+            out[rows, width:] = rest.astype(out.dtype)
 
 
 def gathered(ins):
@@ -424,8 +424,8 @@
         came[c] = [kept, swap(s_a, 4), swap(s_b, 2)]
     held = []
     for c in (0, 1):
-        shapes = [like((2 * sub, own_rows + 128), t) for t in grp_types] + [like((2 * sub, wide), F32)]
-        own, *others = stage(second_sum, shapes, came[c], (), WORK[7][c])[:groups]
+        shapes = [like((2 * sub, own_rows + 128), t) for t in grp_types]
+        own, *others = stage(second_sum, shapes, came[c], (), WORK[7][c])
         came[c] = [own] + [shift(value, step + 1) for step, value in enumerate(others)]
     for c in (0, 1):
         rows = 2 * sub * (c + 1)

time: 86.3 us -> 85.5 us (level)
  Pallas kernels: 19.3 us -> 17.5 us
    pallas_call x19, Pallas kernels: 9.63 us -> 7.89 us  [stage(): pl.pallas_call(body, in_specs=[near] * (len(operands) + len(after)), out_...]
  transfers between devices with their start and end apart: 36 -> 36, of which waited for: 11 -> 12; matrix products, arithmetic and copies ran while one was open for 1% -> 1% of each run, Pallas kernels for 17% -> 15%
where the time goes in v9:
time: 85.5 us; the launch traced here: 85.3 us
  starting transfers between devices  44.9 us (53%)
  waiting for transfers between devices  21.5 us (25%)
  Pallas kernels  17.5 us (20%)
  local copies, waits for them, and re-layouts  0.86 us (1%)
    ppermute x18, starting transfers between devices, shift(): return lax.ppermute(value, 'grp', [(i, (i + step) % n) for i in range(n)])  27.7 us
    ppermute x18, starting transfers between devices, swap(): lax.ppermute(value, 'dp', [(i, i ^ bit) for i in range(lax.axis_size('dp'...  17.2 us
    ppermute x18, waiting for transfers between devices, swap(): lax.ppermute(value, 'dp', [(i, i ^ bit) for i in range(lax.axis_size('dp'...  15.1 us
    pallas_call x19, Pallas kernels, stage(): pl.pallas_call(body, in_specs=[near] * (len(operands) + len(after)), out_...  7.89 us
    ppermute x18, waiting for transfers between devices, shift(): return lax.ppermute(value, 'grp', [(i, (i + step) % n) for i in range(n)])  6.4 us
    pallas_call x1, Pallas kernels, load(): pl.pallas_call(load_kernel, in_specs=[pl.BlockSpec(memory_space=pl.ANY),...  5.09 us
    pallas_call x1, Pallas kernels, grad_parts(): pl.pallas_call(first_kernel, in_specs=[near] * 5, out_specs=[near] * 7, o...  1.85 us
  transfers between devices with their start and end apart: 36, of which 12 were waited for; matrix products, arithmetic and copies ran while one was open for 1% of the time, Pallas kernels for 15%

profile of v9, /device:TPU:0, one launch (start us, length us, event | category | flops | bytes accessed | tf_op | source)
XLA Modules:
  0.0 85.3 jit_solution(7783336194658188264)
XLA Ops:
  0.5 1.3 %shard_map.55 = (bf16[14,14,2,512]{3,2,1,0:T(2,128)(2,1)S(1)}, bf16[14,14,2,512]{3,2,1,0:T(2,128)(2,1)S(1)}, bf16[512,512]{1,0:T(8,128)(2,1)S(1)}) custom-call(bf16[14,14,2,512]{3,2,1,0:T(2,128)(2,1)} %bitcast.12, bf16[14,14,2,512]{3,2,1,0:T(2,128)(2,1)} %bitcast.14, bf16[512,512]{1,0:T(8,128)(2,1)} %refs_2_.1), custom_call_target="tpu_custom_call" | custom-call | tf_op jit(solution)/shard_map/pallas_call | solution.py:222
  2.8 1.9 %shard_map.56 = (bf16[32,4736]{1,0:T(8,128)(2,1)S(1)}, bf16[32,4736]{1,0:T(8,128)(2,1)S(1)}, bf16[32,4736]{1,0:T(8,128)(2,1)S(1)}, bf16[32,4736]{1,0:T(8,128)(2,...) custom-call(bf16[512,512]{1,0:T(8,128)(2,1)S(1)} %bitcast.7, ...), custom_call_target="tpu_custom_call" | custom-call | tf_op jit(solution)/shard_map/pallas_call | solution.py:172
  4.7 3.0 %collective-permute-start.2 = (bf16[32,4736]{1,0:T(8,128)(2,1)S(1)}, bf16[32,4736]{1,0:T(8,128)(2,1)S(1)}, u32[]{:S(2)}, u32[]{:S(2)}) collective-permute-start(bf16[32,4736]{1,0:T(8,128)(2,1)S(1)} %get-tuple-element.56.after), channel_id=1, source_target_pairs={{0,8},{4,12},{8,0},{12,4},{16,24},{20,28},{24,16},{28,20},{1,9},{5... | collective-permute-start | bytes 909320 | tf_op jit(solution)/shard_map/ppermute | solution.py:88
  7.6 1.5 %collective-permute-start.3 = (bf16[32,4736]{1,0:T(8,128)(2,1)S(1)}, bf16[32,4736]{1,0:T(8,128)(2,1)S(1)}, u32[]{:S(2)}, u32[]{:S(2)}) collective-permute-start(bf16[32,4736]{1,0:T(8,128)(2,1)S(1)} %get-tuple-element.58), channel_id=1, source_target_pairs={{0,16},{4,20},{8,24},{12,28},{16,0},{20,4},{24,8},{28,12},{1,17},{... | collective-permute-start | bytes 909320 | tf_op jit(solution)/shard_map/ppermute | solution.py:88
  9.2 1.4 %shard_map.60 = (bf16[32,4736]{1,0:T(8,128)(2,1)S(1)}, bf16[32,4736]{1,0:T(8,128)(2,1)S(1)}, bf16[32,4736]{1,0:T(8,128)(2,1)S(1)}, bf16[32,4736]{1,0:T(8,128)(2,1)S(1)}) custom-call(bf16[1088,512]{1,0:T(8,128)(2,1)S(1)} %get-tuple-element.68.acts, bf16[384,1024]{1,0:T(8,128)(2,1)S(1)} %get-tuple-element.69.later, bf16[128,128]{1,0:T(8,128)(2,1)S(1)} %get-tuple-element.70.squared), custom_call_target="tpu_custom_call" | custom-call | flops 1207959552 | tf_op jit(solution)/shard_map/pallas_call | solution.py:189
  11.5 4.2 %collective-permute-done.2.refs_1_ = bf16[32,4736]{1,0:T(8,128)(2,1)S(1)} collective-permute-done((bf16[32,4736]{1,0:T(8,128)(2,1)S(1)}, bf16[32,4736]{1,0:T(8,128)(2,1)S(1)}, u32[]{:S(2)}, u32[]{:S(2)}) %collective-permute-start.2) | collective-permute-done | bytes 303136 | tf_op jit(solution)/shard_map/ppermute | solution.py:88
  15.6 2.1 %collective-permute-done.3.refs_3_ = bf16[32,4736]{1,0:T(8,128)(2,1)S(1)} collective-permute-done((bf16[32,4736]{1,0:T(8,128)(2,1)S(1)}, bf16[32,4736]{1,0:T(8,128)(2,1)S(1)}, u32[]{:S(2)}, u32[]{:S(2)}) %collective-permute-start.3) | collective-permute-done | bytes 303136 | tf_op jit(solution)/shard_map/ppermute | solution.py:88
  17.9 1.6 %collective-permute-start.4 = (bf16[16,4736]{1,0:T(8,128)(2,1)S(1)}, bf16[16,4736]{1,0:T(8,128)(2,1)S(1)}, u32[]{:S(2)}, u32[]{:S(2)}) collective-permute-start(bf16[16,4736]{1,0:T(8,128)(2,1)S(1)} %get-tuple-element.60.refs_4_), channel_id=1, source_target_pairs={{0,16},{4,20},{8,24},{12,28},{16,0},{20,4},{24,8},{28,12},{1,17},{... | collective-permute-start | bytes 454664 | tf_op jit(solution)/shard_map/ppermute | solution.py:88
  20.0 4.2 %collective-permute-done.10.refs_3_ = bf16[32,4736]{1,0:T(8,128)(2,1)S(1)} collective-permute-done((bf16[32,4736]{1,0:T(8,128)(2,1)S(1)}, bf16[32,4736]{1,0:T(8,128)(2,1)S(1)}, u32[]{:S(2)}, u32[]{:S(2)}) %collective-permute-start.10) | collective-permute-done | bytes 303136 | tf_op jit(solution)/shard_map/ppermute | solution.py:88
  24.4 1.6 %collective-permute-start.11 = (bf16[16,4736]{1,0:T(8,128)(2,1)S(1)}, bf16[16,4736]{1,0:T(8,128)(2,1)S(1)}, u32[]{:S(2)}, u32[]{:S(2)}) collective-permute-start(bf16[16,4736]{1,0:T(8,128)(2,1)S(1)} %get-tuple-element.76), channel_id=1, source_target_pairs={{0,16},{4,20},{8,24},{12,28},{16,0},{20,4},{24,8},{28,12},{1,17},{... | collective-permute-start | bytes 454664 | tf_op jit(solution)/shard_map/ppermute | solution.py:88
  27.5 1.6 %collective-permute-start.6 = (bf16[32,1280]{1,0:T(8,128)(2,1)S(1)}, bf16[32,1280]{1,0:T(8,128)(2,1)S(1)}, u32[]{:S(2)}, u32[]{:S(2)}) collective-permute-start(bf16[32,1280]{1,0:T(8,128)(2,1)S(1)} %get-tuple-element.63), channel_id=1, source_target_pairs={{0,1},{1,2},{2,3},{3,0},{4,5},{5,6},{6,7},{7,4},{8,9},{9,10},{10,1... | collective-permute-start | bytes 245768 | tf_op jit(solution)/shard_map/ppermute | solution.py:93
  29.2 2.6 %collective-permute-start.7 = (bf16[32,1280]{1,0:T(8,128)(2,1)S(1)}, bf16[32,1280]{1,0:T(8,128)(2,1)S(1)}, u32[]{:S(2)}, u32[]{:S(2)}) collective-permute-start(bf16[32,1280]{1,0:T(8,128)(2,1)S(1)} %get-tuple-element.64), channel_id=1, source_target_pairs={{0,2},{1,3},{2,0},{3,1},{4,6},{5,7},{6,4},{7,5},{8,10},{9,11},{10,... | collective-permute-start | bytes 245768 | tf_op jit(solution)/shard_map/ppermute | solution.py:93
  31.8 1.3 %collective-permute-start.8 = (bf16[32,1280]{1,0:T(8,128)(2,1)S(1)}, bf16[32,1280]{1,0:T(8,128)(2,1)S(1)}, u32[]{:S(2)}, u32[]{:S(2)}) collective-permute-start(bf16[32,1280]{1,0:T(8,128)(2,1)S(1)} %get-tuple-element.65), channel_id=1, source_target_pairs={{0,3},{1,0},{2,1},{3,2},{4,7},{5,4},{6,5},{7,6},{8,11},{9,8},{10,9... | collective-permute-start | bytes 245768 | tf_op jit(solution)/shard_map/ppermute | solution.py:93
  33.9 1.5 %collective-permute-start.14 = (bf16[32,1280]{1,0:T(8,128)(2,1)S(1)}, bf16[32,1280]{1,0:T(8,128)(2,1)S(1)}, u32[]{:S(2)}, u32[]{:S(2)}) collective-permute-start(bf16[32,1280]{1,0:T(8,128)(2,1)S(1)} %get-tuple-element.80), channel_id=1, source_target_pairs={{0,2},{1,3},{2,0},{3,1},{4,6},{5,7},{6,4},{7,5},{8,10},{9,11},{10,... | collective-permute-start | bytes 245768 | tf_op jit(solution)/shard_map/ppermute | solution.py:93
  35.4 1.7 %collective-permute-start.15 = (bf16[32,1280]{1,0:T(8,128)(2,1)S(1)}, bf16[32,1280]{1,0:T(8,128)(2,1)S(1)}, u32[]{:S(2)}, u32[]{:S(2)}) collective-permute-start(bf16[32,1280]{1,0:T(8,128)(2,1)S(1)} %get-tuple-element.81), channel_id=1, source_target_pairs={{0,3},{1,0},{2,1},{3,2},{4,7},{5,4},{6,5},{7,6},{8,11},{9,8},{10,9... | collective-permute-start | bytes 245768 | tf_op jit(solution)/shard_map/ppermute | solution.py:93
  37.1 5.1 %shard_map.64.refs_1_.refs_2_.refs_4_ = bf16[1152,4608]{1,0:T(8,128)(2,1)S(1)} custom-call(bf16[1152,4608]{1,0:T(8,128)(2,1)} %source.1, bf16[32,4736]{1,0:T(8,128)(2,1)} %copy-done), custom_call_target="tpu_custom_call" | custom-call | bytes 21233664 | tf_op jit(solution)/shard_map/pallas_call | solution.py:248
  43.1 1.8 %shard_map.65 = (f32[64,512]{1,0:T(8,128)S(1)}, bf16[64,512]{1,0:T(8,128)(2,1)S(1)}, bf16[64,512]{1,0:T(8,128)(2,1)S(1)}, bf16[64,512]{1,0:T(8,128)(2,1)S(1)}, f...) custom-call(bf16[64,1152]{1,0:T(8,128)(2,1)S(1)} %get-tuple-element., ...), custom_call_target="tpu_custom_call" | custom-call | flops 75000000 | tf_op jit(solution)/shard_map/pallas_call | solution.py:265
  44.9 1.5 %collective-permute-start.19 = (bf16[64,512]{1,0:T(8,128)(2,1)S(1)}, bf16[64,512]{1,0:T(8,128)(2,1)S(1)}, u32[]{:S(2)}, u32[]{:S(2)}) collective-permute-start(bf16[64,512]{1,0:T(8,128)(2,1)S(1)} %get-tuple-element.89), channel_id=1, source_target_pairs={{0,1},{1,2},{2,3},{3,0},{4,5},{5,6},{6,7},{7,4},{8,9},{9,10},{10,1... | collective-permute-start | bytes 196616 | tf_op jit(solution)/shard_map/ppermute | solution.py:93
  46.4 2.1 %collective-permute-start.20 = (bf16[64,512]{1,0:T(8,128)(2,1)S(1)}, bf16[64,512]{1,0:T(8,128)(2,1)S(1)}, u32[]{:S(2)}, u32[]{:S(2)}) collective-permute-start(bf16[64,512]{1,0:T(8,128)(2,1)S(1)} %get-tuple-element.90), channel_id=1, source_target_pairs={{0,2},{1,3},{2,0},{3,1},{4,6},{5,7},{6,4},{7,5},{8,10},{9,11},{10,... | collective-permute-start | bytes 196616 | tf_op jit(solution)/shard_map/ppermute | solution.py:93
  49.2 1.3 %collective-permute-start.16 = (bf16[64,640]{1,0:T(8,128)(2,1)S(1)}, bf16[64,640]{1,0:T(8,128)(2,1)S(1)}, u32[]{:S(2)}, u32[]{:S(2)}) collective-permute-start(bf16[64,640]{1,0:T(8,128)(2,1)S(1)} %get-tuple-element.84), channel_id=1, source_target_pairs={{0,1},{1,2},{2,3},{3,0},{4,5},{5,6},{6,7},{7,4},{8,9},{9,10},{10,1... | collective-permute-start | bytes 245768 | tf_op jit(solution)/shard_map/ppermute | solution.py:93
  51.3 2.4 %collective-permute-start.18 = (bf16[64,640]{1,0:T(8,128)(2,1)S(1)}, bf16[64,640]{1,0:T(8,128)(2,1)S(1)}, u32[]{:S(2)}, u32[]{:S(2)}) collective-permute-start(bf16[64,640]{1,0:T(8,128)(2,1)S(1)} %get-tuple-element.86), channel_id=1, source_target_pairs={{0,3},{1,0},{2,1},{3,2},{4,7},{5,4},{6,5},{7,6},{8,11},{9,8},{10,9... | collective-permute-start | bytes 245768 | tf_op jit(solution)/shard_map/ppermute | solution.py:93
  53.7 1.3 %collective-permute-done.20.refs_2_ = bf16[64,512]{1,0:T(8,128)(2,1)S(1)} collective-permute-done((bf16[64,512]{1,0:T(8,128)(2,1)S(1)}, bf16[64,512]{1,0:T(8,128)(2,1)S(1)}, u32[]{:S(2)}, u32[]{:S(2)}) %collective-permute-start.20) | collective-permute-done | bytes 65568 | tf_op jit(solution)/shard_map/ppermute | solution.py:93
  56.2 1.4 %collective-permute-start.30 = (bf16[64,512]{1,0:T(8,128)(2,1)S(1)}, bf16[64,512]{1,0:T(8,128)(2,1)S(1)}, u32[]{:S(2)}, u32[]{:S(2)}) collective-permute-start(bf16[64,512]{1,0:T(8,128)(2,1)S(1)} %shard_map.66.refs_6_.refs_0_), channel_id=1, source_target_pairs={{0,16},{4,20},{8,24},{12,28},{16,0},{20,4},{24,8},{28,12},{1,17},{... | collective-permute-start | bytes 196616 | tf_op jit(solution)/shard_map/ppermute | solution.py:88
  60.1 1.5 %collective-permute-start.23 = (bf16[64,640]{1,0:T(8,128)(2,1)S(1)}, bf16[64,640]{1,0:T(8,128)(2,1)S(1)}, u32[]{:S(2)}, u32[]{:S(2)}) collective-permute-start(bf16[64,640]{1,0:T(8,128)(2,1)S(1)} %shard_map.67.refs_0_), channel_id=1, source_target_pairs={{0,16},{4,20},{8,24},{12,28},{16,0},{20,4},{24,8},{28,12},{1,17},{... | collective-permute-start | bytes 245768 | tf_op jit(solution)/shard_map/ppermute | solution.py:88
  61.6 1.3 %collective-permute-start.24 = (bf16[64,640]{1,0:T(8,128)(2,1)S(1)}, bf16[64,640]{1,0:T(8,128)(2,1)S(1)}, u32[]{:S(2)}, u32[]{:S(2)}) collective-permute-start(bf16[64,640]{1,0:T(8,128)(2,1)S(1)} %shard_map.67.refs_0_), channel_id=1, source_target_pairs={{0,24},{4,28},{8,16},{12,20},{16,8},{20,12},{24,0},{28,4},{1,25},{... | collective-permute-start | bytes 245768 | tf_op jit(solution)/shard_map/ppermute | solution.py:88
  64.5 2.4 %collective-permute-done.24.refs_3_ = bf16[64,640]{1,0:T(8,128)(2,1)S(1)} collective-permute-done((bf16[64,640]{1,0:T(8,128)(2,1)S(1)}, bf16[64,640]{1,0:T(8,128)(2,1)S(1)}, u32[]{:S(2)}, u32[]{:S(2)}) %collective-permute-start.24) | collective-permute-done | bytes 81952 | tf_op jit(solution)/shard_map/ppermute | solution.py:88
  67.4 3.0 %collective-permute-start.33 = (bf16[64,512]{1,0:T(8,128)(2,1)S(1)}, bf16[64,512]{1,0:T(8,128)(2,1)S(1)}, u32[]{:S(2)}, u32[]{:S(2)}) collective-permute-start(bf16[64,512]{1,0:T(8,128)(2,1)S(1)} %shard_map.71.refs_0_), channel_id=1, source_target_pairs={{0,1},{1,2},{2,3},{3,0},{4,5},{5,6},{6,7},{7,4},{8,9},{9,10},{10,1... | collective-permute-start | bytes 196616 | tf_op jit(solution)/shard_map/ppermute | solution.py:93
  70.7 2.2 %collective-permute-start.35 = (bf16[64,512]{1,0:T(8,128)(2,1)S(1)}, bf16[64,512]{1,0:T(8,128)(2,1)S(1)}, u32[]{:S(2)}, u32[]{:S(2)}) collective-permute-start(bf16[64,512]{1,0:T(8,128)(2,1)S(1)} %shard_map.71.refs_0_), channel_id=1, source_target_pairs={{0,3},{1,0},{2,1},{3,2},{4,7},{5,4},{6,5},{7,6},{8,11},{9,8},{10,9... | collective-permute-start | bytes 196616 | tf_op jit(solution)/shard_map/ppermute | solution.py:93
  73.4 2.5 %collective-permute-start.27 = (bf16[64,640]{1,0:T(8,128)(2,1)S(1)}, bf16[64,640]{1,0:T(8,128)(2,1)S(1)}, u32[]{:S(2)}, u32[]{:S(2)}) collective-permute-start(bf16[64,640]{1,0:T(8,128)(2,1)S(1)} %shard_map.69.refs_0_), channel_id=1, source_target_pairs={{0,2},{1,3},{2,0},{3,1},{4,6},{5,7},{6,4},{7,5},{8,10},{9,11},{10,... | collective-permute-start | bytes 245768 | tf_op jit(solution)/shard_map/ppermute | solution.py:93
  76.5 1.4 %collective-permute-start.26 = (bf16[64,640]{1,0:T(8,128)(2,1)S(1)}, bf16[64,640]{1,0:T(8,128)(2,1)S(1)}, u32[]{:S(2)}, u32[]{:S(2)}) collective-permute-start(bf16[64,640]{1,0:T(8,128)(2,1)S(1)} %shard_map.69.refs_0_), channel_id=1, source_target_pairs={{0,3},{1,0},{2,1},{3,2},{4,7},{5,4},{6,5},{7,6},{8,11},{9,8},{10,9... | collective-permute-start | bytes 245768 | tf_op jit(solution)/shard_map/ppermute | solution.py:93
  79.1 1.5 %collective-permute-done.28.refs_0_ = bf16[64,640]{1,0:T(8,128)(2,1)S(1)} collective-permute-done((bf16[64,640]{1,0:T(8,128)(2,1)S(1)}, bf16[64,640]{1,0:T(8,128)(2,1)S(1)}, u32[]{:S(2)}, u32[]{:S(2)}) %collective-permute-start.28) | collective-permute-done | bytes 81952 | tf_op jit(solution)/shard_map/ppermute | solution.py:93
  81.1 2.3 %collective-permute-done.27.refs_0_ = bf16[64,640]{1,0:T(8,128)(2,1)S(1)} collective-permute-done((bf16[64,640]{1,0:T(8,128)(2,1)S(1)}, bf16[64,640]{1,0:T(8,128)(2,1)S(1)}, u32[]{:S(2)}, u32[]{:S(2)}) %collective-permute-start.27) | collective-permute-done | bytes 81952 | tf_op jit(solution)/shard_map/ppermute | solution.py:93
  (79 shorter events, 18.5 us)
Async XLA Ops:
  4.7 10.9 %collective-permute-start.2 = (bf16[32,4736]{1,0:T(8,128)(2,1)S(1)}, bf16[32,4736]{1,0:T(8,128)(2,1)S(1)}, u32[]{:S(2)}, u32[]{:S(2)}) collective-permute-start(bf16[32,4736]{1,0:T(8,128)(2,1)S(1)} %get-tuple-element.56.after), channel_id=1, source_target_pairs={{0,8},{4,12},{8,0},{12,4},{16,24},{20,28},{24,16},{28,20},{1,9},{5... | collective-permute-start | bytes 909320 | tf_op jit(solution)/shard_map/ppermute | solution.py:88
  7.6 10.1 %collective-permute-start.3 = (bf16[32,4736]{1,0:T(8,128)(2,1)S(1)}, bf16[32,4736]{1,0:T(8,128)(2,1)S(1)}, u32[]{:S(2)}, u32[]{:S(2)}) collective-permute-start(bf16[32,4736]{1,0:T(8,128)(2,1)S(1)} %get-tuple-element.58), channel_id=1, source_target_pairs={{0,16},{4,20},{8,24},{12,28},{16,0},{20,4},{24,8},{28,12},{1,17},{... | collective-permute-start | bytes 909320 | tf_op jit(solution)/shard_map/ppermute | solution.py:88
  10.6 13.7 %collective-permute-start.10 = (bf16[32,4736]{1,0:T(8,128)(2,1)S(1)}, bf16[32,4736]{1,0:T(8,128)(2,1)S(1)}, u32[]{:S(2)}, u32[]{:S(2)}) collective-permute-start(bf16[32,4736]{1,0:T(8,128)(2,1)S(1)} %get-tuple-element.74), channel_id=1, source_target_pairs={{0,16},{4,20},{8,24},{12,28},{16,0},{20,4},{24,8},{28,12},{1,17},{... | collective-permute-start | bytes 909320 | tf_op jit(solution)/shard_map/ppermute | solution.py:88
  11.1 13.1 %collective-permute-start.9 = (bf16[32,4736]{1,0:T(8,128)(2,1)S(1)}, bf16[32,4736]{1,0:T(8,128)(2,1)S(1)}, u32[]{:S(2)}, u32[]{:S(2)}) collective-permute-start(bf16[32,4736]{1,0:T(8,128)(2,1)S(1)} %get-tuple-element.72), channel_id=1, source_target_pairs={{0,8},{4,12},{8,0},{12,4},{16,24},{20,28},{24,16},{28,20},{1,9},{5... | collective-permute-start | bytes 909320 | tf_op jit(solution)/shard_map/ppermute | solution.py:88
  17.9 9.6 %collective-permute-start.4 = (bf16[16,4736]{1,0:T(8,128)(2,1)S(1)}, bf16[16,4736]{1,0:T(8,128)(2,1)S(1)}, u32[]{:S(2)}, u32[]{:S(2)}) collective-permute-start(bf16[16,4736]{1,0:T(8,128)(2,1)S(1)} %get-tuple-element.60.refs_4_), channel_id=1, source_target_pairs={{0,16},{4,20},{8,24},{12,28},{16,0},{20,4},{24,8},{28,12},{1,17},{... | collective-permute-start | bytes 454664 | tf_op jit(solution)/shard_map/ppermute | solution.py:88
  19.4 8.0 %collective-permute-start.5 = (bf16[16,4736]{1,0:T(8,128)(2,1)S(1)}, bf16[16,4736]{1,0:T(8,128)(2,1)S(1)}, u32[]{:S(2)}, u32[]{:S(2)}) collective-permute-start(bf16[16,4736]{1,0:T(8,128)(2,1)S(1)} %get-tuple-element.61), channel_id=1, source_target_pairs={{0,8},{4,12},{8,0},{12,4},{16,24},{20,28},{24,16},{28,20},{1,9},{5... | collective-permute-start | bytes 454664 | tf_op jit(solution)/shard_map/ppermute | solution.py:88
  24.4 8.8 %collective-permute-start.11 = (bf16[16,4736]{1,0:T(8,128)(2,1)S(1)}, bf16[16,4736]{1,0:T(8,128)(2,1)S(1)}, u32[]{:S(2)}, u32[]{:S(2)}) collective-permute-start(bf16[16,4736]{1,0:T(8,128)(2,1)S(1)} %get-tuple-element.76), channel_id=1, source_target_pairs={{0,16},{4,20},{8,24},{12,28},{16,0},{20,4},{24,8},{28,12},{1,17},{... | collective-permute-start | bytes 454664 | tf_op jit(solution)/shard_map/ppermute | solution.py:88
  25.9 7.2 %collective-permute-start.12 = (bf16[16,4736]{1,0:T(8,128)(2,1)S(1)}, bf16[16,4736]{1,0:T(8,128)(2,1)S(1)}, u32[]{:S(2)}, u32[]{:S(2)}) collective-permute-start(bf16[16,4736]{1,0:T(8,128)(2,1)S(1)} %get-tuple-element.77), channel_id=1, source_target_pairs={{0,8},{4,12},{8,0},{12,4},{16,24},{20,28},{24,16},{28,20},{1,9},{5... | collective-permute-start | bytes 454664 | tf_op jit(solution)/shard_map/ppermute | solution.py:88
  27.5 7.9 %collective-permute-start.6 = (bf16[32,1280]{1,0:T(8,128)(2,1)S(1)}, bf16[32,1280]{1,0:T(8,128)(2,1)S(1)}, u32[]{:S(2)}, u32[]{:S(2)}) collective-permute-start(bf16[32,1280]{1,0:T(8,128)(2,1)S(1)} %get-tuple-element.63), channel_id=1, source_target_pairs={{0,1},{1,2},{2,3},{3,0},{4,5},{5,6},{6,7},{7,4},{8,9},{9,10},{10,1... | collective-permute-start | bytes 245768 | tf_op jit(solution)/shard_map/ppermute | solution.py:93
  29.2 13.0 %collective-permute-start.7 = (bf16[32,1280]{1,0:T(8,128)(2,1)S(1)}, bf16[32,1280]{1,0:T(8,128)(2,1)S(1)}, u32[]{:S(2)}, u32[]{:S(2)}) collective-permute-start(bf16[32,1280]{1,0:T(8,128)(2,1)S(1)} %get-tuple-element.64), channel_id=1, source_target_pairs={{0,2},{1,3},{2,0},{3,1},{4,6},{5,7},{6,4},{7,5},{8,10},{9,11},{10,... | collective-permute-start | bytes 245768 | tf_op jit(solution)/shard_map/ppermute | solution.py:93
  31.8 10.4 %collective-permute-start.8 = (bf16[32,1280]{1,0:T(8,128)(2,1)S(1)}, bf16[32,1280]{1,0:T(8,128)(2,1)S(1)}, u32[]{:S(2)}, u32[]{:S(2)}) collective-permute-start(bf16[32,1280]{1,0:T(8,128)(2,1)S(1)} %get-tuple-element.65), channel_id=1, source_target_pairs={{0,3},{1,0},{2,1},{3,2},{4,7},{5,4},{6,5},{7,6},{8,11},{9,8},{10,9... | collective-permute-start | bytes 245768 | tf_op jit(solution)/shard_map/ppermute | solution.py:93
  33.2 9.1 %collective-permute-start.13 = (bf16[32,1280]{1,0:T(8,128)(2,1)S(1)}, bf16[32,1280]{1,0:T(8,128)(2,1)S(1)}, u32[]{:S(2)}, u32[]{:S(2)}) collective-permute-start(bf16[32,1280]{1,0:T(8,128)(2,1)S(1)} %get-tuple-element.79), channel_id=1, source_target_pairs={{0,1},{1,2},{2,3},{3,0},{4,5},{5,6},{6,7},{7,4},{8,9},{9,10},{10,1... | collective-permute-start | bytes 245768 | tf_op jit(solution)/shard_map/ppermute | solution.py:93
  33.9 9.0 %collective-permute-start.14 = (bf16[32,1280]{1,0:T(8,128)(2,1)S(1)}, bf16[32,1280]{1,0:T(8,128)(2,1)S(1)}, u32[]{:S(2)}, u32[]{:S(2)}) collective-permute-start(bf16[32,1280]{1,0:T(8,128)(2,1)S(1)} %get-tuple-element.80), channel_id=1, source_target_pairs={{0,2},{1,3},{2,0},{3,1},{4,6},{5,7},{6,4},{7,5},{8,10},{9,11},{10,... | collective-permute-start | bytes 245768 | tf_op jit(solution)/shard_map/ppermute | solution.py:93
  35.4 7.6 %collective-permute-start.15 = (bf16[32,1280]{1,0:T(8,128)(2,1)S(1)}, bf16[32,1280]{1,0:T(8,128)(2,1)S(1)}, u32[]{:S(2)}, u32[]{:S(2)}) collective-permute-start(bf16[32,1280]{1,0:T(8,128)(2,1)S(1)} %get-tuple-element.81), channel_id=1, source_target_pairs={{0,3},{1,0},{2,1},{3,2},{4,7},{5,4},{6,5},{7,6},{8,11},{9,8},{10,9... | collective-permute-start | bytes 245768 | tf_op jit(solution)/shard_map/ppermute | solution.py:93
  44.9 6.5 %collective-permute-start.19 = (bf16[64,512]{1,0:T(8,128)(2,1)S(1)}, bf16[64,512]{1,0:T(8,128)(2,1)S(1)}, u32[]{:S(2)}, u32[]{:S(2)}) collective-permute-start(bf16[64,512]{1,0:T(8,128)(2,1)S(1)} %get-tuple-element.89), channel_id=1, source_target_pairs={{0,1},{1,2},{2,3},{3,0},{4,5},{5,6},{6,7},{7,4},{8,9},{9,10},{10,1... | collective-permute-start | bytes 196616 | tf_op jit(solution)/shard_map/ppermute | solution.py:93
  46.4 8.7 %collective-permute-start.20 = (bf16[64,512]{1,0:T(8,128)(2,1)S(1)}, bf16[64,512]{1,0:T(8,128)(2,1)S(1)}, u32[]{:S(2)}, u32[]{:S(2)}) collective-permute-start(bf16[64,512]{1,0:T(8,128)(2,1)S(1)} %get-tuple-element.90), channel_id=1, source_target_pairs={{0,2},{1,3},{2,0},{3,1},{4,6},{5,7},{6,4},{7,5},{8,10},{9,11},{10,... | collective-permute-start | bytes 196616 | tf_op jit(solution)/shard_map/ppermute | solution.py:93
  48.5 6.6 %collective-permute-start.21 = (bf16[64,512]{1,0:T(8,128)(2,1)S(1)}, bf16[64,512]{1,0:T(8,128)(2,1)S(1)}, u32[]{:S(2)}, u32[]{:S(2)}) collective-permute-start(bf16[64,512]{1,0:T(8,128)(2,1)S(1)} %get-tuple-element.91), channel_id=1, source_target_pairs={{0,3},{1,0},{2,1},{3,2},{4,7},{5,4},{6,5},{7,6},{8,11},{9,8},{10,9... | collective-permute-start | bytes 196616 | tf_op jit(solution)/shard_map/ppermute | solution.py:93
  49.2 8.4 %collective-permute-start.16 = (bf16[64,640]{1,0:T(8,128)(2,1)S(1)}, bf16[64,640]{1,0:T(8,128)(2,1)S(1)}, u32[]{:S(2)}, u32[]{:S(2)}) collective-permute-start(bf16[64,640]{1,0:T(8,128)(2,1)S(1)} %get-tuple-element.84), channel_id=1, source_target_pairs={{0,1},{1,2},{2,3},{3,0},{4,5},{5,6},{6,7},{7,4},{8,9},{9,10},{10,1... | collective-permute-start | bytes 245768 | tf_op jit(solution)/shard_map/ppermute | solution.py:93
  50.5 8.7 %collective-permute-start.17 = (bf16[64,640]{1,0:T(8,128)(2,1)S(1)}, bf16[64,640]{1,0:T(8,128)(2,1)S(1)}, u32[]{:S(2)}, u32[]{:S(2)}) collective-permute-start(bf16[64,640]{1,0:T(8,128)(2,1)S(1)} %get-tuple-element.85), channel_id=1, source_target_pairs={{0,2},{1,3},{2,0},{3,1},{4,6},{5,7},{6,4},{7,5},{8,10},{9,11},{10,... | collective-permute-start | bytes 245768 | tf_op jit(solution)/shard_map/ppermute | solution.py:93
  51.3 7.9 %collective-permute-start.18 = (bf16[64,640]{1,0:T(8,128)(2,1)S(1)}, bf16[64,640]{1,0:T(8,128)(2,1)S(1)}, u32[]{:S(2)}, u32[]{:S(2)}) collective-permute-start(bf16[64,640]{1,0:T(8,128)(2,1)S(1)} %get-tuple-element.86), channel_id=1, source_target_pairs={{0,3},{1,0},{2,1},{3,2},{4,7},{5,4},{6,5},{7,6},{8,11},{9,8},{10,9... | collective-permute-start | bytes 245768 | tf_op jit(solution)/shard_map/ppermute | solution.py:93
  55.2 6.4 %collective-permute-start.29 = (bf16[64,512]{1,0:T(8,128)(2,1)S(1)}, bf16[64,512]{1,0:T(8,128)(2,1)S(1)}, u32[]{:S(2)}, u32[]{:S(2)}) collective-permute-start(bf16[64,512]{1,0:T(8,128)(2,1)S(1)} %shard_map.66.refs_6_.refs_0_), channel_id=1, source_target_pairs={{0,8},{4,12},{8,0},{12,4},{16,24},{20,28},{24,16},{28,20},{1,9},{5... | collective-permute-start | bytes 196616 | tf_op jit(solution)/shard_map/ppermute | solution.py:88
  56.2 6.7 %collective-permute-start.30 = (bf16[64,512]{1,0:T(8,128)(2,1)S(1)}, bf16[64,512]{1,0:T(8,128)(2,1)S(1)}, u32[]{:S(2)}, u32[]{:S(2)}) collective-permute-start(bf16[64,512]{1,0:T(8,128)(2,1)S(1)} %shard_map.66.refs_6_.refs_0_), channel_id=1, source_target_pairs={{0,16},{4,20},{8,24},{12,28},{16,0},{20,4},{24,8},{28,12},{1,17},{... | collective-permute-start | bytes 196616 | tf_op jit(solution)/shard_map/ppermute | solution.py:88
  57.6 5.9 %collective-permute-start.31 = (bf16[64,512]{1,0:T(8,128)(2,1)S(1)}, bf16[64,512]{1,0:T(8,128)(2,1)S(1)}, u32[]{:S(2)}, u32[]{:S(2)}) collective-permute-start(bf16[64,512]{1,0:T(8,128)(2,1)S(1)} %shard_map.66.refs_6_.refs_0_), channel_id=1, source_target_pairs={{0,24},{4,28},{8,16},{12,20},{16,8},{20,12},{24,0},{28,4},{1,25},{... | collective-permute-start | bytes 196616 | tf_op jit(solution)/shard_map/ppermute | solution.py:88
  59.4 4.5 %collective-permute-start.22 = (bf16[64,640]{1,0:T(8,128)(2,1)S(1)}, bf16[64,640]{1,0:T(8,128)(2,1)S(1)}, u32[]{:S(2)}, u32[]{:S(2)}) collective-permute-start(bf16[64,640]{1,0:T(8,128)(2,1)S(1)} %shard_map.67.refs_0_), channel_id=1, source_target_pairs={{0,8},{4,12},{8,0},{12,4},{16,24},{20,28},{24,16},{28,20},{1,9},{5... | collective-permute-start | bytes 245768 | tf_op jit(solution)/shard_map/ppermute | solution.py:88
  61.6 5.3 %collective-permute-start.24 = (bf16[64,640]{1,0:T(8,128)(2,1)S(1)}, bf16[64,640]{1,0:T(8,128)(2,1)S(1)}, u32[]{:S(2)}, u32[]{:S(2)}) collective-permute-start(bf16[64,640]{1,0:T(8,128)(2,1)S(1)} %shard_map.67.refs_0_), channel_id=1, source_target_pairs={{0,24},{4,28},{8,16},{12,20},{16,8},{20,12},{24,0},{28,4},{1,25},{... | collective-permute-start | bytes 245768 | tf_op jit(solution)/shard_map/ppermute | solution.py:88
  67.3 6.1 %collective-permute-start.25 = (f32[64,640]{1,0:T(8,128)S(1)}, f32[64,640]{1,0:T(8,128)S(1)}, u32[]{:S(2)}, u32[]{:S(2)}) collective-permute-start(f32[64,640]{1,0:T(8,128)S(1)} %get-tuple-element.94), channel_id=1, source_target_pairs={{0,4},{4,0},{8,12},{12,8},{16,20},{20,16},{24,28},{28,24},{1,5},{5... | collective-permute-start | bytes 491528 | tf_op jit(solution)/shard_map/ppermute | solution.py:88
  67.4 9.1 %collective-permute-start.33 = (bf16[64,512]{1,0:T(8,128)(2,1)S(1)}, bf16[64,512]{1,0:T(8,128)(2,1)S(1)}, u32[]{:S(2)}, u32[]{:S(2)}) collective-permute-start(bf16[64,512]{1,0:T(8,128)(2,1)S(1)} %shard_map.71.refs_0_), channel_id=1, source_target_pairs={{0,1},{1,2},{2,3},{3,0},{4,5},{5,6},{6,7},{7,4},{8,9},{9,10},{10,1... | collective-permute-start | bytes 196616 | tf_op jit(solution)/shard_map/ppermute | solution.py:93
  70.4 7.5 %collective-permute-start.34 = (bf16[64,512]{1,0:T(8,128)(2,1)S(1)}, bf16[64,512]{1,0:T(8,128)(2,1)S(1)}, u32[]{:S(2)}, u32[]{:S(2)}) collective-permute-start(bf16[64,512]{1,0:T(8,128)(2,1)S(1)} %shard_map.71.refs_0_), channel_id=1, source_target_pairs={{0,2},{1,3},{2,0},{3,1},{4,6},{5,7},{6,4},{7,5},{8,10},{9,11},{10,... | collective-permute-start | bytes 196616 | tf_op jit(solution)/shard_map/ppermute | solution.py:93
  70.7 7.2 %collective-permute-start.35 = (bf16[64,512]{1,0:T(8,128)(2,1)S(1)}, bf16[64,512]{1,0:T(8,128)(2,1)S(1)}, u32[]{:S(2)}, u32[]{:S(2)}) collective-permute-start(bf16[64,512]{1,0:T(8,128)(2,1)S(1)} %shard_map.71.refs_0_), channel_id=1, source_target_pairs={{0,3},{1,0},{2,1},{3,2},{4,7},{5,4},{6,5},{7,6},{8,11},{9,8},{10,9... | collective-permute-start | bytes 196616 | tf_op jit(solution)/shard_map/ppermute | solution.py:93
  73.4 7.2 %collective-permute-start.28 = (bf16[64,640]{1,0:T(8,128)(2,1)S(1)}, bf16[64,640]{1,0:T(8,128)(2,1)S(1)}, u32[]{:S(2)}, u32[]{:S(2)}) collective-permute-start(bf16[64,640]{1,0:T(8,128)(2,1)S(1)} %shard_map.69.refs_0_), channel_id=1, source_target_pairs={{0,1},{1,2},{2,3},{3,0},{4,5},{5,6},{6,7},{7,4},{8,9},{9,10},{10,1... | collective-permute-start | bytes 245768 | tf_op jit(solution)/shard_map/ppermute | solution.py:93
  73.4 10.0 %collective-permute-start.27 = (bf16[64,640]{1,0:T(8,128)(2,1)S(1)}, bf16[64,640]{1,0:T(8,128)(2,1)S(1)}, u32[]{:S(2)}, u32[]{:S(2)}) collective-permute-start(bf16[64,640]{1,0:T(8,128)(2,1)S(1)} %shard_map.69.refs_0_), channel_id=1, source_target_pairs={{0,2},{1,3},{2,0},{3,1},{4,6},{5,7},{6,4},{7,5},{8,10},{9,11},{10,... | collective-permute-start | bytes 245768 | tf_op jit(solution)/shard_map/ppermute | solution.py:93
  76.5 7.5 %collective-permute-start.26 = (bf16[64,640]{1,0:T(8,128)(2,1)S(1)}, bf16[64,640]{1,0:T(8,128)(2,1)S(1)}, u32[]{:S(2)}, u32[]{:S(2)}) collective-permute-start(bf16[64,640]{1,0:T(8,128)(2,1)S(1)} %shard_map.69.refs_0_), channel_id=1, source_target_pairs={{0,3},{1,0},{2,1},{3,2},{4,7},{5,4},{6,5},{7,6},{8,11},{9,8},{10,9... | collective-permute-start | bytes 245768 | tf_op jit(solution)/shard_map/ppermute | solution.py:93
  (6 other events, 53.2 us)
